TPU v7x, 32 devices: a whole 2x2x4 slice. The times are simulated.
32 devices in a mesh: dp: 8 (over z, x), mp: 4 (over y, core).
Axes of the slice: x: 2, y: 2, z: 4, core: 2. Of those that a mesh axis runs over, the one named last changes fastest.
Arguments:
- hidden: bfloat16 [16, 448, 768], P('dp'), may hold values from -6 to 6
- encoder: bfloat16 [16, 1500, 768], P('dp'), may hold values from -6 to 6
- lengths: int32 [16], P('dp'), may hold values from 1 to 448, as said below
- tasks: int32 [16], P('dp'), may hold values from 0 to 2, as said below
- frames: int32 [16], P('dp'), may hold values from 750 to 1500, as said below
- out_grad: bfloat16 [16, 448, 768], P('dp'), may hold values from -6 to 6
- gain_self: bfloat16 [768], replicated, may hold values from 0.099609375 to 1.8984375
- shift_self: bfloat16 [768], replicated, may hold values from -1.75 to 1.75
- query_self: bfloat16 [768, 768], P(None, 'mp'), may hold values from -0.21875 to 0.21875
- qbias_self: bfloat16 [768], P('mp'), may hold values from -3 to 3
- key_self: bfloat16 [768, 768], P(None, 'mp'), may hold values from -0.21875 to 0.21875
- value_self: bfloat16 [768, 768], P(None, 'mp'), may hold values from -0.21875 to 0.21875
- vbias_self: bfloat16 [768], P('mp'), may hold values from -1.75 to 1.75
- output_self: bfloat16 [768, 768], P('mp'), may hold values from -0.875 to 0.875
- obias_self: bfloat16 [768], replicated, may hold values from -1.75 to 1.75
- gain_cross: bfloat16 [768], replicated, may hold values from 0.099609375 to 1.8984375
- shift_cross: bfloat16 [768], replicated, may hold values from -1.75 to 1.75
- query_cross: bfloat16 [768, 768], P(None, 'mp'), may hold values from -0.21875 to 0.21875
- qbias_cross: bfloat16 [768], P('mp'), may hold values from -3 to 3
- key_cross: bfloat16 [768, 768], P(None, 'mp'), may hold values from -0.21875 to 0.21875
- value_cross: bfloat16 [768, 768], P(None, 'mp'), may hold values from -0.21875 to 0.21875
- vbias_cross: bfloat16 [768], P('mp'), may hold values from -1.75 to 1.75
- output_cross: bfloat16 [768, 768], P('mp'), may hold values from -0.875 to 0.875
- obias_cross: bfloat16 [768], replicated, may hold values from -1.75 to 1.75
- gain_feed: bfloat16 [768], replicated, may hold values from 0.099609375 to 1.8984375
- shift_feed: bfloat16 [768], replicated, may hold values from -1.75 to 1.75
- expand_weight: bfloat16 [768, 3072], P(None, 'mp'), may hold values from -0.21875 to 0.21875
- expand_bias: bfloat16 [3072], P('mp'), may hold values from -1.75 to 1.75
- contract_weight: bfloat16 [3072, 768], P('mp'), may hold values from -0.15625 to 0.15625
- contract_bias: bfloat16 [768], replicated, may hold values from -1.75 to 1.75
Outputs:
- block_out: bfloat16 [16, 448, 768], P('dp')
- hidden_grad: float32 [16, 448, 768], P('dp')
- encoder_grad: float32 [16, 1500, 768], P('dp', None, 'mp')
- gain_self_grad: float32 [768], replicated
- shift_self_grad: float32 [768], replicated
- query_self_grad: float32 [768, 768], P(None, 'mp')
- qbias_self_grad: float32 [768], P('mp')
- key_self_grad: float32 [768, 768], P(None, 'mp')
- value_self_grad: float32 [768, 768], P(None, 'mp')
- vbias_self_grad: float32 [768], P('mp')
- output_self_grad: float32 [768, 768], P('mp')
- obias_self_grad: float32 [768], replicated
- gain_cross_grad: float32 [768], replicated
- shift_cross_grad: float32 [768], replicated
- query_cross_grad: float32 [768, 768], P(None, 'mp')
- qbias_cross_grad: float32 [768], P('mp')
- key_cross_grad: float32 [768, 768], P(None, 'mp')
- value_cross_grad: float32 [768, 768], P(None, 'mp')
- vbias_cross_grad: float32 [768], P('mp')
- output_cross_grad: float32 [768, 768], P('mp')
- obias_cross_grad: float32 [768], replicated
- gain_feed_grad: float32 [768], replicated
- shift_feed_grad: float32 [768], replicated
- expand_weight_grad: float32 [768, 3072], P(None, 'mp')
- expand_bias_grad: float32 [3072], P('mp')
- contract_weight_grad: float32 [3072, 768], P('mp')
- contract_bias_grad: float32 [768], replicated
Inputs may be any that keep to these rules, and one draw needn't show every extreme that they name: `tasks`: 0 transcription, 1 translation, 2 language identification. `lengths`: an item of task 2 has at most min(8, 112) tokens, any other item 448 // 2 or more; some item has 448. `frames`: some item has 1500.
All inputs are finite; a program needn't handle non-finite values.
Results may differ from a plain program's by a relative error of at most 0.035.
Values may be sent and summed in bfloat16 or wider, within the bound.
No kernel may reach another device: no remote copies, remote signals or barrier semaphores. Data moves between devices by JAX's collectives and lax.ppermute only.
A program may use at most 192 MiB of HBM per device.

v0:
```python
import jax
import jax.numpy as jnp
from jax import lax
from jax.sharding import PartitionSpec as P

HEAD = 64


epsilon = 1e-05


def layer_norm(values, norm_gain, norm_shift):
    centred = values - jnp.mean(values, axis=-1, keepdims=True)
    spread = jnp.mean(centred * centred, axis=-1, keepdims=True)
    return centred * lax.rsqrt(spread + epsilon) * norm_gain + norm_shift


def norm_back(values, norm_gain, norm_shift, upstream):
    _, pullback = jax.vjp(layer_norm, values, norm_gain, norm_shift)
    return pullback(upstream)


def exact_gelu(values):
    return jax.nn.gelu(values, approximate=False)


def project(operand, weight):
    return jnp.dot(operand, weight, preferred_element_type=jnp.float32)


def project_back(operand, weight):
    return lax.dot_general(
        operand, weight, (((1,), (1,)), ((), ())), preferred_element_type=jnp.float32
    )


def outer_sum(operand, other):
    return lax.dot_general(
        operand, other, (((0,), (0,)), ((), ())), preferred_element_type=jnp.float32
    )


def split_heads(flat, item_count):
    return flat.reshape(item_count, -1, flat.shape[-1] // HEAD, HEAD)


def join_heads(split):
    return split.reshape(-1, split.shape[2] * split.shape[3])


def masked_scores(queries, key_rows, allowed):
    factor = HEAD ** (-0.5)
    scores = (
        jnp.einsum("bqhe,bkhe->bhqk", queries, key_rows, preferred_element_type=jnp.float32)
        * factor
    )
    return jnp.where(allowed[:, None], scores, -1e30)


def attend(queries, key_rows, value_rows, allowed):
    scores = masked_scores(queries, key_rows, allowed)
    largest = jnp.max(scores, axis=-1, keepdims=True)
    powers = jnp.exp(scores - largest)
    totals = jnp.sum(powers, axis=-1, keepdims=True)
    shares = (powers / totals).astype(jnp.bfloat16)
    mixture = jnp.einsum("bhqk,bkhe->bqhe", shares, value_rows, preferred_element_type=jnp.float32)
    return (mixture.astype(jnp.bfloat16), largest + jnp.log(totals))


def attend_back(queries, key_rows, value_rows, allowed, log_totals, upstream):
    factor = HEAD ** (-0.5)
    scores = masked_scores(queries, key_rows, allowed)
    shares = jnp.exp(scores - log_totals)
    pushed = jnp.einsum("bqhe,bkhe->bhqk", upstream, value_rows, preferred_element_type=jnp.float32)
    centre = jnp.sum(shares * pushed, axis=-1, keepdims=True)
    score_grad = (shares * (pushed - centre)).astype(jnp.bfloat16)
    query_grad = (
        jnp.einsum("bhqk,bkhe->bqhe", score_grad, key_rows, preferred_element_type=jnp.float32)
        * factor
    ).astype(jnp.bfloat16)
    key_grad = (
        jnp.einsum("bhqk,bqhe->bkhe", score_grad, queries, preferred_element_type=jnp.float32)
        * factor
    ).astype(jnp.bfloat16)
    value_grad = jnp.einsum(
        "bhqk,bqhe->bkhe", shares.astype(jnp.bfloat16), upstream, preferred_element_type=jnp.float32
    ).astype(jnp.bfloat16)
    return (query_grad, key_grad, value_grad)


def col_sum(values):
    return jnp.sum(values.astype(jnp.float32), axis=0)


def shards(
    hidden,
    encoder,
    lengths,
    tasks,
    frames,
    out_grad,
    gain_self,
    shift_self,
    query_self,
    qbias_self,
    key_self,
    value_self,
    vbias_self,
    output_self,
    obias_self,
    gain_cross,
    shift_cross,
    query_cross,
    qbias_cross,
    key_cross,
    value_cross,
    vbias_cross,
    output_cross,
    obias_cross,
    gain_feed,
    shift_feed,
    expand_weight,
    expand_bias,
    contract_weight,
    contract_bias,
):
    item_count, length, width = hidden.shape
    memory_len = encoder.shape[1]
    row_count = item_count * length
    inputs = hidden.astype(jnp.float32).reshape(row_count, width)
    memory = encoder.reshape(item_count * memory_len, width)
    places = jnp.arange(length)
    causal = (places[None, None, :] <= places[None, :, None]) & (
        places[None, None, :] < lengths[:, None, None]
    )
    heard = jnp.arange(memory_len)[None, None, :] < frames[:, None, None]
    g_self = gain_self.astype(jnp.float32)
    s_self = shift_self.astype(jnp.float32)
    g_cross = gain_cross.astype(jnp.float32)
    s_cross = shift_cross.astype(jnp.float32)
    g_feed = gain_feed.astype(jnp.float32)
    s_feed = shift_feed.astype(jnp.float32)
    normed_self = layer_norm(inputs, g_self, s_self).astype(jnp.bfloat16)
    q_self = (project(normed_self, query_self) + qbias_self.astype(jnp.float32)).astype(
        jnp.bfloat16
    )
    k_self = project(normed_self, key_self).astype(jnp.bfloat16)
    v_self = (project(normed_self, value_self) + vbias_self.astype(jnp.float32)).astype(
        jnp.bfloat16
    )
    q_self_h = split_heads(q_self, item_count)
    k_self_h = split_heads(k_self, item_count)
    v_self_h = split_heads(v_self, item_count)
    mix_self, lse_self = attend(q_self_h, k_self_h, v_self_h, causal)
    o_self = join_heads(mix_self)
    after_self = (
        inputs
        + lax.psum(project(o_self, output_self).astype(jnp.bfloat16), "mp").astype(jnp.float32)
        + obias_self.astype(jnp.float32)
    )
    normed_cross = layer_norm(after_self, g_cross, s_cross).astype(jnp.bfloat16)
    q_cross = (project(normed_cross, query_cross) + qbias_cross.astype(jnp.float32)).astype(
        jnp.bfloat16
    )
    k_cross = project(memory, key_cross).astype(jnp.bfloat16)
    v_cross = (project(memory, value_cross) + vbias_cross.astype(jnp.float32)).astype(jnp.bfloat16)
    q_cross_h = split_heads(q_cross, item_count)
    k_cross_h = split_heads(k_cross, item_count)
    v_cross_h = split_heads(v_cross, item_count)
    mix_cross, lse_cross = attend(q_cross_h, k_cross_h, v_cross_h, heard)
    o_cross = join_heads(mix_cross)
    after_cross = (
        after_self
        + lax.psum(project(o_cross, output_cross).astype(jnp.bfloat16), "mp").astype(jnp.float32)
        + obias_cross.astype(jnp.float32)
    )
    normed_feed = layer_norm(after_cross, g_feed, s_feed).astype(jnp.bfloat16)
    before_act = project(normed_feed, expand_weight) + expand_bias.astype(jnp.float32)
    activated = exact_gelu(before_act).astype(jnp.bfloat16)
    result = (
        after_cross
        + lax.psum(project(activated, contract_weight).astype(jnp.bfloat16), "mp").astype(
            jnp.float32
        )
        + contract_bias.astype(jnp.float32)
    )
    block_out = result.astype(jnp.bfloat16).reshape(item_count, length, width)
    task_weight = jnp.where(tasks == 0, 1.0, jnp.where(tasks == 1, 0.6, 2.0)).astype(jnp.float32)
    valid = places[None, :] < lengths[:, None]
    upstream = (
        out_grad.astype(jnp.float32) * jnp.where(valid, task_weight[:, None], 0.0)[:, :, None]
    )
    grad_out = upstream.reshape(row_count, width)
    grad_low = grad_out.astype(jnp.bfloat16)
    contract_bias_grad = jnp.sum(grad_out, axis=0)
    contract_weight_grad = outer_sum(activated, grad_low)
    act_grad = project_back(grad_low, contract_weight)
    _, gelu_pull = jax.vjp(exact_gelu, before_act)
    pre_grad = gelu_pull(act_grad)[0].astype(jnp.bfloat16)
    expand_bias_grad = col_sum(pre_grad)
    expand_weight_grad = outer_sum(normed_feed, pre_grad)
    feed_in = lax.psum(project_back(pre_grad, expand_weight).astype(jnp.bfloat16), "mp").astype(
        jnp.float32
    )
    norm_grad, gain_feed_grad, shift_feed_grad = norm_back(after_cross, g_feed, s_feed, feed_in)
    grad_two = grad_out + norm_grad
    cross_low = grad_two.astype(jnp.bfloat16)
    obias_cross_grad = jnp.sum(grad_two, axis=0)
    output_cross_grad = outer_sum(o_cross, cross_low)
    mix_cross_grad = split_heads(
        project_back(cross_low, output_cross).astype(jnp.bfloat16), item_count
    )
    dq_cross, dk_cross, dv_cross = attend_back(
        q_cross_h, k_cross_h, v_cross_h, heard, lse_cross, mix_cross_grad
    )
    dq_cross = join_heads(dq_cross)
    dk_cross = join_heads(dk_cross)
    dv_cross = join_heads(dv_cross)
    qbias_cross_grad = col_sum(dq_cross)
    query_cross_grad = outer_sum(normed_cross, dq_cross)
    key_cross_grad = outer_sum(memory, dk_cross)
    value_cross_grad = outer_sum(memory, dv_cross)
    vbias_cross_grad = col_sum(dv_cross)
    cross_in = lax.psum(project_back(dq_cross, query_cross).astype(jnp.bfloat16), "mp").astype(
        jnp.float32
    )
    memory_part = project_back(dk_cross, key_cross) + project_back(dv_cross, value_cross)
    memory_grad = lax.psum_scatter(
        memory_part.astype(jnp.bfloat16), "mp", scatter_dimension=1, tiled=True
    ).astype(jnp.float32)
    encoder_grad = memory_grad.reshape(item_count, memory_len, memory_grad.shape[-1])
    norm_grad, gain_cross_grad, shift_cross_grad = norm_back(after_self, g_cross, s_cross, cross_in)
    grad_one = grad_two + norm_grad
    self_low = grad_one.astype(jnp.bfloat16)
    obias_self_grad = jnp.sum(grad_one, axis=0)
    output_self_grad = outer_sum(o_self, self_low)
    mix_self_grad = split_heads(
        project_back(self_low, output_self).astype(jnp.bfloat16), item_count
    )
    dq_self, dk_self, dv_self = attend_back(
        q_self_h, k_self_h, v_self_h, causal, lse_self, mix_self_grad
    )
    dq_self = join_heads(dq_self)
    dk_self = join_heads(dk_self)
    dv_self = join_heads(dv_self)
    qbias_self_grad = col_sum(dq_self)
    query_self_grad = outer_sum(normed_self, dq_self)
    key_self_grad = outer_sum(normed_self, dk_self)
    value_self_grad = outer_sum(normed_self, dv_self)
    vbias_self_grad = col_sum(dv_self)
    self_part = (
        project_back(dq_self, query_self)
        + project_back(dk_self, key_self)
        + project_back(dv_self, value_self)
    )
    self_in = lax.psum(self_part.astype(jnp.bfloat16), "mp").astype(jnp.float32)
    norm_grad, gain_self_grad, shift_self_grad = norm_back(inputs, g_self, s_self, self_in)
    hidden_grad = (grad_one + norm_grad).reshape(item_count, length, width)
    (
        gain_self_grad,
        shift_self_grad,
        query_self_grad,
        qbias_self_grad,
        key_self_grad,
        value_self_grad,
        vbias_self_grad,
        output_self_grad,
        obias_self_grad,
        gain_cross_grad,
        shift_cross_grad,
        query_cross_grad,
        qbias_cross_grad,
        key_cross_grad,
        value_cross_grad,
        vbias_cross_grad,
        output_cross_grad,
        obias_cross_grad,
        gain_feed_grad,
        shift_feed_grad,
        expand_weight_grad,
        expand_bias_grad,
        contract_weight_grad,
        contract_bias_grad,
    ) = lax.psum(
        (
            gain_self_grad,
            shift_self_grad,
            query_self_grad,
            qbias_self_grad,
            key_self_grad,
            value_self_grad,
            vbias_self_grad,
            output_self_grad,
            obias_self_grad,
            gain_cross_grad,
            shift_cross_grad,
            query_cross_grad,
            qbias_cross_grad,
            key_cross_grad,
            value_cross_grad,
            vbias_cross_grad,
            output_cross_grad,
            obias_cross_grad,
            gain_feed_grad,
            shift_feed_grad,
            expand_weight_grad,
            expand_bias_grad,
            contract_weight_grad,
            contract_bias_grad,
        ),
        "dp",
    )
    return (
        block_out,
        hidden_grad,
        encoder_grad,
        gain_self_grad,
        shift_self_grad,
        query_self_grad,
        qbias_self_grad,
        key_self_grad,
        value_self_grad,
        vbias_self_grad,
        output_self_grad,
        obias_self_grad,
        gain_cross_grad,
        shift_cross_grad,
        query_cross_grad,
        qbias_cross_grad,
        key_cross_grad,
        value_cross_grad,
        vbias_cross_grad,
        output_cross_grad,
        obias_cross_grad,
        gain_feed_grad,
        shift_feed_grad,
        expand_weight_grad,
        expand_bias_grad,
        contract_weight_grad,
        contract_bias_grad,
    )


def solution(mesh):
    placed = (
        P("dp", None, None),
        P("dp", None, None),
        P("dp"),
        P("dp"),
        P("dp"),
        P("dp", None, None),
        P(),
        P(),
        P(None, "mp"),
        P("mp"),
        P(None, "mp"),
        P(None, "mp"),
        P("mp"),
        P("mp", None),
        P(),
        P(),
        P(),
        P(None, "mp"),
        P("mp"),
        P(None, "mp"),
        P(None, "mp"),
        P("mp"),
        P("mp", None),
        P(),
        P(),
        P(),
        P(None, "mp"),
        P("mp"),
        P("mp", None),
        P(),
    )
    return jax.shard_map(
        shards,
        mesh=mesh,
        in_specs=placed,
        out_specs=(
            P("dp", None, None),
            P("dp", None, None),
            P("dp", None, "mp"),
            P(),
            P(),
            P(None, "mp"),
            P("mp"),
            P(None, "mp"),
            P(None, "mp"),
            P("mp"),
            P("mp", None),
            P(),
            P(),
            P(),
            P(None, "mp"),
            P("mp"),
            P(None, "mp"),
            P(None, "mp"),
            P("mp"),
            P("mp", None),
            P(),
            P(),
            P(),
            P(None, "mp"),
            P("mp"),
            P("mp", None),
            P(),
        ),
        check_vma=False,
    )
```

profile of v0, /device:TPU:0, one launch (start us, length us, event | category | flops | bytes accessed | tf_op | source)
XLA Modules:
  0.0 775.0 jit_solution(17953733283435265358)
XLA Ops:
  19.7 2.7 fusion.62
  25.2 2.3 fusion.109
  31.7 2.7 convolution_convert_fusion.5
  34.9 5.0 copy.83
  39.9 5.3 reshape.426
  45.3 5.0 convolution_convert_fusion
  50.3 4.4 reshape.429
  54.9 5.0 fusion.8
  59.9 4.9 reshape.427
  65.0 3.8 fusion.84
  68.9 8.3 %all-reduce.10.cloned.1.call-done = bf16[896,768]{1,0:T(8,128)(2,1)} async-done(((bf16[896,768]{1,0:T(8,128)(2,1)}), bf16[896,768]{1,0:T(8,128)(2,1)}) %all-reduce.10.cloned.1.call-update) | async-done | bytes 1376272 | tf_op jit(solution)/shard_map/psum | solution.py:158
  82.8 9.4 %fusion.110 = (f32[2,3,448]{2,1,0:T(4,128)S(1)}, f32[2,3,448,1500]{3,2,1,0:T(8,128)}) fusion(bf16[2,1500,3,64]{1,0,3,2:T(2,128)(2,1)} %reshape.429, bf16[2,448,3,64]{1,0,3,2:T(2,128)(2,1)S(1)} %reshape.428, pred[2,1500]{1,0:T(4,128)(4,1)S(1)} %iota_compare_fusion.1), kind=kOutput, calls=%fused_computation.196 | convolution fusion | flops 528189312 | bytes 17637816 | tf_op jit(solution)/shard_map/bqhe,bkhe->bhqk/dot_general | solution.py:54
  92.3 8.2 %fusion = f32[2,3,448]{2,1,0:T(4,128)S(1)} fusion(f32[2,3,448,1500]{3,2,1,0:T(8,128)} %get-tuple-element.135, f32[2,3,448]{2,1,0:T(4,128)S(1)} %get-tuple-element.134), kind=kLoop, calls=%fused_computation.6 | loop fusion | flops 8061312 | bytes 16149504 | tf_op jit(solution)/shard_map/reduce_sum | solution.py:64
  100.5 7.3 fusion.72
  110.2 2.7 convolution_convert_fusion.4
  113.3 3.0 bitcast_convert_fusion
  116.3 36.8 %all-reduce.12.cloned.1.call-done = bf16[896,768]{1,0:T(8,128)(2,1)} async-done(((bf16[896,768]{1,0:T(8,128)(2,1)}), bf16[896,768]{1,0:T(8,128)(2,1)}) %all-reduce.12.cloned.1.call-update) | async-done | bytes 1376272 | tf_op jit(solution)/shard_map/psum | solution.py:174
  153.1 2.5 fusion.108
  159.2 8.5 %convert_reduce_fusion.4 = (f32[768]{0:T(1024)S(1)}, bf16[896,768]{1,0:T(8,128)(2,1)S(1)}, f32[896,768]{1,0:T(8,128)}) fusion(f32[896,768]{1,0:T(8,128)S(1)} %fusion.104, f32[768]{0:T(1024)S(1)} %convert_element_type.263, bf16[896,768]{1,0:T(8,128)(2,1)S(1)} %copy-done.47, bf16[768,768]{1,0:T(8,128)(2,1)S(1)} %copy-done), kind=kOutput, calls=%fused_computation.71 | convolution fusion | flops 1108573440 | bytes 9443328 | tf_op jit(solution)/shard_map/dot_general | solution.py:32
  168.8 2.3 convolution_convert_fusion.2
  171.2 3.0 multiply_convert_fusion.2
  175.3 2.3 convolution_convert_fusion.3
  177.6 33.6 %all-reduce.14.cloned.1.call-done = bf16[896,768]{1,0:T(8,128)(2,1)} async-done(((bf16[896,768]{1,0:T(8,128)(2,1)}), bf16[896,768]{1,0:T(8,128)(2,1)}) %all-reduce.14.cloned.1.call-update) | async-done | bytes 1376272 | tf_op jit(solution)/shard_map/psum | solution.py:202
  211.3 3.2 convert_reduce_fusion.2
  221.7 10.8 %multiply_reduce_fusion = (f32[2,3,448]{2,1,0:T(4,128)S(1)}, f32[2,3,448,1500]{3,2,1,0:T(8,128)}) fusion(f32[2,3,448,1500]{3,2,1,0:T(8,128)} %get-tuple-element.135, f32[2,3,448]{2,1,0:T(4,128)S(1)} %log_add_fusion.1, bf16[2,1500,3,64]{1,0,3,2:T(2,128)(2,1)S(1)} %copy-done.26, bf16[2,448,3,64]{1,0,3,2:T(2,128)(2,1)S(1)} %reshape.433), kind=kOutput, calls=%fused_computation.1 | convolution fusion | flops 528189312 | bytes 33773568 | tf_op jit(solution)/shard_map/bqhe,bkhe->bhqk/dot_general | solution.py:74
  232.5 11.7 %multiply_convert_fusion = bf16[2,3,448,1500]{3,2,1,0:T(8,128)(2,1)S(1)} fusion(f32[2,3,448,1500]{3,2,1,0:T(8,128)} %get-tuple-element.137, f32[2,3,448,1500]{3,2,1,0:T(8,128)} %get-tuple-element.135, f32[2,3,448]{2,1,0:T(4,128)S(1)} %get-tuple-element.136, f32[2,3,448]{2,1,0:T(4,128)S(1)} %log_add_fusion.1), kind=kLoop, calls=%fused_computation | loop fusion | flops 16128000 | bytes 40341504 | tf_op jit(solution)/shard_map/convert_element_type | solution.py:76
  244.2 2.5 convert_reduce_fusion.6
  248.1 2.7 convolution_convert_fusion.1
  251.4 9.7 %convert_reduce_fusion.5 = (f32[3,64]{1,0:T(4,128)S(1)}, bf16[2,1500,3,64]{1,3,2,0:T(8,128)(2,1)}) fusion(f32[2,3,448,1500]{3,2,1,0:T(8,128)} %get-tuple-element.135, f32[2,3,448]{2,1,0:T(4,128)S(1)} %log_add_fusion.1, bf16[2,448,3,64]{1,0,3,2:T(2,128)(2,1)S(1)} %reshape.433), kind=kOutput, calls=%fused_computation.101 | convolution fusion | flops 525887808 | bytes 17635584 | tf_op jit(solution)/shard_map/bhqk,bqhe->bkhe/dot_general | solution.py:85
  261.1 29.9 %all-reduce.16.cloned.1.call-done = bf16[896,768]{1,0:T(8,128)(2,1)} async-done(((bf16[896,768]{1,0:T(8,128)(2,1)}), bf16[896,768]{1,0:T(8,128)(2,1)}) %all-reduce.16.cloned.1.call-update) | async-done | bytes 1376272 | tf_op jit(solution)/shard_map/psum | solution.py:224
  291.0 3.1 convert_reduce_fusion.1
  300.3 4.1 multiply_reduce_fusion.1
  304.4 4.3 multiply_convert_fusion.1
  318.8 3.2 fusion.112
  324.4 4.4 add_convert_fusion.1
  329.0 4.9 fusion.50
  336.2 3.7 reshape.440
  339.8 3.5 copy.106
  343.4 4.3 reshape.441
  349.2 3.7 add_convert_fusion
  354.9 2.8 fusion.114
  357.8 3.2 fusion.103
  373.8 17.5 %all-reduce.20.cloned.1.call-done = (bf16[896,768]{1,0:T(8,128)(2,1)}, bf16[896,768]{1,0:T(8,128)(2,1)}) async-done(((bf16[896,768]{1,0:T(8,128)(2,1)}, bf16[896,768]{1,0:T(8,128)(2,1)}), (bf16[896,768]{1,0:T(8,128)(2,1)}, bf16[896,768]{1,0:T(8,128)(2,1)})) %all-reduce.20.cloned.1.call-update) | async-done | bytes 2752528 | tf_op jit(solution)/shard_map/psum | solution.py:182
  391.3 2.4 convert_reduce_fusion
  395.3 38.5 %all-reduce = (f32[768]{0:T(1024)}, f32[768]{0:T(1024)}, f32[192]{0:T(256)}, f32[192]{0:T(256)}, f32[768]{0:T(1024)}, /*index=5*/f32[768]{0:T(1024)}, f32[768]{0...) all-reduce(f32[768]{0:T(1024)S(1)} %get-tuple-element.85, ...), channel_id=1, replica_groups=mesh['dp'=8,'mp'=4] {'dp'}, use_global_device_ids=true, to_apply=%region_26.27 | all-reduce | flops 8448 | bytes 67584 | tf_op jit(solution)/shard_map/psum | solution.py:284
  433.7 3.8 add_convert_fusion.3
  441.6 3.8 reshape.445
  447.3 308.8 %all-reduce.18.cloned.1.call-done = (f32[768,192]{0,1:T(8,128)}, f32[768,192]{0,1:T(8,128)}, f32[768,192]{0,1:T(8,128)}, f32[192,768]{1,0:T(8,128)}, f32[768,192...) async-done(((f32[768,192]{0,1:T(8,128)}, f32[768,192]{0,1:T(8,128)}, ...) | async-done | bytes 9437200 | tf_op jit(solution)/shard_map/psum | solution.py:284
  (331 shorter events, 99.5 us)
Async XLA Ops:
  7.2 152.0 %copy-start = (bf16[768,768]{1,0:T(8,128)(2,1)S(1)}, bf16[768,768]{1,0:T(8,128)(2,1)}, u32[]{:S(2)}) copy-start(bf16[768,768]{1,0:T(8,128)(2,1)} %param.58) | copy-start | bytes 3538948
  7.2 6.5 copy-start.2
  7.2 4.6 copy-start.80
  7.2 4.6 copy-start.81
  7.3 8.1 %copy-start.53 = (bf16[768,192]{0,1:T(8,128)(2,1)S(1)}, bf16[768,192]{0,1:T(8,128)(2,1)}, u32[]{:S(2)}) copy-start(bf16[768,192]{0,1:T(8,128)(2,1)} %param.40) | copy-start | bytes 884740
  7.3 69.9 %all-reduce.10.cloned.1.call-start = ((), (), s32[]{:S(2)}) async-start(), calls=%async_computation.1 | async-start | bytes 2752512 | tf_op jit(solution)/shard_map/psum | solution.py:158
  16.4 8.8 %copy-start.44 = (bf16[2,448,3,64]{1,0,3,2:T(2,128)(2,1)}, bf16[2,448,3,64]{1,0,3,2:T(2,128)(2,1)S(1)}, u32[]{:S(2)}) copy-start(bf16[2,448,3,64]{1,0,3,2:T(2,128)(2,1)S(1)} %reshape.424) | copy-start | bytes 1032196
  23.8 4.6 copy-start.42
  31.7 8.2 %copy-start.33 = (bf16[896,192]{0,1:T(8,128)(2,1)}, bf16[896,192]{0,1:T(8,128)(2,1)S(1)}, u32[]{:S(2)}) copy-start(bf16[896,192]{0,1:T(8,128)(2,1)S(1)} %reshape.425) | copy-start | bytes 1032196
  34.5 118.6 %all-reduce.12.cloned.1.call-start = ((), (), s32[]{:S(2)}) async-start(), calls=%async_computation.2 | async-start | bytes 2752512 | tf_op jit(solution)/shard_map/psum | solution.py:174
  39.9 5.3 copy-start.61
  45.2 9.5 %copy-start.83 = (bf16[768]{0:T(1024)(128)(2,1)S(1)}, bf16[768]{0:T(1024)(128)(2,1)}, u32[]{:S(2)}) copy-start(bf16[768]{0:T(1024)(128)(2,1)} %param.46) | copy-start | bytes 4612
  45.2 9.5 %copy-start.84 = (bf16[768]{0:T(1024)(128)(2,1)S(1)}, bf16[768]{0:T(1024)(128)(2,1)}, u32[]{:S(2)}) copy-start(bf16[768]{0:T(1024)(128)(2,1)} %param.45) | copy-start | bytes 4612
  45.2 9.6 %copy-start.85 = (bf16[768]{0:T(1024)(128)(2,1)S(1)}, bf16[768]{0:T(1024)(128)(2,1)}, u32[]{:S(2)}) copy-start(bf16[768]{0:T(1024)(128)(2,1)} %param.44) | copy-start | bytes 4612
  45.2 9.6 %copy-start.95 = (bf16[192]{0:T(256)(128)(2,1)S(1)}, bf16[192]{0:T(256)(128)(2,1)}, u32[]{:S(2)}) copy-start(bf16[192]{0:T(256)(128)(2,1)} %param.48) | copy-start | bytes 1156
  45.2 9.6 %copy-start.96 = (bf16[192]{0:T(256)(128)(2,1)S(1)}, bf16[192]{0:T(256)(128)(2,1)}, u32[]{:S(2)}) copy-start(bf16[192]{0:T(256)(128)(2,1)} %param.51) | copy-start | bytes 1156
  45.3 9.6 %copy-start.64 = (bf16[768,192]{0,1:T(8,128)(2,1)S(1)}, bf16[768,192]{0,1:T(8,128)(2,1)}, u32[]{:S(2)}) copy-start(bf16[768,192]{0,1:T(8,128)(2,1)} %param.50) | copy-start | bytes 884740
  54.9 10.0 %copy-start.86 = (bf16[768]{0:T(1024)(128)(2,1)S(1)}, bf16[768]{0:T(1024)(128)(2,1)}, u32[]{:S(2)}) copy-start(bf16[768]{0:T(1024)(128)(2,1)} %param.55) | copy-start | bytes 4612
  54.9 10.1 %copy-start.87 = (bf16[768]{0:T(1024)(128)(2,1)S(1)}, bf16[768]{0:T(1024)(128)(2,1)}, u32[]{:S(2)}) copy-start(bf16[768]{0:T(1024)(128)(2,1)} %param.54) | copy-start | bytes 4612
  54.9 10.1 %copy-start.88 = (bf16[768]{0:T(1024)(128)(2,1)S(1)}, bf16[768]{0:T(1024)(128)(2,1)}, u32[]{:S(2)}) copy-start(bf16[768]{0:T(1024)(128)(2,1)} %param.57) | copy-start | bytes 4612
  54.9 10.1 %copy-start.97 = (s32[2]{0:T(128)S(1)}, s32[2]{0:T(128)}, u32[]{:S(2)}) copy-start(s32[2]{0:T(128)} %param.33) | copy-start | bytes 28
  59.9 8.9 %copy-start.91 = (s32[2]{0:T(128)S(1)}, s32[2]{0:T(128)}, u32[]{:S(2)}) copy-start(s32[2]{0:T(128)} %param.34) | copy-start | bytes 28
  92.3 8.2 %copy-start.25 = (bf16[2,1500,3,64]{1,0,3,2:T(2,128)(2,1)S(1)}, bf16[2,1500,3,64]{1,0,3,2:T(2,128)(2,1)}, u32[]{:S(2)}) copy-start(bf16[2,1500,3,64]{1,0,3,2:T(2,128)(2,1)} %reshape.427) | copy-start | bytes 3456004
  110.2 6.0 copy-start.35
  113.0 98.2 %all-reduce.14.cloned.1.call-start = ((), (), s32[]{:S(2)}) async-start(), calls=%async_computation.3 | async-start | bytes 2752512 | tf_op jit(solution)/shard_map/psum | solution.py:202
  159.2 8.5 %copy-start.39 = (f32[896,768]{1,0:T(8,128)}, f32[896,768]{1,0:T(8,128)S(1)}, u32[]{:S(2)}) copy-start(f32[896,768]{1,0:T(8,128)S(1)} %fusion.104) | copy-start | bytes 8257540
  171.2 119.8 %all-reduce.16.cloned.1.call-start = ((), (), s32[]{:S(2)}) async-start(), calls=%async_computation.4 | async-start | bytes 2752512 | tf_op jit(solution)/shard_map/psum | solution.py:224
  232.5 11.7 %copy-start.21 = (bf16[2,1500,3,64]{1,0,3,2:T(2,128)(2,1)S(1)}, bf16[2,1500,3,64]{1,0,3,2:T(2,128)(2,1)}, u32[]{:S(2)}) copy-start(bf16[2,1500,3,64]{1,0,3,2:T(2,128)(2,1)} %reshape.429) | copy-start | bytes 3456004
  248.1 12.9 %copy-start.37 = (bf16[896,192]{0,1:T(8,128)(2,1)}, bf16[896,192]{0,1:T(8,128)(2,1)S(1)}, u32[]{:S(2)}) copy-start(bf16[896,192]{0,1:T(8,128)(2,1)S(1)} %reshape.434) | copy-start | bytes 1032196
  250.9 140.4 %all-reduce.20.cloned.1.call-start = ((), (), s32[]{:S(2)}) async-start(), calls=%async_computation.7 | async-start | bytes 5505024 | tf_op jit(solution)/shard_map/psum | solution.py:182
  300.2 10.3 %slice-start = ((s8[5505024]{0:T(1024)(128)(4,1)}), s8[4194304]{0:T(1024)(128)(4,1)S(1)}, s32[]{:S(2)}) async-start(s8[5505024]{0:T(1024)(128)(4,1)} %bitcast.164), calls=%async_computation.8 | async-start | bytes 8388608
  304.4 6.2 slice-start.1
  314.1 7.9 %copy-start.29 = (bf16[896,192]{0,1:T(8,128)(2,1)}, bf16[896,192]{0,1:T(8,128)(2,1)S(1)}, u32[]{:S(2)}) copy-start(bf16[896,192]{0,1:T(8,128)(2,1)S(1)} %reshape.436) | copy-start | bytes 1032196
  318.8 10.0 %copy-start.31 = (bf16[896,192]{0,1:T(8,128)(2,1)}, bf16[896,192]{0,1:T(8,128)(2,1)S(1)}, u32[]{:S(2)}) copy-start(bf16[896,192]{0,1:T(8,128)(2,1)S(1)} %reshape.437) | copy-start | bytes 1032196
  328.8 112.8 %reduce-scatter.2.cloned.1.call-start = ((), (), s32[]{:S(2)}) async-start(), calls=%async_computation.5 | async-start | bytes 5898240 | tf_op jit(solution)/shard_map/reduce_scatter | solution.py:228
  339.8 7.9 %copy-start.62 = (bf16[768,192]{0,1:T(8,128)(2,1)S(1)}, bf16[768,192]{0,1:T(8,128)(2,1)}, u32[]{:S(2)}) copy-start(bf16[768,192]{0,1:T(8,128)(2,1)} %param.49) | copy-start | bytes 884740
  352.9 403.2 %all-reduce.18.cloned.1.call-start = ((), (), s32[]{:S(2)}) async-start(), calls=%async_computation.6 | async-start | bytes 18874368 | tf_op jit(solution)/shard_map/psum | solution.py:284
  354.9 8.7 %slice-start.2 = ((s8[4608000]{0:T(1024)(128)(4,1)}), s8[4194304]{0:T(1024)(128)(4,1)S(1)}, s32[]{:S(2)}) async-start(s8[4608000]{0:T(1024)(128)(4,1)} %bitcast.169), calls=%async_computation.10 | async-start | bytes 8388608
  357.8 4.5 copy-start.15
  357.8 4.5 copy-start.36
  357.8 5.8 slice-start.3
  372.8 18.5 %copy-start.69 = (f32[896]{0:T(1024)S(1)}, f32[896]{0:T(1024)}, u32[]{:S(2)}) copy-start(f32[896]{0:T(1024)} %copy-done.68) | copy-start | bytes 10756
  373.5 20.2 %copy-start.77 = (f32[896]{0:T(1024)S(1)}, f32[896]{0:T(1024)}, u32[]{:S(2)}) copy-start(f32[896]{0:T(1024)} %copy-done.76) | copy-start | bytes 10756
  373.5 20.2 %copy-start.71 = (f32[896]{0:T(1024)S(1)}, f32[896]{0:T(1024)}, u32[]{:S(2)}) copy-start(f32[896]{0:T(1024)} %copy-done.70) | copy-start | bytes 10756
  756.1 4.9 copy-start.58
  756.1 5.7 copy-start.57
  756.1 6.5 copy-start.56
  758.1 5.3 copy-start.55
  (63 other events, 151.2 us)
Sparse Core Ops, SparseCore 0:
  34.6 42.5 all-reduce.9
  113.1 39.8 all-reduce.11
  171.3 39.8 all-reduce.13
  251.0 39.8 all-reduce.15
  328.9 62.2 all-reduce.19
  393.7 47.9 reduce-scatter.1
  451.2 304.8 all-reduce.17
where the time goes:
time: 783 us; the launch traced here: 775 us
  waiting for transfers between devices  437 us (56%)
  matrix products  128 us (16%)
  local copies, waits for them, and re-layouts  82.7 us (11%)
  other arithmetic  71.6 us (9%)
  blocking collectives  38.5 us (5%)
  between operations  15.6 us (2%)
    psum x1, waiting for transfers between devices, shards(): lax.psum((gain_self_grad, shift_self_grad, query_self_grad, qbias_self_gr...  309 us
    psum x1, blocking collectives, shards(): lax.psum((gain_self_grad, shift_self_grad, query_self_grad, qbias_self_gr...  38.5 us
    psum x1, waiting for transfers between devices, shards(): lax.psum(project(o_cross, output_cross).astype(jnp.bfloat16), 'mp')  36.8 us
    unnamed x220, local copies, waits for them, and re-layouts  34 us
    psum x1, waiting for transfers between devices, shards(): lax.psum(project_back(pre_grad, expand_weight).astype(jnp.bfloat16), 'mp')  33.6 us
    dot_general x10, matrix products, project_back(): lax.dot_general(operand, weight, (((1,), (1,)), ((), ())), preferred_elem...  30.4 us
    psum x1, waiting for transfers between devices, shards(): lax.psum(project_back(dq_cross, query_cross).astype(jnp.bfloat16), 'mp')  29.9 us
    dot_general x10, matrix products, project(): return jnp.dot(operand, weight, preferred_element_type=jnp.float32)  25.4 us
  transfers between devices with their start and end apart: 7, of which 7 were waited for; matrix products, arithmetic and copies ran while one was open for 14% of the time, Pallas kernels for 0%

commit v1 on v0

v1 whole, which is shorter than its diff:
```python
import functools
import math

import jax
import jax.numpy as jnp
from jax import lax
from jax.experimental import pallas as pl
from jax.experimental.pallas import tpu as pltpu
from jax.sharding import PartitionSpec as P

HEAD = 64
AUG = 80
EPS = 1e-05
NEG = -1e30
F32 = jnp.float32
BF16 = jnp.bfloat16
ROOT_HALF = math.sqrt(0.5)
INV_ROOT_TAU = 1.0 / math.sqrt(2.0 * math.pi)
VMEM_BYTES = 28 * 1024 * 1024


def dot(left, right, left_dim, right_dim):
    return lax.dot_general(
        left, right, (((left_dim,), (right_dim,)), ((), ())), preferred_element_type=F32
    )


def nn(left, right):
    return dot(left, right, 1, 0)


def nt(left, right):
    return dot(left, right, 1, 1)


def tn(left, right):
    return dot(left, right, 0, 0)


def iota(shape, axis):
    return lax.broadcasted_iota(jnp.int32, shape, axis)


def norm_parts(values):
    centred = values - jnp.mean(values, axis=-1, keepdims=True)
    spread = jnp.mean(centred * centred, axis=-1, keepdims=True)
    scale = lax.rsqrt(spread + EPS)
    return centred * scale, scale


def norm_back(values, gain, upstream):
    unit, scale = norm_parts(values)
    inner = upstream * gain
    first = jnp.mean(inner, axis=-1, keepdims=True)
    second = jnp.mean(inner * unit, axis=-1, keepdims=True)
    grad = scale * (inner - first - unit * second)
    return (
        grad,
        jnp.sum(upstream * unit, axis=0, keepdims=True),
        jnp.sum(upstream, axis=0, keepdims=True),
    )


def line(ref):
    return ref[...].astype(F32).reshape(1, ref.shape[0])


def column_bias(ref, count):
    first = jnp.where(iota((16, ref.shape[0]), 0) == 0, line(ref), 0.0).astype(BF16)
    return tn(first, jnp.ones((16, count), BF16))


def mp_side():
    return lax.axis_index("mp") % 2


def key_extra(count, limit):
    rows = iota((16, count), 0)
    hidden_keys = jnp.where(iota((16, count), 1) < limit, 0.0, NEG)
    ones = jnp.where(rows < 4, 1.0, 0.0)
    return jnp.where(rows == 0, hidden_keys, ones).astype(BF16)


def value_extra(count):
    return jnp.where(iota((16, count), 0) < 3, 1.0, 0.0).astype(BF16)


def three_parts(row):
    high = row.astype(BF16)
    rest = row - high.astype(F32)
    middle = rest.astype(BF16)
    last = (rest - middle.astype(F32)).astype(BF16)
    return high.astype(F32), middle.astype(F32), last.astype(F32)


def split_rows(rows, row, first, with_one):
    high, middle, last = three_parts(row)
    base = jnp.where(rows == 0, 1.0, 0.0) if with_one else jnp.zeros(rows.shape, F32)
    out = jnp.where(rows == first, high, base)
    out = jnp.where(rows == first + 1, middle, out)
    return jnp.where(rows == first + 2, last, out).astype(BF16)


def store_halves(part, side, keep_ref, send_ref):
    half = part.shape[0] // 2
    low = part.astype(BF16)

    @pl.when(side == 0)
    def _():
        keep_ref[...] = low[:half]
        send_ref[...] = low[half:]

    @pl.when(side == 1)
    def _():
        keep_ref[...] = low[half:]
        send_ref[...] = low[:half]


def join_halves(pieces, side, scratch):
    own, own_far, other, other_far = pieces
    half = own.shape[0]
    here = pl.multiple_of(side * half, 16)
    there = pl.multiple_of((1 - side) * half, 16)
    scratch[pl.ds(here, half), :] = own[...].astype(F32) + own_far[...].astype(F32)
    scratch[pl.ds(there, half), :] = other[...].astype(F32) + other_far[...].astype(F32)
    return scratch[...]


def attend_block(keys, queries, keep):
    scores = tn(keys, queries)
    if keep is not None:
        scores = jnp.where(keep, scores, NEG)
    return scores


def causal_mask(count):
    return iota((count, count), 0) <= iota((count, count), 1)


def attention_forward(q_ref, ka_ref, va_ref, qa, o_ref, lse_ref, chunk, causal):
    heads, _, keys = ka_ref.shape
    count = q_ref.shape[1]
    rows = iota((16, count), 0)
    qa[HEAD:AUG, :] = jnp.where(rows == 0, 1.0, 0.0).astype(BF16)
    keep = causal_mask(count) if causal else None
    lse_rows = iota((8, count), 0)
    lse = jnp.zeros((8, count), F32)
    for head in range(heads):
        spot = slice(head * HEAD, (head + 1) * HEAD)
        qa[0:HEAD, :] = q_ref[spot, :]
        queries = qa[...]
        largest = None
        for start in range(0, keys, chunk):
            part = slice(start, start + chunk)
            scores = attend_block(ka_ref[head, :, part], queries, keep)
            top = jnp.max(scores, axis=0, keepdims=True)
            if largest is None:
                powers = jnp.exp(scores - top).astype(BF16)
                mixed = nn(va_ref[head, :, part], powers)
                largest = top
            else:
                newer = jnp.maximum(largest, top)
                powers = jnp.exp(scores - newer).astype(BF16)
                mixed = mixed * jnp.exp(largest - newer) + nn(va_ref[head, :, part], powers)
                largest = newer
        total = mixed[HEAD : HEAD + 1]
        o_ref[spot, :] = (mixed[0:HEAD] / total).astype(BF16)
        lse = jnp.where(lse_rows == head, largest + jnp.log(total), lse)
    lse_ref[...] = lse


def attention_backward(
    q_ref, ka_ref, va_ref, o_ref, lse_ref, do_ref, qa, doa, dq_ref, dk_ref, dv_ref, chunk, causal
):
    heads, _, keys = ka_ref.shape
    count = q_ref.shape[1]
    rows = iota((16, count), 0)
    keep = causal_mask(count) if causal else None
    for head in range(heads):
        spot = slice(head * HEAD, (head + 1) * HEAD)
        queries = q_ref[spot, :]
        mix_grad = do_ref[spot, :]
        qa[0:HEAD, :] = queries
        doa[0:HEAD, :] = mix_grad
        qa[HEAD:AUG, :] = split_rows(rows, -lse_ref[head : head + 1, :], 1, True)
        centre = jnp.sum(
            mix_grad.astype(F32) * o_ref[spot, :].astype(F32), axis=0, keepdims=True
        )
        doa[HEAD:AUG, :] = split_rows(rows, -centre, 0, False)
        query_side = qa[...]
        grad_side = doa[...]
        query_grad = jnp.zeros((HEAD, count), F32)
        for start in range(0, keys, chunk):
            part = slice(start, start + chunk)
            shares = jnp.exp(attend_block(ka_ref[head, :, part], query_side, keep))
            pushed = tn(va_ref[head, :, part], grad_side)
            score_grad = (shares * pushed).astype(BF16)
            dv_ref[spot, part] = nt(mix_grad, shares.astype(BF16)).astype(BF16)
            dk_ref[spot, part] = nt(queries, score_grad).astype(BF16)
            query_grad = query_grad + nn(ka_ref[head, 0:HEAD, part], score_grad)
        dq_ref[spot, :] = (query_grad * 0.125).astype(BF16)


def row_of_sums(matrix):
    ones = jnp.ones((16, matrix.shape[1]), BF16)
    return nt(ones, matrix)[0:1]


def self_forward(item, lengths, x_ref, gain, shift, wq, qbias, wk, wv, vbias, wo, q_o, ka_o, va_o, o_o, lse_o, keep_o, send_o, qa):
    count = x_ref.shape[1]
    unit, _ = norm_parts(x_ref[item].astype(F32))
    normed = (unit * line(gain) + line(shift)).astype(BF16)
    queries = (nt(wq[...], normed) + column_bias(qbias, count)).astype(BF16)
    q_o[...] = queries * jnp.asarray(0.125, BF16)
    key_rows = nt(wk[...], normed).astype(BF16)
    value_rows = (nt(wv[...], normed) + column_bias(vbias, count)).astype(BF16)
    extra = key_extra(count, lengths[item])
    other = value_extra(count)
    for head in range(ka_o.shape[0]):
        spot = slice(head * HEAD, (head + 1) * HEAD)
        ka_o[head, 0:HEAD, :] = key_rows[spot]
        ka_o[head, HEAD:AUG, :] = extra
        va_o[head, 0:HEAD, :] = value_rows[spot]
        va_o[head, HEAD:AUG, :] = other
    attention_forward(q_o, ka_o, va_o, qa, o_o, lse_o, count, True)
    store_halves(tn(o_o[...], wo[...]), mp_side(), keep_o, send_o)


def cross_keys(item, frames, enc, wk, wv, vbias, ka_o, va_o):
    count = enc.shape[0]
    wide = ka_o.shape[2]
    memory = enc[...]
    key_rows = nt(wk[...], memory).astype(BF16)
    value_rows = (nt(wv[...], memory) + column_bias(vbias, count)).astype(BF16)
    extra = key_extra(wide, frames[item])
    other = value_extra(wide)
    for head in range(ka_o.shape[0]):
        spot = slice(head * HEAD, (head + 1) * HEAD)
        if wide > count:
            ka_o[head, 0:HEAD, wide - 128 :] = jnp.zeros((HEAD, 128), BF16)
            va_o[head, 0:HEAD, wide - 128 :] = jnp.zeros((HEAD, 128), BF16)
        ka_o[head, 0:HEAD, 0:count] = key_rows[spot]
        ka_o[head, HEAD:AUG, :] = extra
        va_o[head, 0:HEAD, 0:count] = value_rows[spot]
        va_o[head, HEAD:AUG, :] = other


def cross_forward(item, chunk, x_ref, s0, s1, s2, s3, obias, gain, shift, wq, qbias, wo, ka, va, x1_o, h2_o, q_o, o_o, lse_o, keep_o, send_o, whole, qa):
    count = x_ref.shape[1]
    side = mp_side()
    after = x_ref[item].astype(F32) + join_halves((s0, s1, s2, s3), side, whole) + line(obias)
    x1_o[...] = after
    unit, _ = norm_parts(after)
    normed = (unit * line(gain) + line(shift)).astype(BF16)
    h2_o[...] = normed
    queries = (nt(wq[...], normed) + column_bias(qbias, count)).astype(BF16)
    q_o[...] = queries * jnp.asarray(0.125, BF16)
    attention_forward(q_o, ka, va, qa, o_o, lse_o, chunk, False)
    store_halves(tn(o_o[...], wo[...]), side, keep_o, send_o)


def upstream_rows(item, lengths, tasks, og):
    task = tasks[item]
    weight = jnp.where(task == 0, 1.0, jnp.where(task == 1, 0.6, 2.0)).astype(F32)
    valid = iota((og.shape[1], 1), 0) < lengths[item]
    return og[item].astype(F32) * jnp.where(valid, weight, 0.0)


def feed(item, lengths, tasks, x1, s0, s1, s2, s3, og, obias, gain, shift, we, ebias, wc, x2_o, h3_o, a_o, dz_o, gy_o, vec_o, keep_o, send_o, bkeep_o, bsend_o, whole):
    side = mp_side()
    after = x1[...] + join_halves((s0, s1, s2, s3), side, whole) + line(obias)
    x2_o[...] = after
    unit, _ = norm_parts(after)
    normed = (unit * line(gain) + line(shift)).astype(BF16)
    h3_o[...] = normed
    before = nn(normed, we[...]) + line(ebias)
    share = 0.5 + 0.5 * lax.erf(before * ROOT_HALF)
    active = (before * share).astype(BF16)
    a_o[...] = active
    slope = share + before * (jnp.exp(before * before * -0.5) * INV_ROOT_TAU)
    grad = upstream_rows(item, lengths, tasks, og)
    low = grad.astype(BF16)
    gy_o[...] = low
    inner = (nt(low, wc[...]) * slope).astype(BF16)
    dz_o[...] = inner
    store_halves(nt(inner, we[...]), side, bkeep_o, bsend_o)
    store_halves(nn(active, wc[...]), side, keep_o, send_o)
    pick = iota((8, vec_o.shape[1]), 0)
    out = jnp.where(pick == 0, jnp.sum(grad, axis=0, keepdims=True), 0.0)
    vec_o[...] = jnp.where(pick == 1, jnp.sum(inner.astype(F32), axis=0, keepdims=True), out)


def sum_of(refs):
    out = refs[0]
    for other in refs[1:]:
        out = out + other
    return out


def feed_weights(items, *refs):
    h3, dz, a, gy, vecs = (refs[k * items : (k + 1) * items] for k in range(5))
    pack = refs[5 * items]
    width = h3[0].shape[1]
    unit = dz[0].shape[1]
    pack[0:width, :] = sum_of([tn(h3[k][...], dz[k][...]) for k in range(items)]).astype(BF16)
    pack[width : width + unit, :] = sum_of([tn(a[k][...], gy[k][...]) for k in range(items)]).astype(BF16)
    tail = pack.shape[0] - width - unit
    pack[width + unit :, :] = jnp.zeros((tail, width), BF16)
    low = sum_of([v[...] for v in vecs]).astype(BF16)
    pack[width + unit : width + unit + 8, :] = low


def cross_backward(item, chunk, lengths, tasks, x2, s0, s1, s2, s3, og, gain, wo, wq, ka, va, q, o, lse, dx2_o, g2_o, dq_o, dk_o, dv_o, vec_o, keep_o, send_o, whole, qa, doa, do):
    side = mp_side()
    grad_in = join_halves((s0, s1, s2, s3), side, whole)
    grad, gain_row, shift_row = norm_back(x2[...], line(gain), grad_in)
    total = upstream_rows(item, lengths, tasks, og) + grad
    dx2_o[...] = total
    low = total.astype(BF16)
    g2_o[...] = low
    do[...] = nt(wo[...], low).astype(BF16)
    attention_backward(q, ka, va, o, lse, do, qa, doa, dq_o, dk_o, dv_o, chunk, False)
    store_halves(tn(dq_o[...], wq[...]), side, keep_o, send_o)
    pick = iota((8, vec_o.shape[1]), 0)
    out = jnp.where(pick == 0, gain_row, 0.0)
    out = jnp.where(pick == 1, shift_row, out)
    vec_o[...] = jnp.where(pick == 2, jnp.sum(total, axis=0, keepdims=True), out)
    vec_o[3:4, 0 : dq_o.shape[0]] = row_of_sums(dq_o[...])
    vec_o[4:5, 0 : dq_o.shape[0]] = row_of_sums(dv_o[...])


def memory_grad(wk, wv, dk, dv, keep_o, send_o):
    count = keep_o.shape[2]
    position = lax.axis_index("mp")
    rows = keep_o.shape[1]
    whole = (tn(wk[...], dk[...]) + tn(wv[...], dv[...])).astype(BF16)
    for block in range(4):
        piece = whole[block * rows : (block + 1) * rows, 0:count]
        relative = lax.bitwise_xor(position, block)
        slot = relative // 2

        @pl.when(relative % 2 == 0)
        def _():
            keep_o[slot] = piece

        @pl.when(relative % 2 == 1)
        def _():
            send_o[slot] = piece


def place_of(block):
    return (block % 2) * 4 + (block // 2 % 2) * 2 + block // 4 % 2


def scatter_blocks(whole, keep_o, send_o):
    position = lax.axis_index("dp") % 8
    rows = keep_o.shape[1]
    for block in range(8):
        place = place_of(lax.bitwise_xor(position, block))
        piece = whole[block * rows : (block + 1) * rows, :].astype(BF16)

        @pl.when(place < 4)
        def _():
            keep_o[place] = piece

        @pl.when(place >= 4)
        def _():
            send_o[place - 4] = piece


def gather_blocks(near, far, whole):
    position = lax.axis_index("dp") % 8
    rows = near.shape[1]
    for block in range(8):
        place = place_of(lax.bitwise_xor(position, block))
        spot = slice(block * rows, (block + 1) * rows)

        @pl.when(place < 4)
        def _():
            whole[spot, :] = near[place].astype(F32)

        @pl.when(place >= 4)
        def _():
            whole[spot, :] = far[place - 4].astype(F32)


def cross_weights(items, enc, *refs):
    dq, h2, o, g2, dk, dv, vecs = (refs[k * items : (k + 1) * items] for k in range(7))
    keep_o, send_o, whole = refs[7 * items :]
    rows = dq[0].shape[0]
    count = enc.shape[1]
    span = range(items)
    whole[0:rows, :] = sum_of([nn(dq[k][...], h2[k][...]) for k in span])
    whole[rows : 2 * rows, :] = sum_of([nn(dk[k][:, 0:count], enc[k]) for k in span])
    whole[2 * rows : 3 * rows, :] = sum_of([nn(dv[k][:, 0:count], enc[k]) for k in span])
    whole[3 * rows : 4 * rows, :] = sum_of([nn(o[k][...], g2[k][...]) for k in span])
    whole[4 * rows :, :] = jnp.zeros((whole.shape[0] - 4 * rows, whole.shape[1]), F32)
    whole[4 * rows : 4 * rows + 8, :] = sum_of([v[...] for v in vecs])
    scatter_blocks(whole, keep_o, send_o)


def self_backward(item, x1, s0, s1, s2, s3, dx2, x_ref, gain, wo, wq, wk, wv, ka, va, q, o, lse, dx1_o, g1_o, dqkv_o, vec_o, keep_o, send_o, whole, qa, doa, do):
    side = mp_side()
    grad_in = join_halves((s0, s1, s2, s3), side, whole)
    grad, gain_row, shift_row = norm_back(x1[...], line(gain), grad_in)
    total = dx2[...] + grad
    dx1_o[...] = total
    low = total.astype(BF16)
    g1_o[...] = low
    do[...] = nt(wo[...], low).astype(BF16)
    rows = do.shape[0]
    dq_o = dqkv_o.at[0:rows]
    dk_o = dqkv_o.at[rows : 2 * rows]
    dv_o = dqkv_o.at[2 * rows : 3 * rows]
    attention_backward(q, ka, va, o, lse, do, qa, doa, dq_o, dk_o, dv_o, q.shape[1], True)
    part = tn(dq_o[...], wq[...]) + tn(dk_o[...], wk[...]) + tn(dv_o[...], wv[...])
    store_halves(part, side, keep_o, send_o)
    unit, _ = norm_parts(x_ref[item].astype(F32))
    pick = iota((8, vec_o.shape[1]), 0)
    out = jnp.where(pick == 0, gain_row, 0.0)
    out = jnp.where(pick == 1, shift_row, out)
    out = jnp.where(pick == 2, jnp.sum(total, axis=0, keepdims=True), out)
    out = jnp.where(pick == 5, jnp.sum(part * unit, axis=0, keepdims=True), out)
    vec_o[...] = jnp.where(pick == 6, jnp.sum(part, axis=0, keepdims=True), out)
    vec_o[3:4, 0:rows] = row_of_sums(dq_o[...])
    vec_o[4:5, 0:rows] = row_of_sums(dv_o[...])


def self_weights(items, x_ref, gain, shift, *refs):
    dqkv, o, g1, vecs = (refs[k * items : (k + 1) * items] for k in range(4))
    keep_o, send_o, whole = refs[4 * items :]
    rows = o[0].shape[0]
    span = range(items)
    normed = []
    for k in span:
        unit, _ = norm_parts(x_ref[k].astype(F32))
        normed.append((unit * line(gain) + line(shift)).astype(BF16))
    whole[0 : 3 * rows, :] = sum_of([nn(dqkv[k][...], normed[k]) for k in span])
    whole[3 * rows : 4 * rows, :] = sum_of([nn(o[k][...], g1[k][...]) for k in span])
    whole[4 * rows :, :] = jnp.zeros((whole.shape[0] - 4 * rows, whole.shape[1]), F32)
    whole[4 * rows : 4 * rows + 8, :] = sum_of([v[...] for v in vecs])
    scatter_blocks(whole, keep_o, send_o)


def unpack(near, far, first, second, third, fourth, vec_o, whole):
    gather_blocks(near, far, whole)
    rows = first.shape[0]
    for k, out in enumerate((first, second, third, fourth)):
        out[...] = whole[k * rows : (k + 1) * rows, :]
    vec_o[...] = whole[4 * rows : 4 * rows + 8, :]


def finish_out(item, x2, s0, s1, s2, s3, bias, *rest):
    out, whole = rest[-2:]
    total = x2[...] + join_halves((s0, s1, s2, s3), mp_side(), whole) + line(bias)
    out[...] = total.astype(BF16)


def finish_grad(item, dx1, s0, s1, s2, s3, x_ref, gain, *rest):
    out, whole = rest[-2:]
    grad_in = join_halves((s0, s1, s2, s3), mp_side(), whole)
    grad, _, _ = norm_back(x_ref[item].astype(F32), line(gain), grad_in)
    out[...] = dx1[...] + grad


SCALARS = pl.BlockSpec(memory_space=pltpu.SMEM)
LEFT = pl.BlockSpec(memory_space=pl.ANY)
NEAR = pl.BlockSpec(memory_space=pltpu.VMEM)


def chosen(array, item):
    rest = (0,) * (len(array.shape) - 1)
    return pl.BlockSpec((None,) + tuple(array.shape[1:]), lambda *_: (item,) + rest)


def shape(dims, dtype):
    return jax.ShapeDtypeStruct(dims, dtype)


def run(body, name, cost, operands, outs, scratch=(), specs=None, out_specs=None, aliases=None):
    specs = specs or {}
    placed, in_specs = [], []
    for k, array in enumerate(operands):
        spec = specs.get(k, SCALARS if array.dtype == jnp.int32 else NEAR)
        if spec is NEAR:
            array = pltpu.with_memory_space_constraint(array, pltpu.VMEM)
        placed.append(array)
        in_specs.append(spec)
    return pl.pallas_call(
        body,
        name=name,
        grid=(1,),
        in_specs=in_specs,
        out_specs=out_specs or [NEAR] * len(outs),
        out_shape=list(outs),
        scratch_shapes=list(scratch),
        input_output_aliases=aliases or {},
        cost_estimate=pl.CostEstimate(flops=int(cost * 1.1e9), transcendentals=0, bytes_accessed=0),
        compiler_params=pltpu.CompilerParams(vmem_limit_bytes=VMEM_BYTES),
    )(*placed)


def swap(value, axis, size, bit):
    return lax.ppermute(value, axis, [(k, k ^ bit) for k in range(size)])


def after(value, *earlier):
    return lax.optimization_barrier((value, earlier))[0]


def add_low(left, right):
    return (left.astype(F32) + right.astype(F32)).astype(BF16)


def mp_near(send, size):
    return swap(send, "mp", size, 1)


def mp_pieces(keep, near, size):
    own = add_low(keep, near)
    far = swap(own, "mp", size, 2)
    other = swap(own, "mp", size, 1)
    other_far = swap(far, "mp", size, 1)
    return own, far, other, other_far


def dp_sum(keep, send, size):
    near = swap(send, "dp", size, 1)
    keep, send = add_low(keep[:2], near[:2]), add_low(keep[2:], near[2:])
    near = swap(send, "dp", size, 2)
    keep, send = add_low(keep[:1], near[:1]), add_low(keep[1:], near[1:])
    total = add_low(keep, swap(send, "dp", size, 4))
    bit = 8
    while bit < size:
        total = add_low(total, swap(total, "dp", size, bit))
        bit *= 2
    total = jnp.concatenate([total, swap(total, "dp", size, 4)])
    total = jnp.concatenate([total, swap(total, "dp", size, 2)])
    return total, swap(total, "dp", size, 1)


def shards(sizes, *arguments):
    (
        hidden, encoder, lengths, tasks, frames, out_grad,
        gain_self, shift_self, query_self, qbias_self, key_self, value_self, vbias_self, output_self, obias_self,
        gain_cross, shift_cross, query_cross, qbias_cross, key_cross, value_cross, vbias_cross, output_cross, obias_cross,
        gain_feed, shift_feed, expand_weight, expand_bias, contract_weight, contract_bias,
    ) = arguments
    n_mp, n_dp = sizes["mp"], sizes["dp"]
    items, length, width = hidden.shape
    memory_len = encoder.shape[1]
    rows = query_self.shape[1]
    heads = rows // HEAD
    units = expand_weight.shape[1]
    wide = -(-memory_len // 512) * 512
    chunk = 512
    half = length // 2
    wq1, wk1, wv1 = query_self.T, key_self.T, value_self.T
    wq2, wk2, wv2 = query_cross.T, key_cross.T, value_cross.T

    def near_shape(dims, dtype=BF16):
        return pltpu.VMEM(dims, dtype)

    low_rows = near_shape((rows, length))
    mem_rows = near_shape((rows, wide))
    half_out = near_shape((half, width))
    state = near_shape((length, width), F32)
    low_state = near_shape((length, width))
    unit_state = near_shape((length, units))
    vec_out = near_shape((8, width), F32)
    lse_out = near_shape((8, length), F32)
    aug_out = near_shape((heads, AUG, length))
    aug_mem = near_shape((heads, AUG, wide))
    whole = pltpu.VMEM((length, width), F32)
    aug = pltpu.VMEM((AUG, length), BF16)
    row_scratch = pltpu.VMEM((rows, length), BF16)
    pack_rows = 4 * rows + 64
    pack_scratch = pltpu.VMEM((pack_rows, width), F32)
    pack_half = shape((4, pack_rows // 8, width), BF16)
    span = range(items)
    last = items - 1
    bind = functools.partial

    self_out, near = [], []
    for i in span:
        out = run(
            bind(self_forward, i), "self_forward", 6,
            (lengths, hidden, gain_self, shift_self, wq1, qbias_self, wk1, wv1, vbias_self, output_self),
            (low_rows, aug_out, aug_out, low_rows, lse_out, half_out, half_out), (aug,),
        )
        self_out.append(out)
        near.append(mp_near(out[6], n_mp))

    def keys(i, start):
        return run(
            bind(cross_keys, i), "cross_keys", 5, (after(frames, start), encoder, wk2, wv2, vbias_cross),
            (aug_mem, aug_mem), (), {1: chosen(encoder, i)},
        )

    cross_kv, pieces = [None] * items, []
    token = self_out[last][4]
    for i in span:
        pieces.append(mp_pieces(self_out[i][5], after(near[i], token), n_mp))
        if i == 0:
            cross_kv[0] = keys(0, token)
            token = cross_kv[0][0]

    cross_out, cross_near = [], []
    for i in span:
        out = run(
            bind(cross_forward, i, chunk), "cross_forward", 9,
            (hidden, *pieces[i], obias_self, gain_cross, shift_cross, wq2, qbias_cross, output_cross, *cross_kv[i]),
            (state, low_state, low_rows, low_rows, lse_out, half_out, half_out), (whole, aug),
        )
        cross_out.append(out)
        cross_near.append(mp_near(out[6], n_mp))
        if i < last:
            cross_kv[i + 1] = keys(i + 1, out[4])
            cross_near[i] = after(cross_near[i], cross_kv[i + 1][0])

    feed_out, feed_near = [], []
    for i in span:
        done = mp_pieces(cross_out[i][5], cross_near[i], n_mp)
        out = run(
            bind(feed, i), "feed", 9,
            (lengths, tasks, cross_out[i][0], *done, out_grad, obias_cross, gain_feed, shift_feed, expand_weight, expand_bias, contract_weight),
            (state, low_state, unit_state, unit_state, low_state, vec_out, half_out, half_out, half_out, half_out), (whole,),
        )
        feed_out.append(out)
        feed_near.append(mp_near(out[9], n_mp))

    token = feed_out[last][5]
    back_pieces = [mp_pieces(feed_out[i][8], after(feed_near[i], token), n_mp) for i in span]
    feed_pack = run(
        bind(feed_weights, items), "feed_weights", 7,
        [feed_out[i][k] for k in (1, 3, 2, 4, 5) for i in span],
        (shape((width + units + 16, width), BF16),),
    )[0]
    feed_pack = lax.psum(feed_pack, "dp")
    block_near = [mp_near(feed_out[i][7], n_mp) for i in span]

    back_out, back_near = [], []
    for i in span:
        _, _, q2, o2, lse2 = cross_out[i][:5]
        out = run(
            bind(cross_backward, i, chunk), "cross_backward", 12,
            (lengths, tasks, feed_out[i][0], *back_pieces[i], out_grad, gain_feed, output_cross, wq2, *cross_kv[i], q2, o2, lse2),
            (state, low_state, low_rows, mem_rows, mem_rows, vec_out, half_out, half_out), (whole, aug, aug, row_scratch),
        )
        back_out.append(out)
        back_near.append(mp_near(out[7], n_mp))
    block_pieces = [mp_pieces(feed_out[i][6], after(block_near[i], back_out[0][5]), n_mp) for i in span]
    token = back_out[last][5]
    dq_pieces = [mp_pieces(back_out[i][6], after(back_near[i], token), n_mp) for i in span]

    memory_parts = []
    for i in span:
        memory_parts.append(
            run(
                memory_grad, "memory_grad", 5, (wk2, wv2, back_out[i][3], back_out[i][4]),
                (near_shape((2, rows, memory_len)), near_shape((2, rows, memory_len))),
            )
        )

    cross_pack = run(
        bind(cross_weights, items), "cross_weights", 8,
        [encoder] + [out[2] for out in back_out] + [out[1] for out in cross_out] + [out[3] for out in cross_out]
        + [out[1] for out in back_out] + [out[3] for out in back_out] + [out[4] for out in back_out]
        + [out[5] for out in back_out],
        (pack_half, pack_half), (pack_scratch,), {0: pl.BlockSpec(encoder.shape, lambda *_: (0, 0, 0))},
    )
    cross_sum = dp_sum(*cross_pack, n_dp)

    self_back, self_near = [], []
    for i in span:
        q1, ka1, va1, o1, lse1 = self_out[i][:5]
        out = run(
            bind(self_backward, i), "self_backward", 9,
            (cross_out[i][0], *dq_pieces[i], back_out[i][0], hidden, gain_cross, output_self, wq1, wk1, wv1, ka1, va1, q1, o1, lse1),
            (state, low_state, near_shape((3 * rows, length)), vec_out, half_out, half_out), (whole, aug, aug, row_scratch),
        )
        self_back.append(out)
        self_near.append(mp_near(out[5], n_mp))

    self_pack = run(
        bind(self_weights, items), "self_weights", 6,
        [hidden, gain_self, shift_self] + [out[2] for out in self_back] + [out[3] for out in self_out]
        + [out[1] for out in self_back] + [out[3] for out in self_back],
        (pack_half, pack_half), (pack_scratch,),
    )
    self_sum = dp_sum(*self_pack, n_dp)
    token = self_back[last][3]
    last_pieces = [mp_pieces(self_back[i][4], after(self_near[i], token), n_mp) for i in span]

    block_out, hidden_grad = None, None
    block_shape = shape(hidden.shape, BF16)
    grad_shape = shape(hidden.shape, F32)
    for i in span:
        extra = () if block_out is None else (block_out,)
        block_out = run(
            bind(finish_out, i), "finish_out", 3,
            (feed_out[i][0], *block_pieces[i], contract_bias, *extra), (block_shape,), (whole,),
            {6: LEFT}, [chosen(block_shape, i)], {6: 0} if extra else {},
        )[0]
    for i in span:
        extra = () if hidden_grad is None else (hidden_grad,)
        hidden_grad = run(
            bind(finish_grad, i), "finish_grad", 4,
            (self_back[i][0], *last_pieces[i], hidden, gain_self, *extra), (grad_shape,), (whole,),
            {7: LEFT}, [chosen(grad_shape, i)], {7: 0} if extra else {},
        )[0]

    memory_grads = []
    for keep, send in memory_parts:
        near_part = swap(send, "mp", n_mp, 1)
        kept, sent = add_low(keep[0], near_part[0]), add_low(keep[1], near_part[1])
        memory_grads.append(kept.astype(F32) + swap(sent, "mp", n_mp, 2).astype(F32))
    encoder_grad = jnp.stack(memory_grads).transpose(0, 2, 1)

    matrix = shape((rows, width), F32)
    outs = (matrix, matrix, matrix, matrix, shape((8, width), F32))
    cross_grads = run(unpack, "unpack", 3, cross_sum, outs, (pack_scratch,))
    self_grads = run(unpack, "unpack", 3, self_sum, outs, (pack_scratch,))
    feed_grads = feed_pack.astype(F32)
    norm_rows = self_grads[4]
    norm_rows = norm_rows + swap(norm_rows, "mp", n_mp, 1)
    norm_rows = norm_rows + swap(norm_rows, "mp", n_mp, 2)
    return (
        block_out,
        hidden_grad,
        encoder_grad,
        norm_rows[5],
        norm_rows[6],
        self_grads[0].T,
        self_grads[4][3, 0:rows],
        self_grads[1].T,
        self_grads[2].T,
        self_grads[4][4, 0:rows],
        self_grads[3],
        self_grads[4][2],
        self_grads[4][0],
        self_grads[4][1],
        cross_grads[0].T,
        cross_grads[4][3, 0:rows],
        cross_grads[1].T,
        cross_grads[2].T,
        cross_grads[4][4, 0:rows],
        cross_grads[3],
        cross_grads[4][2],
        cross_grads[4][0],
        cross_grads[4][1],
        feed_grads[0:width],
        feed_grads[width + units + 1],
        feed_grads[width : width + units],
        feed_grads[width + units],
    )


def solution(mesh):
    column, row, flat = P(None, "mp"), P("mp", None), P("mp")
    cube = P("dp", None, None)
    attention = (P(), P(), column, flat, column, column, flat, row, P())
    grads = (P(), P(), column, flat, column, column, flat, row, P())
    return jax.shard_map(
        functools.partial(shards, dict(mesh.shape)),
        mesh=mesh,
        in_specs=(cube, cube, P("dp"), P("dp"), P("dp"), cube)
        + attention
        + attention
        + (P(), P(), column, flat, row, P()),
        out_specs=(cube, cube, P("dp", None, "mp")) + grads + grads + (P(), P(), column, flat, row, P()),
        check_vma=False,
    )
```

time: 783 us -> 333 us (0.43)
  waiting for transfers between devices: 437 us -> 141 us
  matrix products: 128 us -> 0 us
  Pallas kernels: 0 us -> 83.9 us
  other arithmetic: 71.6 us -> 15.7 us
  local copies, waits for them, and re-layouts: 82.7 us -> 33.1 us
  blocking collectives: 38.5 us -> 0 us
  starting transfers between devices: 1.55 us -> 38.2 us
    psum x6 -> x1, waiting for transfers between devices: 435 us -> 11.3 us  [shards(): feed_pack = lax.psum(feed_pack, 'dp')]
    ppermute x0 -> x66, waiting for transfers between devices: none -> 130 us  [swap(): return lax.ppermute(value, axis, [(k, k ^ bit) for k in range(size)])]
    dot_general x42 -> x0, matrix products: 128 us -> none  [the longest x10 30.4 us: project_back(): lax.dot_general(operand, weight, (((1,), (1,)), ((), ())), preferred_elem...]
    pallas_call x0 -> x23, Pallas kernels: none -> 83.9 us  [run(): pl.pallas_call(body, name=name, grid=(1,), in_specs=in_specs, out_specs=o...]
    reduce_sum x17 -> x0, other arithmetic: 38.5 us -> none  [the longest x6 13.6 us: layer_norm(): return centred * lax.rsqrt(spread + epsilon) * norm_gain + norm_shift]
    psum x1 -> x0, blocking collectives: 38.5 us -> none  [shards(): lax.psum((gain_self_grad, shift_self_grad, query_self_grad, qbias_self_gr...]
    ppermute x0 -> x66, starting transfers between devices: none -> 38.2 us  [swap(): return lax.ppermute(value, axis, [(k, k ^ bit) for k in range(size)])]
    reshape x18 -> x0, local copies, waits for them, and re-layouts: 37 us -> none  [the longest x8 14.1 us: split_heads(): return flat.reshape(item_count, -1, flat.shape[-1] // HEAD, HEAD)]
  transfers between devices with their start and end apart: 7 -> 67, of which waited for: 7 -> 21; matrix products, arithmetic and copies ran while one was open for 14% -> 7% of each run, Pallas kernels for 0% -> 24%
where the time goes in v1:
time: 333 us; the launch traced here: 328 us
  waiting for transfers between devices  141 us (42%)
  Pallas kernels  83.9 us (25%)
  starting transfers between devices  38.2 us (11%)
  local copies, waits for them, and re-layouts  33.1 us (10%)
  between operations  16 us (5%)
  other arithmetic  15.7 us (5%)
    ppermute x66, waiting for transfers between devices, swap(): return lax.ppermute(value, axis, [(k, k ^ bit) for k in range(size)])  130 us
    pallas_call x23, Pallas kernels, run(): pl.pallas_call(body, name=name, grid=(1,), in_specs=in_specs, out_specs=o...  83.9 us
    ppermute x66, starting transfers between devices, swap(): return lax.ppermute(value, axis, [(k, k ^ bit) for k in range(size)])  38.2 us
    unnamed x221, local copies, waits for them, and re-layouts  27 us
    psum x1, waiting for transfers between devices, shards(): feed_pack = lax.psum(feed_pack, 'dp')  11.3 us
    convert_element_type x20, other arithmetic, add_low(): return (left.astype(F32) + right.astype(F32)).astype(BF16)  8.41 us
  transfers between devices with their start and end apart: 67, of which 21 were waited for; matrix products, arithmetic and copies ran while one was open for 7% of the time, Pallas kernels for 24%

profile of v1, /device:TPU:0, one launch (start us, length us, event | category | flops | bytes accessed | tf_op | source)
XLA Modules:
  0.0 328.1 jit_solution(13221365488435298198)
XLA Ops:
  15.8 3.3 self_forward.3
  22.3 3.5 %self_forward.2 = (bf16[192,448]{1,0:T(8,128)(2,1)S(1)}, bf16[3,80,448]{2,1,0:T(8,128)(2,1)S(1)}, bf16[3,80,448]{2,1,0:T(8,128)(2,1)S(1)}, bf16[192,448]{1,0:T(8...) custom-call(s32[2]{0:T(128)S(1)} %copy-done.45, ...), custom_call_target="tpu_custom_call" | custom-call | flops 6600000000 | tf_op jit(solution)/shard_map/self_forward/pallas_call | solution.py:489
  29.3 3.0 collective-permute-start.5
  32.4 2.1 cross_keys.2
  34.9 6.3 %collective-permute-done.5.s1 = bf16[224,768]{1,0:T(8,128)(2,1)S(1)} collective-permute-done((bf16[224,768]{1,0:T(8,128)(2,1)S(1)}, bf16[224,768]{1,0:T(8,128)(2,1)S(1)}, u32[]{:S(2)}, u32[]{:S(2)}) %collective-permute-start.5) | collective-permute-done | bytes 344096 | tf_op jit(solution)/shard_map/ppermute | solution.py:504
  41.7 6.2 %collective-permute-done.1.s1 = bf16[224,768]{1,0:T(8,128)(2,1)S(1)} collective-permute-done((bf16[224,768]{1,0:T(8,128)(2,1)S(1)}, bf16[224,768]{1,0:T(8,128)(2,1)S(1)}, u32[]{:S(2)}, u32[]{:S(2)}) %collective-permute-start.1) | collective-permute-done | bytes 344096 | tf_op jit(solution)/shard_map/ppermute | solution.py:504
  48.0 5.7 %cross_forward.2 = (f32[448,768]{1,0:T(8,128)S(1)}, bf16[448,768]{1,0:T(8,128)(2,1)S(1)}, bf16[192,448]{1,0:T(8,128)(2,1)S(1)}, bf16[192,448]{1,0:T(8,128)(2,1)S...) custom-call(bf16[2,448,768]{2,1,0:T(8,128)(2,1)S(1)} %copy-done.7, ...), custom_call_target="tpu_custom_call" | custom-call | flops 9900000256 | tf_op jit(solution)/shard_map/cross_forward/pallas_call | solution.py:489
  54.4 2.1 cross_keys.3
  56.5 5.5 %cross_forward.3 = (f32[448,768]{1,0:T(8,128)S(1)}, bf16[448,768]{1,0:T(8,128)(2,1)S(1)}, bf16[192,448]{1,0:T(8,128)(2,1)S(1)}, bf16[192,448]{1,0:T(8,128)(2,1)S...) custom-call(bf16[2,448,768]{2,1,0:T(8,128)(2,1)S(1)} %copy-done.7, ...), custom_call_target="tpu_custom_call" | custom-call | flops 9900000256 | tf_op jit(solution)/shard_map/cross_forward/pallas_call | solution.py:489
  64.0 1.8 collective-permute-start.14
  67.4 7.5 %collective-permute-done.14.s1 = bf16[224,768]{1,0:T(8,128)(2,1)S(1)} collective-permute-done((bf16[224,768]{1,0:T(8,128)(2,1)S(1)}, bf16[224,768]{1,0:T(8,128)(2,1)S(1)}, u32[]{:S(2)}, u32[]{:S(2)}) %collective-permute-start.14) | collective-permute-done | bytes 344096 | tf_op jit(solution)/shard_map/ppermute | solution.py:504
  75.5 6.4 %collective-permute-done.9.s1 = bf16[224,768]{1,0:T(8,128)(2,1)S(1)} collective-permute-done((bf16[224,768]{1,0:T(8,128)(2,1)S(1)}, bf16[224,768]{1,0:T(8,128)(2,1)S(1)}, u32[]{:S(2)}, u32[]{:S(2)}) %collective-permute-start.9) | collective-permute-done | bytes 344096 | tf_op jit(solution)/shard_map/ppermute | solution.py:504
  82.0 4.9 %feed.3 = (f32[448,768]{1,0:T(8,128)S(1)}, bf16[448,768]{1,0:T(8,128)(2,1)S(1)}, bf16[448,768]{1,0:T(8,128)(2,1)S(1)}, bf16[448,768]{1,0:T(8,128)(2,1)S(1)}, bf1...) custom-call(s32[2]{0:T(128)S(1)} %copy-done.46, ...), custom_call_target="tpu_custom_call" | custom-call | flops 9900000256 | tf_op jit(solution)/shard_map/feed/pallas_call | solution.py:489
  88.5 4.5 %feed.2 = (f32[448,768]{1,0:T(8,128)S(1)}, bf16[448,768]{1,0:T(8,128)(2,1)S(1)}, bf16[448,768]{1,0:T(8,128)(2,1)S(1)}, bf16[448,768]{1,0:T(8,128)(2,1)S(1)}, bf1...) custom-call(s32[2]{0:T(128)S(1)} %copy-done.46, ...), custom_call_target="tpu_custom_call" | custom-call | flops 9900000256 | tf_op jit(solution)/shard_map/feed/pallas_call | solution.py:489
  93.2 1.8 collective-permute-start.18
  96.6 7.5 %collective-permute-done.18.s1 = bf16[224,768]{1,0:T(8,128)(2,1)S(1)} collective-permute-done((bf16[224,768]{1,0:T(8,128)(2,1)S(1)}, bf16[224,768]{1,0:T(8,128)(2,1)S(1)}, u32[]{:S(2)}, u32[]{:S(2)}) %collective-permute-start.18) | collective-permute-done | bytes 344096 | tf_op jit(solution)/shard_map/ppermute | solution.py:504
  104.1 4.1 %feed_weights.1 = bf16[1552,768]{1,0:T(8,128)(2,1)} custom-call(bf16[448,768]{1,0:T(8,128)(2,1)S(1)} %get-tuple-element.240.refs_0_, bf16[448,768]{1,0:T(8,128)(2,1)S(1)} %get-tuple-element.241.refs_1_, bf16[448,768]{1,0:T(8,128)(2,1)S(1)} %get-tuple-element.242.refs_2_, bf16[448,768]{1,0:T(8,128)(2,1)S(1)} %get-tuple-element.243.refs_3_, ...), custom_call_target="tpu_custom_call" | custom-call | flops 7699999744 | tf_op jit(solution)/shard_map/feed_weights/pallas_call | solution.py:489
  108.8 2.2 collective-permute-done.29.s1
  119.0 9.2 %cross_backward.2 = (f32[448,768]{1,0:T(8,128)S(1)}, bf16[448,768]{1,0:T(8,128)(2,1)S(1)}, bf16[192,448]{1,0:T(8,128)(2,1)S(1)}, bf16[192,1536]{1,0:T(8,128)(2,1...) custom-call(s32[2]{0:T(128)S(1)} %copy-done.46, ...), custom_call_target="tpu_custom_call" | custom-call | flops 13200000000 | tf_op jit(solution)/shard_map/cross_backward/pallas_call | solution.py:489
  129.3 1.8 collective-permute-start.25
  131.2 8.4 %cross_backward.3 = (f32[448,768]{1,0:T(8,128)S(1)}, bf16[448,768]{1,0:T(8,128)(2,1)S(1)}, bf16[192,448]{1,0:T(8,128)(2,1)S(1)}, bf16[192,1536]{1,0:T(8,128)(2,1...) custom-call(s32[2]{0:T(128)S(1)} %copy-done.46, ...), custom_call_target="tpu_custom_call" | custom-call | flops 13200000000 | tf_op jit(solution)/shard_map/cross_backward/pallas_call | solution.py:489
  140.1 1.7 memory_grad.3
  141.9 1.9 memory_grad.2
  143.8 2.9 cross_weights.1
  150.8 8.6 %collective-permute-done.21.s1 = bf16[224,768]{1,0:T(8,128)(2,1)S(1)} collective-permute-done((bf16[224,768]{1,0:T(8,128)(2,1)S(1)}, bf16[224,768]{1,0:T(8,128)(2,1)S(1)}, u32[]{:S(2)}, u32[]{:S(2)}) %collective-permute-start.21) | collective-permute-done | bytes 344096 | tf_op jit(solution)/shard_map/ppermute | solution.py:504
  159.9 7.8 %collective-permute-done.60 = bf16[4,104,768]{2,1,0:T(8,128)(2,1)S(1)} collective-permute-done((bf16[4,104,768]{2,1,0:T(8,128)(2,1)S(1)}, bf16[4,104,768]{2,1,0:T(8,128)(2,1)S(1)}, u32[]{:S(2)}, u32[]{:S(2)}) %collective-permute-start.60) | collective-permute-done | bytes 639008 | tf_op jit(solution)/shard_map/ppermute | solution.py:504
  173.6 6.2 %collective-permute-done.61 = bf16[2,104,768]{2,1,0:T(8,128)(2,1)S(1)} collective-permute-done((bf16[2,104,768]{2,1,0:T(8,128)(2,1)S(1)}, bf16[2,104,768]{2,1,0:T(8,128)(2,1)S(1)}, u32[]{:S(2)}, u32[]{:S(2)}) %collective-permute-start.61) | collective-permute-done | bytes 319520 | tf_op jit(solution)/shard_map/ppermute | solution.py:504
  180.3 1.6 collective-permute-done.41.s1
  182.0 2.5 collective-permute-start.62
  184.6 5.3 %self_backward.2 = (f32[448,768]{1,0:T(8,128)S(1)}, bf16[448,768]{1,0:T(8,128)(2,1)S(1)}, bf16[576,448]{1,0:T(8,128)(2,1)S(1)}, f32[8,768]{1,0:T(8,128)S(1)}, bf...) custom-call(f32[448,768]{1,0:T(8,128)S(1)} %copy-done.68, bf16[224,768]{1,0:T(8,128)(2,1)S(1)} %add_convert_fusion.7.s0, ...), custom_call_target="tpu_custom_call" | custom-call | flops 9900000256 | tf_op jit(solution)/shard_map/self_backward/pallas_call | solution.py:489
  191.3 5.1 %self_backward.3 = (f32[448,768]{1,0:T(8,128)S(1)}, bf16[448,768]{1,0:T(8,128)(2,1)S(1)}, bf16[576,448]{1,0:T(8,128)(2,1)S(1)}, f32[8,768]{1,0:T(8,128)S(1)}, bf...) custom-call(f32[448,768]{1,0:T(8,128)S(1)} %copy-done.66, bf16[224,768]{1,0:T(8,128)(2,1)S(1)} %add_convert_fusion.5.s0, ...), custom_call_target="tpu_custom_call" | custom-call | flops 9900000256 | tf_op jit(solution)/shard_map/self_backward/pallas_call | solution.py:489
  196.7 3.3 %self_weights.1 = (bf16[4,104,768]{2,1,0:T(8,128)(2,1)S(1)}, bf16[4,104,768]{2,1,0:T(8,128)(2,1)}) custom-call(bf16[2,448,768]{2,1,0:T(8,128)(2,1)S(1)} %copy-done.8, bf16[768]{0:T(1024)(128)(2,1)S(1)} %copy-done.39, bf16[768]{0:T(1024)(128)(2,1)S(1)} %copy-done.37, bf16[576,448]{1,0:T(8,128)(2,1)S(1)} %get-tuple-element.215.refs_0_, ...), custom_call_target="tpu_custom_call" | custom-call | flops 6600000000 | tf_op jit(solution)/shard_map/self_weights/pallas_call | solution.py:489
  204.4 17.1 %collective-permute-done.63 = bf16[1,104,768]{2,1,0:T(8,128)(2,1)S(1)} collective-permute-done((bf16[1,104,768]{2,1,0:T(8,128)(2,1)S(1)}, bf16[1,104,768]{2,1,0:T(8,128)(2,1)S(1)}, u32[]{:S(2)}, u32[]{:S(2)}) %collective-permute-start.63) | collective-permute-done | bytes 159776 | tf_op jit(solution)/shard_map/ppermute | solution.py:504
  223.4 11.3 %all-reduce.2.cloned.1.call-done = bf16[1552,768]{1,0:T(8,128)(2,1)} async-done(((bf16[1552,768]{1,0:T(8,128)(2,1)}), bf16[1552,768]{1,0:T(8,128)(2,1)}) %all-reduce.2.cloned.1.call-update) | async-done | bytes 2383888 | tf_op jit(solution)/shard_map/psum | solution.py:639
  234.7 2.2 convert_element_type.357
  237.1 2.5 fusion.6
  244.0 5.4 %collective-permute-done.64 = bf16[2,104,768]{2,1,0:T(8,128)(2,1)S(1)} collective-permute-done((bf16[2,104,768]{2,1,0:T(8,128)(2,1)S(1)}, bf16[2,104,768]{2,1,0:T(8,128)(2,1)S(1)}, u32[]{:S(2)}, u32[]{:S(2)}) %collective-permute-start.64) | collective-permute-done | bytes 319520 | tf_op jit(solution)/shard_map/ppermute | solution.py:504
  253.8 6.2 %collective-permute-done.45.s1 = bf16[224,768]{1,0:T(8,128)(2,1)S(1)} collective-permute-done((bf16[224,768]{1,0:T(8,128)(2,1)S(1)}, bf16[224,768]{1,0:T(8,128)(2,1)S(1)}, u32[]{:S(2)}, u32[]{:S(2)}) %collective-permute-start.45) | collective-permute-done | bytes 344096 | tf_op jit(solution)/shard_map/ppermute | solution.py:504
  261.6 7.6 %collective-permute-done.53 = bf16[2,104,768]{2,1,0:T(8,128)(2,1)S(1)} collective-permute-done((bf16[2,104,768]{2,1,0:T(8,128)(2,1)S(1)}, bf16[2,104,768]{2,1,0:T(8,128)(2,1)S(1)}, u32[]{:S(2)}, u32[]{:S(2)}) %collective-permute-start.53) | collective-permute-done | bytes 319520 | tf_op jit(solution)/shard_map/ppermute | solution.py:504
  272.8 5.4 %collective-permute-done.54 = bf16[1,104,768]{2,1,0:T(8,128)(2,1)S(1)} collective-permute-done((bf16[1,104,768]{2,1,0:T(8,128)(2,1)S(1)}, bf16[1,104,768]{2,1,0:T(8,128)(2,1)S(1)}, u32[]{:S(2)}, u32[]{:S(2)}) %collective-permute-start.54) | collective-permute-done | bytes 159776 | tf_op jit(solution)/shard_map/ppermute | solution.py:504
  278.4 2.2 finish_grad.2.rest_0_
  280.6 7.6 %collective-permute-done.55 = bf16[1,104,768]{2,1,0:T(8,128)(2,1)S(1)} collective-permute-done((bf16[1,104,768]{2,1,0:T(8,128)(2,1)S(1)}, bf16[1,104,768]{2,1,0:T(8,128)(2,1)S(1)}, u32[]{:S(2)}, u32[]{:S(2)}) %collective-permute-start.55) | collective-permute-done | bytes 159776 | tf_op jit(solution)/shard_map/ppermute | solution.py:504
  288.3 2.2 finish_grad.3
  290.5 7.2 %collective-permute-done.56 = bf16[2,104,768]{2,1,0:T(8,128)(2,1)S(1)} collective-permute-done((bf16[2,104,768]{2,1,0:T(8,128)(2,1)S(1)}, bf16[2,104,768]{2,1,0:T(8,128)(2,1)S(1)}, u32[]{:S(2)}, u32[]{:S(2)}) %collective-permute-start.56) | collective-permute-done | bytes 319520 | tf_op jit(solution)/shard_map/ppermute | solution.py:504
  299.4 1.8 unpack.3
  302.4 11.0 %collective-permute-done.57.far = bf16[4,104,768]{2,1,0:T(8,128)(2,1)S(1)} collective-permute-done((bf16[4,104,768]{2,1,0:T(8,128)(2,1)S(1)}, bf16[4,104,768]{2,1,0:T(8,128)(2,1)S(1)}, u32[]{:S(2)}, u32[]{:S(2)}) %collective-permute-start.57) | collective-permute-done | bytes 639008 | tf_op jit(solution)/shard_map/ppermute | solution.py:504
  313.4 1.8 unpack.2
  316.4 1.7 collective-permute-start.59
  (370 shorter events, 74.6 us)
Async XLA Ops:
  7.2 227.5 %all-reduce.2.cloned.1.call-start = ((), (), s32[]{:S(2)}) async-start(), calls=%async_computation | async-start | bytes 4767744 | tf_op jit(solution)/shard_map/psum | solution.py:639
  29.3 11.9 %collective-permute-start.5 = (bf16[224,768]{1,0:T(8,128)(2,1)S(1)}, bf16[224,768]{1,0:T(8,128)(2,1)S(1)}, u32[]{:S(2)}, u32[]{:S(2)}) collective-permute-start(bf16[224,768]{1,0:T(8,128)(2,1)S(1)} %add_convert_fusion.14.s0), channel_id=1, source_target_pairs={{0,2},{1,3},{2,0},{3,1},{4,6},{5,7},{6,4},{7,5},{8,10},{9,11},{10,... | collective-permute-start | bytes 1032200 | tf_op jit(solution)/shard_map/ppermute | solution.py:504
  34.6 13.3 %collective-permute-start.1 = (bf16[224,768]{1,0:T(8,128)(2,1)S(1)}, bf16[224,768]{1,0:T(8,128)(2,1)S(1)}, u32[]{:S(2)}, u32[]{:S(2)}) collective-permute-start(bf16[224,768]{1,0:T(8,128)(2,1)S(1)} %add_convert_fusion.15.s0), channel_id=1, source_target_pairs={{0,2},{1,3},{2,0},{3,1},{4,6},{5,7},{6,4},{7,5},{8,10},{9,11},{10,... | collective-permute-start | bytes 1032200 | tf_op jit(solution)/shard_map/ppermute | solution.py:504
  34.9 13.0 %collective-permute-start.6 = (bf16[224,768]{1,0:T(8,128)(2,1)S(1)}, bf16[224,768]{1,0:T(8,128)(2,1)S(1)}, u32[]{:S(2)}, u32[]{:S(2)}) collective-permute-start(bf16[224,768]{1,0:T(8,128)(2,1)S(1)} %add_convert_fusion.14.s0), channel_id=1, source_target_pairs={{0,1},{1,0},{2,3},{3,2},{4,5},{5,4},{6,7},{7,6},{8,9},{9,8},{10,11... | collective-permute-start | bytes 1032200 | tf_op jit(solution)/shard_map/ppermute | solution.py:504
  41.2 15.3 %collective-permute-start.2 = (bf16[224,768]{1,0:T(8,128)(2,1)S(1)}, bf16[224,768]{1,0:T(8,128)(2,1)S(1)}, u32[]{:S(2)}, u32[]{:S(2)}) collective-permute-start(bf16[224,768]{1,0:T(8,128)(2,1)S(1)} %add_convert_fusion.15.s0), channel_id=1, source_target_pairs={{0,1},{1,0},{2,3},{3,2},{4,5},{5,4},{6,7},{7,6},{8,9},{9,8},{10,11... | collective-permute-start | bytes 1032200 | tf_op jit(solution)/shard_map/ppermute | solution.py:504
  53.8 10.2 %collective-permute-start.13 = (bf16[224,768]{1,0:T(8,128)(2,1)S(1)}, bf16[224,768]{1,0:T(8,128)(2,1)S(1)}, u32[]{:S(2)}, u32[]{:S(2)}) collective-permute-start(bf16[224,768]{1,0:T(8,128)(2,1)S(1)} %get-tuple-element.160), channel_id=1, source_target_pairs={{0,1},{1,0},{2,3},{3,2},{4,5},{5,4},{6,7},{7,6},{8,9},{9,8},{10,11... | collective-permute-start | bytes 1032200 | tf_op jit(solution)/shard_map/ppermute | solution.py:504
  64.0 10.9 %collective-permute-start.14 = (bf16[224,768]{1,0:T(8,128)(2,1)S(1)}, bf16[224,768]{1,0:T(8,128)(2,1)S(1)}, u32[]{:S(2)}, u32[]{:S(2)}) collective-permute-start(bf16[224,768]{1,0:T(8,128)(2,1)S(1)} %add_convert_fusion.12.s0), channel_id=1, source_target_pairs={{0,2},{1,3},{2,0},{3,1},{4,6},{5,7},{6,4},{7,5},{8,10},{9,11},{10,... | collective-permute-start | bytes 1032200 | tf_op jit(solution)/shard_map/ppermute | solution.py:504
  65.9 16.0 %collective-permute-start.9 = (bf16[224,768]{1,0:T(8,128)(2,1)S(1)}, bf16[224,768]{1,0:T(8,128)(2,1)S(1)}, u32[]{:S(2)}, u32[]{:S(2)}) collective-permute-start(bf16[224,768]{1,0:T(8,128)(2,1)S(1)} %add_convert_fusion.13.s0), channel_id=1, source_target_pairs={{0,2},{1,3},{2,0},{3,1},{4,6},{5,7},{6,4},{7,5},{8,10},{9,11},{10,... | collective-permute-start | bytes 1032200 | tf_op jit(solution)/shard_map/ppermute | solution.py:504
  67.4 14.5 %collective-permute-start.15 = (bf16[224,768]{1,0:T(8,128)(2,1)S(1)}, bf16[224,768]{1,0:T(8,128)(2,1)S(1)}, u32[]{:S(2)}, u32[]{:S(2)}) collective-permute-start(bf16[224,768]{1,0:T(8,128)(2,1)S(1)} %add_convert_fusion.12.s0), channel_id=1, source_target_pairs={{0,1},{1,0},{2,3},{3,2},{4,5},{5,4},{6,7},{7,6},{8,9},{9,8},{10,11... | collective-permute-start | bytes 1032200 | tf_op jit(solution)/shard_map/ppermute | solution.py:504
  75.0 13.5 %collective-permute-start.10 = (bf16[224,768]{1,0:T(8,128)(2,1)S(1)}, bf16[224,768]{1,0:T(8,128)(2,1)S(1)}, u32[]{:S(2)}, u32[]{:S(2)}) collective-permute-start(bf16[224,768]{1,0:T(8,128)(2,1)S(1)} %add_convert_fusion.13.s0), channel_id=1, source_target_pairs={{0,1},{1,0},{2,3},{3,2},{4,5},{5,4},{6,7},{7,6},{8,9},{9,8},{10,11... | collective-permute-start | bytes 1032200 | tf_op jit(solution)/shard_map/ppermute | solution.py:504
  93.2 10.9 %collective-permute-start.18 = (bf16[224,768]{1,0:T(8,128)(2,1)S(1)}, bf16[224,768]{1,0:T(8,128)(2,1)S(1)}, u32[]{:S(2)}, u32[]{:S(2)}) collective-permute-start(bf16[224,768]{1,0:T(8,128)(2,1)S(1)} %add_convert_fusion.11.s0), channel_id=1, source_target_pairs={{0,2},{1,3},{2,0},{3,1},{4,6},{5,7},{6,4},{7,5},{8,10},{9,11},{10,... | collective-permute-start | bytes 1032200 | tf_op jit(solution)/shard_map/ppermute | solution.py:504
  95.0 33.3 %collective-permute-start.12 = (bf16[224,768]{1,0:T(8,128)(2,1)S(1)}, bf16[224,768]{1,0:T(8,128)(2,1)}, u32[]{:S(2)}, u32[]{:S(2)}) collective-permute-start(bf16[224,768]{1,0:T(8,128)(2,1)S(1)} %get-tuple-element.157), channel_id=1, source_target_pairs={{0,1},{1,0},{2,3},{3,2},{4,5},{5,4},{6,7},{7,6},{8,9},{9,8},{10,11... | collective-permute-start | bytes 1032200 | tf_op jit(solution)/shard_map/ppermute | solution.py:504
  95.2 33.1 %collective-permute-start.24 = (bf16[224,768]{1,0:T(8,128)(2,1)S(1)}, bf16[224,768]{1,0:T(8,128)(2,1)}, u32[]{:S(2)}, u32[]{:S(2)}) collective-permute-start(bf16[224,768]{1,0:T(8,128)(2,1)S(1)} %get-tuple-element.172), channel_id=1, source_target_pairs={{0,1},{1,0},{2,3},{3,2},{4,5},{5,4},{6,7},{7,6},{8,9},{9,8},{10,11... | collective-permute-start | bytes 1032200 | tf_op jit(solution)/shard_map/ppermute | solution.py:504
  95.5 12.8 %collective-permute-start.19 = (bf16[224,768]{1,0:T(8,128)(2,1)S(1)}, bf16[224,768]{1,0:T(8,128)(2,1)S(1)}, u32[]{:S(2)}, u32[]{:S(2)}) collective-permute-start(bf16[224,768]{1,0:T(8,128)(2,1)S(1)} %add_convert_fusion.11.s0), channel_id=1, source_target_pairs={{0,1},{1,0},{2,3},{3,2},{4,5},{5,4},{6,7},{7,6},{8,9},{9,8},{10,11... | collective-permute-start | bytes 1032200 | tf_op jit(solution)/shard_map/ppermute | solution.py:504
  95.8 15.3 %collective-permute-start.29 = (bf16[224,768]{1,0:T(8,128)(2,1)S(1)}, bf16[224,768]{1,0:T(8,128)(2,1)S(1)}, u32[]{:S(2)}, u32[]{:S(2)}) collective-permute-start(bf16[224,768]{1,0:T(8,128)(2,1)S(1)} %add_convert_fusion.8.s0), channel_id=1, source_target_pairs={{0,2},{1,3},{2,0},{3,1},{4,6},{5,7},{6,4},{7,5},{8,10},{9,11},{10,... | collective-permute-start | bytes 1032200 | tf_op jit(solution)/shard_map/ppermute | solution.py:504
  108.2 22.9 %collective-permute-start.30 = (bf16[224,768]{1,0:T(8,128)(2,1)S(1)}, bf16[224,768]{1,0:T(8,128)(2,1)S(1)}, u32[]{:S(2)}, u32[]{:S(2)}) collective-permute-start(bf16[224,768]{1,0:T(8,128)(2,1)S(1)} %add_convert_fusion.8.s0), channel_id=1, source_target_pairs={{0,1},{1,0},{2,3},{3,2},{4,5},{5,4},{6,7},{7,6},{8,9},{9,8},{10,11... | collective-permute-start | bytes 1032200 | tf_op jit(solution)/shard_map/ppermute | solution.py:504
  111.0 20.1 %collective-permute-start.31 = (bf16[224,768]{1,0:T(8,128)(2,1)S(1)}, bf16[224,768]{1,0:T(8,128)(2,1)S(1)}, u32[]{:S(2)}, u32[]{:S(2)}) collective-permute-start(bf16[224,768]{1,0:T(8,128)(2,1)S(1)} %collective-permute-done.29.s1), channel_id=1, source_target_pairs={{0,1},{1,0},{2,3},{3,2},{4,5},{5,4},{6,7},{7,6},{8,9},{9,8},{10,11... | collective-permute-start | bytes 1032200 | tf_op jit(solution)/shard_map/ppermute | solution.py:504
  129.3 21.3 %collective-permute-start.25 = (bf16[224,768]{1,0:T(8,128)(2,1)S(1)}, bf16[224,768]{1,0:T(8,128)(2,1)S(1)}, u32[]{:S(2)}, u32[]{:S(2)}) collective-permute-start(bf16[224,768]{1,0:T(8,128)(2,1)S(1)} %add_convert_fusion.9.s0), channel_id=1, source_target_pairs={{0,2},{1,3},{2,0},{3,1},{4,6},{5,7},{6,4},{7,5},{8,10},{9,11},{10,... | collective-permute-start | bytes 1032200 | tf_op jit(solution)/shard_map/ppermute | solution.py:504
  139.6 10.3 %collective-permute-start.32 = (bf16[224,768]{1,0:T(8,128)(2,1)S(1)}, bf16[224,768]{1,0:T(8,128)(2,1)S(1)}, u32[]{:S(2)}, u32[]{:S(2)}) collective-permute-start(bf16[224,768]{1,0:T(8,128)(2,1)S(1)} %get-tuple-element.181), channel_id=1, source_target_pairs={{0,1},{1,0},{2,3},{3,2},{4,5},{5,4},{6,7},{7,6},{8,9},{9,8},{10,11... | collective-permute-start | bytes 1032200 | tf_op jit(solution)/shard_map/ppermute | solution.py:504
  139.8 10.2 %collective-permute-start.40 = (bf16[224,768]{1,0:T(8,128)(2,1)S(1)}, bf16[224,768]{1,0:T(8,128)(2,1)S(1)}, u32[]{:S(2)}, u32[]{:S(2)}) collective-permute-start(bf16[224,768]{1,0:T(8,128)(2,1)S(1)} %get-tuple-element.195), channel_id=1, source_target_pairs={{0,1},{1,0},{2,3},{3,2},{4,5},{5,4},{6,7},{7,6},{8,9},{9,8},{10,11... | collective-permute-start | bytes 1032200 | tf_op jit(solution)/shard_map/ppermute | solution.py:504
  146.7 21.0 %collective-permute-start.60 = (bf16[4,104,768]{2,1,0:T(8,128)(2,1)S(1)}, bf16[4,104,768]{2,1,0:T(8,128)(2,1)S(1)}, u32[]{:S(2)}, u32[]{:S(2)}) collective-permute-start(bf16[4,104,768]{2,1,0:T(8,128)(2,1)S(1)} %get-tuple-element.234), channel_id=1, source_target_pairs={{0,4},{4,0},{8,12},{12,8},{16,20},{20,16},{24,28},{28,24},{1,5},{5... | collective-permute-start | bytes 1916936 | tf_op jit(solution)/shard_map/ppermute | solution.py:504
  149.3 10.0 %collective-permute-start.21 = (bf16[224,768]{1,0:T(8,128)(2,1)S(1)}, bf16[224,768]{1,0:T(8,128)(2,1)S(1)}, u32[]{:S(2)}, u32[]{:S(2)}) collective-permute-start(bf16[224,768]{1,0:T(8,128)(2,1)S(1)} %add_convert_fusion.10.s0), channel_id=1, source_target_pairs={{0,2},{1,3},{2,0},{3,1},{4,6},{5,7},{6,4},{7,5},{8,10},{9,11},{10,... | collective-permute-start | bytes 1032200 | tf_op jit(solution)/shard_map/ppermute | solution.py:504
  149.9 21.5 %collective-permute-start.22 = (bf16[224,768]{1,0:T(8,128)(2,1)S(1)}, bf16[224,768]{1,0:T(8,128)(2,1)S(1)}, u32[]{:S(2)}, u32[]{:S(2)}) collective-permute-start(bf16[224,768]{1,0:T(8,128)(2,1)S(1)} %add_convert_fusion.10.s0), channel_id=1, source_target_pairs={{0,1},{1,0},{2,3},{3,2},{4,5},{5,4},{6,7},{7,6},{8,9},{9,8},{10,11... | collective-permute-start | bytes 1032200 | tf_op jit(solution)/shard_map/ppermute | solution.py:504
  150.0 17.8 %collective-permute-start.26 = (bf16[224,768]{1,0:T(8,128)(2,1)S(1)}, bf16[224,768]{1,0:T(8,128)(2,1)S(1)}, u32[]{:S(2)}, u32[]{:S(2)}) collective-permute-start(bf16[224,768]{1,0:T(8,128)(2,1)S(1)} %add_convert_fusion.9.s0), channel_id=1, source_target_pairs={{0,1},{1,0},{2,3},{3,2},{4,5},{5,4},{6,7},{7,6},{8,9},{9,8},{10,11... | collective-permute-start | bytes 1032200 | tf_op jit(solution)/shard_map/ppermute | solution.py:504
  150.6 17.8 %collective-permute-start.27 = (bf16[224,768]{1,0:T(8,128)(2,1)S(1)}, bf16[224,768]{1,0:T(8,128)(2,1)S(1)}, u32[]{:S(2)}, u32[]{:S(2)}) collective-permute-start(bf16[224,768]{1,0:T(8,128)(2,1)S(1)} %collective-permute-done.25.s1), channel_id=1, source_target_pairs={{0,1},{1,0},{2,3},{3,2},{4,5},{5,4},{6,7},{7,6},{8,9},{9,8},{10,11... | collective-permute-start | bytes 1032200 | tf_op jit(solution)/shard_map/ppermute | solution.py:504
  159.3 12.7 %collective-permute-start.33 = (bf16[224,768]{1,0:T(8,128)(2,1)S(1)}, bf16[224,768]{1,0:T(8,128)(2,1)S(1)}, u32[]{:S(2)}, u32[]{:S(2)}) collective-permute-start(bf16[224,768]{1,0:T(8,128)(2,1)S(1)} %add_convert_fusion.7.s0), channel_id=1, source_target_pairs={{0,2},{1,3},{2,0},{3,1},{4,6},{5,7},{6,4},{7,5},{8,10},{9,11},{10,... | collective-permute-start | bytes 1032200 | tf_op jit(solution)/shard_map/ppermute | solution.py:504
  167.9 33.6 %collective-permute-start.50 = (bf16[2,192,1500]{2,1,0:T(8,128)(2,1)S(1)}, bf16[2,192,1500]{2,1,0:T(8,128)(2,1)S(1)}, u32[]{:S(2)}, u32[]{:S(2)}) collective-permute-start(bf16[2,192,1500]{2,1,0:T(8,128)(2,1)S(1)} %get-tuple-element.214), channel_id=1, source_target_pairs={{0,1},{1,0},{2,3},{3,2},{4,5},{5,4},{6,7},{7,6},{8,9},{9,8},{10,11... | collective-permute-start | bytes 3456008 | tf_op jit(solution)/shard_map/ppermute | solution.py:504
  168.4 11.3 %collective-permute-start.61 = (bf16[2,104,768]{2,1,0:T(8,128)(2,1)S(1)}, bf16[2,104,768]{2,1,0:T(8,128)(2,1)S(1)}, u32[]{:S(2)}, u32[]{:S(2)}) collective-permute-start(bf16[2,104,768]{2,1,0:T(8,128)(2,1)S(1)} %get-tuple-element.262), channel_id=1, source_target_pairs={{0,8},{4,12},{8,0},{12,4},{16,24},{20,28},{24,16},{28,20},{1,9},{5... | collective-permute-start | bytes 958472 | tf_op jit(solution)/shard_map/ppermute | solution.py:504
  171.5 10.5 %collective-permute-start.41 = (bf16[224,768]{1,0:T(8,128)(2,1)S(1)}, bf16[224,768]{1,0:T(8,128)(2,1)S(1)}, u32[]{:S(2)}, u32[]{:S(2)}) collective-permute-start(bf16[224,768]{1,0:T(8,128)(2,1)S(1)} %add_convert_fusion.5.s0), channel_id=1, source_target_pairs={{0,2},{1,3},{2,0},{3,1},{4,6},{5,7},{6,4},{7,5},{8,10},{9,11},{10,... | collective-permute-start | bytes 1032200 | tf_op jit(solution)/shard_map/ppermute | solution.py:504
  172.1 9.9 %collective-permute-start.35 = (bf16[224,768]{1,0:T(8,128)(2,1)S(1)}, bf16[224,768]{1,0:T(8,128)(2,1)S(1)}, u32[]{:S(2)}, u32[]{:S(2)}) collective-permute-start(bf16[224,768]{1,0:T(8,128)(2,1)S(1)} %collective-permute-done.33.s1), channel_id=1, source_target_pairs={{0,1},{1,0},{2,3},{3,2},{4,5},{5,4},{6,7},{7,6},{8,9},{9,8},{10,11... | collective-permute-start | bytes 1032200 | tf_op jit(solution)/shard_map/ppermute | solution.py:504
  179.7 23.2 %collective-permute-start.48 = (bf16[2,192,1500]{2,1,0:T(8,128)(2,1)S(1)}, bf16[2,192,1500]{2,1,0:T(8,128)(2,1)S(1)}, u32[]{:S(2)}, u32[]{:S(2)}) collective-permute-start(bf16[2,192,1500]{2,1,0:T(8,128)(2,1)S(1)} %get-tuple-element.210), channel_id=1, source_target_pairs={{0,1},{1,0},{2,3},{3,2},{4,5},{5,4},{6,7},{7,6},{8,9},{9,8},{10,11... | collective-permute-start | bytes 3456008 | tf_op jit(solution)/shard_map/ppermute | solution.py:504
  179.8 11.2 %collective-permute-start.42 = (bf16[224,768]{1,0:T(8,128)(2,1)S(1)}, bf16[224,768]{1,0:T(8,128)(2,1)S(1)}, u32[]{:S(2)}, u32[]{:S(2)}) collective-permute-start(bf16[224,768]{1,0:T(8,128)(2,1)S(1)} %add_convert_fusion.5.s0), channel_id=1, source_target_pairs={{0,1},{1,0},{2,3},{3,2},{4,5},{5,4},{6,7},{7,6},{8,9},{9,8},{10,11... | collective-permute-start | bytes 1032200 | tf_op jit(solution)/shard_map/ppermute | solution.py:504
  182.0 18.1 %collective-permute-start.62 = (bf16[1,104,768]{2,1,0:T(8,128)(2,1)S(1)}, bf16[1,104,768]{2,1,0:T(8,128)(2,1)S(1)}, u32[]{:S(2)}, u32[]{:S(2)}) collective-permute-start(bf16[1,104,768]{2,1,0:T(8,128)(2,1)S(1)} %add_convert_fusion.21), channel_id=1, source_target_pairs={{0,16},{4,20},{8,24},{12,28},{16,0},{20,4},{24,8},{28,12},{1,17},{... | collective-permute-start | bytes 479240 | tf_op jit(solution)/shard_map/ppermute | solution.py:504
  191.0 49.3 %collective-permute-start.36 = (bf16[224,768]{1,0:T(8,128)(2,1)}, bf16[224,768]{1,0:T(8,128)(2,1)}, u32[]{:S(2)}, u32[]{:S(2)}) collective-permute-start(bf16[224,768]{1,0:T(8,128)(2,1)} %get-tuple-element.191), channel_id=1, source_target_pairs={{0,1},{1,0},{2,3},{3,2},{4,5},{5,4},{6,7},{7,6},{8,9},{9,8},{10,11... | collective-permute-start | bytes 1032200 | tf_op jit(solution)/shard_map/ppermute | solution.py:504
  196.4 44.9 %collective-permute-start.44 = (bf16[224,768]{1,0:T(8,128)(2,1)}, bf16[224,768]{1,0:T(8,128)(2,1)}, u32[]{:S(2)}, u32[]{:S(2)}) collective-permute-start(bf16[224,768]{1,0:T(8,128)(2,1)} %get-tuple-element.205), channel_id=1, source_target_pairs={{0,1},{1,0},{2,3},{3,2},{4,5},{5,4},{6,7},{7,6},{8,9},{9,8},{10,11... | collective-permute-start | bytes 1032200 | tf_op jit(solution)/shard_map/ppermute | solution.py:504
  200.0 49.4 %collective-permute-start.52 = (bf16[4,104,768]{2,1,0:T(8,128)(2,1)}, bf16[4,104,768]{2,1,0:T(8,128)(2,1)}, u32[]{:S(2)}, u32[]{:S(2)}) collective-permute-start(bf16[4,104,768]{2,1,0:T(8,128)(2,1)} %get-tuple-element.221), channel_id=1, source_target_pairs={{0,4},{4,0},{8,12},{12,8},{16,20},{20,16},{24,28},{28,24},{1,5},{5... | collective-permute-start | bytes 1916936 | tf_op jit(solution)/shard_map/ppermute | solution.py:504
  201.5 20.1 %collective-permute-start.63 = (bf16[1,104,768]{2,1,0:T(8,128)(2,1)S(1)}, bf16[1,104,768]{2,1,0:T(8,128)(2,1)S(1)}, u32[]{:S(2)}, u32[]{:S(2)}) collective-permute-start(bf16[1,104,768]{2,1,0:T(8,128)(2,1)S(1)} %add_convert_fusion.20), channel_id=1, source_target_pairs={{0,16},{4,20},{8,24},{12,28},{16,0},{20,4},{24,8},{28,12},{1,17},{... | collective-permute-start | bytes 479240 | tf_op jit(solution)/shard_map/ppermute | solution.py:504
  203.0 49.3 %collective-permute-start.51 = (bf16[192,1500]{1,0:T(8,128)(2,1)}, bf16[192,1500]{1,0:T(8,128)(2,1)}, u32[]{:S(2)}, u32[]{:S(2)}) collective-permute-start(bf16[192,1500]{1,0:T(8,128)(2,1)} %fusion.5), channel_id=1, source_target_pairs={{0,2},{1,3},{2,0},{3,1},{4,6},{5,7},{6,4},{7,5},{8,10},{9,11},{10,... | collective-permute-start | bytes 1728008 | tf_op jit(solution)/shard_map/ppermute | solution.py:504
  221.6 38.7 %collective-permute-start.49 = (bf16[192,1500]{1,0:T(8,128)(2,1)}, bf16[192,1500]{1,0:T(8,128)(2,1)}, u32[]{:S(2)}, u32[]{:S(2)}) collective-permute-start(bf16[192,1500]{1,0:T(8,128)(2,1)} %fusion.3), channel_id=1, source_target_pairs={{0,2},{1,3},{2,0},{3,1},{4,6},{5,7},{6,4},{7,5},{8,10},{9,11},{10,... | collective-permute-start | bytes 1728008 | tf_op jit(solution)/shard_map/ppermute | solution.py:504
  241.3 29.9 %collective-permute-start.37 = (bf16[224,768]{1,0:T(8,128)(2,1)S(1)}, bf16[224,768]{1,0:T(8,128)(2,1)S(1)}, u32[]{:S(2)}, u32[]{:S(2)}) collective-permute-start(bf16[224,768]{1,0:T(8,128)(2,1)S(1)} %add_convert_fusion.6.s0), channel_id=1, source_target_pairs={{0,2},{1,3},{2,0},{3,1},{4,6},{5,7},{6,4},{7,5},{8,10},{9,11},{10,... | collective-permute-start | bytes 1032200 | tf_op jit(solution)/shard_map/ppermute | solution.py:504
  249.3 38.9 %collective-permute-start.38 = (bf16[224,768]{1,0:T(8,128)(2,1)S(1)}, bf16[224,768]{1,0:T(8,128)(2,1)S(1)}, u32[]{:S(2)}, u32[]{:S(2)}) collective-permute-start(bf16[224,768]{1,0:T(8,128)(2,1)S(1)} %add_convert_fusion.6.s0), channel_id=1, source_target_pairs={{0,1},{1,0},{2,3},{3,2},{4,5},{5,4},{6,7},{7,6},{8,9},{9,8},{10,11... | collective-permute-start | bytes 1032200 | tf_op jit(solution)/shard_map/ppermute | solution.py:504
  249.4 10.5 %collective-permute-start.45 = (bf16[224,768]{1,0:T(8,128)(2,1)S(1)}, bf16[224,768]{1,0:T(8,128)(2,1)S(1)}, u32[]{:S(2)}, u32[]{:S(2)}) collective-permute-start(bf16[224,768]{1,0:T(8,128)(2,1)S(1)} %add_convert_fusion.4.s0), channel_id=1, source_target_pairs={{0,2},{1,3},{2,0},{3,1},{4,6},{5,7},{6,4},{7,5},{8,10},{9,11},{10,... | collective-permute-start | bytes 1032200 | tf_op jit(solution)/shard_map/ppermute | solution.py:504
  252.2 26.0 %collective-permute-start.46 = (bf16[224,768]{1,0:T(8,128)(2,1)S(1)}, bf16[224,768]{1,0:T(8,128)(2,1)S(1)}, u32[]{:S(2)}, u32[]{:S(2)}) collective-permute-start(bf16[224,768]{1,0:T(8,128)(2,1)S(1)} %add_convert_fusion.4.s0), channel_id=1, source_target_pairs={{0,1},{1,0},{2,3},{3,2},{4,5},{5,4},{6,7},{7,6},{8,9},{9,8},{10,11... | collective-permute-start | bytes 1032200 | tf_op jit(solution)/shard_map/ppermute | solution.py:504
  260.3 18.1 %collective-permute-start.47 = (bf16[224,768]{1,0:T(8,128)(2,1)S(1)}, bf16[224,768]{1,0:T(8,128)(2,1)S(1)}, u32[]{:S(2)}, u32[]{:S(2)}) collective-permute-start(bf16[224,768]{1,0:T(8,128)(2,1)S(1)} %collective-permute-done.45.s1), channel_id=1, source_target_pairs={{0,1},{1,0},{2,3},{3,2},{4,5},{5,4},{6,7},{7,6},{8,9},{9,8},{10,11... | collective-permute-start | bytes 1032200 | tf_op jit(solution)/shard_map/ppermute | solution.py:504
  271.2 28.2 %collective-permute-start.65 = (bf16[4,104,768]{2,1,0:T(8,128)(2,1)S(1)}, bf16[4,104,768]{2,1,0:T(8,128)(2,1)S(1)}, u32[]{:S(2)}, u32[]{:S(2)}) collective-permute-start(bf16[4,104,768]{2,1,0:T(8,128)(2,1)S(1)} %pad_maximum_fusion.1.near), channel_id=1, source_target_pairs={{0,4},{4,0},{8,12},{12,8},{16,20},{20,16},{24,28},{28,24},{1,5},{5... | collective-permute-start | bytes 1916936 | tf_op jit(solution)/shard_map/ppermute | solution.py:504
  278.2 10.1 %collective-permute-start.39 = (bf16[224,768]{1,0:T(8,128)(2,1)S(1)}, bf16[224,768]{1,0:T(8,128)(2,1)S(1)}, u32[]{:S(2)}, u32[]{:S(2)}) collective-permute-start(bf16[224,768]{1,0:T(8,128)(2,1)S(1)} %collective-permute-done.37.s1), channel_id=1, source_target_pairs={{0,1},{1,0},{2,3},{3,2},{4,5},{5,4},{6,7},{7,6},{8,9},{9,8},{10,11... | collective-permute-start | bytes 1032200 | tf_op jit(solution)/shard_map/ppermute | solution.py:504
  278.3 9.9 %collective-permute-start.55 = (bf16[1,104,768]{2,1,0:T(8,128)(2,1)S(1)}, bf16[1,104,768]{2,1,0:T(8,128)(2,1)S(1)}, u32[]{:S(2)}, u32[]{:S(2)}) collective-permute-start(bf16[1,104,768]{2,1,0:T(8,128)(2,1)S(1)} %add_convert_fusion.23), channel_id=1, source_target_pairs={{0,16},{4,20},{8,24},{12,28},{16,0},{20,4},{24,8},{28,12},{1,17},{... | collective-permute-start | bytes 479240 | tf_op jit(solution)/shard_map/ppermute | solution.py:504
  297.8 15.6 %collective-permute-start.57 = (bf16[4,104,768]{2,1,0:T(8,128)(2,1)S(1)}, bf16[4,104,768]{2,1,0:T(8,128)(2,1)S(1)}, u32[]{:S(2)}, u32[]{:S(2)}) collective-permute-start(bf16[4,104,768]{2,1,0:T(8,128)(2,1)S(1)} %pad_maximum_fusion.near), channel_id=1, source_target_pairs={{0,4},{4,0},{8,12},{12,8},{16,20},{20,16},{24,28},{28,24},{1,5},{5... | collective-permute-start | bytes 1916936 | tf_op jit(solution)/shard_map/ppermute | solution.py:504
  (129 other events, 1049.2 us)
Sparse Core Ops, SparseCore 0:
  108.3 126.2 all-reduce.1

commit v2 on v1

--- a/solution.py
+++ b/solution.py
@@ -16,7 +16,8 @@
 BF16 = jnp.bfloat16
 ROOT_HALF = math.sqrt(0.5)
 INV_ROOT_TAU = 1.0 / math.sqrt(2.0 * math.pi)
-VMEM_BYTES = 28 * 1024 * 1024
+VMEM_BYTES = 20 * 1024 * 1024
+COST = 1
 
 
 def dot(left, right, left_dim, right_dim):
@@ -101,19 +102,22 @@
     return jnp.where(rows == first + 2, last, out).astype(BF16)
 
 
-def store_halves(part, side, keep_ref, send_ref):
+def store_halves(part, side, keep_ref, send_ref, rest_ref):
     half = part.shape[0] // 2
+    edge = send_ref.shape[0]
     low = part.astype(BF16)
 
     @pl.when(side == 0)
     def _():
         keep_ref[...] = low[:half]
-        send_ref[...] = low[half:]
+        send_ref[...] = low[half : half + edge]
+        rest_ref[...] = low[half + edge :]
 
     @pl.when(side == 1)
     def _():
         keep_ref[...] = low[half:]
-        send_ref[...] = low[:half]
+        send_ref[...] = low[:edge]
+        rest_ref[...] = low[edge:half]
 
 
 def join_halves(pieces, side, scratch):
@@ -206,7 +210,7 @@
     return nt(ones, matrix)[0:1]
 
 
-def self_forward(item, lengths, x_ref, gain, shift, wq, qbias, wk, wv, vbias, wo, q_o, ka_o, va_o, o_o, lse_o, keep_o, send_o, qa):
+def self_forward(item, lengths, x_ref, gain, shift, wq, qbias, wk, wv, vbias, wo, q_o, ka_o, va_o, o_o, lse_o, keep_o, send_o, rest_o, qa):
     count = x_ref.shape[1]
     unit, _ = norm_parts(x_ref[item].astype(F32))
     normed = (unit * line(gain) + line(shift)).astype(BF16)
@@ -223,7 +227,20 @@
         va_o[head, 0:HEAD, :] = value_rows[spot]
         va_o[head, HEAD:AUG, :] = other
     attention_forward(q_o, ka_o, va_o, qa, o_o, lse_o, count, True)
-    store_halves(tn(o_o[...], wo[...]), mp_side(), keep_o, send_o)
+    store_halves(tn(o_o[...], wo[...]), mp_side(), keep_o, send_o, rest_o)
+
+
+def first_forward(item, first, count, lengths, *refs):
+    sources, targets = refs[:count], refs[count + 8 : 2 * count + 8]
+    outs, qa, sems = refs[count : count + 8], refs[-2], refs[-1]
+    copies = [pltpu.make_async_copy(s, t, sems.at[k]) for k, (s, t) in enumerate(zip(sources, targets))]
+    for copy in copies:
+        copy.start()
+    for copy in copies[:first]:
+        copy.wait()
+    self_forward(item, lengths, *targets[:first], *outs, qa)
+    for copy in copies[first:]:
+        copy.wait()
 
 
 def cross_keys(item, frames, enc, wk, wv, vbias, ka_o, va_o):
@@ -245,7 +262,7 @@
         va_o[head, HEAD:AUG, :] = other
 
 
-def cross_forward(item, chunk, x_ref, s0, s1, s2, s3, obias, gain, shift, wq, qbias, wo, ka, va, x1_o, h2_o, q_o, o_o, lse_o, keep_o, send_o, whole, qa):
+def cross_forward(item, chunk, x_ref, s0, s1, s2, s3, obias, gain, shift, wq, qbias, wo, ka, va, x1_o, h2_o, q_o, o_o, lse_o, keep_o, send_o, rest_o, whole, qa):
     count = x_ref.shape[1]
     side = mp_side()
     after = x_ref[item].astype(F32) + join_halves((s0, s1, s2, s3), side, whole) + line(obias)
@@ -256,7 +273,7 @@
     queries = (nt(wq[...], normed) + column_bias(qbias, count)).astype(BF16)
     q_o[...] = queries * jnp.asarray(0.125, BF16)
     attention_forward(q_o, ka, va, qa, o_o, lse_o, chunk, False)
-    store_halves(tn(o_o[...], wo[...]), side, keep_o, send_o)
+    store_halves(tn(o_o[...], wo[...]), side, keep_o, send_o, rest_o)
 
 
 def upstream_rows(item, lengths, tasks, og):
@@ -266,7 +283,7 @@
     return og[item].astype(F32) * jnp.where(valid, weight, 0.0)
 
 
-def feed(item, lengths, tasks, x1, s0, s1, s2, s3, og, obias, gain, shift, we, ebias, wc, x2_o, h3_o, a_o, dz_o, gy_o, vec_o, keep_o, send_o, bkeep_o, bsend_o, whole):
+def feed(item, lengths, tasks, x1, s0, s1, s2, s3, og, obias, gain, shift, we, ebias, wc, x2_o, h3_o, a_o, dz_o, gy_o, vec_o, bkeep_o, bsend_o, brest_o, whole):
     side = mp_side()
     after = x1[...] + join_halves((s0, s1, s2, s3), side, whole) + line(obias)
     x2_o[...] = after
@@ -283,11 +300,14 @@
     gy_o[...] = low
     inner = (nt(low, wc[...]) * slope).astype(BF16)
     dz_o[...] = inner
-    store_halves(nt(inner, we[...]), side, bkeep_o, bsend_o)
-    store_halves(nn(active, wc[...]), side, keep_o, send_o)
+    store_halves(nt(inner, we[...]), side, bkeep_o, bsend_o, brest_o)
     pick = iota((8, vec_o.shape[1]), 0)
     out = jnp.where(pick == 0, jnp.sum(grad, axis=0, keepdims=True), 0.0)
     vec_o[...] = jnp.where(pick == 1, jnp.sum(inner.astype(F32), axis=0, keepdims=True), out)
+
+
+def feed_out_part(active, wc, keep_o, send_o, rest_o):
+    store_halves(nn(active[...], wc[...]), mp_side(), keep_o, send_o, rest_o)
 
 
 def sum_of(refs):
@@ -299,18 +319,17 @@
 
 def feed_weights(items, *refs):
     h3, dz, a, gy, vecs = (refs[k * items : (k + 1) * items] for k in range(5))
-    pack = refs[5 * items]
+    keep_o, send_o, whole = refs[5 * items :]
     width = h3[0].shape[1]
-    unit = dz[0].shape[1]
-    pack[0:width, :] = sum_of([tn(h3[k][...], dz[k][...]) for k in range(items)]).astype(BF16)
-    pack[width : width + unit, :] = sum_of([tn(a[k][...], gy[k][...]) for k in range(items)]).astype(BF16)
-    tail = pack.shape[0] - width - unit
-    pack[width + unit :, :] = jnp.zeros((tail, width), BF16)
-    low = sum_of([v[...] for v in vecs]).astype(BF16)
-    pack[width + unit : width + unit + 8, :] = low
-
-
-def cross_backward(item, chunk, lengths, tasks, x2, s0, s1, s2, s3, og, gain, wo, wq, ka, va, q, o, lse, dx2_o, g2_o, dq_o, dk_o, dv_o, vec_o, keep_o, send_o, whole, qa, doa, do):
+    edge = width + dz[0].shape[1]
+    whole[0:width, :] = sum_of([tn(h3[k][...], dz[k][...]) for k in range(items)])
+    whole[width:edge, :] = sum_of([tn(a[k][...], gy[k][...]) for k in range(items)])
+    whole[edge:, :] = jnp.zeros((whole.shape[0] - edge, width), F32)
+    whole[edge : edge + 8, :] = sum_of([v[...] for v in vecs])
+    scatter_blocks(whole, keep_o, send_o)
+
+
+def cross_backward(item, chunk, lengths, tasks, x2, s0, s1, s2, s3, og, gain, wo, wq, ka, va, q, o, lse, dx2_o, g2_o, dq_o, dk_o, dv_o, vec_o, keep_o, send_o, rest_o, whole, qa, doa, do):
     side = mp_side()
     grad_in = join_halves((s0, s1, s2, s3), side, whole)
     grad, gain_row, shift_row = norm_back(x2[...], line(gain), grad_in)
@@ -320,7 +339,7 @@
     g2_o[...] = low
     do[...] = nt(wo[...], low).astype(BF16)
     attention_backward(q, ka, va, o, lse, do, qa, doa, dq_o, dk_o, dv_o, chunk, False)
-    store_halves(tn(dq_o[...], wq[...]), side, keep_o, send_o)
+    store_halves(tn(dq_o[...], wq[...]), side, keep_o, send_o, rest_o)
     pick = iota((8, vec_o.shape[1]), 0)
     out = jnp.where(pick == 0, gain_row, 0.0)
     out = jnp.where(pick == 1, shift_row, out)
@@ -399,7 +418,7 @@
     scatter_blocks(whole, keep_o, send_o)
 
 
-def self_backward(item, x1, s0, s1, s2, s3, dx2, x_ref, gain, wo, wq, wk, wv, ka, va, q, o, lse, dx1_o, g1_o, dqkv_o, vec_o, keep_o, send_o, whole, qa, doa, do):
+def self_backward(item, x1, s0, s1, s2, s3, dx2, x_ref, gain, wo, wq, wk, wv, ka, va, q, o, lse, dx1_o, g1_o, dqkv_o, vec_o, keep_o, send_o, rest_o, whole, qa, doa, do):
     side = mp_side()
     grad_in = join_halves((s0, s1, s2, s3), side, whole)
     grad, gain_row, shift_row = norm_back(x1[...], line(gain), grad_in)
@@ -414,7 +433,7 @@
     dv_o = dqkv_o.at[2 * rows : 3 * rows]
     attention_backward(q, ka, va, o, lse, do, qa, doa, dq_o, dk_o, dv_o, q.shape[1], True)
     part = tn(dq_o[...], wq[...]) + tn(dk_o[...], wk[...]) + tn(dv_o[...], wv[...])
-    store_halves(part, side, keep_o, send_o)
+    store_halves(part, side, keep_o, send_o, rest_o)
     unit, _ = norm_parts(x_ref[item].astype(F32))
     pick = iota((8, vec_o.shape[1]), 0)
     out = jnp.where(pick == 0, gain_row, 0.0)
@@ -442,18 +461,20 @@
     scatter_blocks(whole, keep_o, send_o)
 
 
-def unpack(near, far, first, second, third, fourth, vec_o, whole):
+def unpack(near, far, *rest):
+    outs, whole = rest[:-1], rest[-1]
     gather_blocks(near, far, whole)
-    rows = first.shape[0]
-    for k, out in enumerate((first, second, third, fourth)):
-        out[...] = whole[k * rows : (k + 1) * rows, :]
-    vec_o[...] = whole[4 * rows : 4 * rows + 8, :]
-
-
-def finish_out(item, x2, s0, s1, s2, s3, bias, *rest):
-    out, whole = rest[-2:]
-    total = x2[...] + join_halves((s0, s1, s2, s3), mp_side(), whole) + line(bias)
-    out[...] = total.astype(BF16)
+    start = 0
+    for out in outs:
+        out[...] = whole[start : start + out.shape[0], :]
+        start += out.shape[0]
+
+
+def finish_out(items, *refs):
+    x2, pieces, (bias, out, whole) = refs[:items], refs[items : items + 4], refs[items + 4 :]
+    for k in range(items):
+        total = x2[k][...] + join_halves([p.at[k] for p in pieces], mp_side(), whole) + line(bias)
+        out[k] = total.astype(BF16)
 
 
 def finish_grad(item, dx1, s0, s1, s2, s3, x_ref, gain, *rest):
@@ -463,9 +484,59 @@
     out[...] = dx1[...] + grad
 
 
+def finish_memory(kept, far, out):
+    for k in range(kept.shape[0]):
+        out[k] = kept[k].astype(F32) + far[k].astype(F32)
+
+
+def both(left, right):
+    return (left.astype(F32) + right.astype(F32)).astype(BF16)
+
+
+def add_rows(left, right, out):
+    out[...] = both(left[...], right[...])
+
+
+def add_parts(left, *rest):
+    parts, out = rest[:-1], rest[-1]
+    start = 0
+    for part in parts:
+        spot = slice(start, start + part.shape[0])
+        out[spot] = both(left[spot], part[...])
+        start += part.shape[0]
+
+
+def add_stack(count, *refs):
+    out = refs[-1]
+    each = (len(refs) - 1) // count
+    for k in range(count):
+        add_parts(*refs[k * each : (k + 1) * each], out.at[k])
+
+
+def add_memory(count, *refs):
+    left, right, (kept, sent) = refs[:count], refs[count : 2 * count], refs[2 * count :]
+    for k in range(count):
+        kept[k] = both(left[k][0], right[k][0])
+        sent[k] = both(left[k][1], right[k][1])
+
+
+def add_split(left, right, keep, send):
+    half = keep.shape[0]
+    keep[...] = both(left[0:half], right[0:half])
+    send[...] = both(left[half:], right[half:])
+
+
+def stack_pair(left, right, out):
+    half = left.shape[0]
+    out[0:half] = left[...]
+    out[half:] = right[...]
+
+
 SCALARS = pl.BlockSpec(memory_space=pltpu.SMEM)
 LEFT = pl.BlockSpec(memory_space=pl.ANY)
+AWAY = pl.BlockSpec(memory_space=pltpu.HBM)
 NEAR = pl.BlockSpec(memory_space=pltpu.VMEM)
+FAR = pl.BlockSpec(memory_space=pltpu.VMEM)
 
 
 def chosen(array, item):
@@ -477,66 +548,116 @@
     return jax.ShapeDtypeStruct(dims, dtype)
 
 
-def run(body, name, cost, operands, outs, scratch=(), specs=None, out_specs=None, aliases=None):
-    specs = specs or {}
-    placed, in_specs = [], []
-    for k, array in enumerate(operands):
-        spec = specs.get(k, SCALARS if array.dtype == jnp.int32 else NEAR)
-        if spec is NEAR:
-            array = pltpu.with_memory_space_constraint(array, pltpu.VMEM)
-        placed.append(array)
-        in_specs.append(spec)
-    return pl.pallas_call(
-        body,
-        name=name,
-        grid=(1,),
-        in_specs=in_specs,
-        out_specs=out_specs or [NEAR] * len(outs),
-        out_shape=list(outs),
-        scratch_shapes=list(scratch),
-        input_output_aliases=aliases or {},
-        cost_estimate=pl.CostEstimate(flops=int(cost * 1.1e9), transcendentals=0, bytes_accessed=0),
-        compiler_params=pltpu.CompilerParams(vmem_limit_bytes=VMEM_BYTES),
-    )(*placed)
+def near_shape(dims, dtype=BF16):
+    return pltpu.VMEM(dims, dtype)
+
+
+def near_like(array, dims=None):
+    return pltpu.VMEM(tuple(dims or array.shape), array.dtype)
+
+
+class Order:
+    def __init__(self):
+        self.tick = None
+
+    def run(self, body, cost, operands, outs, scratch=(), specs=None, out_specs=None, aliases=None):
+        specs = specs or {}
+        placed, in_specs = [], []
+        for k, array in enumerate(operands):
+            spec = specs.get(k, SCALARS if array.dtype == jnp.int32 else NEAR)
+            if spec is NEAR:
+                array = pltpu.with_memory_space_constraint(array, pltpu.VMEM)
+            elif spec is AWAY:
+                array = pltpu.with_memory_space_constraint(array, pltpu.HBM)
+            placed.append(array)
+            in_specs.append(spec)
+        count = len(placed)
+        if self.tick is not None:
+            placed.append(pltpu.with_memory_space_constraint(self.tick, pltpu.VMEM))
+            in_specs.append(NEAR)
+        given, made = len(placed), len(outs)
+
+        def whole_body(*refs):
+            tick = refs[given + made]
+            tick[...] = jnp.zeros(tick.shape, tick.dtype)
+            body(*refs[:count], *refs[given : given + made], *refs[given + made + 1 :])
+
+        inner = body
+        while isinstance(inner, functools.partial):
+            inner = inner.func
+        results = pl.pallas_call(
+            whole_body,
+            name=inner.__name__,
+            grid=(1,),
+            in_specs=in_specs,
+            out_specs=list(out_specs or [NEAR] * made) + [NEAR],
+            out_shape=list(outs) + [near_shape((8, 128), F32)],
+            scratch_shapes=list(scratch),
+            input_output_aliases=aliases or {},
+            cost_estimate=pl.CostEstimate(flops=int(cost * COST), transcendentals=0, bytes_accessed=1),
+            compiler_params=pltpu.CompilerParams(vmem_limit_bytes=VMEM_BYTES),
+        )(*placed)
+        self.tick = results[-1]
+        return results[:-1]
 
 
 def swap(value, axis, size, bit):
     return lax.ppermute(value, axis, [(k, k ^ bit) for k in range(size)])
 
 
-def after(value, *earlier):
-    return lax.optimization_barrier((value, earlier))[0]
-
-
-def add_low(left, right):
-    return (left.astype(F32) + right.astype(F32)).astype(BF16)
-
-
-def mp_near(send, size):
-    return swap(send, "mp", size, 1)
-
-
-def mp_pieces(keep, near, size):
-    own = add_low(keep, near)
-    far = swap(own, "mp", size, 2)
-    other = swap(own, "mp", size, 1)
-    other_far = swap(far, "mp", size, 1)
-    return own, far, other, other_far
-
-
-def dp_sum(keep, send, size):
-    near = swap(send, "dp", size, 1)
-    keep, send = add_low(keep[:2], near[:2]), add_low(keep[2:], near[2:])
-    near = swap(send, "dp", size, 2)
-    keep, send = add_low(keep[:1], near[:1]), add_low(keep[1:], near[1:])
-    total = add_low(keep, swap(send, "dp", size, 4))
-    bit = 8
-    while bit < size:
-        total = add_low(total, swap(total, "dp", size, bit))
-        bit *= 2
-    total = jnp.concatenate([total, swap(total, "dp", size, 4)])
-    total = jnp.concatenate([total, swap(total, "dp", size, 2)])
-    return total, swap(total, "dp", size, 1)
+class MpSum:
+    def __init__(self, order, size, keep, *sends):
+        self.order, self.size, self.keep = order, size, keep
+        self.near = [swap(send, "mp", size, 1) for send in sends]
+
+    def add(self):
+        own = self.order.run(add_parts, 0.5, (self.keep, *self.near), (near_like(self.keep),))[0]
+        self.spread(own)
+
+    def spread(self, own):
+        self.own = own
+        self.far = swap(own, "mp", self.size, 2)
+        self.other = swap(own, "mp", self.size, 1)
+
+    def pieces(self):
+        far = self.far
+        if self.order.tick is not None:
+            far = lax.optimization_barrier((far, self.order.tick))[0]
+        return self.own, far, self.other, swap(far, "mp", self.size, 1)
+
+
+class DpSum:
+    def __init__(self, order, size, keep, send):
+        self.order, self.size = order, size
+        self.keep, self.near = keep, swap(send, "dp", size, 1)
+        self.stage = 0
+
+    def step(self):
+        dims = self.keep.shape
+        if self.stage < 2:
+            out = near_like(self.keep, (dims[0] // 2,) + dims[1:])
+            self.keep, send = self.order.run(add_split, 0.7, (self.keep, self.near), (out, out))
+            self.near = swap(send, "dp", self.size, 2 << self.stage)
+        elif self.stage == 2:
+            self.keep = self.order.run(add_rows, 0.5, (self.keep, self.near), (near_like(self.keep),))[0]
+            bit = 8
+            while bit < self.size:
+                other = swap(self.keep, "dp", self.size, bit)
+                self.keep = self.order.run(add_rows, 0.5, (self.keep, other), (near_like(self.keep),))[0]
+                bit *= 2
+            self.near = swap(self.keep, "dp", self.size, 4)
+        else:
+            out = near_like(self.keep, (dims[0] * 2,) + dims[1:])
+            self.keep = self.order.run(stack_pair, 0.5, (self.keep, self.near), (out,))[0]
+            self.near = swap(self.keep, "dp", self.size, 2 if self.stage == 3 else 1)
+        self.stage += 1
+
+    def unpack(self, outs):
+        rows = 8 * self.keep.shape[1]
+        specs = [pl.BlockSpec(o.shape, lambda *_: (0, 0)) for o in outs]
+        return self.order.run(
+            unpack, 3, (self.keep, self.near), outs, (pltpu.VMEM((rows, outs[0].shape[1]), F32),), None, specs
+        )
 
 
 def shards(sizes, *arguments):
@@ -558,12 +679,9 @@
     wq1, wk1, wv1 = query_self.T, key_self.T, value_self.T
     wq2, wk2, wv2 = query_cross.T, key_cross.T, value_cross.T
 
-    def near_shape(dims, dtype=BF16):
-        return pltpu.VMEM(dims, dtype)
-
     low_rows = near_shape((rows, length))
     mem_rows = near_shape((rows, wide))
-    half_out = near_shape((half, width))
+    half_outs = (near_shape((half, width)), near_shape((half // 2, width)), near_shape((half - half // 2, width)))
     state = near_shape((length, width), F32)
     low_state = near_shape((length, width))
     unit_state = near_shape((length, units))
@@ -571,157 +689,177 @@
     lse_out = near_shape((8, length), F32)
     aug_out = near_shape((heads, AUG, length))
     aug_mem = near_shape((heads, AUG, wide))
+    mem_half = near_shape((2, rows, memory_len))
     whole = pltpu.VMEM((length, width), F32)
     aug = pltpu.VMEM((AUG, length), BF16)
     row_scratch = pltpu.VMEM((rows, length), BF16)
-    pack_rows = 4 * rows + 64
-    pack_scratch = pltpu.VMEM((pack_rows, width), F32)
-    pack_half = shape((4, pack_rows // 8, width), BF16)
     span = range(items)
-    last = items - 1
     bind = functools.partial
-
-    self_out, near = [], []
-    for i in span:
-        out = run(
-            bind(self_forward, i), "self_forward", 6,
-            (lengths, hidden, gain_self, shift_self, wq1, qbias_self, wk1, wv1, vbias_self, output_self),
-            (low_rows, aug_out, aug_out, low_rows, lse_out, half_out, half_out), (aug,),
-        )
-        self_out.append(out)
-        near.append(mp_near(out[6], n_mp))
-
-    def keys(i, start):
-        return run(
-            bind(cross_keys, i), "cross_keys", 5, (after(frames, start), encoder, wk2, wv2, vbias_cross),
+    order = Order()
+
+    def mp_sum(*parts):
+        return MpSum(order, n_mp, *parts)
+
+    def pack_outs(count):
+        return (near_shape((4, count // 8, width)),) * 2, (pltpu.VMEM((count, width), F32),)
+
+    def keys(i):
+        return order.run(
+            bind(cross_keys, i), 3, (frames, encoder, wk2, wv2, vbias_cross),
             (aug_mem, aug_mem), (), {1: chosen(encoder, i)},
         )
 
-    cross_kv, pieces = [None] * items, []
-    token = self_out[last][4]
+    self_out, self_sum, cross_kv = [], [], []
+    loads = (
+        hidden, gain_self, shift_self, wq1, qbias_self, wk1, wv1, vbias_self, output_self,
+        wk2, wv2, vbias_cross, obias_self, gain_cross, shift_cross, wq2, qbias_cross, output_cross,
+        out_grad, obias_cross, gain_feed, shift_feed, expand_weight, expand_bias, contract_weight, contract_bias,
+    )
+    self_outs = (low_rows, aug_out, aug_out, low_rows, lse_out, *half_outs)
     for i in span:
-        pieces.append(mp_pieces(self_out[i][5], after(near[i], token), n_mp))
         if i == 0:
-            cross_kv[0] = keys(0, token)
-            token = cross_kv[0][0]
-
-    cross_out, cross_near = [], []
+            out = order.run(
+                bind(first_forward, i, 9, len(loads)), 4, (lengths, *loads),
+                self_outs + tuple(near_like(a) for a in loads), (aug, pltpu.SemaphoreType.DMA((len(loads),))),
+                {k + 1: AWAY for k in range(len(loads))},
+            )
+            near = out[8:]
+            hidden, gain_self, shift_self, wq1, qbias_self, wk1, wv1, vbias_self, output_self = near[:9]
+            wk2, wv2, vbias_cross, obias_self, gain_cross, shift_cross, wq2, qbias_cross, output_cross = near[9:18]
+            out_grad, obias_cross, gain_feed, shift_feed, expand_weight, expand_bias, contract_weight, contract_bias = near[18:]
+        else:
+            operands = (lengths, hidden, gain_self, shift_self, wq1, qbias_self, wk1, wv1, vbias_self, output_self)
+            out = order.run(bind(self_forward, i), 4, operands, self_outs, (aug,))
+        self_out.append(out)
+        self_sum.append(mp_sum(*out[5:8]))
     for i in span:
-        out = run(
-            bind(cross_forward, i, chunk), "cross_forward", 9,
-            (hidden, *pieces[i], obias_self, gain_cross, shift_cross, wq2, qbias_cross, output_cross, *cross_kv[i]),
-            (state, low_state, low_rows, low_rows, lse_out, half_out, half_out), (whole, aug),
+        self_sum[i].add()
+        if i == 0:
+            cross_kv.append(keys(0))
+
+    cross_out, cross_sum = [], []
+    for i in span:
+        out = order.run(
+            bind(cross_forward, i, chunk), 6,
+            (hidden, *self_sum[i].pieces(), obias_self, gain_cross, shift_cross, wq2, qbias_cross, output_cross, *cross_kv[i]),
+            (state, low_state, low_rows, low_rows, lse_out, *half_outs), (whole, aug),
         )
         cross_out.append(out)
-        cross_near.append(mp_near(out[6], n_mp))
-        if i < last:
-            cross_kv[i + 1] = keys(i + 1, out[4])
-            cross_near[i] = after(cross_near[i], cross_kv[i + 1][0])
-
-    feed_out, feed_near = [], []
+        cross_sum.append(mp_sum(*out[5:8]))
+        if len(cross_kv) < items:
+            cross_kv.append(keys(i + 1))
+        cross_sum[i].add()
+
+    feed_out, feed_sum, block_sum = [], [], []
     for i in span:
-        done = mp_pieces(cross_out[i][5], cross_near[i], n_mp)
-        out = run(
-            bind(feed, i), "feed", 9,
-            (lengths, tasks, cross_out[i][0], *done, out_grad, obias_cross, gain_feed, shift_feed, expand_weight, expand_bias, contract_weight),
-            (state, low_state, unit_state, unit_state, low_state, vec_out, half_out, half_out, half_out, half_out), (whole,),
+        out = order.run(
+            bind(feed, i), 4,
+            (lengths, tasks, cross_out[i][0], *cross_sum[i].pieces(), out_grad, obias_cross, gain_feed, shift_feed, expand_weight, expand_bias, contract_weight),
+            (state, low_state, unit_state, unit_state, low_state, vec_out, *half_outs), (whole,),
         )
         feed_out.append(out)
-        feed_near.append(mp_near(out[9], n_mp))
-
-    token = feed_out[last][5]
-    back_pieces = [mp_pieces(feed_out[i][8], after(feed_near[i], token), n_mp) for i in span]
-    feed_pack = run(
-        bind(feed_weights, items), "feed_weights", 7,
-        [feed_out[i][k] for k in (1, 3, 2, 4, 5) for i in span],
-        (shape((width + units + 16, width), BF16),),
-    )[0]
-    feed_pack = lax.psum(feed_pack, "dp")
-    block_near = [mp_near(feed_out[i][7], n_mp) for i in span]
-
-    back_out, back_near = [], []
+        feed_sum.append(mp_sum(*out[6:9]))
+        block_sum.append(mp_sum(*order.run(feed_out_part, 1, (out[2], contract_weight), half_outs)))
+        feed_sum[i].add()
+    outs, scratch = pack_outs(width + units + 64)
+    feed_dp = DpSum(
+        order, n_dp, *order.run(
+            bind(feed_weights, items), 4, [out[k] for k in (1, 3, 2, 4, 5) for out in feed_out], outs, scratch
+        )
+    )
+
+    back_out, back_sum, memory_parts = [], [], []
     for i in span:
         _, _, q2, o2, lse2 = cross_out[i][:5]
-        out = run(
-            bind(cross_backward, i, chunk), "cross_backward", 12,
-            (lengths, tasks, feed_out[i][0], *back_pieces[i], out_grad, gain_feed, output_cross, wq2, *cross_kv[i], q2, o2, lse2),
-            (state, low_state, low_rows, mem_rows, mem_rows, vec_out, half_out, half_out), (whole, aug, aug, row_scratch),
+        out = order.run(
+            bind(cross_backward, i, chunk), 9,
+            (lengths, tasks, feed_out[i][0], *feed_sum[i].pieces(), out_grad, gain_feed, output_cross, wq2, *cross_kv[i], q2, o2, lse2),
+            (state, low_state, low_rows, mem_rows, mem_rows, vec_out, *half_outs), (whole, aug, aug, row_scratch),
         )
         back_out.append(out)
-        back_near.append(mp_near(out[7], n_mp))
-    block_pieces = [mp_pieces(feed_out[i][6], after(block_near[i], back_out[0][5]), n_mp) for i in span]
-    token = back_out[last][5]
-    dq_pieces = [mp_pieces(back_out[i][6], after(back_near[i], token), n_mp) for i in span]
-
-    memory_parts = []
-    for i in span:
-        memory_parts.append(
-            run(
-                memory_grad, "memory_grad", 5, (wk2, wv2, back_out[i][3], back_out[i][4]),
-                (near_shape((2, rows, memory_len)), near_shape((2, rows, memory_len))),
-            )
-        )
-
-    cross_pack = run(
-        bind(cross_weights, items), "cross_weights", 8,
-        [encoder] + [out[2] for out in back_out] + [out[1] for out in cross_out] + [out[3] for out in cross_out]
-        + [out[1] for out in back_out] + [out[3] for out in back_out] + [out[4] for out in back_out]
-        + [out[5] for out in back_out],
-        (pack_half, pack_half), (pack_scratch,), {0: pl.BlockSpec(encoder.shape, lambda *_: (0, 0, 0))},
-    )
-    cross_sum = dp_sum(*cross_pack, n_dp)
-
-    self_back, self_near = [], []
+        back_sum.append(mp_sum(*out[6:9]))
+        keep, send = order.run(memory_grad, 2, (wk2, wv2, out[3], out[4]), (mem_half, mem_half))
+        memory_parts.append((keep, swap(send, "mp", n_mp, 1)))
+        back_sum[i].add()
+    feed_dp.step()
+
+    self_back, last_sum = [], []
     for i in span:
         q1, ka1, va1, o1, lse1 = self_out[i][:5]
-        out = run(
-            bind(self_backward, i), "self_backward", 9,
-            (cross_out[i][0], *dq_pieces[i], back_out[i][0], hidden, gain_cross, output_self, wq1, wk1, wv1, ka1, va1, q1, o1, lse1),
-            (state, low_state, near_shape((3 * rows, length)), vec_out, half_out, half_out), (whole, aug, aug, row_scratch),
+        out = order.run(
+            bind(self_backward, i), 5,
+            (cross_out[i][0], *back_sum[i].pieces(), back_out[i][0], hidden, gain_cross, output_self, wq1, wk1, wv1, ka1, va1, q1, o1, lse1),
+            (state, low_state, near_shape((3 * rows, length)), vec_out, *half_outs), (whole, aug, aug, row_scratch),
         )
         self_back.append(out)
-        self_near.append(mp_near(out[5], n_mp))
-
-    self_pack = run(
-        bind(self_weights, items), "self_weights", 6,
-        [hidden, gain_self, shift_self] + [out[2] for out in self_back] + [out[3] for out in self_out]
-        + [out[1] for out in self_back] + [out[3] for out in self_back],
-        (pack_half, pack_half), (pack_scratch,),
+        last_sum.append(mp_sum(*out[4:7]))
+        outs, scratch = pack_outs(4 * rows + 64)
+        if i == 0:
+            operands = [encoder] + [out[2] for out in back_out] + [out[1] for out in cross_out] + [out[3] for out in cross_out]
+            operands += [out[1] for out in back_out] + [out[3] for out in back_out] + [out[4] for out in back_out]
+            operands += [out[5] for out in back_out]
+            cross_dp = DpSum(
+                order, n_dp, *order.run(
+                    bind(cross_weights, items), 3, operands, outs, scratch,
+                    {0: pl.BlockSpec(encoder.shape, lambda *_: (0, 0, 0))},
+                )
+            )
+            last_sum[i].add()
+            feed_dp.step()
+        if i == items - 1:
+            operands = [hidden, gain_self, shift_self] + [out[2] for out in self_back] + [out[3] for out in self_out]
+            operands += [out[1] for out in self_back] + [out[3] for out in self_back]
+            self_dp = DpSum(order, n_dp, *order.run(bind(self_weights, items), 3, operands, outs, scratch))
+        if i > 0:
+            last_sum[i].add()
+
+    feed_dp.step()
+    cross_dp.step()
+    block_half = near_shape((items, half, width))
+    stacked = order.run(
+        bind(add_stack, items), 1, [a for s in block_sum for a in (s.keep, *s.near)], (block_half,)
+    )[0]
+    block_sum[0].spread(stacked)
+    memory_out = near_shape((items, rows, memory_len))
+    kept, sent = order.run(
+        bind(add_memory, items), 1, [p[0] for p in memory_parts] + [p[1] for p in memory_parts], (memory_out, memory_out)
     )
-    self_sum = dp_sum(*self_pack, n_dp)
-    token = self_back[last][3]
-    last_pieces = [mp_pieces(self_back[i][4], after(self_near[i], token), n_mp) for i in span]
-
-    block_out, hidden_grad = None, None
-    block_shape = shape(hidden.shape, BF16)
+    memory_far = swap(sent, "mp", n_mp, 2)
+    cross_dp.step()
+    hidden_grad = None
     grad_shape = shape(hidden.shape, F32)
     for i in span:
-        extra = () if block_out is None else (block_out,)
-        block_out = run(
-            bind(finish_out, i), "finish_out", 3,
-            (feed_out[i][0], *block_pieces[i], contract_bias, *extra), (block_shape,), (whole,),
-            {6: LEFT}, [chosen(block_shape, i)], {6: 0} if extra else {},
-        )[0]
-    for i in span:
         extra = () if hidden_grad is None else (hidden_grad,)
-        hidden_grad = run(
-            bind(finish_grad, i), "finish_grad", 4,
-            (self_back[i][0], *last_pieces[i], hidden, gain_self, *extra), (grad_shape,), (whole,),
+        hidden_grad = order.run(
+            bind(finish_grad, i), 2,
+            (self_back[i][0], *last_sum[i].pieces(), hidden, gain_self, *extra), (grad_shape,), (whole,),
             {7: LEFT}, [chosen(grad_shape, i)], {7: 0} if extra else {},
         )[0]
-
-    memory_grads = []
-    for keep, send in memory_parts:
-        near_part = swap(send, "mp", n_mp, 1)
-        kept, sent = add_low(keep[0], near_part[0]), add_low(keep[1], near_part[1])
-        memory_grads.append(kept.astype(F32) + swap(sent, "mp", n_mp, 2).astype(F32))
-    encoder_grad = jnp.stack(memory_grads).transpose(0, 2, 1)
+    self_dp.step()
+    feed_dp.step()
+    cross_dp.step()
+    self_dp.step()
+    block_shape = shape(hidden.shape, BF16)
+    block_out = order.run(
+        bind(finish_out, items), 3, [out[0] for out in feed_out] + list(block_sum[0].pieces()) + [contract_bias],
+        (block_shape,), (whole,), None, [pl.BlockSpec(hidden.shape, lambda *_: (0, 0, 0))],
+    )[0]
+    feed_dp.step()
+    cross_dp.step()
+    self_dp.step()
+    encoder_grad = order.run(
+        finish_memory, 2, (kept, memory_far), (shape((items, rows, memory_len), F32),), (), None,
+        [pl.BlockSpec((items, rows, memory_len), lambda *_: (0, 0, 0))],
+    )[0].transpose(0, 2, 1)
+    cross_dp.step()
+    self_dp.step()
+    self_dp.step()
 
     matrix = shape((rows, width), F32)
     outs = (matrix, matrix, matrix, matrix, shape((8, width), F32))
-    cross_grads = run(unpack, "unpack", 3, cross_sum, outs, (pack_scratch,))
-    self_grads = run(unpack, "unpack", 3, self_sum, outs, (pack_scratch,))
-    feed_grads = feed_pack.astype(F32)
+    feed_grads = feed_dp.unpack((shape((width, width), F32), shape((units, width), F32), shape((8, width), F32)))
+    cross_grads = cross_dp.unpack(outs)
+    self_grads = self_dp.unpack(outs)
     norm_rows = self_grads[4]
     norm_rows = norm_rows + swap(norm_rows, "mp", n_mp, 1)
     norm_rows = norm_rows + swap(norm_rows, "mp", n_mp, 2)
@@ -749,10 +887,10 @@
         cross_grads[4][2],
         cross_grads[4][0],
         cross_grads[4][1],
-        feed_grads[0:width],
-        feed_grads[width + units + 1],
-        feed_grads[width : width + units],
-        feed_grads[width + units],
+        feed_grads[0],
+        feed_grads[2][1],
+        feed_grads[1],
+        feed_grads[2][0],
     )
 
 

time: 333 us -> 272 us (0.82)
  local copies, waits for them, and re-layouts: 33.1 us -> 4.87 us
  waiting for transfers between devices: 141 us -> 117 us
  starting transfers between devices: 38.2 us -> 55 us
  other arithmetic: 15.7 us -> 0.01 us
  between operations: 16 us -> 1.73 us
  Pallas kernels: 83.9 us -> 89.2 us
    unnamed x221 -> x11, local copies, waits for them, and re-layouts: 27 us -> 1.26 us
    ppermute x66 -> x80, starting transfers between devices: 38.2 us -> 55 us  [swap(): return lax.ppermute(value, axis, [(k, k ^ bit) for k in range(size)])]
    ppermute x66 -> x80, waiting for transfers between devices: 130 us -> 117 us  [swap(): return lax.ppermute(value, axis, [(k, k ^ bit) for k in range(size)])]
    psum x1 -> x0, waiting for transfers between devices: 11.3 us -> none  [shards(): feed_pack = lax.psum(feed_pack, 'dp')]
    convert_element_type x21 -> x0, other arithmetic: 10.6 us -> none  [the longest x20 8.41 us: add_low(): return (left.astype(F32) + right.astype(F32)).astype(BF16)]
    pallas_call x23 -> x53, Pallas kernels: 83.9 us -> 89.2 us  [run(): pl.pallas_call(whole_body, name=inner.__name__, grid=(1,), in_specs=in_sp...]
  transfers between devices with their start and end apart: 67 -> 80, of which waited for: 21 -> 31; matrix products, arithmetic and copies ran while one was open for 7% -> 1% of each run, Pallas kernels for 24% -> 29%
where the time goes in v2:
time: 272 us; the launch traced here: 267 us
  waiting for transfers between devices  117 us (43%)
  Pallas kernels  89.2 us (33%)
  starting transfers between devices  55 us (20%)
  local copies, waits for them, and re-layouts  4.87 us (2%)
    ppermute x80, waiting for transfers between devices, swap(): return lax.ppermute(value, axis, [(k, k ^ bit) for k in range(size)])  117 us
    pallas_call x53, Pallas kernels, run(): pl.pallas_call(whole_body, name=inner.__name__, grid=(1,), in_specs=in_sp...  89.2 us
    ppermute x80, starting transfers between devices, swap(): return lax.ppermute(value, axis, [(k, k ^ bit) for k in range(size)])  55 us
  transfers between devices with their start and end apart: 80, of which 31 were waited for; matrix products, arithmetic and copies ran while one was open for 1% of the time, Pallas kernels for 29%

profile of v2, /device:TPU:0, one launch (start us, length us, event | category | flops | bytes accessed | tf_op | source)
XLA Modules:
  0.0 267.4 jit_solution(7398999959417302977)
XLA Ops:
  1.3 5.5 %first_forward.1 = (bf16[192,448]{1,0:T(8,128)(2,1)S(1)}, bf16[3,80,448]{2,1,0:T(8,128)(2,1)S(1)}, bf16[3,80,448]{2,1,0:T(8,128)(2,1)S(1)}, bf16[192,448]{1,0:T(...) custom-call(s32[2]{0:T(128)S(1)} %copy-done, ...), custom_call_target="tpu_custom_call" | custom-call | flops 4 | bytes 1 | tf_op jit(solution)/shard_map/first_forward/pallas_call | solution.py:588
  7.4 3.4 %self_forward.1 = (bf16[192,448]{1,0:T(8,128)(2,1)S(1)}, bf16[3,80,448]{2,1,0:T(8,128)(2,1)S(1)}, bf16[3,80,448]{2,1,0:T(8,128)(2,1)S(1)}, bf16[192,448]{1,0:T(8...) custom-call(s32[2]{0:T(128)S(1)} %copy-done, ...), custom_call_target="tpu_custom_call" | custom-call | flops 4 | bytes 1 | tf_op jit(solution)/shard_map/self_forward/pallas_call | solution.py:588
  11.0 3.0 %collective-permute-start.2 = (bf16[224,768]{1,0:T(8,128)(2,1)S(1)}, bf16[224,768]{1,0:T(8,128)(2,1)S(1)}, u32[]{:S(2)}, u32[]{:S(2)}) collective-permute-start(bf16[224,768]{1,0:T(8,128)(2,1)S(1)} %get-tuple-element.283.refs_1_), channel_id=1, source_target_pairs={{0,2},{1,3},{2,0},{3,1},{4,6},{5,7},{6,4},{7,5},{8,10},{9,11},{10,... | collective-permute-start | bytes 1032200 | tf_op jit(solution)/shard_map/ppermute | solution.py:605
  15.2 2.1 cross_keys.2
  17.4 4.9 %collective-permute-done.2.refs_2_ = bf16[224,768]{1,0:T(8,128)(2,1)S(1)} collective-permute-done((bf16[224,768]{1,0:T(8,128)(2,1)S(1)}, bf16[224,768]{1,0:T(8,128)(2,1)S(1)}, u32[]{:S(2)}, u32[]{:S(2)}) %collective-permute-start.2) | collective-permute-done | bytes 344096 | tf_op jit(solution)/shard_map/ppermute | solution.py:605
  22.3 1.7 collective-permute-start.10
  24.1 5.6 %cross_forward.2 = (f32[448,768]{1,0:T(8,128)S(1)}, bf16[448,768]{1,0:T(8,128)(2,1)S(1)}, bf16[192,448]{1,0:T(8,128)(2,1)S(1)}, bf16[192,448]{1,0:T(8,128)(2,1)S...) custom-call(bf16[2,448,768]{2,1,0:T(8,128)(2,1)S(1)} %get-tuple-elem, ...), custom_call_target="tpu_custom_call" | custom-call | flops 6 | bytes 1 | tf_op jit(solution)/shard_map/cross_forward/pallas_call | solution.py:588
  30.5 2.1 cross_keys.3
  34.7 5.4 %cross_forward.3 = (f32[448,768]{1,0:T(8,128)S(1)}, bf16[448,768]{1,0:T(8,128)(2,1)S(1)}, bf16[192,448]{1,0:T(8,128)(2,1)S(1)}, bf16[192,448]{1,0:T(8,128)(2,1)S...) custom-call(bf16[2,448,768]{2,1,0:T(8,128)(2,1)S(1)} %get-tuple-elem, ...), custom_call_target="tpu_custom_call" | custom-call | flops 6 | bytes 1 | tf_op jit(solution)/shard_map/cross_forward/pallas_call | solution.py:588
  43.3 1.7 collective-permute-start.17
  45.0 3.5 %feed.2 = (f32[448,768]{1,0:T(8,128)S(1)}, bf16[448,768]{1,0:T(8,128)(2,1)S(1)}, bf16[448,768]{1,0:T(8,128)(2,1)S(1)}, bf16[448,768]{1,0:T(8,128)(2,1)S(1)}, bf1...) custom-call(s32[2]{0:T(128)S(1)} %copy-done.1, ...), custom_call_target="tpu_custom_call" | custom-call | flops 4 | bytes 1 | tf_op jit(solution)/shard_map/feed/pallas_call | solution.py:588
  50.5 3.3 %collective-permute-done.17.refs_4_ = bf16[224,768]{1,0:T(8,128)(2,1)S(1)} collective-permute-done((bf16[224,768]{1,0:T(8,128)(2,1)S(1)}, bf16[224,768]{1,0:T(8,128)(2,1)S(1)}, u32[]{:S(2)}, u32[]{:S(2)}) %collective-permute-start.17) | collective-permute-done | bytes 344096 | tf_op jit(solution)/shard_map/ppermute | solution.py:605
  55.4 3.4 %feed.3 = (f32[448,768]{1,0:T(8,128)S(1)}, bf16[448,768]{1,0:T(8,128)(2,1)S(1)}, bf16[448,768]{1,0:T(8,128)(2,1)S(1)}, bf16[448,768]{1,0:T(8,128)(2,1)S(1)}, bf1...) custom-call(s32[2]{0:T(128)S(1)} %copy-done.1, ...), custom_call_target="tpu_custom_call" | custom-call | flops 4 | bytes 1 | tf_op jit(solution)/shard_map/feed/pallas_call | solution.py:588
  59.4 1.7 collective-permute-start.26
  62.1 3.6 %feed_weights.1 = (bf16[4,200,768]{2,1,0:T(8,128)(2,1)S(1)}, bf16[4,200,768]{2,1,0:T(8,128)(2,1)S(1)}, f32[8,128]{1,0:T(8,128)S(1)}) custom-call(bf16[448,768]{1,0:T(8,128)(2,1)S(1)} %get-tuple-element.348.refs_0_, bf16[448,768]{1,0:T(8,128)(2,1)S(1)} %get-tuple-element.349.refs_1_, bf16[448,768]{1,0:T(8,128)(2,1)S(1)} %get-tuple-element.350.refs_2_, ...), custom_call_target="tpu_custom_call" | custom-call | flops 4 | bytes 1 | tf_op jit(solution)/shard_map/feed_weights/pallas_call | solution.py:588
  67.2 2.3 collective-permute-done.26.refs_4_
  69.5 1.7 collective-permute-start.31
  71.3 8.4 %cross_backward.2 = (f32[448,768]{1,0:T(8,128)S(1)}, bf16[448,768]{1,0:T(8,128)(2,1)S(1)}, bf16[192,448]{1,0:T(8,128)(2,1)S(1)}, bf16[192,1536]{1,0:T(8,128)(2,1...) custom-call(s32[2]{0:T(128)S(1)} %copy-done.1, ...), custom_call_target="tpu_custom_call" | custom-call | flops 9 | bytes 1 | tf_op jit(solution)/shard_map/cross_backward/pallas_call | solution.py:588
  80.5 1.9 memory_grad.2
  84.4 8.4 %cross_backward.3 = (f32[448,768]{1,0:T(8,128)S(1)}, bf16[448,768]{1,0:T(8,128)(2,1)S(1)}, bf16[192,448]{1,0:T(8,128)(2,1)S(1)}, bf16[192,1536]{1,0:T(8,128)(2,1...) custom-call(s32[2]{0:T(128)S(1)} %copy-done.1, ...), custom_call_target="tpu_custom_call" | custom-call | flops 9 | bytes 1 | tf_op jit(solution)/shard_map/cross_backward/pallas_call | solution.py:588
  93.3 1.9 memory_grad.3
  99.4 4.8 %self_backward.2 = (f32[448,768]{1,0:T(8,128)S(1)}, bf16[448,768]{1,0:T(8,128)(2,1)S(1)}, bf16[576,448]{1,0:T(8,128)(2,1)S(1)}, f32[8,768]{1,0:T(8,128)S(1)}, bf...) custom-call(f32[448,768]{1,0:T(8,128)S(1)} %get-tuple-element.302.re, ...), custom_call_target="tpu_custom_call" | custom-call | flops 5 | bytes 1 | tf_op jit(solution)/shard_map/self_backward/pallas_call | solution.py:588
  106.2 2.9 %cross_weights.1 = (bf16[4,104,768]{2,1,0:T(8,128)(2,1)S(1)}, bf16[4,104,768]{2,1,0:T(8,128)(2,1)S(1)}, f32[8,128]{1,0:T(8,128)S(1)}) custom-call(bf16[2,1500,768]{2,1,0:T(8,128)(2,1)S(1)} %copy.58.refs_1_.refs_0_, bf16[192,448]{1,0:T(8,128)(2,1)S(1)} %get-tuple-element.366.refs_1_, bf16[192,448]{1,0:T(8,128)(2,1)S(1)} %get-tuple-element.380.refs_2_, ...), custom_call_target="tpu_custom_call" | custom-call | flops 3 | bytes 1 | tf_op jit(solution)/shard_map/cross_weights/pallas_call | solution.py:588
  109.1 2.4 collective-permute-done.43.refs_1_
  113.5 2.7 collective-permute-start.46
  116.3 5.0 %self_backward.3 = (f32[448,768]{1,0:T(8,128)S(1)}, bf16[448,768]{1,0:T(8,128)(2,1)S(1)}, bf16[576,448]{1,0:T(8,128)(2,1)S(1)}, f32[8,768]{1,0:T(8,128)S(1)}, bf...) custom-call(f32[448,768]{1,0:T(8,128)S(1)} %get-tuple-element.328.re, ...), custom_call_target="tpu_custom_call" | custom-call | flops 5 | bytes 1 | tf_op jit(solution)/shard_map/self_backward/pallas_call | solution.py:588
  121.7 8.9 %collective-permute-done.46.refs_1_ = bf16[1,200,768]{2,1,0:T(8,128)(2,1)S(1)} collective-permute-done((bf16[1,200,768]{2,1,0:T(8,128)(2,1)S(1)}, bf16[1,200,768]{2,1,0:T(8,128)(2,1)S(1)}, u32[]{:S(2)}, u32[]{:S(2)}) %collective-permute-start.46) | collective-permute-done | bytes 307232 | tf_op jit(solution)/shard_map/ppermute | solution.py:605
  133.5 2.2 self_weights.1
  139.2 6.3 %collective-permute-done.56.refs_1_ = bf16[2,104,768]{2,1,0:T(8,128)(2,1)S(1)} collective-permute-done((bf16[2,104,768]{2,1,0:T(8,128)(2,1)S(1)}, bf16[2,104,768]{2,1,0:T(8,128)(2,1)S(1)}, u32[]{:S(2)}, u32[]{:S(2)}) %collective-permute-start.56) | collective-permute-done | bytes 319520 | tf_op jit(solution)/shard_map/ppermute | solution.py:605
  148.3 2.2 finish_grad.2
  150.5 6.1 %collective-permute-done.54.refs_2_ = bf16[224,768]{1,0:T(8,128)(2,1)S(1)} collective-permute-done((bf16[224,768]{1,0:T(8,128)(2,1)S(1)}, bf16[224,768]{1,0:T(8,128)(2,1)S(1)}, u32[]{:S(2)}, u32[]{:S(2)}) %collective-permute-start.54) | collective-permute-done | bytes 344096 | tf_op jit(solution)/shard_map/ppermute | solution.py:605
  158.2 2.2 finish_grad.3
  160.4 2.3 collective-permute-done.53.refs_1_
  163.6 3.4 %collective-permute-start.65 = (bf16[1,200,768]{2,1,0:T(8,128)(2,1)S(1)}, bf16[1,200,768]{2,1,0:T(8,128)(2,1)S(1)}, u32[]{:S(2)}, u32[]{:S(2)}) collective-permute-start(bf16[1,200,768]{2,1,0:T(8,128)(2,1)S(1)} %get-tuple-element.466.refs_0_), channel_id=1, source_target_pairs={{0,16},{4,20},{8,24},{12,28},{16,0},{20,4},{24,8},{28,12},{1,17},{... | collective-permute-start | bytes 921608 | tf_op jit(solution)/shard_map/ppermute | solution.py:605
  167.0 18.2 %collective-permute-done.65.refs_1_ = bf16[1,200,768]{2,1,0:T(8,128)(2,1)S(1)} collective-permute-done((bf16[1,200,768]{2,1,0:T(8,128)(2,1)S(1)}, bf16[1,200,768]{2,1,0:T(8,128)(2,1)S(1)}, u32[]{:S(2)}, u32[]{:S(2)}) %collective-permute-start.65) | collective-permute-done | bytes 307232 | tf_op jit(solution)/shard_map/ppermute | solution.py:605
  185.2 1.7 collective-permute-done.64.refs_1_
  189.3 2.1 finish_out.1
  191.3 12.1 %collective-permute-done.71.refs_1_ = bf16[2,200,768]{2,1,0:T(8,128)(2,1)S(1)} collective-permute-done((bf16[2,200,768]{2,1,0:T(8,128)(2,1)S(1)}, bf16[2,200,768]{2,1,0:T(8,128)(2,1)S(1)}, u32[]{:S(2)}, u32[]{:S(2)}) %collective-permute-start.71) | collective-permute-done | bytes 614432 | tf_op jit(solution)/shard_map/ppermute | solution.py:605
  205.3 8.4 %collective-permute-done.70.refs_1_ = bf16[1,104,768]{2,1,0:T(8,128)(2,1)S(1)} collective-permute-done((bf16[1,104,768]{2,1,0:T(8,128)(2,1)S(1)}, bf16[1,104,768]{2,1,0:T(8,128)(2,1)S(1)}, u32[]{:S(2)}, u32[]{:S(2)}) %collective-permute-start.70) | collective-permute-done | bytes 159776 | tf_op jit(solution)/shard_map/ppermute | solution.py:605
  213.8 3.0 %collective-permute-start.69 = (bf16[1,104,768]{2,1,0:T(8,128)(2,1)S(1)}, bf16[1,104,768]{2,1,0:T(8,128)(2,1)S(1)}, u32[]{:S(2)}, u32[]{:S(2)}) collective-permute-start(bf16[1,104,768]{2,1,0:T(8,128)(2,1)S(1)} %get-tuple-element.478), channel_id=1, source_target_pairs={{0,16},{4,20},{8,24},{12,28},{16,0},{20,4},{24,8},{28,12},{1,17},{... | collective-permute-start | bytes 479240 | tf_op jit(solution)/shard_map/ppermute | solution.py:605
  216.8 7.7 %collective-permute-done.69.refs_1_ = bf16[1,104,768]{2,1,0:T(8,128)(2,1)S(1)} collective-permute-done((bf16[1,104,768]{2,1,0:T(8,128)(2,1)S(1)}, bf16[1,104,768]{2,1,0:T(8,128)(2,1)S(1)}, u32[]{:S(2)}, u32[]{:S(2)}) %collective-permute-start.69) | collective-permute-done | bytes 159776 | tf_op jit(solution)/shard_map/ppermute | solution.py:605
  224.5 3.4 %collective-permute-start.72 = (bf16[1,104,768]{2,1,0:T(8,128)(2,1)S(1)}, bf16[1,104,768]{2,1,0:T(8,128)(2,1)S(1)}, u32[]{:S(2)}, u32[]{:S(2)}) collective-permute-start(bf16[1,104,768]{2,1,0:T(8,128)(2,1)S(1)} %get-tuple-element.486.refs_0_), channel_id=1, source_target_pairs={{0,16},{4,20},{8,24},{12,28},{16,0},{20,4},{24,8},{28,12},{1,17},{... | collective-permute-start | bytes 479240 | tf_op jit(solution)/shard_map/ppermute | solution.py:605
  231.2 4.0 %collective-permute-done.72.refs_1_ = bf16[1,104,768]{2,1,0:T(8,128)(2,1)S(1)} collective-permute-done((bf16[1,104,768]{2,1,0:T(8,128)(2,1)S(1)}, bf16[1,104,768]{2,1,0:T(8,128)(2,1)S(1)}, u32[]{:S(2)}, u32[]{:S(2)}) %collective-permute-start.72) | collective-permute-done | bytes 159776 | tf_op jit(solution)/shard_map/ppermute | solution.py:605
  235.3 7.0 %collective-permute-done.74.refs_1_ = bf16[2,104,768]{2,1,0:T(8,128)(2,1)S(1)} collective-permute-done((bf16[2,104,768]{2,1,0:T(8,128)(2,1)S(1)}, bf16[2,104,768]{2,1,0:T(8,128)(2,1)S(1)}, u32[]{:S(2)}, u32[]{:S(2)}) %collective-permute-start.74) | collective-permute-done | bytes 319520 | tf_op jit(solution)/shard_map/ppermute | solution.py:605
  243.9 2.8 %unpack.3 = (f32[768,768]{1,0:T(8,128)}, f32[768,768]{1,0:T(8,128)}, f32[8,768]{1,0:T(8,128)S(1)}, f32[8,128]{1,0:T(8,128)S(1)}) custom-call(bf16[4,200,768]{2,1,0:T(8,128)(2,1)S(1)} %get-tuple-element.494.refs_0_, bf16[4,200,768]{2,1,0:T(8,128)(2,1)S(1)} %collective-permute-done.77.refs_1_, f32[8,128]{1,0:T(8,128)S(1)} %get-tuple-element.495.refs_2_), custom_call_target="tpu_custom_call" | custom-call | flops 3 | bytes 1 | tf_op jit(solution)/shard_map/unpack/pallas_call | solution.py:588
  247.0 1.8 unpack.4
  250.6 8.9 %collective-permute-done.75.refs_1_ = bf16[4,104,768]{2,1,0:T(8,128)(2,1)S(1)} collective-permute-done((bf16[4,104,768]{2,1,0:T(8,128)(2,1)S(1)}, bf16[4,104,768]{2,1,0:T(8,128)(2,1)S(1)}, u32[]{:S(2)}, u32[]{:S(2)}) %collective-permute-start.75) | collective-permute-done | bytes 639008 | tf_op jit(solution)/shard_map/ppermute | solution.py:605
  259.5 1.8 unpack.5
  (184 shorter events, 56.0 us)
Async XLA Ops:
  6.8 4.0 %collective-permute-start = (bf16[112,768]{1,0:T(8,128)(2,1)S(1)}, bf16[112,768]{1,0:T(8,128)(2,1)S(1)}, u32[]{:S(2)}, u32[]{:S(2)}) collective-permute-start(bf16[112,768]{1,0:T(8,128)(2,1)S(1)} %get-tuple-element.271), channel_id=1, source_target_pairs={{0,1},{1,0},{2,3},{3,2},{4,5},{5,4},{6,7},{7,6},{8,9},{9,8},{10,11... | collective-permute-start | bytes 516104 | tf_op jit(solution)/shard_map/ppermute | solution.py:605
  11.0 11.3 %collective-permute-start.2 = (bf16[224,768]{1,0:T(8,128)(2,1)S(1)}, bf16[224,768]{1,0:T(8,128)(2,1)S(1)}, u32[]{:S(2)}, u32[]{:S(2)}) collective-permute-start(bf16[224,768]{1,0:T(8,128)(2,1)S(1)} %get-tuple-element.283.refs_1_), channel_id=1, source_target_pairs={{0,2},{1,3},{2,0},{3,1},{4,6},{5,7},{6,4},{7,5},{8,10},{9,11},{10,... | collective-permute-start | bytes 1032200 | tf_op jit(solution)/shard_map/ppermute | solution.py:605
  15.1 8.9 %collective-permute-start.5 = (bf16[224,768]{1,0:T(8,128)(2,1)S(1)}, bf16[224,768]{1,0:T(8,128)(2,1)S(1)}, u32[]{:S(2)}, u32[]{:S(2)}) collective-permute-start(bf16[224,768]{1,0:T(8,128)(2,1)S(1)} %get-tuple-element.283.refs_1_), channel_id=1, source_target_pairs={{0,1},{1,0},{2,3},{3,2},{4,5},{5,4},{6,7},{7,6},{8,9},{9,8},{10,11... | collective-permute-start | bytes 1032200 | tf_op jit(solution)/shard_map/ppermute | solution.py:605
  22.3 10.5 %collective-permute-start.10 = (bf16[224,768]{1,0:T(8,128)(2,1)S(1)}, bf16[224,768]{1,0:T(8,128)(2,1)S(1)}, u32[]{:S(2)}, u32[]{:S(2)}) collective-permute-start(bf16[224,768]{1,0:T(8,128)(2,1)S(1)} %get-tuple-element.309.refs_1_), channel_id=1, source_target_pairs={{0,2},{1,3},{2,0},{3,1},{4,6},{5,7},{6,4},{7,5},{8,10},{9,11},{10,... | collective-permute-start | bytes 1032200 | tf_op jit(solution)/shard_map/ppermute | solution.py:605
  30.3 4.4 %collective-permute-start.11 = (bf16[224,768]{1,0:T(8,128)(2,1)S(1)}, bf16[224,768]{1,0:T(8,128)(2,1)S(1)}, u32[]{:S(2)}, u32[]{:S(2)}) collective-permute-start(bf16[224,768]{1,0:T(8,128)(2,1)S(1)} %get-tuple-element.309.refs_1_), channel_id=1, source_target_pairs={{0,1},{1,0},{2,3},{3,2},{4,5},{5,4},{6,7},{7,6},{8,9},{9,8},{10,11... | collective-permute-start | bytes 1032200 | tf_op jit(solution)/shard_map/ppermute | solution.py:605
  33.0 10.2 %collective-permute-start.9 = (bf16[224,768]{1,0:T(8,128)(2,1)S(1)}, bf16[224,768]{1,0:T(8,128)(2,1)S(1)}, u32[]{:S(2)}, u32[]{:S(2)}) collective-permute-start(bf16[224,768]{1,0:T(8,128)(2,1)S(1)} %get-tuple-element.308.refs_3_), channel_id=1, source_target_pairs={{0,2},{1,3},{2,0},{3,1},{4,6},{5,7},{6,4},{7,5},{8,10},{9,11},{10,... | collective-permute-start | bytes 1032200 | tf_op jit(solution)/shard_map/ppermute | solution.py:605
  40.7 4.3 %collective-permute-start.15 = (bf16[224,768]{1,0:T(8,128)(2,1)S(1)}, bf16[224,768]{1,0:T(8,128)(2,1)S(1)}, u32[]{:S(2)}, u32[]{:S(2)}) collective-permute-start(bf16[224,768]{1,0:T(8,128)(2,1)S(1)} %get-tuple-element.308.refs_3_), channel_id=1, source_target_pairs={{0,1},{1,0},{2,3},{3,2},{4,5},{5,4},{6,7},{7,6},{8,9},{9,8},{10,11... | collective-permute-start | bytes 1032200 | tf_op jit(solution)/shard_map/ppermute | solution.py:605
  43.3 10.5 %collective-permute-start.17 = (bf16[224,768]{1,0:T(8,128)(2,1)S(1)}, bf16[224,768]{1,0:T(8,128)(2,1)S(1)}, u32[]{:S(2)}, u32[]{:S(2)}) collective-permute-start(bf16[224,768]{1,0:T(8,128)(2,1)S(1)} %get-tuple-element.329.refs_3_), channel_id=1, source_target_pairs={{0,2},{1,3},{2,0},{3,1},{4,6},{5,7},{6,4},{7,5},{8,10},{9,11},{10,... | collective-permute-start | bytes 1032200 | tf_op jit(solution)/shard_map/ppermute | solution.py:605
  49.1 4.7 %collective-permute-start.20 = (bf16[224,768]{1,0:T(8,128)(2,1)S(1)}, bf16[224,768]{1,0:T(8,128)(2,1)S(1)}, u32[]{:S(2)}, u32[]{:S(2)}) collective-permute-start(bf16[224,768]{1,0:T(8,128)(2,1)S(1)} %get-tuple-element.329.refs_3_), channel_id=1, source_target_pairs={{0,1},{1,0},{2,3},{3,2},{4,5},{5,4},{6,7},{7,6},{8,9},{9,8},{10,11... | collective-permute-start | bytes 1032200 | tf_op jit(solution)/shard_map/ppermute | solution.py:605
  59.4 10.1 %collective-permute-start.26 = (bf16[224,768]{1,0:T(8,128)(2,1)S(1)}, bf16[224,768]{1,0:T(8,128)(2,1)S(1)}, u32[]{:S(2)}, u32[]{:S(2)}) collective-permute-start(bf16[224,768]{1,0:T(8,128)(2,1)S(1)} %get-tuple-element.347.refs_3_), channel_id=1, source_target_pairs={{0,2},{1,3},{2,0},{3,1},{4,6},{5,7},{6,4},{7,5},{8,10},{9,11},{10,... | collective-permute-start | bytes 1032200 | tf_op jit(solution)/shard_map/ppermute | solution.py:605
  65.7 29.7 %collective-permute-start.37 = (bf16[4,200,768]{2,1,0:T(8,128)(2,1)S(1)}, bf16[4,200,768]{2,1,0:T(8,128)(2,1)S(1)}, u32[]{:S(2)}, u32[]{:S(2)}) collective-permute-start(bf16[4,200,768]{2,1,0:T(8,128)(2,1)S(1)} %get-tuple-element.391), channel_id=1, source_target_pairs={{0,4},{4,0},{8,12},{12,8},{16,20},{20,16},{24,28},{28,24},{1,5},{5... | collective-permute-start | bytes 3686408 | tf_op jit(solution)/shard_map/ppermute | solution.py:605
  67.2 4.0 %collective-permute-start.29 = (bf16[224,768]{1,0:T(8,128)(2,1)S(1)}, bf16[224,768]{1,0:T(8,128)(2,1)S(1)}, u32[]{:S(2)}, u32[]{:S(2)}) collective-permute-start(bf16[224,768]{1,0:T(8,128)(2,1)S(1)} %get-tuple-element.347.refs_3_), channel_id=1, source_target_pairs={{0,1},{1,0},{2,3},{3,2},{4,5},{5,4},{6,7},{7,6},{8,9},{9,8},{10,11... | collective-permute-start | bytes 1032200 | tf_op jit(solution)/shard_map/ppermute | solution.py:605
  69.5 12.9 %collective-permute-start.31 = (bf16[224,768]{1,0:T(8,128)(2,1)S(1)}, bf16[224,768]{1,0:T(8,128)(2,1)S(1)}, u32[]{:S(2)}, u32[]{:S(2)}) collective-permute-start(bf16[224,768]{1,0:T(8,128)(2,1)S(1)} %get-tuple-element.367.refs_3_), channel_id=1, source_target_pairs={{0,2},{1,3},{2,0},{3,1},{4,6},{5,7},{6,4},{7,5},{8,10},{9,11},{10,... | collective-permute-start | bytes 1032200 | tf_op jit(solution)/shard_map/ppermute | solution.py:605
  80.2 4.2 %collective-permute-start.34 = (bf16[224,768]{1,0:T(8,128)(2,1)S(1)}, bf16[224,768]{1,0:T(8,128)(2,1)S(1)}, u32[]{:S(2)}, u32[]{:S(2)}) collective-permute-start(bf16[224,768]{1,0:T(8,128)(2,1)S(1)} %get-tuple-element.367.refs_3_), channel_id=1, source_target_pairs={{0,1},{1,0},{2,3},{3,2},{4,5},{5,4},{6,7},{7,6},{8,9},{9,8},{10,11... | collective-permute-start | bytes 1032200 | tf_op jit(solution)/shard_map/ppermute | solution.py:605
  82.8 14.5 %collective-permute-start.36 = (bf16[224,768]{1,0:T(8,128)(2,1)S(1)}, bf16[224,768]{1,0:T(8,128)(2,1)S(1)}, u32[]{:S(2)}, u32[]{:S(2)}) collective-permute-start(bf16[224,768]{1,0:T(8,128)(2,1)S(1)} %get-tuple-element.389.refs_1_), channel_id=1, source_target_pairs={{0,2},{1,3},{2,0},{3,1},{4,6},{5,7},{6,4},{7,5},{8,10},{9,11},{10,... | collective-permute-start | bytes 1032200 | tf_op jit(solution)/shard_map/ppermute | solution.py:605
  95.7 15.9 %collective-permute-start.43 = (bf16[2,200,768]{2,1,0:T(8,128)(2,1)S(1)}, bf16[2,200,768]{2,1,0:T(8,128)(2,1)S(1)}, u32[]{:S(2)}, u32[]{:S(2)}) collective-permute-start(bf16[2,200,768]{2,1,0:T(8,128)(2,1)S(1)} %get-tuple-element.410), channel_id=1, source_target_pairs={{0,8},{4,12},{8,0},{12,4},{16,24},{20,28},{24,16},{28,20},{1,9},{5... | collective-permute-start | bytes 1843208 | tf_op jit(solution)/shard_map/ppermute | solution.py:605
  97.8 15.5 %collective-permute-start.47 = (bf16[224,768]{1,0:T(8,128)(2,1)S(1)}, bf16[224,768]{1,0:T(8,128)(2,1)S(1)}, u32[]{:S(2)}, u32[]{:S(2)}) collective-permute-start(bf16[224,768]{1,0:T(8,128)(2,1)S(1)} %get-tuple-element.418.refs_1_), channel_id=1, source_target_pairs={{0,2},{1,3},{2,0},{3,1},{4,6},{5,7},{6,4},{7,5},{8,10},{9,11},{10,... | collective-permute-start | bytes 1032200 | tf_op jit(solution)/shard_map/ppermute | solution.py:605
  104.8 8.7 %collective-permute-start.48 = (bf16[224,768]{1,0:T(8,128)(2,1)S(1)}, bf16[224,768]{1,0:T(8,128)(2,1)S(1)}, u32[]{:S(2)}, u32[]{:S(2)}) collective-permute-start(bf16[224,768]{1,0:T(8,128)(2,1)S(1)} %get-tuple-element.418.refs_1_), channel_id=1, source_target_pairs={{0,1},{1,0},{2,3},{3,2},{4,5},{5,4},{6,7},{7,6},{8,9},{9,8},{10,11... | collective-permute-start | bytes 1032200 | tf_op jit(solution)/shard_map/ppermute | solution.py:605
  105.7 32.9 %collective-permute-start.57 = (bf16[2,192,1500]{2,1,0:T(8,128)(2,1)S(1)}, bf16[2,192,1500]{2,1,0:T(8,128)(2,1)S(1)}, u32[]{:S(2)}, u32[]{:S(2)}) collective-permute-start(bf16[2,192,1500]{2,1,0:T(8,128)(2,1)S(1)} %get-tuple-element.452), channel_id=1, source_target_pairs={{0,1},{1,0},{2,3},{3,2},{4,5},{5,4},{6,7},{7,6},{8,9},{9,8},{10,11... | collective-permute-start | bytes 3456008 | tf_op jit(solution)/shard_map/ppermute | solution.py:605
  105.9 32.7 %collective-permute-start.58 = (bf16[2,192,1500]{2,1,0:T(8,128)(2,1)S(1)}, bf16[2,192,1500]{2,1,0:T(8,128)(2,1)S(1)}, u32[]{:S(2)}, u32[]{:S(2)}) collective-permute-start(bf16[2,192,1500]{2,1,0:T(8,128)(2,1)S(1)} %get-tuple-element.453), channel_id=1, source_target_pairs={{0,1},{1,0},{2,3},{3,2},{4,5},{5,4},{6,7},{7,6},{8,9},{9,8},{10,11... | collective-permute-start | bytes 3456008 | tf_op jit(solution)/shard_map/ppermute | solution.py:605
  111.5 19.1 %collective-permute-start.42 = (bf16[4,104,768]{2,1,0:T(8,128)(2,1)S(1)}, bf16[4,104,768]{2,1,0:T(8,128)(2,1)S(1)}, u32[]{:S(2)}, u32[]{:S(2)}) collective-permute-start(bf16[4,104,768]{2,1,0:T(8,128)(2,1)S(1)} %get-tuple-element.408), channel_id=1, source_target_pairs={{0,4},{4,0},{8,12},{12,8},{16,20},{20,16},{24,28},{28,24},{1,5},{5... | collective-permute-start | bytes 1916936 | tf_op jit(solution)/shard_map/ppermute | solution.py:605
  113.5 17.2 %collective-permute-start.46 = (bf16[1,200,768]{2,1,0:T(8,128)(2,1)S(1)}, bf16[1,200,768]{2,1,0:T(8,128)(2,1)S(1)}, u32[]{:S(2)}, u32[]{:S(2)}) collective-permute-start(bf16[1,200,768]{2,1,0:T(8,128)(2,1)S(1)} %get-tuple-element.417), channel_id=1, source_target_pairs={{0,16},{4,20},{8,24},{12,28},{16,0},{20,4},{24,8},{28,12},{1,17},{... | collective-permute-start | bytes 921608 | tf_op jit(solution)/shard_map/ppermute | solution.py:605
  116.1 5.2 %collective-permute-start.22 = (bf16[112,768]{1,0:T(8,128)(2,1)S(1)}, bf16[112,768]{1,0:T(8,128)(2,1)S(1)}, u32[]{:S(2)}, u32[]{:S(2)}) collective-permute-start(bf16[112,768]{1,0:T(8,128)(2,1)S(1)} %get-tuple-element.340), channel_id=1, source_target_pairs={{0,1},{1,0},{2,3},{3,2},{4,5},{5,4},{6,7},{7,6},{8,9},{9,8},{10,11... | collective-permute-start | bytes 516104 | tf_op jit(solution)/shard_map/ppermute | solution.py:605
  121.3 9.8 %collective-permute-start.50 = (bf16[112,768]{1,0:T(8,128)(2,1)S(1)}, bf16[112,768]{1,0:T(8,128)(2,1)S(1)}, u32[]{:S(2)}, u32[]{:S(2)}) collective-permute-start(bf16[112,768]{1,0:T(8,128)(2,1)S(1)} %get-tuple-element.428), channel_id=1, source_target_pairs={{0,1},{1,0},{2,3},{3,2},{4,5},{5,4},{6,7},{7,6},{8,9},{9,8},{10,11... | collective-permute-start | bytes 516104 | tf_op jit(solution)/shard_map/ppermute | solution.py:605
  130.6 5.5 %collective-permute-start.23 = (bf16[112,768]{1,0:T(8,128)(2,1)S(1)}, bf16[112,768]{1,0:T(8,128)(2,1)S(1)}, u32[]{:S(2)}, u32[]{:S(2)}) collective-permute-start(bf16[112,768]{1,0:T(8,128)(2,1)S(1)} %get-tuple-element.341), channel_id=1, source_target_pairs={{0,1},{1,0},{2,3},{3,2},{4,5},{5,4},{6,7},{7,6},{8,9},{9,8},{10,11... | collective-permute-start | bytes 516104 | tf_op jit(solution)/shard_map/ppermute | solution.py:605
  131.1 5.7 %collective-permute-start.24 = (bf16[112,768]{1,0:T(8,128)(2,1)S(1)}, bf16[112,768]{1,0:T(8,128)(2,1)S(1)}, u32[]{:S(2)}, u32[]{:S(2)}) collective-permute-start(bf16[112,768]{1,0:T(8,128)(2,1)S(1)} %get-tuple-element.345), channel_id=1, source_target_pairs={{0,1},{1,0},{2,3},{3,2},{4,5},{5,4},{6,7},{7,6},{8,9},{9,8},{10,11... | collective-permute-start | bytes 516104 | tf_op jit(solution)/shard_map/ppermute | solution.py:605
  132.0 13.5 %collective-permute-start.55 = (bf16[224,768]{1,0:T(8,128)(2,1)S(1)}, bf16[224,768]{1,0:T(8,128)(2,1)S(1)}, u32[]{:S(2)}, u32[]{:S(2)}) collective-permute-start(bf16[224,768]{1,0:T(8,128)(2,1)S(1)} %get-tuple-element.447.refs_1_), channel_id=1, source_target_pairs={{0,2},{1,3},{2,0},{3,1},{4,6},{5,7},{6,4},{7,5},{8,10},{9,11},{10,... | collective-permute-start | bytes 1032200 | tf_op jit(solution)/shard_map/ppermute | solution.py:605
  136.1 9.4 %collective-permute-start.56 = (bf16[2,104,768]{2,1,0:T(8,128)(2,1)S(1)}, bf16[2,104,768]{2,1,0:T(8,128)(2,1)S(1)}, u32[]{:S(2)}, u32[]{:S(2)}) collective-permute-start(bf16[2,104,768]{2,1,0:T(8,128)(2,1)S(1)} %get-tuple-element.449), channel_id=1, source_target_pairs={{0,8},{4,12},{8,0},{12,4},{16,24},{20,28},{24,16},{28,20},{1,9},{5... | collective-permute-start | bytes 958472 | tf_op jit(solution)/shard_map/ppermute | solution.py:605
  138.3 10.0 %collective-permute-start.59 = (bf16[224,768]{1,0:T(8,128)(2,1)S(1)}, bf16[224,768]{1,0:T(8,128)(2,1)S(1)}, u32[]{:S(2)}, u32[]{:S(2)}) collective-permute-start(bf16[224,768]{1,0:T(8,128)(2,1)S(1)} %get-tuple-element.447.refs_1_), channel_id=1, source_target_pairs={{0,1},{1,0},{2,3},{3,2},{4,5},{5,4},{6,7},{7,6},{8,9},{9,8},{10,11... | collective-permute-start | bytes 1032200 | tf_op jit(solution)/shard_map/ppermute | solution.py:605
  145.6 10.9 %collective-permute-start.54 = (bf16[224,768]{1,0:T(8,128)(2,1)S(1)}, bf16[224,768]{1,0:T(8,128)(2,1)S(1)}, u32[]{:S(2)}, u32[]{:S(2)}) collective-permute-start(bf16[224,768]{1,0:T(8,128)(2,1)S(1)} %get-tuple-element.445.refs_1_), channel_id=1, source_target_pairs={{0,2},{1,3},{2,0},{3,1},{4,6},{5,7},{6,4},{7,5},{8,10},{9,11},{10,... | collective-permute-start | bytes 1032200 | tf_op jit(solution)/shard_map/ppermute | solution.py:605
  146.2 16.5 %collective-permute-start.53 = (bf16[4,104,768]{2,1,0:T(8,128)(2,1)S(1)}, bf16[4,104,768]{2,1,0:T(8,128)(2,1)S(1)}, u32[]{:S(2)}, u32[]{:S(2)}) collective-permute-start(bf16[4,104,768]{2,1,0:T(8,128)(2,1)S(1)} %get-tuple-element.443), channel_id=1, source_target_pairs={{0,4},{4,0},{8,12},{12,8},{16,20},{20,16},{24,28},{28,24},{1,5},{5... | collective-permute-start | bytes 1916936 | tf_op jit(solution)/shard_map/ppermute | solution.py:605
  146.7 40.4 %collective-permute-start.52 = (bf16[2,224,768]{2,1,0:T(8,128)(2,1)S(1)}, bf16[2,224,768]{2,1,0:T(8,128)(2,1)S(1)}, u32[]{:S(2)}, u32[]{:S(2)}) collective-permute-start(bf16[2,224,768]{2,1,0:T(8,128)(2,1)S(1)} %get-tuple-element.441.refs_2_), channel_id=1, source_target_pairs={{0,2},{1,3},{2,0},{3,1},{4,6},{5,7},{6,4},{7,5},{8,10},{9,11},{10,... | collective-permute-start | bytes 2064392 | tf_op jit(solution)/shard_map/ppermute | solution.py:605
  148.3 8.3 %collective-permute-start.61 = (bf16[224,768]{1,0:T(8,128)(2,1)S(1)}, bf16[224,768]{1,0:T(8,128)(2,1)S(1)}, u32[]{:S(2)}, u32[]{:S(2)}) collective-permute-start(bf16[224,768]{1,0:T(8,128)(2,1)S(1)} %get-tuple-element.445.refs_1_), channel_id=1, source_target_pairs={{0,1},{1,0},{2,3},{3,2},{4,5},{5,4},{6,7},{7,6},{8,9},{9,8},{10,11... | collective-permute-start | bytes 1032200 | tf_op jit(solution)/shard_map/ppermute | solution.py:605
  162.8 24.1 %collective-permute-start.63 = (bf16[2,104,768]{2,1,0:T(8,128)(2,1)S(1)}, bf16[2,104,768]{2,1,0:T(8,128)(2,1)S(1)}, u32[]{:S(2)}, u32[]{:S(2)}) collective-permute-start(bf16[2,104,768]{2,1,0:T(8,128)(2,1)S(1)} %get-tuple-element.463), channel_id=1, source_target_pairs={{0,8},{4,12},{8,0},{12,4},{16,24},{20,28},{24,16},{28,20},{1,9},{5... | collective-permute-start | bytes 958472 | tf_op jit(solution)/shard_map/ppermute | solution.py:605
  163.6 21.6 %collective-permute-start.65 = (bf16[1,200,768]{2,1,0:T(8,128)(2,1)S(1)}, bf16[1,200,768]{2,1,0:T(8,128)(2,1)S(1)}, u32[]{:S(2)}, u32[]{:S(2)}) collective-permute-start(bf16[1,200,768]{2,1,0:T(8,128)(2,1)S(1)} %get-tuple-element.466.refs_0_), channel_id=1, source_target_pairs={{0,16},{4,20},{8,24},{12,28},{16,0},{20,4},{24,8},{28,12},{1,17},{... | collective-permute-start | bytes 921608 | tf_op jit(solution)/shard_map/ppermute | solution.py:605
  166.9 20.0 %collective-permute-start.64 = (bf16[1,104,768]{2,1,0:T(8,128)(2,1)S(1)}, bf16[1,104,768]{2,1,0:T(8,128)(2,1)S(1)}, u32[]{:S(2)}, u32[]{:S(2)}) collective-permute-start(bf16[1,104,768]{2,1,0:T(8,128)(2,1)S(1)} %get-tuple-element.465), channel_id=1, source_target_pairs={{0,16},{4,20},{8,24},{12,28},{16,0},{20,4},{24,8},{28,12},{1,17},{... | collective-permute-start | bytes 479240 | tf_op jit(solution)/shard_map/ppermute | solution.py:605
  167.0 21.8 %collective-permute-start.66 = (bf16[2,224,768]{2,1,0:T(8,128)(2,1)S(1)}, bf16[2,224,768]{2,1,0:T(8,128)(2,1)S(1)}, u32[]{:S(2)}, u32[]{:S(2)}) collective-permute-start(bf16[2,224,768]{2,1,0:T(8,128)(2,1)S(1)} %get-tuple-element.441.refs_2_), channel_id=1, source_target_pairs={{0,1},{1,0},{2,3},{3,2},{4,5},{5,4},{6,7},{7,6},{8,9},{9,8},{10,11... | collective-permute-start | bytes 2064392 | tf_op jit(solution)/shard_map/ppermute | solution.py:605
  187.1 16.3 %collective-permute-start.71 = (bf16[2,200,768]{2,1,0:T(8,128)(2,1)S(1)}, bf16[2,200,768]{2,1,0:T(8,128)(2,1)S(1)}, u32[]{:S(2)}, u32[]{:S(2)}) collective-permute-start(bf16[2,200,768]{2,1,0:T(8,128)(2,1)S(1)} %get-tuple-element.480.refs_0_), channel_id=1, source_target_pairs={{0,8},{4,12},{8,0},{12,4},{16,24},{20,28},{24,16},{28,20},{1,9},{5... | collective-permute-start | bytes 1843208 | tf_op jit(solution)/shard_map/ppermute | solution.py:605
  187.2 40.8 %collective-permute-start.68 = (bf16[2,192,1500]{2,1,0:T(8,128)(2,1)S(1)}, bf16[2,192,1500]{2,1,0:T(8,128)(2,1)S(1)}, u32[]{:S(2)}, u32[]{:S(2)}) collective-permute-start(bf16[2,192,1500]{2,1,0:T(8,128)(2,1)S(1)} %get-tuple-element.476), channel_id=1, source_target_pairs={{0,2},{1,3},{2,0},{3,1},{4,6},{5,7},{6,4},{7,5},{8,10},{9,11},{10,... | collective-permute-start | bytes 3456008 | tf_op jit(solution)/shard_map/ppermute | solution.py:605
  203.5 40.4 %collective-permute-start.77 = (bf16[4,200,768]{2,1,0:T(8,128)(2,1)S(1)}, bf16[4,200,768]{2,1,0:T(8,128)(2,1)S(1)}, u32[]{:S(2)}, u32[]{:S(2)}) collective-permute-start(bf16[4,200,768]{2,1,0:T(8,128)(2,1)S(1)} %get-tuple-element.494.refs_0_), channel_id=1, source_target_pairs={{0,4},{4,0},{8,12},{12,8},{16,20},{20,16},{24,28},{28,24},{1,5},{5... | collective-permute-start | bytes 3686408 | tf_op jit(solution)/shard_map/ppermute | solution.py:605
  204.1 9.6 %collective-permute-start.70 = (bf16[1,104,768]{2,1,0:T(8,128)(2,1)S(1)}, bf16[1,104,768]{2,1,0:T(8,128)(2,1)S(1)}, u32[]{:S(2)}, u32[]{:S(2)}) collective-permute-start(bf16[1,104,768]{2,1,0:T(8,128)(2,1)S(1)} %get-tuple-element.479.refs_0_), channel_id=1, source_target_pairs={{0,16},{4,20},{8,24},{12,28},{16,0},{20,4},{24,8},{28,12},{1,17},{... | collective-permute-start | bytes 479240 | tf_op jit(solution)/shard_map/ppermute | solution.py:605
  213.7 15.9 %collective-permute-start.73 = (bf16[2,104,768]{2,1,0:T(8,128)(2,1)S(1)}, bf16[2,104,768]{2,1,0:T(8,128)(2,1)S(1)}, u32[]{:S(2)}, u32[]{:S(2)}) collective-permute-start(bf16[2,104,768]{2,1,0:T(8,128)(2,1)S(1)} %get-tuple-element.487.refs_0_), channel_id=1, source_target_pairs={{0,8},{4,12},{8,0},{12,4},{16,24},{20,28},{24,16},{28,20},{1,9},{5... | collective-permute-start | bytes 958472 | tf_op jit(solution)/shard_map/ppermute | solution.py:605
  213.8 10.7 %collective-permute-start.69 = (bf16[1,104,768]{2,1,0:T(8,128)(2,1)S(1)}, bf16[1,104,768]{2,1,0:T(8,128)(2,1)S(1)}, u32[]{:S(2)}, u32[]{:S(2)}) collective-permute-start(bf16[1,104,768]{2,1,0:T(8,128)(2,1)S(1)} %get-tuple-element.478), channel_id=1, source_target_pairs={{0,16},{4,20},{8,24},{12,28},{16,0},{20,4},{24,8},{28,12},{1,17},{... | collective-permute-start | bytes 479240 | tf_op jit(solution)/shard_map/ppermute | solution.py:605
  224.5 10.7 %collective-permute-start.72 = (bf16[1,104,768]{2,1,0:T(8,128)(2,1)S(1)}, bf16[1,104,768]{2,1,0:T(8,128)(2,1)S(1)}, u32[]{:S(2)}, u32[]{:S(2)}) collective-permute-start(bf16[1,104,768]{2,1,0:T(8,128)(2,1)S(1)} %get-tuple-element.486.refs_0_), channel_id=1, source_target_pairs={{0,16},{4,20},{8,24},{12,28},{16,0},{20,4},{24,8},{28,12},{1,17},{... | collective-permute-start | bytes 479240 | tf_op jit(solution)/shard_map/ppermute | solution.py:605
  229.7 17.4 %collective-permute-start.76 = (bf16[4,104,768]{2,1,0:T(8,128)(2,1)S(1)}, bf16[4,104,768]{2,1,0:T(8,128)(2,1)S(1)}, u32[]{:S(2)}, u32[]{:S(2)}) collective-permute-start(bf16[4,104,768]{2,1,0:T(8,128)(2,1)S(1)} %get-tuple-element.493.refs_0_), channel_id=1, source_target_pairs={{0,4},{4,0},{8,12},{12,8},{16,20},{20,16},{24,28},{28,24},{1,5},{5... | collective-permute-start | bytes 1916936 | tf_op jit(solution)/shard_map/ppermute | solution.py:605
  235.2 7.1 %collective-permute-start.74 = (bf16[2,104,768]{2,1,0:T(8,128)(2,1)S(1)}, bf16[2,104,768]{2,1,0:T(8,128)(2,1)S(1)}, u32[]{:S(2)}, u32[]{:S(2)}) collective-permute-start(bf16[2,104,768]{2,1,0:T(8,128)(2,1)S(1)} %get-tuple-element.490.refs_0_), channel_id=1, source_target_pairs={{0,8},{4,12},{8,0},{12,4},{16,24},{20,28},{24,16},{28,20},{1,9},{5... | collective-permute-start | bytes 958472 | tf_op jit(solution)/shard_map/ppermute | solution.py:605
  242.3 17.2 %collective-permute-start.75 = (bf16[4,104,768]{2,1,0:T(8,128)(2,1)S(1)}, bf16[4,104,768]{2,1,0:T(8,128)(2,1)S(1)}, u32[]{:S(2)}, u32[]{:S(2)}) collective-permute-start(bf16[4,104,768]{2,1,0:T(8,128)(2,1)S(1)} %get-tuple-element.492.refs_0_), channel_id=1, source_target_pairs={{0,4},{4,0},{8,12},{12,8},{16,20},{20,16},{24,28},{28,24},{1,5},{5... | collective-permute-start | bytes 1916936 | tf_op jit(solution)/shard_map/ppermute | solution.py:605
  262.5 3.8 %collective-permute-start.79 = (f32[8,768]{1,0:T(8,128)S(1)}, f32[8,768]{1,0:T(8,128)S(1)}, u32[]{:S(2)}, u32[]{:S(2)}) collective-permute-start(f32[8,768]{1,0:T(8,128)S(1)} %add.6), channel_id=1, source_target_pairs={{0,2},{1,3},{2,0},{3,1},{4,6},{5,7},{6,4},{7,5},{8,10},{9,11},{10,... | collective-permute-start | bytes 73736 | tf_op jit(solution)/shard_map/ppermute | solution.py:605
  (37 other events, 104.6 us)

commit v3 on v2

--- a/solution.py
+++ b/solution.py
@@ -18,6 +18,7 @@
 INV_ROOT_TAU = 1.0 / math.sqrt(2.0 * math.pi)
 VMEM_BYTES = 20 * 1024 * 1024
 COST = 1
+ORDER = ("P", "AB", "FXl", "M", "a", "FXSm", "N", "b", "FXS", "ge", "FXSc", "XS", "u", "S", "v", "o", "w")
 
 
 def dot(left, right, left_dim, right_dim):
@@ -102,7 +103,7 @@
     return jnp.where(rows == first + 2, last, out).astype(BF16)
 
 
-def store_halves(part, side, keep_ref, send_ref, rest_ref):
+def store_halves(part, side, keep_ref, send_ref, rest_ref=None):
     half = part.shape[0] // 2
     edge = send_ref.shape[0]
     low = part.astype(BF16)
@@ -111,22 +112,22 @@
     def _():
         keep_ref[...] = low[:half]
         send_ref[...] = low[half : half + edge]
-        rest_ref[...] = low[half + edge :]
+        if rest_ref is not None:
+            rest_ref[...] = low[half + edge :]
 
     @pl.when(side == 1)
     def _():
         keep_ref[...] = low[half:]
         send_ref[...] = low[:edge]
-        rest_ref[...] = low[edge:half]
+        if rest_ref is not None:
+            rest_ref[...] = low[edge:half]
 
 
 def join_halves(pieces, side, scratch):
-    own, own_far, other, other_far = pieces
+    own, other = pieces
     half = own.shape[0]
-    here = pl.multiple_of(side * half, 16)
-    there = pl.multiple_of((1 - side) * half, 16)
-    scratch[pl.ds(here, half), :] = own[...].astype(F32) + own_far[...].astype(F32)
-    scratch[pl.ds(there, half), :] = other[...].astype(F32) + other_far[...].astype(F32)
+    scratch[pl.ds(pl.multiple_of(side * half, 16), half), :] = own[...].astype(F32)
+    scratch[pl.ds(pl.multiple_of((1 - side) * half, 16), half), :] = other[...].astype(F32)
     return scratch[...]
 
 
@@ -262,10 +263,10 @@
         va_o[head, HEAD:AUG, :] = other
 
 
-def cross_forward(item, chunk, x_ref, s0, s1, s2, s3, obias, gain, shift, wq, qbias, wo, ka, va, x1_o, h2_o, q_o, o_o, lse_o, keep_o, send_o, rest_o, whole, qa):
+def cross_forward(item, chunk, x_ref, s0, s1, obias, gain, shift, wq, qbias, wo, ka, va, x1_o, h2_o, q_o, o_o, lse_o, keep_o, send_o, rest_o, whole, qa):
     count = x_ref.shape[1]
     side = mp_side()
-    after = x_ref[item].astype(F32) + join_halves((s0, s1, s2, s3), side, whole) + line(obias)
+    after = x_ref[item].astype(F32) + join_halves((s0, s1), side, whole) + line(obias)
     x1_o[...] = after
     unit, _ = norm_parts(after)
     normed = (unit * line(gain) + line(shift)).astype(BF16)
@@ -283,9 +284,9 @@
     return og[item].astype(F32) * jnp.where(valid, weight, 0.0)
 
 
-def feed(item, lengths, tasks, x1, s0, s1, s2, s3, og, obias, gain, shift, we, ebias, wc, x2_o, h3_o, a_o, dz_o, gy_o, vec_o, bkeep_o, bsend_o, brest_o, whole):
+def feed(item, lengths, tasks, x1, s0, s1, og, obias, gain, shift, we, ebias, wc, x2_o, h3_o, a_o, dz_o, gy_o, vec_o, bkeep_o, bsend_o, brest_o, whole):
     side = mp_side()
-    after = x1[...] + join_halves((s0, s1, s2, s3), side, whole) + line(obias)
+    after = x1[...] + join_halves((s0, s1), side, whole) + line(obias)
     x2_o[...] = after
     unit, _ = norm_parts(after)
     normed = (unit * line(gain) + line(shift)).astype(BF16)
@@ -306,8 +307,8 @@
     vec_o[...] = jnp.where(pick == 1, jnp.sum(inner.astype(F32), axis=0, keepdims=True), out)
 
 
-def feed_out_part(active, wc, keep_o, send_o, rest_o):
-    store_halves(nn(active[...], wc[...]), mp_side(), keep_o, send_o, rest_o)
+def feed_out_part(active, wc, keep_o, send_o):
+    store_halves(nn(active[...], wc[...]), mp_side(), keep_o, send_o)
 
 
 def sum_of(refs):
@@ -326,12 +327,12 @@
     whole[width:edge, :] = sum_of([tn(a[k][...], gy[k][...]) for k in range(items)])
     whole[edge:, :] = jnp.zeros((whole.shape[0] - edge, width), F32)
     whole[edge : edge + 8, :] = sum_of([v[...] for v in vecs])
-    scatter_blocks(whole, keep_o, send_o)
-
-
-def cross_backward(item, chunk, lengths, tasks, x2, s0, s1, s2, s3, og, gain, wo, wq, ka, va, q, o, lse, dx2_o, g2_o, dq_o, dk_o, dv_o, vec_o, keep_o, send_o, rest_o, whole, qa, doa, do):
+    scatter_blocks(whole, keep_o, send_o, X_FIRST)
+
+
+def cross_backward(item, chunk, lengths, tasks, x2, s0, s1, og, gain, wo, wq, ka, va, q, o, lse, dx2_o, g2_o, dq_o, dk_o, dv_o, vec_o, keep_o, send_o, rest_o, whole, qa, doa, do):
     side = mp_side()
-    grad_in = join_halves((s0, s1, s2, s3), side, whole)
+    grad_in = join_halves((s0, s1), side, whole)
     grad, gain_row, shift_row = norm_back(x2[...], line(gain), grad_in)
     total = upstream_rows(item, lengths, tasks, og) + grad
     dx2_o[...] = total
@@ -367,15 +368,22 @@
             send_o[slot] = piece
 
 
-def place_of(block):
-    return (block % 2) * 4 + (block // 2 % 2) * 2 + block // 4 % 2
-
-
-def scatter_blocks(whole, keep_o, send_o):
+X_FIRST = (1, 2, 4)
+Z_FIRST = (2, 4, 1)
+
+
+def place_of(block, steps):
+    place = 0
+    for bit in steps:
+        place = place * 2 + block // bit % 2
+    return place
+
+
+def scatter_blocks(whole, keep_o, send_o, steps):
     position = lax.axis_index("dp") % 8
     rows = keep_o.shape[1]
     for block in range(8):
-        place = place_of(lax.bitwise_xor(position, block))
+        place = place_of(lax.bitwise_xor(position, block), steps)
         piece = whole[block * rows : (block + 1) * rows, :].astype(BF16)
 
         @pl.when(place < 4)
@@ -387,11 +395,11 @@
             send_o[place - 4] = piece
 
 
-def gather_blocks(near, far, whole):
+def gather_blocks(near, far, whole, steps):
     position = lax.axis_index("dp") % 8
     rows = near.shape[1]
     for block in range(8):
-        place = place_of(lax.bitwise_xor(position, block))
+        place = place_of(lax.bitwise_xor(position, block), steps)
         spot = slice(block * rows, (block + 1) * rows)
 
         @pl.when(place < 4)
@@ -415,12 +423,12 @@
     whole[3 * rows : 4 * rows, :] = sum_of([nn(o[k][...], g2[k][...]) for k in span])
     whole[4 * rows :, :] = jnp.zeros((whole.shape[0] - 4 * rows, whole.shape[1]), F32)
     whole[4 * rows : 4 * rows + 8, :] = sum_of([v[...] for v in vecs])
-    scatter_blocks(whole, keep_o, send_o)
-
-
-def self_backward(item, x1, s0, s1, s2, s3, dx2, x_ref, gain, wo, wq, wk, wv, ka, va, q, o, lse, dx1_o, g1_o, dqkv_o, vec_o, keep_o, send_o, rest_o, whole, qa, doa, do):
+    scatter_blocks(whole, keep_o, send_o, X_FIRST)
+
+
+def self_backward(item, x1, s0, s1, dx2, x_ref, gain, wo, wq, wk, wv, ka, va, q, o, lse, dx1_o, g1_o, dqkv_o, vec_o, keep_o, send_o, whole, qa, doa, do):
     side = mp_side()
-    grad_in = join_halves((s0, s1, s2, s3), side, whole)
+    grad_in = join_halves((s0, s1), side, whole)
     grad, gain_row, shift_row = norm_back(x1[...], line(gain), grad_in)
     total = dx2[...] + grad
     dx1_o[...] = total
@@ -433,7 +441,7 @@
     dv_o = dqkv_o.at[2 * rows : 3 * rows]
     attention_backward(q, ka, va, o, lse, do, qa, doa, dq_o, dk_o, dv_o, q.shape[1], True)
     part = tn(dq_o[...], wq[...]) + tn(dk_o[...], wk[...]) + tn(dv_o[...], wv[...])
-    store_halves(part, side, keep_o, send_o, rest_o)
+    store_halves(part, side, keep_o, send_o)
     unit, _ = norm_parts(x_ref[item].astype(F32))
     pick = iota((8, vec_o.shape[1]), 0)
     out = jnp.where(pick == 0, gain_row, 0.0)
@@ -458,30 +466,35 @@
     whole[3 * rows : 4 * rows, :] = sum_of([nn(o[k][...], g1[k][...]) for k in span])
     whole[4 * rows :, :] = jnp.zeros((whole.shape[0] - 4 * rows, whole.shape[1]), F32)
     whole[4 * rows : 4 * rows + 8, :] = sum_of([v[...] for v in vecs])
-    scatter_blocks(whole, keep_o, send_o)
-
-
-def unpack(near, far, *rest):
+    scatter_blocks(whole, keep_o, send_o, X_FIRST)
+
+
+def unpack(matrices, lines, steps, near, far, *rest):
     outs, whole = rest[:-1], rest[-1]
-    gather_blocks(near, far, whole)
+    gather_blocks(near, far, whole, steps)
     start = 0
-    for out in outs:
+    for out in outs[:matrices]:
         out[...] = whole[start : start + out.shape[0], :]
         start += out.shape[0]
+    for k, out in enumerate(outs[matrices : matrices + lines]):
+        out[...] = whole[start + k : start + k + 1, 0 : out.shape[0]].reshape(out.shape)
+    for out in outs[matrices + lines :]:
+        out[...] = whole[start : start + out.shape[0], :]
 
 
 def finish_out(items, *refs):
-    x2, pieces, (bias, out, whole) = refs[:items], refs[items : items + 4], refs[items + 4 :]
+    x2, pieces, (bias, out, whole) = refs[:items], refs[items : items + 2], refs[items + 2 :]
     for k in range(items):
         total = x2[k][...] + join_halves([p.at[k] for p in pieces], mp_side(), whole) + line(bias)
         out[k] = total.astype(BF16)
 
 
-def finish_grad(item, dx1, s0, s1, s2, s3, x_ref, gain, *rest):
-    out, whole = rest[-2:]
-    grad_in = join_halves((s0, s1, s2, s3), mp_side(), whole)
-    grad, _, _ = norm_back(x_ref[item].astype(F32), line(gain), grad_in)
-    out[...] = dx1[...] + grad
+def finish_grad(items, *refs):
+    dx1, pieces, (x_ref, gain, out, whole) = refs[:items], refs[items : items + 2], refs[items + 2 :]
+    for k in range(items):
+        grad_in = join_halves([p.at[k] for p in pieces], mp_side(), whole)
+        grad, _, _ = norm_back(x_ref[k].astype(F32), line(gain), grad_in)
+        out[k] = dx1[k][...] + grad
 
 
 def finish_memory(kept, far, out):
@@ -526,6 +539,14 @@
     send[...] = both(left[half:], right[half:])
 
 
+def together(steps, *refs):
+    given = sum(step[1] for step in steps)
+    ins, outs = refs[:given], refs[given:]
+    for body, takes, gives in steps:
+        body(*ins[:takes], *outs[:gives])
+        ins, outs = ins[takes:], outs[gives:]
+
+
 def stack_pair(left, right, out):
     half = left.shape[0]
     out[0:half] = left[...]
@@ -559,6 +580,9 @@
 class Order:
     def __init__(self):
         self.tick = None
+
+    def later(self, value):
+        return lax.optimization_barrier((value, self.tick))[0]
 
     def run(self, body, cost, operands, outs, scratch=(), specs=None, out_specs=None, aliases=None):
         specs = specs or {}
@@ -601,6 +625,16 @@
         return results[:-1]
 
 
+def run_together(order, jobs):
+    steps = [(body, len(operands), len(outs)) for body, operands, outs, _ in jobs]
+    results = order.run(
+        functools.partial(together, steps), 1, [a for job in jobs for a in job[1]], [o for job in jobs for o in job[2]]
+    )
+    for _, _, outs, then in jobs:
+        then(*results[: len(outs)])
+        results = results[len(outs) :]
+
+
 def swap(value, axis, size, bit):
     return lax.ppermute(value, axis, [(k, k ^ bit) for k in range(size)])
 
@@ -617,46 +651,77 @@
     def spread(self, own):
         self.own = own
         self.far = swap(own, "mp", self.size, 2)
-        self.other = swap(own, "mp", self.size, 1)
-
-    def pieces(self):
-        far = self.far
-        if self.order.tick is not None:
-            far = lax.optimization_barrier((far, self.order.tick))[0]
-        return self.own, far, self.other, swap(far, "mp", self.size, 1)
+
+    def meet(self):
+        run_together(self.order, [self.meet_job()])
+
+    def meet_job(self):
+        return add_rows, (self.own, self.far), (near_like(self.own),), self.share
+
+    def share(self, total):
+        self.pieces = total, swap(total, "mp", self.size, 1)
+
+
+class PairSum(MpSum):
+    def __init__(self, order, size, keeps, sends):
+        self.order, self.size, self.keeps = order, size, keeps
+        self.near = [swap(send, "mp", size, 1) for send in sends]
+
+    def job(self):
+        count = len(self.keeps)
+        stack = near_like(self.keeps[0], (count,) + self.keeps[0].shape)
+        parts = [part for pair in zip(self.keeps, self.near) for part in pair]
+        return functools.partial(add_stack, count), parts, (stack,), self.spread
 
 
 class DpSum:
-    def __init__(self, order, size, keep, send):
-        self.order, self.size = order, size
-        self.keep, self.near = keep, swap(send, "dp", size, 1)
+    def __init__(self, order, size, steps, keep, send):
+        self.order, self.size, self.steps = order, size, steps
+        self.keep, self.near = keep, self.swap(send, 0)
         self.stage = 0
 
+    def swap(self, value, step):
+        return swap(value, "dp", self.size, self.steps[step])
+
     def step(self):
-        dims = self.keep.shape
-        if self.stage < 2:
+        run_together(self.order, [self.job()])
+
+    def job(self):
+        dims, stage = self.keep.shape, self.stage
+        self.stage += 1
+        both_parts = (self.keep, self.near)
+        if stage < 2:
             out = near_like(self.keep, (dims[0] // 2,) + dims[1:])
-            self.keep, send = self.order.run(add_split, 0.7, (self.keep, self.near), (out, out))
-            self.near = swap(send, "dp", self.size, 2 << self.stage)
-        elif self.stage == 2:
-            self.keep = self.order.run(add_rows, 0.5, (self.keep, self.near), (near_like(self.keep),))[0]
-            bit = 8
-            while bit < self.size:
-                other = swap(self.keep, "dp", self.size, bit)
-                self.keep = self.order.run(add_rows, 0.5, (self.keep, other), (near_like(self.keep),))[0]
-                bit *= 2
-            self.near = swap(self.keep, "dp", self.size, 4)
-        else:
-            out = near_like(self.keep, (dims[0] * 2,) + dims[1:])
-            self.keep = self.order.run(stack_pair, 0.5, (self.keep, self.near), (out,))[0]
-            self.near = swap(self.keep, "dp", self.size, 2 if self.stage == 3 else 1)
-        self.stage += 1
-
-    def unpack(self, outs):
+
+            def then(keep, send):
+                self.keep, self.near = keep, self.swap(send, stage + 1)
+
+            return add_split, both_parts, (out, out), then
+        if stage == 2:
+
+            def then(total):
+                bit = 8
+                while bit < self.size:
+                    other = swap(total, "dp", self.size, bit)
+                    total = self.order.run(add_rows, 0.5, (total, other), (near_like(total),))[0]
+                    bit *= 2
+                self.keep, self.near = total, self.swap(total, 2)
+
+            return add_rows, both_parts, (near_like(self.keep),), then
+        out = near_like(self.keep, (dims[0] * 2,) + dims[1:])
+
+        def then(total):
+            self.keep, self.near = total, self.swap(total, 4 - stage)
+
+        return stack_pair, both_parts, (out,), then
+
+    def unpack(self, matrices, lines, *more):
         rows = 8 * self.keep.shape[1]
-        specs = [pl.BlockSpec(o.shape, lambda *_: (0, 0)) for o in outs]
+        specs = [pl.BlockSpec(o.shape, lambda *_: (0, 0)) for o in matrices]
+        specs += [pl.BlockSpec(o.shape, lambda *_: (0,)) for o in lines] + [NEAR] * len(more)
         return self.order.run(
-            unpack, 3, (self.keep, self.near), outs, (pltpu.VMEM((rows, outs[0].shape[1]), F32),), None, specs
+            functools.partial(unpack, len(matrices), len(lines), self.steps), 3, (self.keep, self.near),
+            tuple(matrices) + tuple(lines) + more, (pltpu.VMEM((rows, matrices[0].shape[1]), F32),), None, specs,
         )
 
 
@@ -690,6 +755,7 @@
     aug_out = near_shape((heads, AUG, length))
     aug_mem = near_shape((heads, AUG, wide))
     mem_half = near_shape((2, rows, memory_len))
+    pair_outs = (near_shape((half, width)), near_shape((half, width)))
     whole = pltpu.VMEM((length, width), F32)
     aug = pltpu.VMEM((AUG, length), BF16)
     row_scratch = pltpu.VMEM((rows, length), BF16)
@@ -734,135 +800,161 @@
         self_sum.append(mp_sum(*out[5:8]))
     for i in span:
         self_sum[i].add()
-        if i == 0:
-            cross_kv.append(keys(0))
+        cross_kv.append(keys(i))
 
     cross_out, cross_sum = [], []
     for i in span:
+        self_sum[i].meet()
         out = order.run(
             bind(cross_forward, i, chunk), 6,
-            (hidden, *self_sum[i].pieces(), obias_self, gain_cross, shift_cross, wq2, qbias_cross, output_cross, *cross_kv[i]),
+            (hidden, *self_sum[i].pieces, obias_self, gain_cross, shift_cross, wq2, qbias_cross, output_cross, *cross_kv[i]),
             (state, low_state, low_rows, low_rows, lse_out, *half_outs), (whole, aug),
         )
         cross_out.append(out)
         cross_sum.append(mp_sum(*out[5:8]))
-        if len(cross_kv) < items:
-            cross_kv.append(keys(i + 1))
         cross_sum[i].add()
 
-    feed_out, feed_sum, block_sum = [], [], []
+    feed_out, feed_sum = [], []
     for i in span:
+        cross_sum[i].meet()
         out = order.run(
             bind(feed, i), 4,
-            (lengths, tasks, cross_out[i][0], *cross_sum[i].pieces(), out_grad, obias_cross, gain_feed, shift_feed, expand_weight, expand_bias, contract_weight),
+            (lengths, tasks, cross_out[i][0], *cross_sum[i].pieces, out_grad, obias_cross, gain_feed, shift_feed, expand_weight, expand_bias, contract_weight),
             (state, low_state, unit_state, unit_state, low_state, vec_out, *half_outs), (whole,),
         )
         feed_out.append(out)
         feed_sum.append(mp_sum(*out[6:9]))
-        block_sum.append(mp_sum(*order.run(feed_out_part, 1, (out[2], contract_weight), half_outs)))
         feed_sum[i].add()
-    outs, scratch = pack_outs(width + units + 64)
-    feed_dp = DpSum(
-        order, n_dp, *order.run(
-            bind(feed_weights, items), 4, [out[k] for k in (1, 3, 2, 4, 5) for out in feed_out], outs, scratch
-        )
-    )
-
-    back_out, back_sum, memory_parts = [], [], []
+    back_out, back_sum = [], []
     for i in span:
         _, _, q2, o2, lse2 = cross_out[i][:5]
+        feed_sum[i].meet()
+        if i == 0:
+            outs, scratch = pack_outs(width + units + 64)
+            operands = [out[k] for k in (1, 3, 2, 4, 5) for out in feed_out]
+            feed_dp = DpSum(order, n_dp, X_FIRST, *order.run(bind(feed_weights, items), 2, operands, outs, scratch))
         out = order.run(
             bind(cross_backward, i, chunk), 9,
-            (lengths, tasks, feed_out[i][0], *feed_sum[i].pieces(), out_grad, gain_feed, output_cross, wq2, *cross_kv[i], q2, o2, lse2),
+            (lengths, tasks, feed_out[i][0], *feed_sum[i].pieces, out_grad, gain_feed, output_cross, wq2, *cross_kv[i], q2, o2, lse2),
             (state, low_state, low_rows, mem_rows, mem_rows, vec_out, *half_outs), (whole, aug, aug, row_scratch),
         )
         back_out.append(out)
         back_sum.append(mp_sum(*out[6:9]))
-        keep, send = order.run(memory_grad, 2, (wk2, wv2, out[3], out[4]), (mem_half, mem_half))
-        memory_parts.append((keep, swap(send, "mp", n_mp, 1)))
         back_sum[i].add()
-    feed_dp.step()
-
-    self_back, last_sum = [], []
+
+    self_back = []
+    outs, scratch = pack_outs(4 * rows + 64)
     for i in span:
         q1, ka1, va1, o1, lse1 = self_out[i][:5]
+        back_sum[i].meet()
+        if i == 0:
+            feed_dp.step()
         out = order.run(
             bind(self_backward, i), 5,
-            (cross_out[i][0], *back_sum[i].pieces(), back_out[i][0], hidden, gain_cross, output_self, wq1, wk1, wv1, ka1, va1, q1, o1, lse1),
-            (state, low_state, near_shape((3 * rows, length)), vec_out, *half_outs), (whole, aug, aug, row_scratch),
+            (cross_out[i][0], *back_sum[i].pieces, back_out[i][0], hidden, gain_cross, output_self, wq1, wk1, wv1, ka1, va1, q1, o1, lse1),
+            (state, low_state, near_shape((3 * rows, length)), vec_out, *pair_outs), (whole, aug, aug, row_scratch),
         )
         self_back.append(out)
-        last_sum.append(mp_sum(*out[4:7]))
-        outs, scratch = pack_outs(4 * rows + 64)
         if i == 0:
             operands = [encoder] + [out[2] for out in back_out] + [out[1] for out in cross_out] + [out[3] for out in cross_out]
             operands += [out[1] for out in back_out] + [out[3] for out in back_out] + [out[4] for out in back_out]
             operands += [out[5] for out in back_out]
-            cross_dp = DpSum(
-                order, n_dp, *order.run(
-                    bind(cross_weights, items), 3, operands, outs, scratch,
-                    {0: pl.BlockSpec(encoder.shape, lambda *_: (0, 0, 0))},
-                )
+            made = order.run(
+                bind(cross_weights, items), 3, operands, outs, scratch,
+                {0: pl.BlockSpec(encoder.shape, lambda *_: (0, 0, 0))},
             )
-            last_sum[i].add()
-            feed_dp.step()
-        if i == items - 1:
-            operands = [hidden, gain_self, shift_self] + [out[2] for out in self_back] + [out[3] for out in self_out]
-            operands += [out[1] for out in self_back] + [out[3] for out in self_back]
-            self_dp = DpSum(order, n_dp, *order.run(bind(self_weights, items), 3, operands, outs, scratch))
-        if i > 0:
-            last_sum[i].add()
-
-    feed_dp.step()
-    cross_dp.step()
-    block_half = near_shape((items, half, width))
-    stacked = order.run(
-        bind(add_stack, items), 1, [a for s in block_sum for a in (s.keep, *s.near)], (block_half,)
-    )[0]
-    block_sum[0].spread(stacked)
-    memory_out = near_shape((items, rows, memory_len))
-    kept, sent = order.run(
-        bind(add_memory, items), 1, [p[0] for p in memory_parts] + [p[1] for p in memory_parts], (memory_out, memory_out)
+            cross_dp = DpSum(order, n_dp, X_FIRST, *made)
+    operands = [hidden, gain_self, shift_self] + [out[2] for out in self_back] + [out[3] for out in self_out]
+    operands += [out[1] for out in self_back] + [out[3] for out in self_back]
+    grad_shape, block_shape = shape(hidden.shape, F32), shape(hidden.shape, BF16)
+    mem_half, memory_out = near_shape((2, rows, memory_len)), near_shape((items, rows, memory_len))
+    line_out, bias_out, matrix = shape((width,), F32), shape((rows,), F32), shape((rows, width), F32)
+    lines = (line_out, line_out, line_out, bias_out, bias_out)
+    whole_cube = [pl.BlockSpec(hidden.shape, lambda *_: (0, 0, 0))]
+    got = {}
+
+    def pack_self():
+        got["S"] = DpSum(order, n_dp, X_FIRST, *order.run(bind(self_weights, items), 3, operands, outs, scratch))
+
+    def last_finish():
+        got["hidden"] = order.run(
+            bind(finish_grad, items), 4, [out[0] for out in self_back] + list(got["last"].pieces) + [hidden, gain_self],
+            (grad_shape,), (whole,), None, whole_cube,
+        )[0]
+
+    def memory(i):
+        part = order.run(memory_grad, 2, (wk2, wv2, back_out[i][3], back_out[i][4]), (mem_half, mem_half))
+        got["m", i] = part
+
+    def memory_swap():
+        for i in span:
+            keep, send = got["m", i]
+            got["m", i] = keep, swap(order.later(send), "mp", n_mp, 1)
+
+    def memory_finish():
+        got["encoder"] = order.run(
+            finish_memory, 2, got["far"], (shape((items, rows, memory_len), F32),), (), None,
+            [pl.BlockSpec((items, rows, memory_len), lambda *_: (0, 0, 0))],
+        )[0].transpose(0, 2, 1)
+
+    def block_part(i):
+        keep, send = order.run(feed_out_part, 1, (feed_out[i][2], contract_weight), pair_outs)
+        got["b", i] = keep, send
+
+    def block_finish():
+        got["out"] = order.run(
+            bind(finish_out, items), 3, [out[0] for out in feed_out] + list(got["block"].pieces) + [contract_bias],
+            (block_shape,), (whole,), None, whole_cube,
+        )[0]
+
+    def unpack_feed():
+        got["f"] = feed_dp.unpack(
+            (shape((width, width), F32), shape((units, width), F32)), (line_out, shape((units,), F32))
+        )
+
+    def unpack_cross():
+        got["x"] = cross_dp.unpack((matrix,) * 4, lines)
+
+    def unpack_self():
+        got["s"] = got["S"].unpack((matrix,) * 4, lines, near_shape((8, width), F32))
+
+    def job(which):
+        if which in "FXS":
+            return {"F": feed_dp, "X": cross_dp, "S": got.get("S")}[which].job()
+        if which == "l":
+            got["last"] = PairSum(order, n_mp, [out[4] for out in self_back], [out[5] for out in self_back])
+            return got["last"].job()
+        if which == "b":
+            return got["block"].job()
+        if which == "m":
+            return got["last"].meet_job()
+        if which == "c":
+            return got["block"].meet_job()
+        parts = [got["m", i] for i in span]
+
+        def then(kept, sent):
+            got["far"] = kept, swap(sent, "mp", n_mp, 2)
+
+        return bind(add_memory, items), [p[0] for p in parts] + [p[1] for p in parts], (memory_out, memory_out), then
+
+    def block_swap():
+        sends = [order.later(got["b", i][1]) for i in span]
+        got["block"] = PairSum(order, n_mp, [got["b", i][0] for i in span], sends)
+
+    acts = dict(
+        M=memory_swap, N=block_swap, P=pack_self, g=last_finish, A=lambda: [memory(i) for i in span], e=memory_finish,
+        B=lambda: [block_part(i) for i in span], o=block_finish, u=unpack_feed, v=unpack_cross, w=unpack_self,
     )
-    memory_far = swap(sent, "mp", n_mp, 2)
-    cross_dp.step()
-    hidden_grad = None
-    grad_shape = shape(hidden.shape, F32)
-    for i in span:
-        extra = () if hidden_grad is None else (hidden_grad,)
-        hidden_grad = order.run(
-            bind(finish_grad, i), 2,
-            (self_back[i][0], *last_sum[i].pieces(), hidden, gain_self, *extra), (grad_shape,), (whole,),
-            {7: LEFT}, [chosen(grad_shape, i)], {7: 0} if extra else {},
-        )[0]
-    self_dp.step()
-    feed_dp.step()
-    cross_dp.step()
-    self_dp.step()
-    block_shape = shape(hidden.shape, BF16)
-    block_out = order.run(
-        bind(finish_out, items), 3, [out[0] for out in feed_out] + list(block_sum[0].pieces()) + [contract_bias],
-        (block_shape,), (whole,), None, [pl.BlockSpec(hidden.shape, lambda *_: (0, 0, 0))],
-    )[0]
-    feed_dp.step()
-    cross_dp.step()
-    self_dp.step()
-    encoder_grad = order.run(
-        finish_memory, 2, (kept, memory_far), (shape((items, rows, memory_len), F32),), (), None,
-        [pl.BlockSpec((items, rows, memory_len), lambda *_: (0, 0, 0))],
-    )[0].transpose(0, 2, 1)
-    cross_dp.step()
-    self_dp.step()
-    self_dp.step()
-
-    matrix = shape((rows, width), F32)
-    outs = (matrix, matrix, matrix, matrix, shape((8, width), F32))
-    feed_grads = feed_dp.unpack((shape((width, width), F32), shape((units, width), F32), shape((8, width), F32)))
-    cross_grads = cross_dp.unpack(outs)
-    self_grads = self_dp.unpack(outs)
-    norm_rows = self_grads[4]
-    norm_rows = norm_rows + swap(norm_rows, "mp", n_mp, 1)
-    norm_rows = norm_rows + swap(norm_rows, "mp", n_mp, 2)
+    for word in ORDER:
+        if word[0] in acts:
+            for act in word:
+                acts[act]()
+        else:
+            run_together(order, [job(which) for which in word])
+    cross_grads, self_grads, feed_grads = got["x"], got["s"], got["f"]
+    hidden_grad, encoder_grad, block_out = got["hidden"], got["encoder"], got["out"]
+    norm_rows = self_grads[9]
+    norm_rows = norm_rows + swap(norm_rows, "mp", n_mp, 1) + (swap(norm_rows, "mp", n_mp, 2) + swap(norm_rows, "mp", n_mp, 3))
     return (
         block_out,
         hidden_grad,
@@ -870,27 +962,27 @@
         norm_rows[5],
         norm_rows[6],
         self_grads[0].T,
-        self_grads[4][3, 0:rows],
+        self_grads[7],
         self_grads[1].T,
         self_grads[2].T,
-        self_grads[4][4, 0:rows],
+        self_grads[8],
         self_grads[3],
-        self_grads[4][2],
-        self_grads[4][0],
-        self_grads[4][1],
+        self_grads[6],
+        self_grads[4],
+        self_grads[5],
         cross_grads[0].T,
-        cross_grads[4][3, 0:rows],
+        cross_grads[7],
         cross_grads[1].T,
         cross_grads[2].T,
-        cross_grads[4][4, 0:rows],
+        cross_grads[8],
         cross_grads[3],
-        cross_grads[4][2],
-        cross_grads[4][0],
-        cross_grads[4][1],
+        cross_grads[6],
+        cross_grads[4],
+        cross_grads[5],
         feed_grads[0],
-        feed_grads[2][1],
+        feed_grads[3],
         feed_grads[1],
-        feed_grads[2][0],
+        feed_grads[2],
     )
 
 

time: 272 us -> 260 us (0.956)
  waiting for transfers between devices: 117 us -> 112 us
  starting transfers between devices: 55 us -> 51.5 us
  local copies, waits for them, and re-layouts: 4.87 us -> 1.87 us
    ppermute x80 -> x64, waiting for transfers between devices: 117 us -> 112 us  [swap(): return lax.ppermute(value, axis, [(k, k ^ bit) for k in range(size)])]
    ppermute x80 -> x64, starting transfers between devices: 55 us -> 51.5 us  [swap(): return lax.ppermute(value, axis, [(k, k ^ bit) for k in range(size)])]
    slice x5 -> x0, local copies, waits for them, and re-layouts: 2.99 us -> none  [the longest x1 0.62 us: shards(): self_grads[4][1]]
    pallas_call x53 -> x50, Pallas kernels: 89.2 us -> 89.1 us  [run(): pl.pallas_call(whole_body, name=inner.__name__, grid=(1,), in_specs=in_sp...]
  transfers between devices with their start and end apart: 80 -> 64, of which waited for: 31 -> 33; matrix products, arithmetic and copies ran while one was open for 1% -> 0% of each run, Pallas kernels for 29% -> 31%
where the time goes in v3:
time: 260 us; the launch traced here: 255 us
  waiting for transfers between devices  112 us (43%)
  Pallas kernels  89.1 us (34%)
  starting transfers between devices  51.5 us (20%)
    ppermute x64, waiting for transfers between devices, swap(): return lax.ppermute(value, axis, [(k, k ^ bit) for k in range(size)])  112 us
    pallas_call x50, Pallas kernels, run(): pl.pallas_call(whole_body, name=inner.__name__, grid=(1,), in_specs=in_sp...  89.1 us
    ppermute x64, starting transfers between devices, swap(): return lax.ppermute(value, axis, [(k, k ^ bit) for k in range(size)])  51.5 us
  transfers between devices with their start and end apart: 64, of which 33 were waited for; matrix products, arithmetic and copies ran while one was open for 0% of the time, Pallas kernels for 31%

profile of v3, /device:TPU:0, one launch (start us, length us, event | category | flops | bytes accessed | tf_op | source)
XLA Modules:
  0.0 255.5 jit_solution(12911366345025326170)
XLA Ops:
  1.3 5.5 %first_forward.1 = (bf16[192,448]{1,0:T(8,128)(2,1)S(1)}, bf16[3,80,448]{2,1,0:T(8,128)(2,1)S(1)}, bf16[3,80,448]{2,1,0:T(8,128)(2,1)S(1)}, bf16[192,448]{1,0:T(...) custom-call(s32[2]{0:T(128)S(1)} %copy-done, ...), custom_call_target="tpu_custom_call" | custom-call | flops 4 | bytes 1 | tf_op jit(solution)/shard_map/first_forward/pallas_call | solution.py:612
  7.4 3.5 %self_forward.1 = (bf16[192,448]{1,0:T(8,128)(2,1)S(1)}, bf16[3,80,448]{2,1,0:T(8,128)(2,1)S(1)}, bf16[3,80,448]{2,1,0:T(8,128)(2,1)S(1)}, bf16[192,448]{1,0:T(8...) custom-call(s32[2]{0:T(128)S(1)} %copy-done, ...), custom_call_target="tpu_custom_call" | custom-call | flops 4 | bytes 1 | tf_op jit(solution)/shard_map/self_forward/pallas_call | solution.py:612
  11.0 3.0 %collective-permute-start.2 = (bf16[224,768]{1,0:T(8,128)(2,1)S(1)}, bf16[224,768]{1,0:T(8,128)(2,1)S(1)}, u32[]{:S(2)}, u32[]{:S(2)}) collective-permute-start(bf16[224,768]{1,0:T(8,128)(2,1)S(1)} %get-tuple-element.287.refs_0_), channel_id=1, source_target_pairs={{0,2},{1,3},{2,0},{3,1},{4,6},{5,7},{6,4},{7,5},{8,10},{9,11},{10,... | collective-permute-start | bytes 1032200 | tf_op jit(solution)/shard_map/ppermute | solution.py:639
  15.2 2.1 cross_keys.2
  17.4 2.1 cross_keys.3
  19.4 2.9 %collective-permute-done.2.refs_1_ = bf16[224,768]{1,0:T(8,128)(2,1)S(1)} collective-permute-done((bf16[224,768]{1,0:T(8,128)(2,1)S(1)}, bf16[224,768]{1,0:T(8,128)(2,1)S(1)}, u32[]{:S(2)}, u32[]{:S(2)}) %collective-permute-start.2) | collective-permute-done | bytes 344096 | tf_op jit(solution)/shard_map/ppermute | solution.py:639
  22.5 1.8 collective-permute-start.9
  24.3 5.7 %cross_forward.2 = (f32[448,768]{1,0:T(8,128)S(1)}, bf16[448,768]{1,0:T(8,128)(2,1)S(1)}, bf16[192,448]{1,0:T(8,128)(2,1)S(1)}, bf16[192,448]{1,0:T(8,128)(2,1)S...) custom-call(bf16[2,448,768]{2,1,0:T(8,128)(2,1)S(1)} %get-tuple-elem, ...), custom_call_target="tpu_custom_call" | custom-call | flops 6 | bytes 1 | tf_op jit(solution)/shard_map/cross_forward/pallas_call | solution.py:612
  33.2 1.8 collective-permute-start.8
  35.0 5.4 %cross_forward.3 = (f32[448,768]{1,0:T(8,128)S(1)}, bf16[448,768]{1,0:T(8,128)(2,1)S(1)}, bf16[192,448]{1,0:T(8,128)(2,1)S(1)}, bf16[192,448]{1,0:T(8,128)(2,1)S...) custom-call(bf16[2,448,768]{2,1,0:T(8,128)(2,1)S(1)} %get-tuple-elem, ...), custom_call_target="tpu_custom_call" | custom-call | flops 6 | bytes 1 | tf_op jit(solution)/shard_map/cross_forward/pallas_call | solution.py:612
  43.8 1.8 collective-permute-start.14
  45.6 3.4 %feed.2 = (f32[448,768]{1,0:T(8,128)S(1)}, bf16[448,768]{1,0:T(8,128)(2,1)S(1)}, bf16[448,768]{1,0:T(8,128)(2,1)S(1)}, bf16[448,768]{1,0:T(8,128)(2,1)S(1)}, bf1...) custom-call(s32[2]{0:T(128)S(1)} %copy-done.1, ...), custom_call_target="tpu_custom_call" | custom-call | flops 4 | bytes 1 | tf_op jit(solution)/shard_map/feed/pallas_call | solution.py:612
  50.8 3.5 %collective-permute-done.14.refs_1_ = bf16[224,768]{1,0:T(8,128)(2,1)S(1)} collective-permute-done((bf16[224,768]{1,0:T(8,128)(2,1)S(1)}, bf16[224,768]{1,0:T(8,128)(2,1)S(1)}, u32[]{:S(2)}, u32[]{:S(2)}) %collective-permute-start.14) | collective-permute-done | bytes 344096 | tf_op jit(solution)/shard_map/ppermute | solution.py:639
  54.4 1.8 collective-permute-start.18
  56.3 3.8 %feed.3 = (f32[448,768]{1,0:T(8,128)S(1)}, bf16[448,768]{1,0:T(8,128)(2,1)S(1)}, bf16[448,768]{1,0:T(8,128)(2,1)S(1)}, bf16[448,768]{1,0:T(8,128)(2,1)S(1)}, bf1...) custom-call(s32[2]{0:T(128)S(1)} %copy-done.1, ...), custom_call_target="tpu_custom_call" | custom-call | flops 4 | bytes 1 | tf_op jit(solution)/shard_map/feed/pallas_call | solution.py:612
  61.8 3.1 %collective-permute-done.18.refs_1_ = bf16[224,768]{1,0:T(8,128)(2,1)S(1)} collective-permute-done((bf16[224,768]{1,0:T(8,128)(2,1)S(1)}, bf16[224,768]{1,0:T(8,128)(2,1)S(1)}, u32[]{:S(2)}, u32[]{:S(2)}) %collective-permute-start.18) | collective-permute-done | bytes 344096 | tf_op jit(solution)/shard_map/ppermute | solution.py:639
  65.1 3.2 %feed_weights.1 = (bf16[4,200,768]{2,1,0:T(8,128)(2,1)S(1)}, bf16[4,200,768]{2,1,0:T(8,128)(2,1)S(1)}, f32[8,128]{1,0:T(8,128)S(1)}) custom-call(bf16[448,768]{1,0:T(8,128)(2,1)S(1)} %get-tuple-element.345.refs_0_, bf16[448,768]{1,0:T(8,128)(2,1)S(1)} %get-tuple-element.346.refs_1_, bf16[448,768]{1,0:T(8,128)(2,1)S(1)} %get-tuple-element.347.refs_2_, ...), custom_call_target="tpu_custom_call" | custom-call | flops 2 | bytes 1 | tf_op jit(solution)/shard_map/feed_weights/pallas_call | solution.py:612
  68.3 1.8 collective-permute-start.21
  71.6 8.6 %cross_backward.2 = (f32[448,768]{1,0:T(8,128)S(1)}, bf16[448,768]{1,0:T(8,128)(2,1)S(1)}, bf16[192,448]{1,0:T(8,128)(2,1)S(1)}, bf16[192,1536]{1,0:T(8,128)(2,1...) custom-call(s32[2]{0:T(128)S(1)} %copy-done.1, ...), custom_call_target="tpu_custom_call" | custom-call | flops 9 | bytes 1 | tf_op jit(solution)/shard_map/cross_backward/pallas_call | solution.py:612
  83.7 8.4 %cross_backward.3 = (f32[448,768]{1,0:T(8,128)S(1)}, bf16[448,768]{1,0:T(8,128)(2,1)S(1)}, bf16[192,448]{1,0:T(8,128)(2,1)S(1)}, bf16[192,1536]{1,0:T(8,128)(2,1...) custom-call(s32[2]{0:T(128)S(1)} %copy-done.1, ...), custom_call_target="tpu_custom_call" | custom-call | flops 9 | bytes 1 | tf_op jit(solution)/shard_map/cross_backward/pallas_call | solution.py:612
  94.9 2.8 %collective-permute-done.21.refs_1_ = bf16[4,200,768]{2,1,0:T(8,128)(2,1)S(1)} collective-permute-done((bf16[4,200,768]{2,1,0:T(8,128)(2,1)S(1)}, bf16[4,200,768]{2,1,0:T(8,128)(2,1)S(1)}, u32[]{:S(2)}, u32[]{:S(2)}) %collective-permute-start.21) | collective-permute-done | bytes 1228832 | tf_op jit(solution)/shard_map/ppermute | solution.py:639
  98.0 5.1 %self_backward.2 = (f32[448,768]{1,0:T(8,128)S(1)}, bf16[448,768]{1,0:T(8,128)(2,1)S(1)}, bf16[576,448]{1,0:T(8,128)(2,1)S(1)}, f32[8,768]{1,0:T(8,128)S(1)}, bf...) custom-call(f32[448,768]{1,0:T(8,128)S(1)} %get-tuple-element.308.refs_2_.refs_0_, ...), custom_call_target="tpu_custom_call" | custom-call | flops 5 | bytes 1 | tf_op jit(solution)/shard_map/self_backward/pallas_call | solution.py:612
  103.2 2.9 %cross_weights.1 = (bf16[4,104,768]{2,1,0:T(8,128)(2,1)S(1)}, bf16[4,104,768]{2,1,0:T(8,128)(2,1)S(1)}, f32[8,128]{1,0:T(8,128)S(1)}) custom-call(bf16[2,1500,768]{2,1,0:T(8,128)(2,1)S(1)} %copy.58.refs_1_.refs_0_, bf16[192,448]{1,0:T(8,128)(2,1)S(1)} %get-tuple-element.389.refs_1_, bf16[192,448]{1,0:T(8,128)(2,1)S(1)} %get-tuple-element.390.refs_2_, ...), custom_call_target="tpu_custom_call" | custom-call | flops 3 | bytes 1 | tf_op jit(solution)/shard_map/cross_weights/pallas_call | solution.py:612
  106.2 1.8 collective-permute-start.32
  109.6 4.7 %self_backward.3 = (f32[448,768]{1,0:T(8,128)S(1)}, bf16[448,768]{1,0:T(8,128)(2,1)S(1)}, bf16[576,448]{1,0:T(8,128)(2,1)S(1)}, f32[8,768]{1,0:T(8,128)S(1)}, bf...) custom-call(f32[448,768]{1,0:T(8,128)S(1)} %get-tuple-element.335.refs_2_.refs_0_, ...), custom_call_target="tpu_custom_call" | custom-call | flops 5 | bytes 1 | tf_op jit(solution)/shard_map/self_backward/pallas_call | solution.py:612
  114.9 2.2 self_weights.1
  117.2 1.9 memory_grad.2
  119.0 1.7 memory_grad.3
  128.9 2.6 %collective-permute-start.37 = (bf16[1,200,768]{2,1,0:T(8,128)(2,1)S(1)}, bf16[1,200,768]{2,1,0:T(8,128)(2,1)S(1)}, u32[]{:S(2)}, u32[]{:S(2)}) collective-permute-start(bf16[1,200,768]{2,1,0:T(8,128)(2,1)S(1)} %get-tuple-element.439), channel_id=1, source_target_pairs={{0,16},{4,20},{8,24},{12,28},{16,0},{20,4},{24,8},{28,12},{1,17},{... | collective-permute-start | bytes 921608 | tf_op jit(solution)/shard_map/ppermute | solution.py:639
  132.0 10.6 %collective-permute-done.39.refs_5_ = bf16[4,104,768]{2,1,0:T(8,128)(2,1)S(1)} collective-permute-done((bf16[4,104,768]{2,1,0:T(8,128)(2,1)S(1)}, bf16[4,104,768]{2,1,0:T(8,128)(2,1)S(1)}, u32[]{:S(2)}, u32[]{:S(2)}) %collective-permute-start.39) | collective-permute-done | bytes 639008 | tf_op jit(solution)/shard_map/ppermute | solution.py:639
  143.9 2.8 %collective-permute-start.52 = (bf16[2,192,1500]{2,1,0:T(8,128)(2,1)S(1)}, bf16[2,192,1500]{2,1,0:T(8,128)(2,1)S(1)}, u32[]{:S(2)}, u32[]{:S(2)}) collective-permute-start(bf16[2,192,1500]{2,1,0:T(8,128)(2,1)S(1)} %get-tuple-element.472), channel_id=1, source_target_pairs={{0,2},{1,3},{2,0},{3,1},{4,6},{5,7},{6,4},{7,5},{8,10},{9,11},{10,... | collective-permute-start | bytes 3456008 | tf_op jit(solution)/shard_map/ppermute | solution.py:639
  147.5 3.4 %collective-permute-start.43 = (bf16[1,200,768]{2,1,0:T(8,128)(2,1)S(1)}, bf16[1,200,768]{2,1,0:T(8,128)(2,1)S(1)}, u32[]{:S(2)}, u32[]{:S(2)}) collective-permute-start(bf16[1,200,768]{2,1,0:T(8,128)(2,1)S(1)} %get-tuple-element.453.refs_0_), channel_id=1, source_target_pairs={{0,16},{4,20},{8,24},{12,28},{16,0},{20,4},{24,8},{28,12},{1,17},{... | collective-permute-start | bytes 921608 | tf_op jit(solution)/shard_map/ppermute | solution.py:639
  151.1 20.2 %collective-permute-done.44.refs_3_ = bf16[1,104,768]{2,1,0:T(8,128)(2,1)S(1)} collective-permute-done((bf16[1,104,768]{2,1,0:T(8,128)(2,1)S(1)}, bf16[1,104,768]{2,1,0:T(8,128)(2,1)S(1)}, u32[]{:S(2)}, u32[]{:S(2)}) %collective-permute-start.44) | collective-permute-done | bytes 159776 | tf_op jit(solution)/shard_map/ppermute | solution.py:639
  172.1 2.9 %collective-permute-start.50 = (bf16[1,104,768]{2,1,0:T(8,128)(2,1)S(1)}, bf16[1,104,768]{2,1,0:T(8,128)(2,1)S(1)}, u32[]{:S(2)}, u32[]{:S(2)}) collective-permute-start(bf16[1,104,768]{2,1,0:T(8,128)(2,1)S(1)} %get-tuple-element.469), channel_id=1, source_target_pairs={{0,16},{4,20},{8,24},{12,28},{16,0},{20,4},{24,8},{28,12},{1,17},{... | collective-permute-start | bytes 479240 | tf_op jit(solution)/shard_map/ppermute | solution.py:639
  175.1 3.7 %finish_grad.1 = (f32[2,448,768]{2,1,0:T(8,128)}, f32[8,128]{1,0:T(8,128)S(1)}) custom-call(f32[448,768]{1,0:T(8,128)S(1)} %get-tuple-element.473.refs_0_, f32[448,768]{1,0:T(8,128)S(1)} %get-tuple-element.474.refs_1_, bf16[2,224,768]{2,1,0:T(8,128)(2,1)S(1)} %get-tuple-element.475.refs_2_, bf16[2,224,768]{2,1,0:T(8,128)(2,1)S(1)} %collective-permute-done.53.refs_3_, ...), custom_call_target="tpu_custom_call" | custom-call | flops 4 | bytes 1 | tf_op jit(solution)/shard_map/finish_grad/pallas_call | solution.py:612
  180.4 9.0 %collective-permute-done.50.refs_5_ = bf16[1,104,768]{2,1,0:T(8,128)(2,1)S(1)} collective-permute-done((bf16[1,104,768]{2,1,0:T(8,128)(2,1)S(1)}, bf16[1,104,768]{2,1,0:T(8,128)(2,1)S(1)}, u32[]{:S(2)}, u32[]{:S(2)}) %collective-permute-start.50) | collective-permute-done | bytes 159776 | tf_op jit(solution)/shard_map/ppermute | solution.py:639
  189.4 1.7 collective-permute-done.49.refs_3_
  191.1 2.2 collective-permute-done.48.refs_1_
  195.7 1.7 collective-permute-start.56
  197.5 6.4 %collective-permute-done.56.refs_3_ = bf16[1,104,768]{2,1,0:T(8,128)(2,1)S(1)} collective-permute-done((bf16[1,104,768]{2,1,0:T(8,128)(2,1)S(1)}, bf16[1,104,768]{2,1,0:T(8,128)(2,1)S(1)}, u32[]{:S(2)}, u32[]{:S(2)}) %collective-permute-start.56) | collective-permute-done | bytes 159776 | tf_op jit(solution)/shard_map/ppermute | solution.py:639
  203.9 2.0 collective-permute-done.55.refs_1_
  208.6 15.0 %collective-permute-done.59.refs_1_ = bf16[4,200,768]{2,1,0:T(8,128)(2,1)S(1)} collective-permute-done((bf16[4,200,768]{2,1,0:T(8,128)(2,1)S(1)}, bf16[4,200,768]{2,1,0:T(8,128)(2,1)S(1)}, u32[]{:S(2)}, u32[]{:S(2)}) %collective-permute-start.59) | collective-permute-done | bytes 1228832 | tf_op jit(solution)/shard_map/ppermute | solution.py:639
  223.6 2.8 %unpack.3 = (f32[768,768]{1,0:T(8,128)}, f32[768,768]{1,0:T(8,128)}, f32[768]{0:T(1024)}, f32[768]{0:T(1024)}, f32[8,128]{1,0:T(8,128)S(1)}) custom-call(bf16[4,200,768]{2,1,0:T(8,128)(2,1)S(1)} %get-tuple-element.486.refs_0_, bf16[4,200,768]{2,1,0:T(8,128)(2,1)S(1)} %collective-permute-done.59.refs_1_, f32[8,128]{1,0:T(8,128)S(1)} %get-tuple-element.487.refs_2_), custom_call_target="tpu_custom_call" | custom-call | flops 3 | bytes 1 | tf_op jit(solution)/shard_map/unpack/pallas_call | solution.py:612
  227.3 10.0 %collective-permute-done.57.refs_1_ = bf16[4,104,768]{2,1,0:T(8,128)(2,1)S(1)} collective-permute-done((bf16[4,104,768]{2,1,0:T(8,128)(2,1)S(1)}, bf16[4,104,768]{2,1,0:T(8,128)(2,1)S(1)}, u32[]{:S(2)}, u32[]{:S(2)}) %collective-permute-start.57) | collective-permute-done | bytes 639008 | tf_op jit(solution)/shard_map/ppermute | solution.py:639
  237.3 1.8 unpack.4
  239.1 1.9 finish_out.1
  241.1 7.9 %collective-permute-done.60.refs_1_ = bf16[4,104,768]{2,1,0:T(8,128)(2,1)S(1)} collective-permute-done((bf16[4,104,768]{2,1,0:T(8,128)(2,1)S(1)}, bf16[4,104,768]{2,1,0:T(8,128)(2,1)S(1)}, u32[]{:S(2)}, u32[]{:S(2)}) %collective-permute-start.60) | collective-permute-done | bytes 639008 | tf_op jit(solution)/shard_map/ppermute | solution.py:639
  249.0 1.8 unpack.5
  (143 shorter events, 47.5 us)
Async XLA Ops:
  6.8 4.1 %collective-permute-start = (bf16[112,768]{1,0:T(8,128)(2,1)S(1)}, bf16[112,768]{1,0:T(8,128)(2,1)S(1)}, u32[]{:S(2)}, u32[]{:S(2)}) collective-permute-start(bf16[112,768]{1,0:T(8,128)(2,1)S(1)} %get-tuple-element.275), channel_id=1, source_target_pairs={{0,1},{1,0},{2,3},{3,2},{4,5},{5,4},{6,7},{7,6},{8,9},{9,8},{10,11... | collective-permute-start | bytes 516104 | tf_op jit(solution)/shard_map/ppermute | solution.py:639
  7.4 3.6 %collective-permute-start.1 = (bf16[112,768]{1,0:T(8,128)(2,1)S(1)}, bf16[112,768]{1,0:T(8,128)(2,1)S(1)}, u32[]{:S(2)}, u32[]{:S(2)}) collective-permute-start(bf16[112,768]{1,0:T(8,128)(2,1)S(1)} %get-tuple-element.276), channel_id=1, source_target_pairs={{0,1},{1,0},{2,3},{3,2},{4,5},{5,4},{6,7},{7,6},{8,9},{9,8},{10,11... | collective-permute-start | bytes 516104 | tf_op jit(solution)/shard_map/ppermute | solution.py:639
  11.0 11.3 %collective-permute-start.2 = (bf16[224,768]{1,0:T(8,128)(2,1)S(1)}, bf16[224,768]{1,0:T(8,128)(2,1)S(1)}, u32[]{:S(2)}, u32[]{:S(2)}) collective-permute-start(bf16[224,768]{1,0:T(8,128)(2,1)S(1)} %get-tuple-element.287.refs_0_), channel_id=1, source_target_pairs={{0,2},{1,3},{2,0},{3,1},{4,6},{5,7},{6,4},{7,5},{8,10},{9,11},{10,... | collective-permute-start | bytes 1032200 | tf_op jit(solution)/shard_map/ppermute | solution.py:639
  14.0 3.2 %collective-permute-start.3 = (bf16[112,768]{1,0:T(8,128)(2,1)S(1)}, bf16[112,768]{1,0:T(8,128)(2,1)S(1)}, u32[]{:S(2)}, u32[]{:S(2)}) collective-permute-start(bf16[112,768]{1,0:T(8,128)(2,1)S(1)} %get-tuple-element.292), channel_id=1, source_target_pairs={{0,1},{1,0},{2,3},{3,2},{4,5},{5,4},{6,7},{7,6},{8,9},{9,8},{10,11... | collective-permute-start | bytes 516104 | tf_op jit(solution)/shard_map/ppermute | solution.py:639
  14.1 3.2 %collective-permute-start.4 = (bf16[112,768]{1,0:T(8,128)(2,1)S(1)}, bf16[112,768]{1,0:T(8,128)(2,1)S(1)}, u32[]{:S(2)}, u32[]{:S(2)}) collective-permute-start(bf16[112,768]{1,0:T(8,128)(2,1)S(1)} %get-tuple-element.293), channel_id=1, source_target_pairs={{0,1},{1,0},{2,3},{3,2},{4,5},{5,4},{6,7},{7,6},{8,9},{9,8},{10,11... | collective-permute-start | bytes 516104 | tf_op jit(solution)/shard_map/ppermute | solution.py:639
  22.4 1.9 collective-permute-start.5
  22.5 10.5 %collective-permute-start.9 = (bf16[224,768]{1,0:T(8,128)(2,1)S(1)}, bf16[224,768]{1,0:T(8,128)(2,1)S(1)}, u32[]{:S(2)}, u32[]{:S(2)}) collective-permute-start(bf16[224,768]{1,0:T(8,128)(2,1)S(1)} %get-tuple-element.314.refs_0_), channel_id=1, source_target_pairs={{0,2},{1,3},{2,0},{3,1},{4,6},{5,7},{6,4},{7,5},{8,10},{9,11},{10,... | collective-permute-start | bytes 1032200 | tf_op jit(solution)/shard_map/ppermute | solution.py:639
  33.2 10.5 %collective-permute-start.8 = (bf16[224,768]{1,0:T(8,128)(2,1)S(1)}, bf16[224,768]{1,0:T(8,128)(2,1)S(1)}, u32[]{:S(2)}, u32[]{:S(2)}) collective-permute-start(bf16[224,768]{1,0:T(8,128)(2,1)S(1)} %get-tuple-element.313.refs_0_), channel_id=1, source_target_pairs={{0,2},{1,3},{2,0},{3,1},{4,6},{5,7},{6,4},{7,5},{8,10},{9,11},{10,... | collective-permute-start | bytes 1032200 | tf_op jit(solution)/shard_map/ppermute | solution.py:639
  43.8 10.5 %collective-permute-start.14 = (bf16[224,768]{1,0:T(8,128)(2,1)S(1)}, bf16[224,768]{1,0:T(8,128)(2,1)S(1)}, u32[]{:S(2)}, u32[]{:S(2)}) collective-permute-start(bf16[224,768]{1,0:T(8,128)(2,1)S(1)} %get-tuple-element.336.refs_0_), channel_id=1, source_target_pairs={{0,2},{1,3},{2,0},{3,1},{4,6},{5,7},{6,4},{7,5},{8,10},{9,11},{10,... | collective-permute-start | bytes 1032200 | tf_op jit(solution)/shard_map/ppermute | solution.py:639
  54.4 10.5 %collective-permute-start.18 = (bf16[224,768]{1,0:T(8,128)(2,1)S(1)}, bf16[224,768]{1,0:T(8,128)(2,1)S(1)}, u32[]{:S(2)}, u32[]{:S(2)}) collective-permute-start(bf16[224,768]{1,0:T(8,128)(2,1)S(1)} %get-tuple-element.355.refs_0_), channel_id=1, source_target_pairs={{0,2},{1,3},{2,0},{3,1},{4,6},{5,7},{6,4},{7,5},{8,10},{9,11},{10,... | collective-permute-start | bytes 1032200 | tf_op jit(solution)/shard_map/ppermute | solution.py:639
  65.0 6.5 %collective-permute-start.22 = (bf16[224,768]{1,0:T(8,128)(2,1)S(1)}, bf16[224,768]{1,0:T(8,128)(2,1)S(1)}, u32[]{:S(2)}, u32[]{:S(2)}) collective-permute-start(bf16[224,768]{1,0:T(8,128)(2,1)S(1)} %get-tuple-element.364.refs_3_), channel_id=1, source_target_pairs={{0,1},{1,0},{2,3},{3,2},{4,5},{5,4},{6,7},{7,6},{8,9},{9,8},{10,11... | collective-permute-start | bytes 1032200 | tf_op jit(solution)/shard_map/ppermute | solution.py:639
  68.3 29.5 %collective-permute-start.21 = (bf16[4,200,768]{2,1,0:T(8,128)(2,1)S(1)}, bf16[4,200,768]{2,1,0:T(8,128)(2,1)S(1)}, u32[]{:S(2)}, u32[]{:S(2)}) collective-permute-start(bf16[4,200,768]{2,1,0:T(8,128)(2,1)S(1)} %get-tuple-element.363), channel_id=1, source_target_pairs={{0,4},{4,0},{8,12},{12,8},{16,20},{20,16},{24,28},{28,24},{1,5},{5... | collective-permute-start | bytes 3686408 | tf_op jit(solution)/shard_map/ppermute | solution.py:639
  70.0 11.9 %collective-permute-start.26 = (bf16[224,768]{1,0:T(8,128)(2,1)S(1)}, bf16[224,768]{1,0:T(8,128)(2,1)S(1)}, u32[]{:S(2)}, u32[]{:S(2)}) collective-permute-start(bf16[224,768]{1,0:T(8,128)(2,1)S(1)} %get-tuple-element.374.refs_0_), channel_id=1, source_target_pairs={{0,2},{1,3},{2,0},{3,1},{4,6},{5,7},{6,4},{7,5},{8,10},{9,11},{10,... | collective-permute-start | bytes 1032200 | tf_op jit(solution)/shard_map/ppermute | solution.py:639
  82.3 11.6 %collective-permute-start.25 = (bf16[224,768]{1,0:T(8,128)(2,1)S(1)}, bf16[224,768]{1,0:T(8,128)(2,1)S(1)}, u32[]{:S(2)}, u32[]{:S(2)}) collective-permute-start(bf16[224,768]{1,0:T(8,128)(2,1)S(1)} %get-tuple-element.373.refs_0_), channel_id=1, source_target_pairs={{0,2},{1,3},{2,0},{3,1},{4,6},{5,7},{6,4},{7,5},{8,10},{9,11},{10,... | collective-permute-start | bytes 1032200 | tf_op jit(solution)/shard_map/ppermute | solution.py:639
  94.0 4.0 %collective-permute-start.31 = (bf16[224,768]{1,0:T(8,128)(2,1)S(1)}, bf16[224,768]{1,0:T(8,128)(2,1)S(1)}, u32[]{:S(2)}, u32[]{:S(2)}) collective-permute-start(bf16[224,768]{1,0:T(8,128)(2,1)S(1)} %get-tuple-element.401.refs_1_), channel_id=1, source_target_pairs={{0,1},{1,0},{2,3},{3,2},{4,5},{5,4},{6,7},{7,6},{8,9},{9,8},{10,11... | collective-permute-start | bytes 1032200 | tf_op jit(solution)/shard_map/ppermute | solution.py:639
  94.3 11.7 %collective-permute-start.34 = (bf16[224,768]{1,0:T(8,128)(2,1)S(1)}, bf16[224,768]{1,0:T(8,128)(2,1)S(1)}, u32[]{:S(2)}, u32[]{:S(2)}) collective-permute-start(bf16[224,768]{1,0:T(8,128)(2,1)S(1)} %get-tuple-element.414.refs_0_), channel_id=1, source_target_pairs={{0,2},{1,3},{2,0},{3,1},{4,6},{5,7},{6,4},{7,5},{8,10},{9,11},{10,... | collective-permute-start | bytes 1032200 | tf_op jit(solution)/shard_map/ppermute | solution.py:639
  106.2 3.5 %collective-permute-start.35 = (bf16[224,768]{1,0:T(8,128)(2,1)S(1)}, bf16[224,768]{1,0:T(8,128)(2,1)S(1)}, u32[]{:S(2)}, u32[]{:S(2)}) collective-permute-start(bf16[224,768]{1,0:T(8,128)(2,1)S(1)} %get-tuple-element.416.refs_1_), channel_id=1, source_target_pairs={{0,1},{1,0},{2,3},{3,2},{4,5},{5,4},{6,7},{7,6},{8,9},{9,8},{10,11... | collective-permute-start | bytes 1032200 | tf_op jit(solution)/shard_map/ppermute | solution.py:639
  106.2 17.7 %collective-permute-start.32 = (bf16[4,104,768]{2,1,0:T(8,128)(2,1)S(1)}, bf16[4,104,768]{2,1,0:T(8,128)(2,1)S(1)}, u32[]{:S(2)}, u32[]{:S(2)}) collective-permute-start(bf16[4,104,768]{2,1,0:T(8,128)(2,1)S(1)} %get-tuple-element.411), channel_id=1, source_target_pairs={{0,4},{4,0},{8,12},{12,8},{16,20},{20,16},{24,28},{28,24},{1,5},{5... | collective-permute-start | bytes 1916936 | tf_op jit(solution)/shard_map/ppermute | solution.py:639
  108.0 15.9 %collective-permute-start.30 = (bf16[2,200,768]{2,1,0:T(8,128)(2,1)S(1)}, bf16[2,200,768]{2,1,0:T(8,128)(2,1)S(1)}, u32[]{:S(2)}, u32[]{:S(2)}) collective-permute-start(bf16[2,200,768]{2,1,0:T(8,128)(2,1)S(1)} %get-tuple-element.388), channel_id=1, source_target_pairs={{0,8},{4,12},{8,0},{12,4},{16,24},{20,28},{24,16},{28,20},{1,9},{5... | collective-permute-start | bytes 1843208 | tf_op jit(solution)/shard_map/ppermute | solution.py:639
  109.6 12.7 %collective-permute-start.33 = (bf16[224,768]{1,0:T(8,128)(2,1)S(1)}, bf16[224,768]{1,0:T(8,128)(2,1)S(1)}, u32[]{:S(2)}, u32[]{:S(2)}) collective-permute-start(bf16[224,768]{1,0:T(8,128)(2,1)S(1)} %get-tuple-element.413), channel_id=1, source_target_pairs={{0,1},{1,0},{2,3},{3,2},{4,5},{5,4},{6,7},{7,6},{8,9},{9,8},{10,11... | collective-permute-start | bytes 1032200 | tf_op jit(solution)/shard_map/ppermute | solution.py:639
  114.3 9.6 %collective-permute-start.36 = (bf16[224,768]{1,0:T(8,128)(2,1)S(1)}, bf16[224,768]{1,0:T(8,128)(2,1)S(1)}, u32[]{:S(2)}, u32[]{:S(2)}) collective-permute-start(bf16[224,768]{1,0:T(8,128)(2,1)S(1)} %get-tuple-element.425), channel_id=1, source_target_pairs={{0,1},{1,0},{2,3},{3,2},{4,5},{5,4},{6,7},{7,6},{8,9},{9,8},{10,11... | collective-permute-start | bytes 1032200 | tf_op jit(solution)/shard_map/ppermute | solution.py:639
  124.4 4.5 %collective-permute-start.41 = (bf16[2,192,1500]{2,1,0:T(8,128)(2,1)S(1)}, bf16[2,192,1500]{2,1,0:T(8,128)(2,1)S(1)}, u32[]{:S(2)}, u32[]{:S(2)}) collective-permute-start(bf16[2,192,1500]{2,1,0:T(8,128)(2,1)S(1)} %get-tuple-element.449), channel_id=1, source_target_pairs={{0,1},{1,0},{2,3},{3,2},{4,5},{5,4},{6,7},{7,6},{8,9},{9,8},{10,11... | collective-permute-start | bytes 3456008 | tf_op jit(solution)/shard_map/ppermute | solution.py:639
  124.5 7.0 %collective-permute-start.42 = (bf16[2,192,1500]{2,1,0:T(8,128)(2,1)S(1)}, bf16[2,192,1500]{2,1,0:T(8,128)(2,1)S(1)}, u32[]{:S(2)}, u32[]{:S(2)}) collective-permute-start(bf16[2,192,1500]{2,1,0:T(8,128)(2,1)S(1)} %get-tuple-element.451), channel_id=1, source_target_pairs={{0,1},{1,0},{2,3},{3,2},{4,5},{5,4},{6,7},{7,6},{8,9},{9,8},{10,11... | collective-permute-start | bytes 3456008 | tf_op jit(solution)/shard_map/ppermute | solution.py:639
  125.0 17.9 %collective-permute-start.40 = (bf16[2,224,768]{2,1,0:T(8,128)(2,1)S(1)}, bf16[2,224,768]{2,1,0:T(8,128)(2,1)S(1)}, u32[]{:S(2)}, u32[]{:S(2)}) collective-permute-start(bf16[2,224,768]{2,1,0:T(8,128)(2,1)S(1)} %get-tuple-element.444.refs_6_), channel_id=1, source_target_pairs={{0,2},{1,3},{2,0},{3,1},{4,6},{5,7},{6,4},{7,5},{8,10},{9,11},{10,... | collective-permute-start | bytes 2064392 | tf_op jit(solution)/shard_map/ppermute | solution.py:639
  126.5 16.1 %collective-permute-start.39 = (bf16[4,104,768]{2,1,0:T(8,128)(2,1)S(1)}, bf16[4,104,768]{2,1,0:T(8,128)(2,1)S(1)}, u32[]{:S(2)}, u32[]{:S(2)}) collective-permute-start(bf16[4,104,768]{2,1,0:T(8,128)(2,1)S(1)} %get-tuple-element.443), channel_id=1, source_target_pairs={{0,4},{4,0},{8,12},{12,8},{16,20},{20,16},{24,28},{28,24},{1,5},{5... | collective-permute-start | bytes 1916936 | tf_op jit(solution)/shard_map/ppermute | solution.py:639
  127.3 15.5 %collective-permute-start.38 = (bf16[2,104,768]{2,1,0:T(8,128)(2,1)S(1)}, bf16[2,104,768]{2,1,0:T(8,128)(2,1)S(1)}, u32[]{:S(2)}, u32[]{:S(2)}) collective-permute-start(bf16[2,104,768]{2,1,0:T(8,128)(2,1)S(1)} %get-tuple-element.441), channel_id=1, source_target_pairs={{0,8},{4,12},{8,0},{12,4},{16,24},{20,28},{24,16},{28,20},{1,9},{5... | collective-permute-start | bytes 958472 | tf_op jit(solution)/shard_map/ppermute | solution.py:639
  128.9 13.7 %collective-permute-start.37 = (bf16[1,200,768]{2,1,0:T(8,128)(2,1)S(1)}, bf16[1,200,768]{2,1,0:T(8,128)(2,1)S(1)}, u32[]{:S(2)}, u32[]{:S(2)}) collective-permute-start(bf16[1,200,768]{2,1,0:T(8,128)(2,1)S(1)} %get-tuple-element.439), channel_id=1, source_target_pairs={{0,16},{4,20},{8,24},{12,28},{16,0},{20,4},{24,8},{28,12},{1,17},{... | collective-permute-start | bytes 921608 | tf_op jit(solution)/shard_map/ppermute | solution.py:639
  143.3 7.6 %collective-permute-start.46 = (bf16[224,768]{1,0:T(8,128)(2,1)S(1)}, bf16[224,768]{1,0:T(8,128)(2,1)S(1)}, u32[]{:S(2)}, u32[]{:S(2)}) collective-permute-start(bf16[224,768]{1,0:T(8,128)(2,1)S(1)} %get-tuple-element.461), channel_id=1, source_target_pairs={{0,1},{1,0},{2,3},{3,2},{4,5},{5,4},{6,7},{7,6},{8,9},{9,8},{10,11... | collective-permute-start | bytes 1032200 | tf_op jit(solution)/shard_map/ppermute | solution.py:639
  143.4 7.5 %collective-permute-start.47 = (bf16[224,768]{1,0:T(8,128)(2,1)S(1)}, bf16[224,768]{1,0:T(8,128)(2,1)S(1)}, u32[]{:S(2)}, u32[]{:S(2)}) collective-permute-start(bf16[224,768]{1,0:T(8,128)(2,1)S(1)} %get-tuple-element.464), channel_id=1, source_target_pairs={{0,1},{1,0},{2,3},{3,2},{4,5},{5,4},{6,7},{7,6},{8,9},{9,8},{10,11... | collective-permute-start | bytes 1032200 | tf_op jit(solution)/shard_map/ppermute | solution.py:639
  143.9 34.9 %collective-permute-start.52 = (bf16[2,192,1500]{2,1,0:T(8,128)(2,1)S(1)}, bf16[2,192,1500]{2,1,0:T(8,128)(2,1)S(1)}, u32[]{:S(2)}, u32[]{:S(2)}) collective-permute-start(bf16[2,192,1500]{2,1,0:T(8,128)(2,1)S(1)} %get-tuple-element.472), channel_id=1, source_target_pairs={{0,2},{1,3},{2,0},{3,1},{4,6},{5,7},{6,4},{7,5},{8,10},{9,11},{10,... | collective-permute-start | bytes 3456008 | tf_op jit(solution)/shard_map/ppermute | solution.py:639
  146.7 25.1 %collective-permute-start.45 = (bf16[2,104,768]{2,1,0:T(8,128)(2,1)S(1)}, bf16[2,104,768]{2,1,0:T(8,128)(2,1)S(1)}, u32[]{:S(2)}, u32[]{:S(2)}) collective-permute-start(bf16[2,104,768]{2,1,0:T(8,128)(2,1)S(1)} %get-tuple-element.457), channel_id=1, source_target_pairs={{0,8},{4,12},{8,0},{12,4},{16,24},{20,28},{24,16},{28,20},{1,9},{5... | collective-permute-start | bytes 958472 | tf_op jit(solution)/shard_map/ppermute | solution.py:639
  147.5 24.3 %collective-permute-start.43 = (bf16[1,200,768]{2,1,0:T(8,128)(2,1)S(1)}, bf16[1,200,768]{2,1,0:T(8,128)(2,1)S(1)}, u32[]{:S(2)}, u32[]{:S(2)}) collective-permute-start(bf16[1,200,768]{2,1,0:T(8,128)(2,1)S(1)} %get-tuple-element.453.refs_0_), channel_id=1, source_target_pairs={{0,16},{4,20},{8,24},{12,28},{16,0},{20,4},{24,8},{28,12},{1,17},{... | collective-permute-start | bytes 921608 | tf_op jit(solution)/shard_map/ppermute | solution.py:639
  150.9 24.1 %collective-permute-start.53 = (bf16[2,224,768]{2,1,0:T(8,128)(2,1)S(1)}, bf16[2,224,768]{2,1,0:T(8,128)(2,1)S(1)}, u32[]{:S(2)}, u32[]{:S(2)}) collective-permute-start(bf16[2,224,768]{2,1,0:T(8,128)(2,1)S(1)} %get-tuple-element.475.refs_2_), channel_id=1, source_target_pairs={{0,1},{1,0},{2,3},{3,2},{4,5},{5,4},{6,7},{7,6},{8,9},{9,8},{10,11... | collective-permute-start | bytes 2064392 | tf_op jit(solution)/shard_map/ppermute | solution.py:639
  150.9 20.4 %collective-permute-start.44 = (bf16[1,104,768]{2,1,0:T(8,128)(2,1)S(1)}, bf16[1,104,768]{2,1,0:T(8,128)(2,1)S(1)}, u32[]{:S(2)}, u32[]{:S(2)}) collective-permute-start(bf16[1,104,768]{2,1,0:T(8,128)(2,1)S(1)} %get-tuple-element.455), channel_id=1, source_target_pairs={{0,16},{4,20},{8,24},{12,28},{16,0},{20,4},{24,8},{28,12},{1,17},{... | collective-permute-start | bytes 479240 | tf_op jit(solution)/shard_map/ppermute | solution.py:639
  171.3 22.0 %collective-permute-start.51 = (bf16[2,224,768]{2,1,0:T(8,128)(2,1)S(1)}, bf16[2,224,768]{2,1,0:T(8,128)(2,1)S(1)}, u32[]{:S(2)}, u32[]{:S(2)}) collective-permute-start(bf16[2,224,768]{2,1,0:T(8,128)(2,1)S(1)} %get-tuple-element.470.refs_6_), channel_id=1, source_target_pairs={{0,2},{1,3},{2,0},{3,1},{4,6},{5,7},{6,4},{7,5},{8,10},{9,11},{10,... | collective-permute-start | bytes 2064392 | tf_op jit(solution)/shard_map/ppermute | solution.py:639
  172.0 21.3 %collective-permute-start.48 = (bf16[2,200,768]{2,1,0:T(8,128)(2,1)S(1)}, bf16[2,200,768]{2,1,0:T(8,128)(2,1)S(1)}, u32[]{:S(2)}, u32[]{:S(2)}) collective-permute-start(bf16[2,200,768]{2,1,0:T(8,128)(2,1)S(1)} %get-tuple-element.466.refs_0_), channel_id=1, source_target_pairs={{0,8},{4,12},{8,0},{12,4},{16,24},{20,28},{24,16},{28,20},{1,9},{5... | collective-permute-start | bytes 1843208 | tf_op jit(solution)/shard_map/ppermute | solution.py:639
  172.1 17.3 %collective-permute-start.50 = (bf16[1,104,768]{2,1,0:T(8,128)(2,1)S(1)}, bf16[1,104,768]{2,1,0:T(8,128)(2,1)S(1)}, u32[]{:S(2)}, u32[]{:S(2)}) collective-permute-start(bf16[1,104,768]{2,1,0:T(8,128)(2,1)S(1)} %get-tuple-element.469), channel_id=1, source_target_pairs={{0,16},{4,20},{8,24},{12,28},{16,0},{20,4},{24,8},{28,12},{1,17},{... | collective-permute-start | bytes 479240 | tf_op jit(solution)/shard_map/ppermute | solution.py:639
  175.0 16.1 %collective-permute-start.49 = (bf16[1,104,768]{2,1,0:T(8,128)(2,1)S(1)}, bf16[1,104,768]{2,1,0:T(8,128)(2,1)S(1)}, u32[]{:S(2)}, u32[]{:S(2)}) collective-permute-start(bf16[1,104,768]{2,1,0:T(8,128)(2,1)S(1)} %get-tuple-element.467.refs_2_), channel_id=1, source_target_pairs={{0,16},{4,20},{8,24},{12,28},{16,0},{20,4},{24,8},{28,12},{1,17},{... | collective-permute-start | bytes 479240 | tf_op jit(solution)/shard_map/ppermute | solution.py:639
  193.6 30.0 %collective-permute-start.59 = (bf16[4,200,768]{2,1,0:T(8,128)(2,1)S(1)}, bf16[4,200,768]{2,1,0:T(8,128)(2,1)S(1)}, u32[]{:S(2)}, u32[]{:S(2)}) collective-permute-start(bf16[4,200,768]{2,1,0:T(8,128)(2,1)S(1)} %get-tuple-element.486.refs_0_), channel_id=1, source_target_pairs={{0,4},{4,0},{8,12},{12,8},{16,20},{20,16},{24,28},{28,24},{1,5},{5... | collective-permute-start | bytes 3686408 | tf_op jit(solution)/shard_map/ppermute | solution.py:639
  194.4 11.5 %collective-permute-start.55 = (bf16[2,104,768]{2,1,0:T(8,128)(2,1)S(1)}, bf16[2,104,768]{2,1,0:T(8,128)(2,1)S(1)}, u32[]{:S(2)}, u32[]{:S(2)}) collective-permute-start(bf16[2,104,768]{2,1,0:T(8,128)(2,1)S(1)} %get-tuple-element.481.refs_0_), channel_id=1, source_target_pairs={{0,8},{4,12},{8,0},{12,4},{16,24},{20,28},{24,16},{28,20},{1,9},{5... | collective-permute-start | bytes 958472 | tf_op jit(solution)/shard_map/ppermute | solution.py:639
  195.7 8.1 %collective-permute-start.56 = (bf16[1,104,768]{2,1,0:T(8,128)(2,1)S(1)}, bf16[1,104,768]{2,1,0:T(8,128)(2,1)S(1)}, u32[]{:S(2)}, u32[]{:S(2)}) collective-permute-start(bf16[1,104,768]{2,1,0:T(8,128)(2,1)S(1)} %get-tuple-element.482.refs_2_), channel_id=1, source_target_pairs={{0,16},{4,20},{8,24},{12,28},{16,0},{20,4},{24,8},{28,12},{1,17},{... | collective-permute-start | bytes 479240 | tf_op jit(solution)/shard_map/ppermute | solution.py:639
  206.0 20.5 %collective-permute-start.58 = (bf16[2,104,768]{2,1,0:T(8,128)(2,1)S(1)}, bf16[2,104,768]{2,1,0:T(8,128)(2,1)S(1)}, u32[]{:S(2)}, u32[]{:S(2)}) collective-permute-start(bf16[2,104,768]{2,1,0:T(8,128)(2,1)S(1)} %get-tuple-element.485.refs_0_), channel_id=1, source_target_pairs={{0,8},{4,12},{8,0},{12,4},{16,24},{20,28},{24,16},{28,20},{1,9},{5... | collective-permute-start | bytes 958472 | tf_op jit(solution)/shard_map/ppermute | solution.py:639
  207.4 31.7 %collective-permute-start.54 = (bf16[2,224,768]{2,1,0:T(8,128)(2,1)S(1)}, bf16[2,224,768]{2,1,0:T(8,128)(2,1)S(1)}, u32[]{:S(2)}, u32[]{:S(2)}) collective-permute-start(bf16[2,224,768]{2,1,0:T(8,128)(2,1)S(1)} %get-tuple-element.479.refs_2_), channel_id=1, source_target_pairs={{0,1},{1,0},{2,3},{3,2},{4,5},{5,4},{6,7},{7,6},{8,9},{9,8},{10,11... | collective-permute-start | bytes 2064392 | tf_op jit(solution)/shard_map/ppermute | solution.py:639
  207.4 29.9 %collective-permute-start.57 = (bf16[4,104,768]{2,1,0:T(8,128)(2,1)S(1)}, bf16[4,104,768]{2,1,0:T(8,128)(2,1)S(1)}, u32[]{:S(2)}, u32[]{:S(2)}) collective-permute-start(bf16[4,104,768]{2,1,0:T(8,128)(2,1)S(1)} %get-tuple-element.484.refs_0_), channel_id=1, source_target_pairs={{0,4},{4,0},{8,12},{12,8},{16,20},{20,16},{24,28},{28,24},{1,5},{5... | collective-permute-start | bytes 1916936 | tf_op jit(solution)/shard_map/ppermute | solution.py:639
  226.5 22.4 %collective-permute-start.60 = (bf16[4,104,768]{2,1,0:T(8,128)(2,1)S(1)}, bf16[4,104,768]{2,1,0:T(8,128)(2,1)S(1)}, u32[]{:S(2)}, u32[]{:S(2)}) collective-permute-start(bf16[4,104,768]{2,1,0:T(8,128)(2,1)S(1)} %get-tuple-element.494.refs_0_), channel_id=1, source_target_pairs={{0,4},{4,0},{8,12},{12,8},{16,20},{20,16},{24,28},{28,24},{1,5},{5... | collective-permute-start | bytes 1916936 | tf_op jit(solution)/shard_map/ppermute | solution.py:639
  250.8 3.4 %collective-permute-start.63 = (f32[8,768]{1,0:T(8,128)S(1)}, f32[8,768]{1,0:T(8,128)S(1)}, u32[]{:S(2)}, u32[]{:S(2)}) collective-permute-start(f32[8,768]{1,0:T(8,128)S(1)} %get-tuple-element.496), channel_id=1, source_target_pairs={{0,3},{1,2},{2,1},{3,0},{4,7},{5,6},{6,5},{7,4},{8,11},{9,10},{10,... | collective-permute-start | bytes 73736 | tf_op jit(solution)/shard_map/ppermute | solution.py:639
  250.8 3.9 %collective-permute-start.62 = (f32[8,768]{1,0:T(8,128)S(1)}, f32[8,768]{1,0:T(8,128)S(1)}, u32[]{:S(2)}, u32[]{:S(2)}) collective-permute-start(f32[8,768]{1,0:T(8,128)S(1)} %get-tuple-element.496), channel_id=1, source_target_pairs={{0,2},{1,3},{2,0},{3,1},{4,6},{5,7},{6,4},{7,5},{8,10},{9,11},{10,... | collective-permute-start | bytes 73736 | tf_op jit(solution)/shard_map/ppermute | solution.py:639
  252.4 2.3 collective-permute-start.61
  (21 other events, 50.6 us)

commit v4 on v3

--- a/solution.py
+++ b/solution.py
@@ -18,7 +18,7 @@
 INV_ROOT_TAU = 1.0 / math.sqrt(2.0 * math.pi)
 VMEM_BYTES = 20 * 1024 * 1024
 COST = 1
-ORDER = ("P", "AB", "FXl", "M", "a", "FXSm", "N", "b", "FXS", "ge", "FXSc", "XS", "u", "S", "v", "o", "w")
+ORDER = ("VAP", "B", "FX", "M", "FXSa", "FXSl", "e", "N", "b", "FXSm", "XSc", "u", "S", "g", "v", "o", "w")
 
 
 def dot(left, right, left_dim, right_dim):
@@ -453,9 +453,13 @@
     vec_o[4:5, 0:rows] = row_of_sums(dv_o[...])
 
 
+def sum_rows(*refs):
+    refs[-1][...] = sum_of([ref[...] for ref in refs[:-1]])
+
+
 def self_weights(items, x_ref, gain, shift, *refs):
-    dqkv, o, g1, vecs = (refs[k * items : (k + 1) * items] for k in range(4))
-    keep_o, send_o, whole = refs[4 * items :]
+    dqkv, o, g1 = (refs[k * items : (k + 1) * items] for k in range(3))
+    vec, near, far, across, keep_o, send_o, whole = refs[3 * items :]
     rows = o[0].shape[0]
     span = range(items)
     normed = []
@@ -465,7 +469,9 @@
     whole[0 : 3 * rows, :] = sum_of([nn(dqkv[k][...], normed[k]) for k in span])
     whole[3 * rows : 4 * rows, :] = sum_of([nn(o[k][...], g1[k][...]) for k in span])
     whole[4 * rows :, :] = jnp.zeros((whole.shape[0] - 4 * rows, whole.shape[1]), F32)
-    whole[4 * rows : 4 * rows + 8, :] = sum_of([v[...] for v in vecs])
+    summed = (vec[...] + near[...]) + (far[...] + across[...])
+    pick = iota((8, whole.shape[1]), 0)
+    whole[4 * rows : 4 * rows + 8, :] = jnp.where((pick == 5) | (pick == 6), summed, vec[...])
     scatter_blocks(whole, keep_o, send_o, X_FIRST)
 
 
@@ -806,7 +812,7 @@
     for i in span:
         self_sum[i].meet()
         out = order.run(
-            bind(cross_forward, i, chunk), 6,
+            bind(cross_forward, i, wide), 6,
             (hidden, *self_sum[i].pieces, obias_self, gain_cross, shift_cross, wq2, qbias_cross, output_cross, *cross_kv[i]),
             (state, low_state, low_rows, low_rows, lse_out, *half_outs), (whole, aug),
         )
@@ -865,7 +871,7 @@
             )
             cross_dp = DpSum(order, n_dp, X_FIRST, *made)
     operands = [hidden, gain_self, shift_self] + [out[2] for out in self_back] + [out[3] for out in self_out]
-    operands += [out[1] for out in self_back] + [out[3] for out in self_back]
+    operands += [out[1] for out in self_back]
     grad_shape, block_shape = shape(hidden.shape, F32), shape(hidden.shape, BF16)
     mem_half, memory_out = near_shape((2, rows, memory_len)), near_shape((items, rows, memory_len))
     line_out, bias_out, matrix = shape((width,), F32), shape((rows,), F32), shape((rows, width), F32)
@@ -873,8 +879,13 @@
     whole_cube = [pl.BlockSpec(hidden.shape, lambda *_: (0, 0, 0))]
     got = {}
 
+    def rows_self():
+        vec = order.run(sum_rows, 0.3, [out[3] for out in self_back], (vec_out,))[0]
+        got["V"] = [vec] + [swap(vec, "mp", n_mp, bit) for bit in (1, 2, 3)]
+
     def pack_self():
-        got["S"] = DpSum(order, n_dp, X_FIRST, *order.run(bind(self_weights, items), 3, operands, outs, scratch))
+        made = order.run(bind(self_weights, items), 3, operands + got["V"], outs, scratch)
+        got["S"] = DpSum(order, n_dp, X_FIRST, *made)
 
     def last_finish():
         got["hidden"] = order.run(
@@ -916,13 +927,13 @@
         got["x"] = cross_dp.unpack((matrix,) * 4, lines)
 
     def unpack_self():
-        got["s"] = got["S"].unpack((matrix,) * 4, lines, near_shape((8, width), F32))
+        got["s"] = got["S"].unpack((matrix,) * 4, lines + (line_out, line_out))
 
     def job(which):
         if which in "FXS":
             return {"F": feed_dp, "X": cross_dp, "S": got.get("S")}[which].job()
         if which == "l":
-            got["last"] = PairSum(order, n_mp, [out[4] for out in self_back], [out[5] for out in self_back])
+            got["last"] = PairSum(order, n_mp, [out[4] for out in self_back], [order.later(out[5]) for out in self_back])
             return got["last"].job()
         if which == "b":
             return got["block"].job()
@@ -942,7 +953,7 @@
         got["block"] = PairSum(order, n_mp, [got["b", i][0] for i in span], sends)
 
     acts = dict(
-        M=memory_swap, N=block_swap, P=pack_self, g=last_finish, A=lambda: [memory(i) for i in span], e=memory_finish,
+        M=memory_swap, N=block_swap, P=pack_self, V=rows_self, g=last_finish, A=lambda: [memory(i) for i in span], e=memory_finish,
         B=lambda: [block_part(i) for i in span], o=block_finish, u=unpack_feed, v=unpack_cross, w=unpack_self,
     )
     for word in ORDER:
@@ -953,14 +964,12 @@
             run_together(order, [job(which) for which in word])
     cross_grads, self_grads, feed_grads = got["x"], got["s"], got["f"]
     hidden_grad, encoder_grad, block_out = got["hidden"], got["encoder"], got["out"]
-    norm_rows = self_grads[9]
-    norm_rows = norm_rows + swap(norm_rows, "mp", n_mp, 1) + (swap(norm_rows, "mp", n_mp, 2) + swap(norm_rows, "mp", n_mp, 3))
     return (
         block_out,
         hidden_grad,
         encoder_grad,
-        norm_rows[5],
-        norm_rows[6],
+        self_grads[9],
+        self_grads[10],
         self_grads[0].T,
         self_grads[7],
         self_grads[1].T,

time: 260 us -> 255 us (0.981)
  waiting for transfers between devices: 112 us -> 101 us
  starting transfers between devices: 51.5 us -> 58.5 us
    ppermute x64, waiting for transfers between devices: 112 us -> 101 us  [swap(): return lax.ppermute(value, axis, [(k, k ^ bit) for k in range(size)])]
    ppermute x64, starting transfers between devices: 51.5 us -> 58.5 us  [swap(): return lax.ppermute(value, axis, [(k, k ^ bit) for k in range(size)])]
where the time goes in v4:
time: 255 us; the launch traced here: 250 us
  waiting for transfers between devices  101 us (40%)
  Pallas kernels  88 us (35%)
  starting transfers between devices  58.5 us (23%)
    ppermute x64, waiting for transfers between devices, swap(): return lax.ppermute(value, axis, [(k, k ^ bit) for k in range(size)])  101 us
    pallas_call x50, Pallas kernels, run(): pl.pallas_call(whole_body, name=inner.__name__, grid=(1,), in_specs=in_sp...  88 us
    ppermute x64, starting transfers between devices, swap(): return lax.ppermute(value, axis, [(k, k ^ bit) for k in range(size)])  58.5 us
  transfers between devices with their start and end apart: 64, of which 33 were waited for; matrix products, arithmetic and copies ran while one was open for 0% of the time, Pallas kernels for 31%

profile of v4, /device:TPU:0, one launch (start us, length us, event | category | flops | bytes accessed | tf_op | source)
XLA Modules:
  0.0 250.5 jit_solution(9073245479646105858)
XLA Ops:
  1.3 5.5 %first_forward.1 = (bf16[192,448]{1,0:T(8,128)(2,1)S(1)}, bf16[3,80,448]{2,1,0:T(8,128)(2,1)S(1)}, bf16[3,80,448]{2,1,0:T(8,128)(2,1)S(1)}, bf16[192,448]{1,0:T(...) custom-call(s32[2]{0:T(128)S(1)} %copy-done, ...), custom_call_target="tpu_custom_call" | custom-call | flops 4 | bytes 1 | tf_op jit(solution)/shard_map/first_forward/pallas_call | solution.py:618
  7.4 3.5 %self_forward.1 = (bf16[192,448]{1,0:T(8,128)(2,1)S(1)}, bf16[3,80,448]{2,1,0:T(8,128)(2,1)S(1)}, bf16[3,80,448]{2,1,0:T(8,128)(2,1)S(1)}, bf16[192,448]{1,0:T(8...) custom-call(s32[2]{0:T(128)S(1)} %copy-done, ...), custom_call_target="tpu_custom_call" | custom-call | flops 4 | bytes 1 | tf_op jit(solution)/shard_map/self_forward/pallas_call | solution.py:618
  11.0 3.0 %collective-permute-start.2 = (bf16[224,768]{1,0:T(8,128)(2,1)S(1)}, bf16[224,768]{1,0:T(8,128)(2,1)S(1)}, u32[]{:S(2)}, u32[]{:S(2)}) collective-permute-start(bf16[224,768]{1,0:T(8,128)(2,1)S(1)} %get-tuple-element.291.refs_0_), channel_id=1, source_target_pairs={{0,2},{1,3},{2,0},{3,1},{4,6},{5,7},{6,4},{7,5},{8,10},{9,11},{10,... | collective-permute-start | bytes 1032200 | tf_op jit(solution)/shard_map/ppermute | solution.py:645
  15.2 2.1 cross_keys.2
  17.4 2.1 cross_keys.3
  19.4 2.9 %collective-permute-done.2.refs_1_ = bf16[224,768]{1,0:T(8,128)(2,1)S(1)} collective-permute-done((bf16[224,768]{1,0:T(8,128)(2,1)S(1)}, bf16[224,768]{1,0:T(8,128)(2,1)S(1)}, u32[]{:S(2)}, u32[]{:S(2)}) %collective-permute-start.2) | collective-permute-done | bytes 344096 | tf_op jit(solution)/shard_map/ppermute | solution.py:645
  22.5 1.8 collective-permute-start.9
  24.3 5.2 %cross_forward.2 = (f32[448,768]{1,0:T(8,128)S(1)}, bf16[448,768]{1,0:T(8,128)(2,1)S(1)}, bf16[192,448]{1,0:T(8,128)(2,1)S(1)}, bf16[192,448]{1,0:T(8,128)(2,1)S...) custom-call(bf16[2,448,768]{2,1,0:T(8,128)(2,1)S(1)} %get-tuple-elem, ...), custom_call_target="tpu_custom_call" | custom-call | flops 6 | bytes 1 | tf_op jit(solution)/shard_map/cross_forward/pallas_call | solution.py:618
  33.2 1.8 collective-permute-start.8
  35.0 4.9 %cross_forward.3 = (f32[448,768]{1,0:T(8,128)S(1)}, bf16[448,768]{1,0:T(8,128)(2,1)S(1)}, bf16[192,448]{1,0:T(8,128)(2,1)S(1)}, bf16[192,448]{1,0:T(8,128)(2,1)S...) custom-call(bf16[2,448,768]{2,1,0:T(8,128)(2,1)S(1)} %get-tuple-elem, ...), custom_call_target="tpu_custom_call" | custom-call | flops 6 | bytes 1 | tf_op jit(solution)/shard_map/cross_forward/pallas_call | solution.py:618
  41.7 2.0 collective-permute-done.8.refs_1_
  43.8 1.8 collective-permute-start.14
  45.6 3.4 %feed.2 = (f32[448,768]{1,0:T(8,128)S(1)}, bf16[448,768]{1,0:T(8,128)(2,1)S(1)}, bf16[448,768]{1,0:T(8,128)(2,1)S(1)}, bf16[448,768]{1,0:T(8,128)(2,1)S(1)}, bf1...) custom-call(s32[2]{0:T(128)S(1)} %copy-done.1, ...), custom_call_target="tpu_custom_call" | custom-call | flops 4 | bytes 1 | tf_op jit(solution)/shard_map/feed/pallas_call | solution.py:618
  50.8 3.5 %collective-permute-done.14.refs_1_ = bf16[224,768]{1,0:T(8,128)(2,1)S(1)} collective-permute-done((bf16[224,768]{1,0:T(8,128)(2,1)S(1)}, bf16[224,768]{1,0:T(8,128)(2,1)S(1)}, u32[]{:S(2)}, u32[]{:S(2)}) %collective-permute-start.14) | collective-permute-done | bytes 344096 | tf_op jit(solution)/shard_map/ppermute | solution.py:645
  54.4 1.8 collective-permute-start.18
  56.3 3.8 %feed.3 = (f32[448,768]{1,0:T(8,128)S(1)}, bf16[448,768]{1,0:T(8,128)(2,1)S(1)}, bf16[448,768]{1,0:T(8,128)(2,1)S(1)}, bf16[448,768]{1,0:T(8,128)(2,1)S(1)}, bf1...) custom-call(s32[2]{0:T(128)S(1)} %copy-done.1, ...), custom_call_target="tpu_custom_call" | custom-call | flops 4 | bytes 1 | tf_op jit(solution)/shard_map/feed/pallas_call | solution.py:618
  61.8 3.1 %collective-permute-done.18.refs_1_ = bf16[224,768]{1,0:T(8,128)(2,1)S(1)} collective-permute-done((bf16[224,768]{1,0:T(8,128)(2,1)S(1)}, bf16[224,768]{1,0:T(8,128)(2,1)S(1)}, u32[]{:S(2)}, u32[]{:S(2)}) %collective-permute-start.18) | collective-permute-done | bytes 344096 | tf_op jit(solution)/shard_map/ppermute | solution.py:645
  65.1 3.2 %feed_weights.1 = (bf16[4,200,768]{2,1,0:T(8,128)(2,1)S(1)}, bf16[4,200,768]{2,1,0:T(8,128)(2,1)S(1)}, f32[8,128]{1,0:T(8,128)S(1)}) custom-call(bf16[448,768]{1,0:T(8,128)(2,1)S(1)} %get-tuple-element.349.refs_0_, bf16[448,768]{1,0:T(8,128)(2,1)S(1)} %get-tuple-element.350.refs_1_, bf16[448,768]{1,0:T(8,128)(2,1)S(1)} %get-tuple-element.351.refs_2_, ...), custom_call_target="tpu_custom_call" | custom-call | flops 2 | bytes 1 | tf_op jit(solution)/shard_map/feed_weights/pallas_call | solution.py:618
  71.6 8.6 %cross_backward.2 = (f32[448,768]{1,0:T(8,128)S(1)}, bf16[448,768]{1,0:T(8,128)(2,1)S(1)}, bf16[192,448]{1,0:T(8,128)(2,1)S(1)}, bf16[192,1536]{1,0:T(8,128)(2,1...) custom-call(s32[2]{0:T(128)S(1)} %copy-done.1, ...), custom_call_target="tpu_custom_call" | custom-call | flops 9 | bytes 1 | tf_op jit(solution)/shard_map/cross_backward/pallas_call | solution.py:618
  83.7 8.4 %cross_backward.3 = (f32[448,768]{1,0:T(8,128)S(1)}, bf16[448,768]{1,0:T(8,128)(2,1)S(1)}, bf16[192,448]{1,0:T(8,128)(2,1)S(1)}, bf16[192,1536]{1,0:T(8,128)(2,1...) custom-call(s32[2]{0:T(128)S(1)} %copy-done.1, ...), custom_call_target="tpu_custom_call" | custom-call | flops 9 | bytes 1 | tf_op jit(solution)/shard_map/cross_backward/pallas_call | solution.py:618
  94.9 2.8 %collective-permute-done.21.refs_1_ = bf16[4,200,768]{2,1,0:T(8,128)(2,1)S(1)} collective-permute-done((bf16[4,200,768]{2,1,0:T(8,128)(2,1)S(1)}, bf16[4,200,768]{2,1,0:T(8,128)(2,1)S(1)}, u32[]{:S(2)}, u32[]{:S(2)}) %collective-permute-start.21) | collective-permute-done | bytes 1228832 | tf_op jit(solution)/shard_map/ppermute | solution.py:645
  98.0 5.1 %self_backward.2 = (f32[448,768]{1,0:T(8,128)S(1)}, bf16[448,768]{1,0:T(8,128)(2,1)S(1)}, bf16[576,448]{1,0:T(8,128)(2,1)S(1)}, f32[8,768]{1,0:T(8,128)S(1)}, bf...) custom-call(f32[448,768]{1,0:T(8,128)S(1)} %get-tuple-element.312.refs_2_.refs_0_, ...), custom_call_target="tpu_custom_call" | custom-call | flops 5 | bytes 1 | tf_op jit(solution)/shard_map/self_backward/pallas_call | solution.py:618
  103.2 2.9 %cross_weights.1 = (bf16[4,104,768]{2,1,0:T(8,128)(2,1)S(1)}, bf16[4,104,768]{2,1,0:T(8,128)(2,1)S(1)}, f32[8,128]{1,0:T(8,128)S(1)}) custom-call(bf16[2,1500,768]{2,1,0:T(8,128)(2,1)S(1)} %copy.58.refs_1_.refs_0_, bf16[192,448]{1,0:T(8,128)(2,1)S(1)} %get-tuple-element.393.refs_1_, bf16[192,448]{1,0:T(8,128)(2,1)S(1)} %get-tuple-element.394.refs_2_, ...), custom_call_target="tpu_custom_call" | custom-call | flops 3 | bytes 1 | tf_op jit(solution)/shard_map/cross_weights/pallas_call | solution.py:618
  106.1 1.8 collective-permute-start.32
  111.2 4.7 %self_backward.3 = (f32[448,768]{1,0:T(8,128)S(1)}, bf16[448,768]{1,0:T(8,128)(2,1)S(1)}, bf16[576,448]{1,0:T(8,128)(2,1)S(1)}, f32[8,768]{1,0:T(8,128)S(1)}, bf...) custom-call(f32[448,768]{1,0:T(8,128)S(1)} %get-tuple-element.339.refs_2_.refs_0_, ...), custom_call_target="tpu_custom_call" | custom-call | flops 5 | bytes 1 | tf_op jit(solution)/shard_map/self_backward/pallas_call | solution.py:618
  119.6 1.9 memory_grad.3
  121.5 2.2 self_weights.1
  127.0 2.8 %collective-permute-start.38 = (bf16[1,200,768]{2,1,0:T(8,128)(2,1)S(1)}, bf16[1,200,768]{2,1,0:T(8,128)(2,1)S(1)}, u32[]{:S(2)}, u32[]{:S(2)}) collective-permute-start(bf16[1,200,768]{2,1,0:T(8,128)(2,1)S(1)} %get-tuple-element.441), channel_id=1, source_target_pairs={{0,16},{4,20},{8,24},{12,28},{16,0},{20,4},{24,8},{28,12},{1,17},{... | collective-permute-start | bytes 921608 | tf_op jit(solution)/shard_map/ppermute | solution.py:645
  129.8 11.0 %collective-permute-done.38.refs_1_ = bf16[1,200,768]{2,1,0:T(8,128)(2,1)S(1)} collective-permute-done((bf16[1,200,768]{2,1,0:T(8,128)(2,1)S(1)}, bf16[1,200,768]{2,1,0:T(8,128)(2,1)S(1)}, u32[]{:S(2)}, u32[]{:S(2)}) %collective-permute-start.38) | collective-permute-done | bytes 307232 | tf_op jit(solution)/shard_map/ppermute | solution.py:645
  140.7 2.2 collective-permute-done.39.refs_3_
  145.3 2.6 %collective-permute-start.44 = (bf16[1,104,768]{2,1,0:T(8,128)(2,1)S(1)}, bf16[1,104,768]{2,1,0:T(8,128)(2,1)S(1)}, u32[]{:S(2)}, u32[]{:S(2)}) collective-permute-start(bf16[1,104,768]{2,1,0:T(8,128)(2,1)S(1)} %get-tuple-element.455), channel_id=1, source_target_pairs={{0,16},{4,20},{8,24},{12,28},{16,0},{20,4},{24,8},{28,12},{1,17},{... | collective-permute-start | bytes 479240 | tf_op jit(solution)/shard_map/ppermute | solution.py:645
  148.4 2.4 collective-permute-start.45
  150.9 4.5 %collective-permute-done.44.refs_3_ = bf16[1,104,768]{2,1,0:T(8,128)(2,1)S(1)} collective-permute-done((bf16[1,104,768]{2,1,0:T(8,128)(2,1)S(1)}, bf16[1,104,768]{2,1,0:T(8,128)(2,1)S(1)}, u32[]{:S(2)}, u32[]{:S(2)}) %collective-permute-start.44) | collective-permute-done | bytes 159776 | tf_op jit(solution)/shard_map/ppermute | solution.py:645
  155.4 14.2 %collective-permute-done.43.refs_1_ = bf16[1,200,768]{2,1,0:T(8,128)(2,1)S(1)} collective-permute-done((bf16[1,200,768]{2,1,0:T(8,128)(2,1)S(1)}, bf16[1,200,768]{2,1,0:T(8,128)(2,1)S(1)}, u32[]{:S(2)}, u32[]{:S(2)}) %collective-permute-start.43) | collective-permute-done | bytes 307232 | tf_op jit(solution)/shard_map/ppermute | solution.py:645
  170.5 2.4 collective-permute-start.48
  175.1 3.4 %collective-permute-start.50 = (bf16[1,104,768]{2,1,0:T(8,128)(2,1)S(1)}, bf16[1,104,768]{2,1,0:T(8,128)(2,1)S(1)}, u32[]{:S(2)}, u32[]{:S(2)}) collective-permute-start(bf16[1,104,768]{2,1,0:T(8,128)(2,1)S(1)} %get-tuple-element.468), channel_id=1, source_target_pairs={{0,16},{4,20},{8,24},{12,28},{16,0},{20,4},{24,8},{28,12},{1,17},{... | collective-permute-start | bytes 479240 | tf_op jit(solution)/shard_map/ppermute | solution.py:645
  179.8 10.8 %collective-permute-done.50.refs_5_ = bf16[1,104,768]{2,1,0:T(8,128)(2,1)S(1)} collective-permute-done((bf16[1,104,768]{2,1,0:T(8,128)(2,1)S(1)}, bf16[1,104,768]{2,1,0:T(8,128)(2,1)S(1)}, u32[]{:S(2)}, u32[]{:S(2)}) %collective-permute-start.50) | collective-permute-done | bytes 159776 | tf_op jit(solution)/shard_map/ppermute | solution.py:645
  195.9 3.4 %collective-permute-start.55 = (bf16[2,104,768]{2,1,0:T(8,128)(2,1)S(1)}, bf16[2,104,768]{2,1,0:T(8,128)(2,1)S(1)}, u32[]{:S(2)}, u32[]{:S(2)}) collective-permute-start(bf16[2,104,768]{2,1,0:T(8,128)(2,1)S(1)} %get-tuple-element.481.refs_0_), channel_id=1, source_target_pairs={{0,8},{4,12},{8,0},{12,4},{16,24},{20,28},{24,16},{28,20},{1,9},{5... | collective-permute-start | bytes 958472 | tf_op jit(solution)/shard_map/ppermute | solution.py:645
  201.0 6.7 %collective-permute-done.56.refs_3_ = bf16[1,104,768]{2,1,0:T(8,128)(2,1)S(1)} collective-permute-done((bf16[1,104,768]{2,1,0:T(8,128)(2,1)S(1)}, bf16[1,104,768]{2,1,0:T(8,128)(2,1)S(1)}, u32[]{:S(2)}, u32[]{:S(2)}) %collective-permute-start.56) | collective-permute-done | bytes 159776 | tf_op jit(solution)/shard_map/ppermute | solution.py:645
  210.3 3.4 %collective-permute-start.61 = (bf16[2,104,768]{2,1,0:T(8,128)(2,1)S(1)}, bf16[2,104,768]{2,1,0:T(8,128)(2,1)S(1)}, u32[]{:S(2)}, u32[]{:S(2)}) collective-permute-start(bf16[2,104,768]{2,1,0:T(8,128)(2,1)S(1)} %get-tuple-element.491.refs_0_), channel_id=1, source_target_pairs={{0,8},{4,12},{8,0},{12,4},{16,24},{20,28},{24,16},{28,20},{1,9},{5... | collective-permute-start | bytes 958472 | tf_op jit(solution)/shard_map/ppermute | solution.py:645
  215.4 8.0 %collective-permute-done.62.refs_1_ = bf16[4,200,768]{2,1,0:T(8,128)(2,1)S(1)} collective-permute-done((bf16[4,200,768]{2,1,0:T(8,128)(2,1)S(1)}, bf16[4,200,768]{2,1,0:T(8,128)(2,1)S(1)}, u32[]{:S(2)}, u32[]{:S(2)}) %collective-permute-start.62) | collective-permute-done | bytes 1228832 | tf_op jit(solution)/shard_map/ppermute | solution.py:645
  223.4 2.8 %unpack.3 = (f32[768,768]{1,0:T(8,128)}, f32[768,768]{1,0:T(8,128)}, f32[768]{0:T(1024)}, f32[768]{0:T(1024)}, f32[8,128]{1,0:T(8,128)S(1)}) custom-call(bf16[4,200,768]{2,1,0:T(8,128)(2,1)S(1)} %get-tuple-element.492.refs_0_, bf16[4,200,768]{2,1,0:T(8,128)(2,1)S(1)} %collective-permute-done.62.refs_1_, f32[8,128]{1,0:T(8,128)S(1)} %get-tuple-element.493.refs_2_), custom_call_target="tpu_custom_call" | custom-call | flops 3 | bytes 1 | tf_op jit(solution)/shard_map/unpack/pallas_call | solution.py:618
  227.3 3.7 %finish_grad.1 = (f32[2,448,768]{2,1,0:T(8,128)}, f32[8,128]{1,0:T(8,128)S(1)}) custom-call(f32[448,768]{1,0:T(8,128)S(1)} %get-tuple-element.488.refs_0_, f32[448,768]{1,0:T(8,128)S(1)} %get-tuple-element.489.refs_1_, bf16[2,224,768]{2,1,0:T(8,128)(2,1)S(1)} %get-tuple-element.490.refs_2_, bf16[2,224,768]{2,1,0:T(8,128)(2,1)S(1)} %collective-permute-done.60.refs_3_, ...), custom_call_target="tpu_custom_call" | custom-call | flops 4 | bytes 1 | tf_op jit(solution)/shard_map/finish_grad/pallas_call | solution.py:618
  231.0 6.1 %collective-permute-done.59.refs_1_ = bf16[4,104,768]{2,1,0:T(8,128)(2,1)S(1)} collective-permute-done((bf16[4,104,768]{2,1,0:T(8,128)(2,1)S(1)}, bf16[4,104,768]{2,1,0:T(8,128)(2,1)S(1)}, u32[]{:S(2)}, u32[]{:S(2)}) %collective-permute-start.59) | collective-permute-done | bytes 639008 | tf_op jit(solution)/shard_map/ppermute | solution.py:645
  237.1 1.8 unpack.4
  238.9 1.9 finish_out.1
  240.8 7.6 %collective-permute-done.63.refs_1_ = bf16[4,104,768]{2,1,0:T(8,128)(2,1)S(1)} collective-permute-done((bf16[4,104,768]{2,1,0:T(8,128)(2,1)S(1)}, bf16[4,104,768]{2,1,0:T(8,128)(2,1)S(1)}, u32[]{:S(2)}, u32[]{:S(2)}) %collective-permute-start.63) | collective-permute-done | bytes 639008 | tf_op jit(solution)/shard_map/ppermute | solution.py:645
  248.5 1.8 unpack.5
  (141 shorter events, 52.1 us)
Async XLA Ops:
  6.8 4.1 %collective-permute-start = (bf16[112,768]{1,0:T(8,128)(2,1)S(1)}, bf16[112,768]{1,0:T(8,128)(2,1)S(1)}, u32[]{:S(2)}, u32[]{:S(2)}) collective-permute-start(bf16[112,768]{1,0:T(8,128)(2,1)S(1)} %get-tuple-element.279), channel_id=1, source_target_pairs={{0,1},{1,0},{2,3},{3,2},{4,5},{5,4},{6,7},{7,6},{8,9},{9,8},{10,11... | collective-permute-start | bytes 516104 | tf_op jit(solution)/shard_map/ppermute | solution.py:645
  7.4 3.6 %collective-permute-start.1 = (bf16[112,768]{1,0:T(8,128)(2,1)S(1)}, bf16[112,768]{1,0:T(8,128)(2,1)S(1)}, u32[]{:S(2)}, u32[]{:S(2)}) collective-permute-start(bf16[112,768]{1,0:T(8,128)(2,1)S(1)} %get-tuple-element.280), channel_id=1, source_target_pairs={{0,1},{1,0},{2,3},{3,2},{4,5},{5,4},{6,7},{7,6},{8,9},{9,8},{10,11... | collective-permute-start | bytes 516104 | tf_op jit(solution)/shard_map/ppermute | solution.py:645
  11.0 11.3 %collective-permute-start.2 = (bf16[224,768]{1,0:T(8,128)(2,1)S(1)}, bf16[224,768]{1,0:T(8,128)(2,1)S(1)}, u32[]{:S(2)}, u32[]{:S(2)}) collective-permute-start(bf16[224,768]{1,0:T(8,128)(2,1)S(1)} %get-tuple-element.291.refs_0_), channel_id=1, source_target_pairs={{0,2},{1,3},{2,0},{3,1},{4,6},{5,7},{6,4},{7,5},{8,10},{9,11},{10,... | collective-permute-start | bytes 1032200 | tf_op jit(solution)/shard_map/ppermute | solution.py:645
  14.0 3.2 %collective-permute-start.3 = (bf16[112,768]{1,0:T(8,128)(2,1)S(1)}, bf16[112,768]{1,0:T(8,128)(2,1)S(1)}, u32[]{:S(2)}, u32[]{:S(2)}) collective-permute-start(bf16[112,768]{1,0:T(8,128)(2,1)S(1)} %get-tuple-element.296), channel_id=1, source_target_pairs={{0,1},{1,0},{2,3},{3,2},{4,5},{5,4},{6,7},{7,6},{8,9},{9,8},{10,11... | collective-permute-start | bytes 516104 | tf_op jit(solution)/shard_map/ppermute | solution.py:645
  14.1 3.2 %collective-permute-start.4 = (bf16[112,768]{1,0:T(8,128)(2,1)S(1)}, bf16[112,768]{1,0:T(8,128)(2,1)S(1)}, u32[]{:S(2)}, u32[]{:S(2)}) collective-permute-start(bf16[112,768]{1,0:T(8,128)(2,1)S(1)} %get-tuple-element.297), channel_id=1, source_target_pairs={{0,1},{1,0},{2,3},{3,2},{4,5},{5,4},{6,7},{7,6},{8,9},{9,8},{10,11... | collective-permute-start | bytes 516104 | tf_op jit(solution)/shard_map/ppermute | solution.py:645
  22.4 1.9 collective-permute-start.5
  22.5 10.5 %collective-permute-start.9 = (bf16[224,768]{1,0:T(8,128)(2,1)S(1)}, bf16[224,768]{1,0:T(8,128)(2,1)S(1)}, u32[]{:S(2)}, u32[]{:S(2)}) collective-permute-start(bf16[224,768]{1,0:T(8,128)(2,1)S(1)} %get-tuple-element.318.refs_0_), channel_id=1, source_target_pairs={{0,2},{1,3},{2,0},{3,1},{4,6},{5,7},{6,4},{7,5},{8,10},{9,11},{10,... | collective-permute-start | bytes 1032200 | tf_op jit(solution)/shard_map/ppermute | solution.py:645
  33.1 1.9 collective-permute-start.10
  33.2 10.5 %collective-permute-start.8 = (bf16[224,768]{1,0:T(8,128)(2,1)S(1)}, bf16[224,768]{1,0:T(8,128)(2,1)S(1)}, u32[]{:S(2)}, u32[]{:S(2)}) collective-permute-start(bf16[224,768]{1,0:T(8,128)(2,1)S(1)} %get-tuple-element.317.refs_0_), channel_id=1, source_target_pairs={{0,2},{1,3},{2,0},{3,1},{4,6},{5,7},{6,4},{7,5},{8,10},{9,11},{10,... | collective-permute-start | bytes 1032200 | tf_op jit(solution)/shard_map/ppermute | solution.py:645
  43.8 10.5 %collective-permute-start.14 = (bf16[224,768]{1,0:T(8,128)(2,1)S(1)}, bf16[224,768]{1,0:T(8,128)(2,1)S(1)}, u32[]{:S(2)}, u32[]{:S(2)}) collective-permute-start(bf16[224,768]{1,0:T(8,128)(2,1)S(1)} %get-tuple-element.340.refs_0_), channel_id=1, source_target_pairs={{0,2},{1,3},{2,0},{3,1},{4,6},{5,7},{6,4},{7,5},{8,10},{9,11},{10,... | collective-permute-start | bytes 1032200 | tf_op jit(solution)/shard_map/ppermute | solution.py:645
  54.4 10.5 %collective-permute-start.18 = (bf16[224,768]{1,0:T(8,128)(2,1)S(1)}, bf16[224,768]{1,0:T(8,128)(2,1)S(1)}, u32[]{:S(2)}, u32[]{:S(2)}) collective-permute-start(bf16[224,768]{1,0:T(8,128)(2,1)S(1)} %get-tuple-element.359.refs_0_), channel_id=1, source_target_pairs={{0,2},{1,3},{2,0},{3,1},{4,6},{5,7},{6,4},{7,5},{8,10},{9,11},{10,... | collective-permute-start | bytes 1032200 | tf_op jit(solution)/shard_map/ppermute | solution.py:645
  65.0 6.5 %collective-permute-start.22 = (bf16[224,768]{1,0:T(8,128)(2,1)S(1)}, bf16[224,768]{1,0:T(8,128)(2,1)S(1)}, u32[]{:S(2)}, u32[]{:S(2)}) collective-permute-start(bf16[224,768]{1,0:T(8,128)(2,1)S(1)} %get-tuple-element.368.refs_3_), channel_id=1, source_target_pairs={{0,1},{1,0},{2,3},{3,2},{4,5},{5,4},{6,7},{7,6},{8,9},{9,8},{10,11... | collective-permute-start | bytes 1032200 | tf_op jit(solution)/shard_map/ppermute | solution.py:645
  68.3 29.5 %collective-permute-start.21 = (bf16[4,200,768]{2,1,0:T(8,128)(2,1)S(1)}, bf16[4,200,768]{2,1,0:T(8,128)(2,1)S(1)}, u32[]{:S(2)}, u32[]{:S(2)}) collective-permute-start(bf16[4,200,768]{2,1,0:T(8,128)(2,1)S(1)} %get-tuple-element.367), channel_id=1, source_target_pairs={{0,4},{4,0},{8,12},{12,8},{16,20},{20,16},{24,28},{28,24},{1,5},{5... | collective-permute-start | bytes 3686408 | tf_op jit(solution)/shard_map/ppermute | solution.py:645
  70.0 11.9 %collective-permute-start.26 = (bf16[224,768]{1,0:T(8,128)(2,1)S(1)}, bf16[224,768]{1,0:T(8,128)(2,1)S(1)}, u32[]{:S(2)}, u32[]{:S(2)}) collective-permute-start(bf16[224,768]{1,0:T(8,128)(2,1)S(1)} %get-tuple-element.378.refs_0_), channel_id=1, source_target_pairs={{0,2},{1,3},{2,0},{3,1},{4,6},{5,7},{6,4},{7,5},{8,10},{9,11},{10,... | collective-permute-start | bytes 1032200 | tf_op jit(solution)/shard_map/ppermute | solution.py:645
  82.3 11.6 %collective-permute-start.25 = (bf16[224,768]{1,0:T(8,128)(2,1)S(1)}, bf16[224,768]{1,0:T(8,128)(2,1)S(1)}, u32[]{:S(2)}, u32[]{:S(2)}) collective-permute-start(bf16[224,768]{1,0:T(8,128)(2,1)S(1)} %get-tuple-element.377.refs_0_), channel_id=1, source_target_pairs={{0,2},{1,3},{2,0},{3,1},{4,6},{5,7},{6,4},{7,5},{8,10},{9,11},{10,... | collective-permute-start | bytes 1032200 | tf_op jit(solution)/shard_map/ppermute | solution.py:645
  94.0 4.0 %collective-permute-start.31 = (bf16[224,768]{1,0:T(8,128)(2,1)S(1)}, bf16[224,768]{1,0:T(8,128)(2,1)S(1)}, u32[]{:S(2)}, u32[]{:S(2)}) collective-permute-start(bf16[224,768]{1,0:T(8,128)(2,1)S(1)} %get-tuple-element.405.refs_1_), channel_id=1, source_target_pairs={{0,1},{1,0},{2,3},{3,2},{4,5},{5,4},{6,7},{7,6},{8,9},{9,8},{10,11... | collective-permute-start | bytes 1032200 | tf_op jit(solution)/shard_map/ppermute | solution.py:645
  94.3 15.1 %collective-permute-start.33 = (bf16[224,768]{1,0:T(8,128)(2,1)S(1)}, bf16[224,768]{1,0:T(8,128)(2,1)S(1)}, u32[]{:S(2)}, u32[]{:S(2)}) collective-permute-start(bf16[224,768]{1,0:T(8,128)(2,1)S(1)} %get-tuple-element.417.refs_0_), channel_id=1, source_target_pairs={{0,2},{1,3},{2,0},{3,1},{4,6},{5,7},{6,4},{7,5},{8,10},{9,11},{10,... | collective-permute-start | bytes 1032200 | tf_op jit(solution)/shard_map/ppermute | solution.py:645
  106.1 19.3 %collective-permute-start.32 = (bf16[4,104,768]{2,1,0:T(8,128)(2,1)S(1)}, bf16[4,104,768]{2,1,0:T(8,128)(2,1)S(1)}, u32[]{:S(2)}, u32[]{:S(2)}) collective-permute-start(bf16[4,104,768]{2,1,0:T(8,128)(2,1)S(1)} %get-tuple-element.415), channel_id=1, source_target_pairs={{0,4},{4,0},{8,12},{12,8},{16,20},{20,16},{24,28},{28,24},{1,5},{5... | collective-permute-start | bytes 1916936 | tf_op jit(solution)/shard_map/ppermute | solution.py:645
  107.8 17.5 %collective-permute-start.30 = (bf16[2,200,768]{2,1,0:T(8,128)(2,1)S(1)}, bf16[2,200,768]{2,1,0:T(8,128)(2,1)S(1)}, u32[]{:S(2)}, u32[]{:S(2)}) collective-permute-start(bf16[2,200,768]{2,1,0:T(8,128)(2,1)S(1)} %get-tuple-element.392), channel_id=1, source_target_pairs={{0,8},{4,12},{8,0},{12,4},{16,24},{20,28},{24,16},{28,20},{1,9},{5... | collective-permute-start | bytes 1843208 | tf_op jit(solution)/shard_map/ppermute | solution.py:645
  116.0 5.5 %collective-permute-start.37 = (f32[8,768]{1,0:T(8,128)S(1)}, f32[8,768]{1,0:T(8,128)S(1)}, u32[]{:S(2)}, u32[]{:S(2)}) collective-permute-start(f32[8,768]{1,0:T(8,128)S(1)} %get-tuple-element.433.refs_9_), channel_id=1, source_target_pairs={{0,3},{1,2},{2,1},{3,0},{4,7},{5,6},{6,5},{7,4},{8,11},{9,10},{10,... | collective-permute-start | bytes 73736 | tf_op jit(solution)/shard_map/ppermute | solution.py:645
  117.3 4.2 %collective-permute-start.36 = (f32[8,768]{1,0:T(8,128)S(1)}, f32[8,768]{1,0:T(8,128)S(1)}, u32[]{:S(2)}, u32[]{:S(2)}) collective-permute-start(f32[8,768]{1,0:T(8,128)S(1)} %get-tuple-element.433.refs_9_), channel_id=1, source_target_pairs={{0,2},{1,3},{2,0},{3,1},{4,6},{5,7},{6,4},{7,5},{8,10},{9,11},{10,... | collective-permute-start | bytes 73736 | tf_op jit(solution)/shard_map/ppermute | solution.py:645
  117.8 3.7 %collective-permute-start.35 = (f32[8,768]{1,0:T(8,128)S(1)}, f32[8,768]{1,0:T(8,128)S(1)}, u32[]{:S(2)}, u32[]{:S(2)}) collective-permute-start(f32[8,768]{1,0:T(8,128)S(1)} %get-tuple-element.433.refs_9_), channel_id=1, source_target_pairs={{0,1},{1,0},{2,3},{3,2},{4,5},{5,4},{6,7},{7,6},{8,9},{9,8},{10,11... | collective-permute-start | bytes 73736 | tf_op jit(solution)/shard_map/ppermute | solution.py:645
  125.6 17.3 %collective-permute-start.41 = (bf16[2,192,1500]{2,1,0:T(8,128)(2,1)S(1)}, bf16[2,192,1500]{2,1,0:T(8,128)(2,1)S(1)}, u32[]{:S(2)}, u32[]{:S(2)}) collective-permute-start(bf16[2,192,1500]{2,1,0:T(8,128)(2,1)S(1)} %get-tuple-element.450), channel_id=1, source_target_pairs={{0,1},{1,0},{2,3},{3,2},{4,5},{5,4},{6,7},{7,6},{8,9},{9,8},{10,11... | collective-permute-start | bytes 3456008 | tf_op jit(solution)/shard_map/ppermute | solution.py:645
  126.1 16.8 %collective-permute-start.42 = (bf16[2,192,1500]{2,1,0:T(8,128)(2,1)S(1)}, bf16[2,192,1500]{2,1,0:T(8,128)(2,1)S(1)}, u32[]{:S(2)}, u32[]{:S(2)}) collective-permute-start(bf16[2,192,1500]{2,1,0:T(8,128)(2,1)S(1)} %get-tuple-element.452), channel_id=1, source_target_pairs={{0,1},{1,0},{2,3},{3,2},{4,5},{5,4},{6,7},{7,6},{8,9},{9,8},{10,11... | collective-permute-start | bytes 3456008 | tf_op jit(solution)/shard_map/ppermute | solution.py:645
  126.2 16.7 %collective-permute-start.40 = (bf16[4,104,768]{2,1,0:T(8,128)(2,1)S(1)}, bf16[4,104,768]{2,1,0:T(8,128)(2,1)S(1)}, u32[]{:S(2)}, u32[]{:S(2)}) collective-permute-start(bf16[4,104,768]{2,1,0:T(8,128)(2,1)S(1)} %get-tuple-element.445), channel_id=1, source_target_pairs={{0,4},{4,0},{8,12},{12,8},{16,20},{20,16},{24,28},{28,24},{1,5},{5... | collective-permute-start | bytes 1916936 | tf_op jit(solution)/shard_map/ppermute | solution.py:645
  126.7 16.2 %collective-permute-start.39 = (bf16[2,104,768]{2,1,0:T(8,128)(2,1)S(1)}, bf16[2,104,768]{2,1,0:T(8,128)(2,1)S(1)}, u32[]{:S(2)}, u32[]{:S(2)}) collective-permute-start(bf16[2,104,768]{2,1,0:T(8,128)(2,1)S(1)} %get-tuple-element.443), channel_id=1, source_target_pairs={{0,8},{4,12},{8,0},{12,4},{16,24},{20,28},{24,16},{28,20},{1,9},{5... | collective-permute-start | bytes 958472 | tf_op jit(solution)/shard_map/ppermute | solution.py:645
  127.0 13.8 %collective-permute-start.38 = (bf16[1,200,768]{2,1,0:T(8,128)(2,1)S(1)}, bf16[1,200,768]{2,1,0:T(8,128)(2,1)S(1)}, u32[]{:S(2)}, u32[]{:S(2)}) collective-permute-start(bf16[1,200,768]{2,1,0:T(8,128)(2,1)S(1)} %get-tuple-element.441), channel_id=1, source_target_pairs={{0,16},{4,20},{8,24},{12,28},{16,0},{20,4},{24,8},{28,12},{1,17},{... | collective-permute-start | bytes 921608 | tf_op jit(solution)/shard_map/ppermute | solution.py:645
  143.8 29.1 %collective-permute-start.52 = (bf16[2,192,1500]{2,1,0:T(8,128)(2,1)S(1)}, bf16[2,192,1500]{2,1,0:T(8,128)(2,1)S(1)}, u32[]{:S(2)}, u32[]{:S(2)}) collective-permute-start(bf16[2,192,1500]{2,1,0:T(8,128)(2,1)S(1)} %get-tuple-element.473), channel_id=1, source_target_pairs={{0,2},{1,3},{2,0},{3,1},{4,6},{5,7},{6,4},{7,5},{8,10},{9,11},{10,... | collective-permute-start | bytes 3456008 | tf_op jit(solution)/shard_map/ppermute | solution.py:645
  145.3 10.0 %collective-permute-start.44 = (bf16[1,104,768]{2,1,0:T(8,128)(2,1)S(1)}, bf16[1,104,768]{2,1,0:T(8,128)(2,1)S(1)}, u32[]{:S(2)}, u32[]{:S(2)}) collective-permute-start(bf16[1,104,768]{2,1,0:T(8,128)(2,1)S(1)} %get-tuple-element.455), channel_id=1, source_target_pairs={{0,16},{4,20},{8,24},{12,28},{16,0},{20,4},{24,8},{28,12},{1,17},{... | collective-permute-start | bytes 479240 | tf_op jit(solution)/shard_map/ppermute | solution.py:645
  147.9 21.6 %collective-permute-start.46 = (bf16[224,768]{1,0:T(8,128)(2,1)S(1)}, bf16[224,768]{1,0:T(8,128)(2,1)S(1)}, u32[]{:S(2)}, u32[]{:S(2)}) collective-permute-start(bf16[224,768]{1,0:T(8,128)(2,1)S(1)} %get-tuple-element.461), channel_id=1, source_target_pairs={{0,1},{1,0},{2,3},{3,2},{4,5},{5,4},{6,7},{7,6},{8,9},{9,8},{10,11... | collective-permute-start | bytes 1032200 | tf_op jit(solution)/shard_map/ppermute | solution.py:645
  147.9 21.6 %collective-permute-start.47 = (bf16[224,768]{1,0:T(8,128)(2,1)S(1)}, bf16[224,768]{1,0:T(8,128)(2,1)S(1)}, u32[]{:S(2)}, u32[]{:S(2)}) collective-permute-start(bf16[224,768]{1,0:T(8,128)(2,1)S(1)} %get-tuple-element.464), channel_id=1, source_target_pairs={{0,1},{1,0},{2,3},{3,2},{4,5},{5,4},{6,7},{7,6},{8,9},{9,8},{10,11... | collective-permute-start | bytes 1032200 | tf_op jit(solution)/shard_map/ppermute | solution.py:645
  148.4 21.1 %collective-permute-start.45 = (bf16[2,104,768]{2,1,0:T(8,128)(2,1)S(1)}, bf16[2,104,768]{2,1,0:T(8,128)(2,1)S(1)}, u32[]{:S(2)}, u32[]{:S(2)}) collective-permute-start(bf16[2,104,768]{2,1,0:T(8,128)(2,1)S(1)} %get-tuple-element.457), channel_id=1, source_target_pairs={{0,8},{4,12},{8,0},{12,4},{16,24},{20,28},{24,16},{28,20},{1,9},{5... | collective-permute-start | bytes 958472 | tf_op jit(solution)/shard_map/ppermute | solution.py:645
  155.4 14.2 %collective-permute-start.43 = (bf16[1,200,768]{2,1,0:T(8,128)(2,1)S(1)}, bf16[1,200,768]{2,1,0:T(8,128)(2,1)S(1)}, u32[]{:S(2)}, u32[]{:S(2)}) collective-permute-start(bf16[1,200,768]{2,1,0:T(8,128)(2,1)S(1)} %get-tuple-element.453.refs_0_), channel_id=1, source_target_pairs={{0,16},{4,20},{8,24},{12,28},{16,0},{20,4},{24,8},{28,12},{1,17},{... | collective-permute-start | bytes 921608 | tf_op jit(solution)/shard_map/ppermute | solution.py:645
  169.9 23.2 %collective-permute-start.51 = (bf16[2,224,768]{2,1,0:T(8,128)(2,1)S(1)}, bf16[2,224,768]{2,1,0:T(8,128)(2,1)S(1)}, u32[]{:S(2)}, u32[]{:S(2)}) collective-permute-start(bf16[2,224,768]{2,1,0:T(8,128)(2,1)S(1)} %get-tuple-element.469.refs_6_), channel_id=1, source_target_pairs={{0,2},{1,3},{2,0},{3,1},{4,6},{5,7},{6,4},{7,5},{8,10},{9,11},{10,... | collective-permute-start | bytes 2064392 | tf_op jit(solution)/shard_map/ppermute | solution.py:645
  170.5 22.6 %collective-permute-start.48 = (bf16[2,200,768]{2,1,0:T(8,128)(2,1)S(1)}, bf16[2,200,768]{2,1,0:T(8,128)(2,1)S(1)}, u32[]{:S(2)}, u32[]{:S(2)}) collective-permute-start(bf16[2,200,768]{2,1,0:T(8,128)(2,1)S(1)} %get-tuple-element.465.refs_0_), channel_id=1, source_target_pairs={{0,8},{4,12},{8,0},{12,4},{16,24},{20,28},{24,16},{28,20},{1,9},{5... | collective-permute-start | bytes 1843208 | tf_op jit(solution)/shard_map/ppermute | solution.py:645
  174.6 3.9 %collective-permute-start.53 = (bf16[224,768]{1,0:T(8,128)(2,1)S(1)}, bf16[224,768]{1,0:T(8,128)(2,1)S(1)}, u32[]{:S(2)}, u32[]{:S(2)}) collective-permute-start(bf16[224,768]{1,0:T(8,128)(2,1)S(1)} %get-tuple-element.476), channel_id=1, source_target_pairs={{0,1},{1,0},{2,3},{3,2},{4,5},{5,4},{6,7},{7,6},{8,9},{9,8},{10,11... | collective-permute-start | bytes 1032200 | tf_op jit(solution)/shard_map/ppermute | solution.py:645
  174.6 5.0 %collective-permute-start.54 = (bf16[224,768]{1,0:T(8,128)(2,1)S(1)}, bf16[224,768]{1,0:T(8,128)(2,1)S(1)}, u32[]{:S(2)}, u32[]{:S(2)}) collective-permute-start(bf16[224,768]{1,0:T(8,128)(2,1)S(1)} %get-tuple-element.479), channel_id=1, source_target_pairs={{0,1},{1,0},{2,3},{3,2},{4,5},{5,4},{6,7},{7,6},{8,9},{9,8},{10,11... | collective-permute-start | bytes 1032200 | tf_op jit(solution)/shard_map/ppermute | solution.py:645
  175.1 15.5 %collective-permute-start.50 = (bf16[1,104,768]{2,1,0:T(8,128)(2,1)S(1)}, bf16[1,104,768]{2,1,0:T(8,128)(2,1)S(1)}, u32[]{:S(2)}, u32[]{:S(2)}) collective-permute-start(bf16[1,104,768]{2,1,0:T(8,128)(2,1)S(1)} %get-tuple-element.468), channel_id=1, source_target_pairs={{0,16},{4,20},{8,24},{12,28},{16,0},{20,4},{24,8},{28,12},{1,17},{... | collective-permute-start | bytes 479240 | tf_op jit(solution)/shard_map/ppermute | solution.py:645
  178.5 13.8 %collective-permute-start.49 = (bf16[1,104,768]{2,1,0:T(8,128)(2,1)S(1)}, bf16[1,104,768]{2,1,0:T(8,128)(2,1)S(1)}, u32[]{:S(2)}, u32[]{:S(2)}) collective-permute-start(bf16[1,104,768]{2,1,0:T(8,128)(2,1)S(1)} %get-tuple-element.466.refs_2_), channel_id=1, source_target_pairs={{0,16},{4,20},{8,24},{12,28},{16,0},{20,4},{24,8},{28,12},{1,17},{... | collective-permute-start | bytes 479240 | tf_op jit(solution)/shard_map/ppermute | solution.py:645
  193.4 30.0 %collective-permute-start.62 = (bf16[4,200,768]{2,1,0:T(8,128)(2,1)S(1)}, bf16[4,200,768]{2,1,0:T(8,128)(2,1)S(1)}, u32[]{:S(2)}, u32[]{:S(2)}) collective-permute-start(bf16[4,200,768]{2,1,0:T(8,128)(2,1)S(1)} %get-tuple-element.492.refs_0_), channel_id=1, source_target_pairs={{0,4},{4,0},{8,12},{12,8},{16,20},{20,16},{24,28},{28,24},{1,5},{5... | collective-permute-start | bytes 3686408 | tf_op jit(solution)/shard_map/ppermute | solution.py:645
  194.4 15.7 %collective-permute-start.57 = (bf16[2,224,768]{2,1,0:T(8,128)(2,1)S(1)}, bf16[2,224,768]{2,1,0:T(8,128)(2,1)S(1)}, u32[]{:S(2)}, u32[]{:S(2)}) collective-permute-start(bf16[2,224,768]{2,1,0:T(8,128)(2,1)S(1)} %get-tuple-element.483.refs_4_), channel_id=1, source_target_pairs={{0,2},{1,3},{2,0},{3,1},{4,6},{5,7},{6,4},{7,5},{8,10},{9,11},{10,... | collective-permute-start | bytes 2064392 | tf_op jit(solution)/shard_map/ppermute | solution.py:645
  195.9 12.6 %collective-permute-start.55 = (bf16[2,104,768]{2,1,0:T(8,128)(2,1)S(1)}, bf16[2,104,768]{2,1,0:T(8,128)(2,1)S(1)}, u32[]{:S(2)}, u32[]{:S(2)}) collective-permute-start(bf16[2,104,768]{2,1,0:T(8,128)(2,1)S(1)} %get-tuple-element.481.refs_0_), channel_id=1, source_target_pairs={{0,8},{4,12},{8,0},{12,4},{16,24},{20,28},{24,16},{28,20},{1,9},{5... | collective-permute-start | bytes 958472 | tf_op jit(solution)/shard_map/ppermute | solution.py:645
  199.3 8.5 %collective-permute-start.56 = (bf16[1,104,768]{2,1,0:T(8,128)(2,1)S(1)}, bf16[1,104,768]{2,1,0:T(8,128)(2,1)S(1)}, u32[]{:S(2)}, u32[]{:S(2)}) collective-permute-start(bf16[1,104,768]{2,1,0:T(8,128)(2,1)S(1)} %get-tuple-element.482.refs_2_), channel_id=1, source_target_pairs={{0,16},{4,20},{8,24},{12,28},{16,0},{20,4},{24,8},{28,12},{1,17},{... | collective-permute-start | bytes 479240 | tf_op jit(solution)/shard_map/ppermute | solution.py:645
  210.3 15.9 %collective-permute-start.61 = (bf16[2,104,768]{2,1,0:T(8,128)(2,1)S(1)}, bf16[2,104,768]{2,1,0:T(8,128)(2,1)S(1)}, u32[]{:S(2)}, u32[]{:S(2)}) collective-permute-start(bf16[2,104,768]{2,1,0:T(8,128)(2,1)S(1)} %get-tuple-element.491.refs_0_), channel_id=1, source_target_pairs={{0,8},{4,12},{8,0},{12,4},{16,24},{20,28},{24,16},{28,20},{1,9},{5... | collective-permute-start | bytes 958472 | tf_op jit(solution)/shard_map/ppermute | solution.py:645
  213.8 13.5 %collective-permute-start.60 = (bf16[2,224,768]{2,1,0:T(8,128)(2,1)S(1)}, bf16[2,224,768]{2,1,0:T(8,128)(2,1)S(1)}, u32[]{:S(2)}, u32[]{:S(2)}) collective-permute-start(bf16[2,224,768]{2,1,0:T(8,128)(2,1)S(1)} %get-tuple-element.490.refs_2_), channel_id=1, source_target_pairs={{0,1},{1,0},{2,3},{3,2},{4,5},{5,4},{6,7},{7,6},{8,9},{9,8},{10,11... | collective-permute-start | bytes 2064392 | tf_op jit(solution)/shard_map/ppermute | solution.py:645
  213.8 25.1 %collective-permute-start.58 = (bf16[2,224,768]{2,1,0:T(8,128)(2,1)S(1)}, bf16[2,224,768]{2,1,0:T(8,128)(2,1)S(1)}, u32[]{:S(2)}, u32[]{:S(2)}) collective-permute-start(bf16[2,224,768]{2,1,0:T(8,128)(2,1)S(1)} %get-tuple-element.485.refs_2_), channel_id=1, source_target_pairs={{0,1},{1,0},{2,3},{3,2},{4,5},{5,4},{6,7},{7,6},{8,9},{9,8},{10,11... | collective-permute-start | bytes 2064392 | tf_op jit(solution)/shard_map/ppermute | solution.py:645
  214.3 22.8 %collective-permute-start.59 = (bf16[4,104,768]{2,1,0:T(8,128)(2,1)S(1)}, bf16[4,104,768]{2,1,0:T(8,128)(2,1)S(1)}, u32[]{:S(2)}, u32[]{:S(2)}) collective-permute-start(bf16[4,104,768]{2,1,0:T(8,128)(2,1)S(1)} %get-tuple-element.487.refs_0_), channel_id=1, source_target_pairs={{0,4},{4,0},{8,12},{12,8},{16,20},{20,16},{24,28},{28,24},{1,5},{5... | collective-permute-start | bytes 1916936 | tf_op jit(solution)/shard_map/ppermute | solution.py:645
  226.3 22.2 %collective-permute-start.63 = (bf16[4,104,768]{2,1,0:T(8,128)(2,1)S(1)}, bf16[4,104,768]{2,1,0:T(8,128)(2,1)S(1)}, u32[]{:S(2)}, u32[]{:S(2)}) collective-permute-start(bf16[4,104,768]{2,1,0:T(8,128)(2,1)S(1)} %get-tuple-element.501.refs_0_), channel_id=1, source_target_pairs={{0,4},{4,0},{8,12},{12,8},{16,20},{20,16},{24,28},{28,24},{1,5},{5... | collective-permute-start | bytes 1916936 | tf_op jit(solution)/shard_map/ppermute | solution.py:645
  (21 other events, 51.5 us)

commit v5 on v4

--- a/solution.py
+++ b/solution.py
@@ -834,11 +834,11 @@
     back_out, back_sum = [], []
     for i in span:
         _, _, q2, o2, lse2 = cross_out[i][:5]
-        feed_sum[i].meet()
         if i == 0:
             outs, scratch = pack_outs(width + units + 64)
             operands = [out[k] for k in (1, 3, 2, 4, 5) for out in feed_out]
             feed_dp = DpSum(order, n_dp, X_FIRST, *order.run(bind(feed_weights, items), 2, operands, outs, scratch))
+        feed_sum[i].meet()
         out = order.run(
             bind(cross_backward, i, chunk), 9,
             (lengths, tasks, feed_out[i][0], *feed_sum[i].pieces, out_grad, gain_feed, output_cross, wq2, *cross_kv[i], q2, o2, lse2),

time: 255 us -> 252 us (0.988)
  waiting for transfers between devices: 101 us -> 98.2 us
    ppermute x64, waiting for transfers between devices: 101 us -> 98.2 us  [swap(): return lax.ppermute(value, axis, [(k, k ^ bit) for k in range(size)])]
  transfers between devices with their start and end apart: 64 -> 64, of which waited for: 33 -> 32; matrix products, arithmetic and copies ran while one was open for 0% -> 0% of each run, Pallas kernels for 31% -> 32%
where the time goes in v5:
time: 252 us; the launch traced here: 247 us
  waiting for transfers between devices  98.2 us (39%)
  Pallas kernels  88 us (35%)
  starting transfers between devices  58.4 us (23%)
    ppermute x64, waiting for transfers between devices, swap(): return lax.ppermute(value, axis, [(k, k ^ bit) for k in range(size)])  98.2 us
    pallas_call x50, Pallas kernels, run(): pl.pallas_call(whole_body, name=inner.__name__, grid=(1,), in_specs=in_sp...  88 us
    ppermute x64, starting transfers between devices, swap(): return lax.ppermute(value, axis, [(k, k ^ bit) for k in range(size)])  58.4 us
  transfers between devices with their start and end apart: 64, of which 32 were waited for; matrix products, arithmetic and copies ran while one was open for 0% of the time, Pallas kernels for 32%

profile of v5, /device:TPU:0, one launch (start us, length us, event | category | flops | bytes accessed | tf_op | source)
XLA Modules:
  0.0 247.2 jit_solution(17146559589423817017)
XLA Ops:
  1.3 5.5 %first_forward.1 = (bf16[192,448]{1,0:T(8,128)(2,1)S(1)}, bf16[3,80,448]{2,1,0:T(8,128)(2,1)S(1)}, bf16[3,80,448]{2,1,0:T(8,128)(2,1)S(1)}, bf16[192,448]{1,0:T(...) custom-call(s32[2]{0:T(128)S(1)} %copy-done, ...), custom_call_target="tpu_custom_call" | custom-call | flops 4 | bytes 1 | tf_op jit(solution)/shard_map/first_forward/pallas_call | solution.py:618
  7.4 3.5 %self_forward.1 = (bf16[192,448]{1,0:T(8,128)(2,1)S(1)}, bf16[3,80,448]{2,1,0:T(8,128)(2,1)S(1)}, bf16[3,80,448]{2,1,0:T(8,128)(2,1)S(1)}, bf16[192,448]{1,0:T(8...) custom-call(s32[2]{0:T(128)S(1)} %copy-done, ...), custom_call_target="tpu_custom_call" | custom-call | flops 4 | bytes 1 | tf_op jit(solution)/shard_map/self_forward/pallas_call | solution.py:618
  11.0 3.0 %collective-permute-start.2 = (bf16[224,768]{1,0:T(8,128)(2,1)S(1)}, bf16[224,768]{1,0:T(8,128)(2,1)S(1)}, u32[]{:S(2)}, u32[]{:S(2)}) collective-permute-start(bf16[224,768]{1,0:T(8,128)(2,1)S(1)} %get-tuple-element.291.refs_0_), channel_id=1, source_target_pairs={{0,2},{1,3},{2,0},{3,1},{4,6},{5,7},{6,4},{7,5},{8,10},{9,11},{10,... | collective-permute-start | bytes 1032200 | tf_op jit(solution)/shard_map/ppermute | solution.py:645
  15.2 2.1 cross_keys.2
  17.4 2.1 cross_keys.3
  19.4 2.9 %collective-permute-done.2.refs_1_ = bf16[224,768]{1,0:T(8,128)(2,1)S(1)} collective-permute-done((bf16[224,768]{1,0:T(8,128)(2,1)S(1)}, bf16[224,768]{1,0:T(8,128)(2,1)S(1)}, u32[]{:S(2)}, u32[]{:S(2)}) %collective-permute-start.2) | collective-permute-done | bytes 344096 | tf_op jit(solution)/shard_map/ppermute | solution.py:645
  22.5 1.8 collective-permute-start.9
  24.3 5.2 %cross_forward.2 = (f32[448,768]{1,0:T(8,128)S(1)}, bf16[448,768]{1,0:T(8,128)(2,1)S(1)}, bf16[192,448]{1,0:T(8,128)(2,1)S(1)}, bf16[192,448]{1,0:T(8,128)(2,1)S...) custom-call(bf16[2,448,768]{2,1,0:T(8,128)(2,1)S(1)} %get-tuple-elem, ...), custom_call_target="tpu_custom_call" | custom-call | flops 6 | bytes 1 | tf_op jit(solution)/shard_map/cross_forward/pallas_call | solution.py:618
  33.2 1.8 collective-permute-start.8
  35.0 4.9 %cross_forward.3 = (f32[448,768]{1,0:T(8,128)S(1)}, bf16[448,768]{1,0:T(8,128)(2,1)S(1)}, bf16[192,448]{1,0:T(8,128)(2,1)S(1)}, bf16[192,448]{1,0:T(8,128)(2,1)S...) custom-call(bf16[2,448,768]{2,1,0:T(8,128)(2,1)S(1)} %get-tuple-elem, ...), custom_call_target="tpu_custom_call" | custom-call | flops 6 | bytes 1 | tf_op jit(solution)/shard_map/cross_forward/pallas_call | solution.py:618
  41.7 2.0 collective-permute-done.8.refs_1_
  43.8 1.8 collective-permute-start.14
  45.6 3.4 %feed.2 = (f32[448,768]{1,0:T(8,128)S(1)}, bf16[448,768]{1,0:T(8,128)(2,1)S(1)}, bf16[448,768]{1,0:T(8,128)(2,1)S(1)}, bf16[448,768]{1,0:T(8,128)(2,1)S(1)}, bf1...) custom-call(s32[2]{0:T(128)S(1)} %copy-done.1, ...), custom_call_target="tpu_custom_call" | custom-call | flops 4 | bytes 1 | tf_op jit(solution)/shard_map/feed/pallas_call | solution.py:618
  50.8 3.5 %collective-permute-done.14.refs_1_ = bf16[224,768]{1,0:T(8,128)(2,1)S(1)} collective-permute-done((bf16[224,768]{1,0:T(8,128)(2,1)S(1)}, bf16[224,768]{1,0:T(8,128)(2,1)S(1)}, u32[]{:S(2)}, u32[]{:S(2)}) %collective-permute-start.14) | collective-permute-done | bytes 344096 | tf_op jit(solution)/shard_map/ppermute | solution.py:645
  54.4 1.8 collective-permute-start.21
  56.3 3.8 %feed.3 = (f32[448,768]{1,0:T(8,128)S(1)}, bf16[448,768]{1,0:T(8,128)(2,1)S(1)}, bf16[448,768]{1,0:T(8,128)(2,1)S(1)}, bf16[448,768]{1,0:T(8,128)(2,1)S(1)}, bf1...) custom-call(s32[2]{0:T(128)S(1)} %copy-done.1, ...), custom_call_target="tpu_custom_call" | custom-call | flops 4 | bytes 1 | tf_op jit(solution)/shard_map/feed/pallas_call | solution.py:618
  61.8 3.1 %feed_weights.1 = (bf16[4,200,768]{2,1,0:T(8,128)(2,1)S(1)}, bf16[4,200,768]{2,1,0:T(8,128)(2,1)S(1)}, f32[8,128]{1,0:T(8,128)S(1)}) custom-call(bf16[448,768]{1,0:T(8,128)(2,1)S(1)} %get-tuple-element.349.refs_0_, bf16[448,768]{1,0:T(8,128)(2,1)S(1)} %get-tuple-element.350.refs_1_, bf16[448,768]{1,0:T(8,128)(2,1)S(1)} %get-tuple-element.351.refs_2_, ...), custom_call_target="tpu_custom_call" | custom-call | flops 2 | bytes 1 | tf_op jit(solution)/shard_map/feed_weights/pallas_call | solution.py:618
  68.5 8.6 %cross_backward.2 = (f32[448,768]{1,0:T(8,128)S(1)}, bf16[448,768]{1,0:T(8,128)(2,1)S(1)}, bf16[192,448]{1,0:T(8,128)(2,1)S(1)}, bf16[192,1536]{1,0:T(8,128)(2,1...) custom-call(s32[2]{0:T(128)S(1)} %copy-done.1, ...), custom_call_target="tpu_custom_call" | custom-call | flops 9 | bytes 1 | tf_op jit(solution)/shard_map/cross_backward/pallas_call | solution.py:618
  80.7 8.4 %cross_backward.3 = (f32[448,768]{1,0:T(8,128)S(1)}, bf16[448,768]{1,0:T(8,128)(2,1)S(1)}, bf16[192,448]{1,0:T(8,128)(2,1)S(1)}, bf16[192,1536]{1,0:T(8,128)(2,1...) custom-call(s32[2]{0:T(128)S(1)} %copy-done.1, ...), custom_call_target="tpu_custom_call" | custom-call | flops 9 | bytes 1 | tf_op jit(solution)/shard_map/cross_backward/pallas_call | solution.py:618
  91.9 2.7 %collective-permute-done.20.refs_1_ = bf16[4,200,768]{2,1,0:T(8,128)(2,1)S(1)} collective-permute-done((bf16[4,200,768]{2,1,0:T(8,128)(2,1)S(1)}, bf16[4,200,768]{2,1,0:T(8,128)(2,1)S(1)}, u32[]{:S(2)}, u32[]{:S(2)}) %collective-permute-start.20) | collective-permute-done | bytes 1228832 | tf_op jit(solution)/shard_map/ppermute | solution.py:645
  94.9 5.1 %self_backward.2 = (f32[448,768]{1,0:T(8,128)S(1)}, bf16[448,768]{1,0:T(8,128)(2,1)S(1)}, bf16[576,448]{1,0:T(8,128)(2,1)S(1)}, f32[8,768]{1,0:T(8,128)S(1)}, bf...) custom-call(f32[448,768]{1,0:T(8,128)S(1)} %get-tuple-element.312.refs_2_.refs_0_, ...), custom_call_target="tpu_custom_call" | custom-call | flops 5 | bytes 1 | tf_op jit(solution)/shard_map/self_backward/pallas_call | solution.py:618
  100.0 2.9 %cross_weights.1 = (bf16[4,104,768]{2,1,0:T(8,128)(2,1)S(1)}, bf16[4,104,768]{2,1,0:T(8,128)(2,1)S(1)}, f32[8,128]{1,0:T(8,128)S(1)}) custom-call(bf16[2,1500,768]{2,1,0:T(8,128)(2,1)S(1)} %copy.58.refs_1_.refs_0_, bf16[192,448]{1,0:T(8,128)(2,1)S(1)} %get-tuple-element.393.refs_1_, bf16[192,448]{1,0:T(8,128)(2,1)S(1)} %get-tuple-element.394.refs_2_, ...), custom_call_target="tpu_custom_call" | custom-call | flops 3 | bytes 1 | tf_op jit(solution)/shard_map/cross_weights/pallas_call | solution.py:618
  108.0 4.7 %self_backward.3 = (f32[448,768]{1,0:T(8,128)S(1)}, bf16[448,768]{1,0:T(8,128)(2,1)S(1)}, bf16[576,448]{1,0:T(8,128)(2,1)S(1)}, f32[8,768]{1,0:T(8,128)S(1)}, bf...) custom-call(f32[448,768]{1,0:T(8,128)S(1)} %get-tuple-element.339.refs_2_.refs_0_, ...), custom_call_target="tpu_custom_call" | custom-call | flops 5 | bytes 1 | tf_op jit(solution)/shard_map/self_backward/pallas_call | solution.py:618
  116.4 1.9 memory_grad.3
  118.3 2.2 self_weights.1
  123.8 2.7 %collective-permute-start.38 = (bf16[1,200,768]{2,1,0:T(8,128)(2,1)S(1)}, bf16[1,200,768]{2,1,0:T(8,128)(2,1)S(1)}, u32[]{:S(2)}, u32[]{:S(2)}) collective-permute-start(bf16[1,200,768]{2,1,0:T(8,128)(2,1)S(1)} %get-tuple-element.441), channel_id=1, source_target_pairs={{0,16},{4,20},{8,24},{12,28},{16,0},{20,4},{24,8},{28,12},{1,17},{... | collective-permute-start | bytes 921608 | tf_op jit(solution)/shard_map/ppermute | solution.py:645
  126.5 11.0 %collective-permute-done.38.refs_1_ = bf16[1,200,768]{2,1,0:T(8,128)(2,1)S(1)} collective-permute-done((bf16[1,200,768]{2,1,0:T(8,128)(2,1)S(1)}, bf16[1,200,768]{2,1,0:T(8,128)(2,1)S(1)}, u32[]{:S(2)}, u32[]{:S(2)}) %collective-permute-start.38) | collective-permute-done | bytes 307232 | tf_op jit(solution)/shard_map/ppermute | solution.py:645
  137.6 2.1 collective-permute-done.39.refs_3_
  142.1 2.6 %collective-permute-start.44 = (bf16[1,104,768]{2,1,0:T(8,128)(2,1)S(1)}, bf16[1,104,768]{2,1,0:T(8,128)(2,1)S(1)}, u32[]{:S(2)}, u32[]{:S(2)}) collective-permute-start(bf16[1,104,768]{2,1,0:T(8,128)(2,1)S(1)} %get-tuple-element.455), channel_id=1, source_target_pairs={{0,16},{4,20},{8,24},{12,28},{16,0},{20,4},{24,8},{28,12},{1,17},{... | collective-permute-start | bytes 479240 | tf_op jit(solution)/shard_map/ppermute | solution.py:645
  145.2 2.4 collective-permute-start.45
  147.7 4.5 %collective-permute-done.44.refs_3_ = bf16[1,104,768]{2,1,0:T(8,128)(2,1)S(1)} collective-permute-done((bf16[1,104,768]{2,1,0:T(8,128)(2,1)S(1)}, bf16[1,104,768]{2,1,0:T(8,128)(2,1)S(1)}, u32[]{:S(2)}, u32[]{:S(2)}) %collective-permute-start.44) | collective-permute-done | bytes 159776 | tf_op jit(solution)/shard_map/ppermute | solution.py:645
  152.1 14.2 %collective-permute-done.43.refs_1_ = bf16[1,200,768]{2,1,0:T(8,128)(2,1)S(1)} collective-permute-done((bf16[1,200,768]{2,1,0:T(8,128)(2,1)S(1)}, bf16[1,200,768]{2,1,0:T(8,128)(2,1)S(1)}, u32[]{:S(2)}, u32[]{:S(2)}) %collective-permute-start.43) | collective-permute-done | bytes 307232 | tf_op jit(solution)/shard_map/ppermute | solution.py:645
  167.3 2.4 collective-permute-start.48
  171.9 3.4 %collective-permute-start.50 = (bf16[1,104,768]{2,1,0:T(8,128)(2,1)S(1)}, bf16[1,104,768]{2,1,0:T(8,128)(2,1)S(1)}, u32[]{:S(2)}, u32[]{:S(2)}) collective-permute-start(bf16[1,104,768]{2,1,0:T(8,128)(2,1)S(1)} %get-tuple-element.468), channel_id=1, source_target_pairs={{0,16},{4,20},{8,24},{12,28},{16,0},{20,4},{24,8},{28,12},{1,17},{... | collective-permute-start | bytes 479240 | tf_op jit(solution)/shard_map/ppermute | solution.py:645
  176.6 10.8 %collective-permute-done.50.refs_5_ = bf16[1,104,768]{2,1,0:T(8,128)(2,1)S(1)} collective-permute-done((bf16[1,104,768]{2,1,0:T(8,128)(2,1)S(1)}, bf16[1,104,768]{2,1,0:T(8,128)(2,1)S(1)}, u32[]{:S(2)}, u32[]{:S(2)}) %collective-permute-start.50) | collective-permute-done | bytes 159776 | tf_op jit(solution)/shard_map/ppermute | solution.py:645
  187.4 1.7 collective-permute-done.49.refs_3_
  192.7 3.4 %collective-permute-start.55 = (bf16[2,104,768]{2,1,0:T(8,128)(2,1)S(1)}, bf16[2,104,768]{2,1,0:T(8,128)(2,1)S(1)}, u32[]{:S(2)}, u32[]{:S(2)}) collective-permute-start(bf16[2,104,768]{2,1,0:T(8,128)(2,1)S(1)} %get-tuple-element.481.refs_0_), channel_id=1, source_target_pairs={{0,8},{4,12},{8,0},{12,4},{16,24},{20,28},{24,16},{28,20},{1,9},{5... | collective-permute-start | bytes 958472 | tf_op jit(solution)/shard_map/ppermute | solution.py:645
  196.1 1.7 collective-permute-start.56
  197.8 6.7 %collective-permute-done.56.refs_3_ = bf16[1,104,768]{2,1,0:T(8,128)(2,1)S(1)} collective-permute-done((bf16[1,104,768]{2,1,0:T(8,128)(2,1)S(1)}, bf16[1,104,768]{2,1,0:T(8,128)(2,1)S(1)}, u32[]{:S(2)}, u32[]{:S(2)}) %collective-permute-start.56) | collective-permute-done | bytes 159776 | tf_op jit(solution)/shard_map/ppermute | solution.py:645
  207.2 3.4 %collective-permute-start.61 = (bf16[2,104,768]{2,1,0:T(8,128)(2,1)S(1)}, bf16[2,104,768]{2,1,0:T(8,128)(2,1)S(1)}, u32[]{:S(2)}, u32[]{:S(2)}) collective-permute-start(bf16[2,104,768]{2,1,0:T(8,128)(2,1)S(1)} %get-tuple-element.491.refs_0_), channel_id=1, source_target_pairs={{0,8},{4,12},{8,0},{12,4},{16,24},{20,28},{24,16},{28,20},{1,9},{5... | collective-permute-start | bytes 958472 | tf_op jit(solution)/shard_map/ppermute | solution.py:645
  212.2 8.0 %collective-permute-done.62.refs_1_ = bf16[4,200,768]{2,1,0:T(8,128)(2,1)S(1)} collective-permute-done((bf16[4,200,768]{2,1,0:T(8,128)(2,1)S(1)}, bf16[4,200,768]{2,1,0:T(8,128)(2,1)S(1)}, u32[]{:S(2)}, u32[]{:S(2)}) %collective-permute-start.62) | collective-permute-done | bytes 1228832 | tf_op jit(solution)/shard_map/ppermute | solution.py:645
  220.2 2.8 %unpack.3 = (f32[768,768]{1,0:T(8,128)}, f32[768,768]{1,0:T(8,128)}, f32[768]{0:T(1024)}, f32[768]{0:T(1024)}, f32[8,128]{1,0:T(8,128)S(1)}) custom-call(bf16[4,200,768]{2,1,0:T(8,128)(2,1)S(1)} %get-tuple-element.492.refs_0_, bf16[4,200,768]{2,1,0:T(8,128)(2,1)S(1)} %collective-permute-done.62.refs_1_, f32[8,128]{1,0:T(8,128)S(1)} %get-tuple-element.493.refs_2_), custom_call_target="tpu_custom_call" | custom-call | flops 3 | bytes 1 | tf_op jit(solution)/shard_map/unpack/pallas_call | solution.py:618
  224.1 3.7 %finish_grad.1 = (f32[2,448,768]{2,1,0:T(8,128)}, f32[8,128]{1,0:T(8,128)S(1)}) custom-call(f32[448,768]{1,0:T(8,128)S(1)} %get-tuple-element.488.refs_0_, f32[448,768]{1,0:T(8,128)S(1)} %get-tuple-element.489.refs_1_, bf16[2,224,768]{2,1,0:T(8,128)(2,1)S(1)} %get-tuple-element.490.refs_2_, bf16[2,224,768]{2,1,0:T(8,128)(2,1)S(1)} %collective-permute-done.60.refs_3_, ...), custom_call_target="tpu_custom_call" | custom-call | flops 4 | bytes 1 | tf_op jit(solution)/shard_map/finish_grad/pallas_call | solution.py:618
  227.8 6.1 %collective-permute-done.59.refs_1_ = bf16[4,104,768]{2,1,0:T(8,128)(2,1)S(1)} collective-permute-done((bf16[4,104,768]{2,1,0:T(8,128)(2,1)S(1)}, bf16[4,104,768]{2,1,0:T(8,128)(2,1)S(1)}, u32[]{:S(2)}, u32[]{:S(2)}) %collective-permute-start.59) | collective-permute-done | bytes 639008 | tf_op jit(solution)/shard_map/ppermute | solution.py:645
  233.9 1.8 unpack.4
  235.7 1.9 finish_out.1
  237.6 7.6 %collective-permute-done.63.refs_1_ = bf16[4,104,768]{2,1,0:T(8,128)(2,1)S(1)} collective-permute-done((bf16[4,104,768]{2,1,0:T(8,128)(2,1)S(1)}, bf16[4,104,768]{2,1,0:T(8,128)(2,1)S(1)}, u32[]{:S(2)}, u32[]{:S(2)}) %collective-permute-start.63) | collective-permute-done | bytes 639008 | tf_op jit(solution)/shard_map/ppermute | solution.py:645
  245.2 1.8 unpack.5
  (141 shorter events, 50.4 us)
Async XLA Ops:
  6.8 4.1 %collective-permute-start = (bf16[112,768]{1,0:T(8,128)(2,1)S(1)}, bf16[112,768]{1,0:T(8,128)(2,1)S(1)}, u32[]{:S(2)}, u32[]{:S(2)}) collective-permute-start(bf16[112,768]{1,0:T(8,128)(2,1)S(1)} %get-tuple-element.279), channel_id=1, source_target_pairs={{0,1},{1,0},{2,3},{3,2},{4,5},{5,4},{6,7},{7,6},{8,9},{9,8},{10,11... | collective-permute-start | bytes 516104 | tf_op jit(solution)/shard_map/ppermute | solution.py:645
  7.4 3.6 %collective-permute-start.1 = (bf16[112,768]{1,0:T(8,128)(2,1)S(1)}, bf16[112,768]{1,0:T(8,128)(2,1)S(1)}, u32[]{:S(2)}, u32[]{:S(2)}) collective-permute-start(bf16[112,768]{1,0:T(8,128)(2,1)S(1)} %get-tuple-element.280), channel_id=1, source_target_pairs={{0,1},{1,0},{2,3},{3,2},{4,5},{5,4},{6,7},{7,6},{8,9},{9,8},{10,11... | collective-permute-start | bytes 516104 | tf_op jit(solution)/shard_map/ppermute | solution.py:645
  11.0 11.3 %collective-permute-start.2 = (bf16[224,768]{1,0:T(8,128)(2,1)S(1)}, bf16[224,768]{1,0:T(8,128)(2,1)S(1)}, u32[]{:S(2)}, u32[]{:S(2)}) collective-permute-start(bf16[224,768]{1,0:T(8,128)(2,1)S(1)} %get-tuple-element.291.refs_0_), channel_id=1, source_target_pairs={{0,2},{1,3},{2,0},{3,1},{4,6},{5,7},{6,4},{7,5},{8,10},{9,11},{10,... | collective-permute-start | bytes 1032200 | tf_op jit(solution)/shard_map/ppermute | solution.py:645
  14.0 3.2 %collective-permute-start.3 = (bf16[112,768]{1,0:T(8,128)(2,1)S(1)}, bf16[112,768]{1,0:T(8,128)(2,1)S(1)}, u32[]{:S(2)}, u32[]{:S(2)}) collective-permute-start(bf16[112,768]{1,0:T(8,128)(2,1)S(1)} %get-tuple-element.296), channel_id=1, source_target_pairs={{0,1},{1,0},{2,3},{3,2},{4,5},{5,4},{6,7},{7,6},{8,9},{9,8},{10,11... | collective-permute-start | bytes 516104 | tf_op jit(solution)/shard_map/ppermute | solution.py:645
  14.1 3.2 %collective-permute-start.4 = (bf16[112,768]{1,0:T(8,128)(2,1)S(1)}, bf16[112,768]{1,0:T(8,128)(2,1)S(1)}, u32[]{:S(2)}, u32[]{:S(2)}) collective-permute-start(bf16[112,768]{1,0:T(8,128)(2,1)S(1)} %get-tuple-element.297), channel_id=1, source_target_pairs={{0,1},{1,0},{2,3},{3,2},{4,5},{5,4},{6,7},{7,6},{8,9},{9,8},{10,11... | collective-permute-start | bytes 516104 | tf_op jit(solution)/shard_map/ppermute | solution.py:645
  22.4 1.9 collective-permute-start.5
  22.5 10.5 %collective-permute-start.9 = (bf16[224,768]{1,0:T(8,128)(2,1)S(1)}, bf16[224,768]{1,0:T(8,128)(2,1)S(1)}, u32[]{:S(2)}, u32[]{:S(2)}) collective-permute-start(bf16[224,768]{1,0:T(8,128)(2,1)S(1)} %get-tuple-element.318.refs_0_), channel_id=1, source_target_pairs={{0,2},{1,3},{2,0},{3,1},{4,6},{5,7},{6,4},{7,5},{8,10},{9,11},{10,... | collective-permute-start | bytes 1032200 | tf_op jit(solution)/shard_map/ppermute | solution.py:645
  33.1 1.9 collective-permute-start.10
  33.2 10.5 %collective-permute-start.8 = (bf16[224,768]{1,0:T(8,128)(2,1)S(1)}, bf16[224,768]{1,0:T(8,128)(2,1)S(1)}, u32[]{:S(2)}, u32[]{:S(2)}) collective-permute-start(bf16[224,768]{1,0:T(8,128)(2,1)S(1)} %get-tuple-element.317.refs_0_), channel_id=1, source_target_pairs={{0,2},{1,3},{2,0},{3,1},{4,6},{5,7},{6,4},{7,5},{8,10},{9,11},{10,... | collective-permute-start | bytes 1032200 | tf_op jit(solution)/shard_map/ppermute | solution.py:645
  43.8 10.5 %collective-permute-start.14 = (bf16[224,768]{1,0:T(8,128)(2,1)S(1)}, bf16[224,768]{1,0:T(8,128)(2,1)S(1)}, u32[]{:S(2)}, u32[]{:S(2)}) collective-permute-start(bf16[224,768]{1,0:T(8,128)(2,1)S(1)} %get-tuple-element.340.refs_0_), channel_id=1, source_target_pairs={{0,2},{1,3},{2,0},{3,1},{4,6},{5,7},{6,4},{7,5},{8,10},{9,11},{10,... | collective-permute-start | bytes 1032200 | tf_op jit(solution)/shard_map/ppermute | solution.py:645
  54.4 10.6 %collective-permute-start.21 = (bf16[224,768]{1,0:T(8,128)(2,1)S(1)}, bf16[224,768]{1,0:T(8,128)(2,1)S(1)}, u32[]{:S(2)}, u32[]{:S(2)}) collective-permute-start(bf16[224,768]{1,0:T(8,128)(2,1)S(1)} %get-tuple-element.366.refs_0_), channel_id=1, source_target_pairs={{0,2},{1,3},{2,0},{3,1},{4,6},{5,7},{6,4},{7,5},{8,10},{9,11},{10,... | collective-permute-start | bytes 1032200 | tf_op jit(solution)/shard_map/ppermute | solution.py:645
  65.1 3.4 %collective-permute-start.22 = (bf16[224,768]{1,0:T(8,128)(2,1)S(1)}, bf16[224,768]{1,0:T(8,128)(2,1)S(1)}, u32[]{:S(2)}, u32[]{:S(2)}) collective-permute-start(bf16[224,768]{1,0:T(8,128)(2,1)S(1)} %get-tuple-element.368.refs_3_), channel_id=1, source_target_pairs={{0,1},{1,0},{2,3},{3,2},{4,5},{5,4},{6,7},{7,6},{8,9},{9,8},{10,11... | collective-permute-start | bytes 1032200 | tf_op jit(solution)/shard_map/ppermute | solution.py:645
  65.4 29.2 %collective-permute-start.20 = (bf16[4,200,768]{2,1,0:T(8,128)(2,1)S(1)}, bf16[4,200,768]{2,1,0:T(8,128)(2,1)S(1)}, u32[]{:S(2)}, u32[]{:S(2)}) collective-permute-start(bf16[4,200,768]{2,1,0:T(8,128)(2,1)S(1)} %get-tuple-element.365), channel_id=1, source_target_pairs={{0,4},{4,0},{8,12},{12,8},{16,20},{20,16},{24,28},{28,24},{1,5},{5... | collective-permute-start | bytes 3686408 | tf_op jit(solution)/shard_map/ppermute | solution.py:645
  67.0 11.9 %collective-permute-start.26 = (bf16[224,768]{1,0:T(8,128)(2,1)S(1)}, bf16[224,768]{1,0:T(8,128)(2,1)S(1)}, u32[]{:S(2)}, u32[]{:S(2)}) collective-permute-start(bf16[224,768]{1,0:T(8,128)(2,1)S(1)} %get-tuple-element.378.refs_0_), channel_id=1, source_target_pairs={{0,2},{1,3},{2,0},{3,1},{4,6},{5,7},{6,4},{7,5},{8,10},{9,11},{10,... | collective-permute-start | bytes 1032200 | tf_op jit(solution)/shard_map/ppermute | solution.py:645
  79.3 11.6 %collective-permute-start.25 = (bf16[224,768]{1,0:T(8,128)(2,1)S(1)}, bf16[224,768]{1,0:T(8,128)(2,1)S(1)}, u32[]{:S(2)}, u32[]{:S(2)}) collective-permute-start(bf16[224,768]{1,0:T(8,128)(2,1)S(1)} %get-tuple-element.377.refs_0_), channel_id=1, source_target_pairs={{0,2},{1,3},{2,0},{3,1},{4,6},{5,7},{6,4},{7,5},{8,10},{9,11},{10,... | collective-permute-start | bytes 1032200 | tf_op jit(solution)/shard_map/ppermute | solution.py:645
  90.9 4.0 %collective-permute-start.31 = (bf16[224,768]{1,0:T(8,128)(2,1)S(1)}, bf16[224,768]{1,0:T(8,128)(2,1)S(1)}, u32[]{:S(2)}, u32[]{:S(2)}) collective-permute-start(bf16[224,768]{1,0:T(8,128)(2,1)S(1)} %get-tuple-element.405.refs_1_), channel_id=1, source_target_pairs={{0,1},{1,0},{2,3},{3,2},{4,5},{5,4},{6,7},{7,6},{8,9},{9,8},{10,11... | collective-permute-start | bytes 1032200 | tf_op jit(solution)/shard_map/ppermute | solution.py:645
  91.3 15.0 %collective-permute-start.33 = (bf16[224,768]{1,0:T(8,128)(2,1)S(1)}, bf16[224,768]{1,0:T(8,128)(2,1)S(1)}, u32[]{:S(2)}, u32[]{:S(2)}) collective-permute-start(bf16[224,768]{1,0:T(8,128)(2,1)S(1)} %get-tuple-element.417.refs_0_), channel_id=1, source_target_pairs={{0,2},{1,3},{2,0},{3,1},{4,6},{5,7},{6,4},{7,5},{8,10},{9,11},{10,... | collective-permute-start | bytes 1032200 | tf_op jit(solution)/shard_map/ppermute | solution.py:645
  102.9 19.2 %collective-permute-start.32 = (bf16[4,104,768]{2,1,0:T(8,128)(2,1)S(1)}, bf16[4,104,768]{2,1,0:T(8,128)(2,1)S(1)}, u32[]{:S(2)}, u32[]{:S(2)}) collective-permute-start(bf16[4,104,768]{2,1,0:T(8,128)(2,1)S(1)} %get-tuple-element.415), channel_id=1, source_target_pairs={{0,4},{4,0},{8,12},{12,8},{16,20},{20,16},{24,28},{28,24},{1,5},{5... | collective-permute-start | bytes 1916936 | tf_op jit(solution)/shard_map/ppermute | solution.py:645
  104.6 17.5 %collective-permute-start.30 = (bf16[2,200,768]{2,1,0:T(8,128)(2,1)S(1)}, bf16[2,200,768]{2,1,0:T(8,128)(2,1)S(1)}, u32[]{:S(2)}, u32[]{:S(2)}) collective-permute-start(bf16[2,200,768]{2,1,0:T(8,128)(2,1)S(1)} %get-tuple-element.392), channel_id=1, source_target_pairs={{0,8},{4,12},{8,0},{12,4},{16,24},{20,28},{24,16},{28,20},{1,9},{5... | collective-permute-start | bytes 1843208 | tf_op jit(solution)/shard_map/ppermute | solution.py:645
  112.7 5.5 %collective-permute-start.37 = (f32[8,768]{1,0:T(8,128)S(1)}, f32[8,768]{1,0:T(8,128)S(1)}, u32[]{:S(2)}, u32[]{:S(2)}) collective-permute-start(f32[8,768]{1,0:T(8,128)S(1)} %get-tuple-element.433.refs_9_), channel_id=1, source_target_pairs={{0,3},{1,2},{2,1},{3,0},{4,7},{5,6},{6,5},{7,4},{8,11},{9,10},{10,... | collective-permute-start | bytes 73736 | tf_op jit(solution)/shard_map/ppermute | solution.py:645
  114.1 4.2 %collective-permute-start.36 = (f32[8,768]{1,0:T(8,128)S(1)}, f32[8,768]{1,0:T(8,128)S(1)}, u32[]{:S(2)}, u32[]{:S(2)}) collective-permute-start(f32[8,768]{1,0:T(8,128)S(1)} %get-tuple-element.433.refs_9_), channel_id=1, source_target_pairs={{0,2},{1,3},{2,0},{3,1},{4,6},{5,7},{6,4},{7,5},{8,10},{9,11},{10,... | collective-permute-start | bytes 73736 | tf_op jit(solution)/shard_map/ppermute | solution.py:645
  114.6 3.7 %collective-permute-start.35 = (f32[8,768]{1,0:T(8,128)S(1)}, f32[8,768]{1,0:T(8,128)S(1)}, u32[]{:S(2)}, u32[]{:S(2)}) collective-permute-start(f32[8,768]{1,0:T(8,128)S(1)} %get-tuple-element.433.refs_9_), channel_id=1, source_target_pairs={{0,1},{1,0},{2,3},{3,2},{4,5},{5,4},{6,7},{7,6},{8,9},{9,8},{10,11... | collective-permute-start | bytes 73736 | tf_op jit(solution)/shard_map/ppermute | solution.py:645
  122.4 17.3 %collective-permute-start.41 = (bf16[2,192,1500]{2,1,0:T(8,128)(2,1)S(1)}, bf16[2,192,1500]{2,1,0:T(8,128)(2,1)S(1)}, u32[]{:S(2)}, u32[]{:S(2)}) collective-permute-start(bf16[2,192,1500]{2,1,0:T(8,128)(2,1)S(1)} %get-tuple-element.450), channel_id=1, source_target_pairs={{0,1},{1,0},{2,3},{3,2},{4,5},{5,4},{6,7},{7,6},{8,9},{9,8},{10,11... | collective-permute-start | bytes 3456008 | tf_op jit(solution)/shard_map/ppermute | solution.py:645
  122.9 16.8 %collective-permute-start.42 = (bf16[2,192,1500]{2,1,0:T(8,128)(2,1)S(1)}, bf16[2,192,1500]{2,1,0:T(8,128)(2,1)S(1)}, u32[]{:S(2)}, u32[]{:S(2)}) collective-permute-start(bf16[2,192,1500]{2,1,0:T(8,128)(2,1)S(1)} %get-tuple-element.452), channel_id=1, source_target_pairs={{0,1},{1,0},{2,3},{3,2},{4,5},{5,4},{6,7},{7,6},{8,9},{9,8},{10,11... | collective-permute-start | bytes 3456008 | tf_op jit(solution)/shard_map/ppermute | solution.py:645
  123.0 16.7 %collective-permute-start.40 = (bf16[4,104,768]{2,1,0:T(8,128)(2,1)S(1)}, bf16[4,104,768]{2,1,0:T(8,128)(2,1)S(1)}, u32[]{:S(2)}, u32[]{:S(2)}) collective-permute-start(bf16[4,104,768]{2,1,0:T(8,128)(2,1)S(1)} %get-tuple-element.445), channel_id=1, source_target_pairs={{0,4},{4,0},{8,12},{12,8},{16,20},{20,16},{24,28},{28,24},{1,5},{5... | collective-permute-start | bytes 1916936 | tf_op jit(solution)/shard_map/ppermute | solution.py:645
  123.5 16.2 %collective-permute-start.39 = (bf16[2,104,768]{2,1,0:T(8,128)(2,1)S(1)}, bf16[2,104,768]{2,1,0:T(8,128)(2,1)S(1)}, u32[]{:S(2)}, u32[]{:S(2)}) collective-permute-start(bf16[2,104,768]{2,1,0:T(8,128)(2,1)S(1)} %get-tuple-element.443), channel_id=1, source_target_pairs={{0,8},{4,12},{8,0},{12,4},{16,24},{20,28},{24,16},{28,20},{1,9},{5... | collective-permute-start | bytes 958472 | tf_op jit(solution)/shard_map/ppermute | solution.py:645
  123.8 13.8 %collective-permute-start.38 = (bf16[1,200,768]{2,1,0:T(8,128)(2,1)S(1)}, bf16[1,200,768]{2,1,0:T(8,128)(2,1)S(1)}, u32[]{:S(2)}, u32[]{:S(2)}) collective-permute-start(bf16[1,200,768]{2,1,0:T(8,128)(2,1)S(1)} %get-tuple-element.441), channel_id=1, source_target_pairs={{0,16},{4,20},{8,24},{12,28},{16,0},{20,4},{24,8},{28,12},{1,17},{... | collective-permute-start | bytes 921608 | tf_op jit(solution)/shard_map/ppermute | solution.py:645
  140.5 29.1 %collective-permute-start.52 = (bf16[2,192,1500]{2,1,0:T(8,128)(2,1)S(1)}, bf16[2,192,1500]{2,1,0:T(8,128)(2,1)S(1)}, u32[]{:S(2)}, u32[]{:S(2)}) collective-permute-start(bf16[2,192,1500]{2,1,0:T(8,128)(2,1)S(1)} %get-tuple-element.473), channel_id=1, source_target_pairs={{0,2},{1,3},{2,0},{3,1},{4,6},{5,7},{6,4},{7,5},{8,10},{9,11},{10,... | collective-permute-start | bytes 3456008 | tf_op jit(solution)/shard_map/ppermute | solution.py:645
  142.1 10.0 %collective-permute-start.44 = (bf16[1,104,768]{2,1,0:T(8,128)(2,1)S(1)}, bf16[1,104,768]{2,1,0:T(8,128)(2,1)S(1)}, u32[]{:S(2)}, u32[]{:S(2)}) collective-permute-start(bf16[1,104,768]{2,1,0:T(8,128)(2,1)S(1)} %get-tuple-element.455), channel_id=1, source_target_pairs={{0,16},{4,20},{8,24},{12,28},{16,0},{20,4},{24,8},{28,12},{1,17},{... | collective-permute-start | bytes 479240 | tf_op jit(solution)/shard_map/ppermute | solution.py:645
  144.7 21.6 %collective-permute-start.46 = (bf16[224,768]{1,0:T(8,128)(2,1)S(1)}, bf16[224,768]{1,0:T(8,128)(2,1)S(1)}, u32[]{:S(2)}, u32[]{:S(2)}) collective-permute-start(bf16[224,768]{1,0:T(8,128)(2,1)S(1)} %get-tuple-element.461), channel_id=1, source_target_pairs={{0,1},{1,0},{2,3},{3,2},{4,5},{5,4},{6,7},{7,6},{8,9},{9,8},{10,11... | collective-permute-start | bytes 1032200 | tf_op jit(solution)/shard_map/ppermute | solution.py:645
  144.7 21.6 %collective-permute-start.47 = (bf16[224,768]{1,0:T(8,128)(2,1)S(1)}, bf16[224,768]{1,0:T(8,128)(2,1)S(1)}, u32[]{:S(2)}, u32[]{:S(2)}) collective-permute-start(bf16[224,768]{1,0:T(8,128)(2,1)S(1)} %get-tuple-element.464), channel_id=1, source_target_pairs={{0,1},{1,0},{2,3},{3,2},{4,5},{5,4},{6,7},{7,6},{8,9},{9,8},{10,11... | collective-permute-start | bytes 1032200 | tf_op jit(solution)/shard_map/ppermute | solution.py:645
  145.2 21.1 %collective-permute-start.45 = (bf16[2,104,768]{2,1,0:T(8,128)(2,1)S(1)}, bf16[2,104,768]{2,1,0:T(8,128)(2,1)S(1)}, u32[]{:S(2)}, u32[]{:S(2)}) collective-permute-start(bf16[2,104,768]{2,1,0:T(8,128)(2,1)S(1)} %get-tuple-element.457), channel_id=1, source_target_pairs={{0,8},{4,12},{8,0},{12,4},{16,24},{20,28},{24,16},{28,20},{1,9},{5... | collective-permute-start | bytes 958472 | tf_op jit(solution)/shard_map/ppermute | solution.py:645
  152.1 14.2 %collective-permute-start.43 = (bf16[1,200,768]{2,1,0:T(8,128)(2,1)S(1)}, bf16[1,200,768]{2,1,0:T(8,128)(2,1)S(1)}, u32[]{:S(2)}, u32[]{:S(2)}) collective-permute-start(bf16[1,200,768]{2,1,0:T(8,128)(2,1)S(1)} %get-tuple-element.453.refs_0_), channel_id=1, source_target_pairs={{0,16},{4,20},{8,24},{12,28},{16,0},{20,4},{24,8},{28,12},{1,17},{... | collective-permute-start | bytes 921608 | tf_op jit(solution)/shard_map/ppermute | solution.py:645
  166.7 23.2 %collective-permute-start.51 = (bf16[2,224,768]{2,1,0:T(8,128)(2,1)S(1)}, bf16[2,224,768]{2,1,0:T(8,128)(2,1)S(1)}, u32[]{:S(2)}, u32[]{:S(2)}) collective-permute-start(bf16[2,224,768]{2,1,0:T(8,128)(2,1)S(1)} %get-tuple-element.469.refs_6_), channel_id=1, source_target_pairs={{0,2},{1,3},{2,0},{3,1},{4,6},{5,7},{6,4},{7,5},{8,10},{9,11},{10,... | collective-permute-start | bytes 2064392 | tf_op jit(solution)/shard_map/ppermute | solution.py:645
  167.3 22.6 %collective-permute-start.48 = (bf16[2,200,768]{2,1,0:T(8,128)(2,1)S(1)}, bf16[2,200,768]{2,1,0:T(8,128)(2,1)S(1)}, u32[]{:S(2)}, u32[]{:S(2)}) collective-permute-start(bf16[2,200,768]{2,1,0:T(8,128)(2,1)S(1)} %get-tuple-element.465.refs_0_), channel_id=1, source_target_pairs={{0,8},{4,12},{8,0},{12,4},{16,24},{20,28},{24,16},{28,20},{1,9},{5... | collective-permute-start | bytes 1843208 | tf_op jit(solution)/shard_map/ppermute | solution.py:645
  171.4 3.9 %collective-permute-start.53 = (bf16[224,768]{1,0:T(8,128)(2,1)S(1)}, bf16[224,768]{1,0:T(8,128)(2,1)S(1)}, u32[]{:S(2)}, u32[]{:S(2)}) collective-permute-start(bf16[224,768]{1,0:T(8,128)(2,1)S(1)} %get-tuple-element.476), channel_id=1, source_target_pairs={{0,1},{1,0},{2,3},{3,2},{4,5},{5,4},{6,7},{7,6},{8,9},{9,8},{10,11... | collective-permute-start | bytes 1032200 | tf_op jit(solution)/shard_map/ppermute | solution.py:645
  171.4 5.0 %collective-permute-start.54 = (bf16[224,768]{1,0:T(8,128)(2,1)S(1)}, bf16[224,768]{1,0:T(8,128)(2,1)S(1)}, u32[]{:S(2)}, u32[]{:S(2)}) collective-permute-start(bf16[224,768]{1,0:T(8,128)(2,1)S(1)} %get-tuple-element.479), channel_id=1, source_target_pairs={{0,1},{1,0},{2,3},{3,2},{4,5},{5,4},{6,7},{7,6},{8,9},{9,8},{10,11... | collective-permute-start | bytes 1032200 | tf_op jit(solution)/shard_map/ppermute | solution.py:645
  171.9 15.5 %collective-permute-start.50 = (bf16[1,104,768]{2,1,0:T(8,128)(2,1)S(1)}, bf16[1,104,768]{2,1,0:T(8,128)(2,1)S(1)}, u32[]{:S(2)}, u32[]{:S(2)}) collective-permute-start(bf16[1,104,768]{2,1,0:T(8,128)(2,1)S(1)} %get-tuple-element.468), channel_id=1, source_target_pairs={{0,16},{4,20},{8,24},{12,28},{16,0},{20,4},{24,8},{28,12},{1,17},{... | collective-permute-start | bytes 479240 | tf_op jit(solution)/shard_map/ppermute | solution.py:645
  175.3 13.8 %collective-permute-start.49 = (bf16[1,104,768]{2,1,0:T(8,128)(2,1)S(1)}, bf16[1,104,768]{2,1,0:T(8,128)(2,1)S(1)}, u32[]{:S(2)}, u32[]{:S(2)}) collective-permute-start(bf16[1,104,768]{2,1,0:T(8,128)(2,1)S(1)} %get-tuple-element.466.refs_2_), channel_id=1, source_target_pairs={{0,16},{4,20},{8,24},{12,28},{16,0},{20,4},{24,8},{28,12},{1,17},{... | collective-permute-start | bytes 479240 | tf_op jit(solution)/shard_map/ppermute | solution.py:645
  190.2 30.0 %collective-permute-start.62 = (bf16[4,200,768]{2,1,0:T(8,128)(2,1)S(1)}, bf16[4,200,768]{2,1,0:T(8,128)(2,1)S(1)}, u32[]{:S(2)}, u32[]{:S(2)}) collective-permute-start(bf16[4,200,768]{2,1,0:T(8,128)(2,1)S(1)} %get-tuple-element.492.refs_0_), channel_id=1, source_target_pairs={{0,4},{4,0},{8,12},{12,8},{16,20},{20,16},{24,28},{28,24},{1,5},{5... | collective-permute-start | bytes 3686408 | tf_op jit(solution)/shard_map/ppermute | solution.py:645
  191.2 15.7 %collective-permute-start.57 = (bf16[2,224,768]{2,1,0:T(8,128)(2,1)S(1)}, bf16[2,224,768]{2,1,0:T(8,128)(2,1)S(1)}, u32[]{:S(2)}, u32[]{:S(2)}) collective-permute-start(bf16[2,224,768]{2,1,0:T(8,128)(2,1)S(1)} %get-tuple-element.483.refs_4_), channel_id=1, source_target_pairs={{0,2},{1,3},{2,0},{3,1},{4,6},{5,7},{6,4},{7,5},{8,10},{9,11},{10,... | collective-permute-start | bytes 2064392 | tf_op jit(solution)/shard_map/ppermute | solution.py:645
  192.7 12.6 %collective-permute-start.55 = (bf16[2,104,768]{2,1,0:T(8,128)(2,1)S(1)}, bf16[2,104,768]{2,1,0:T(8,128)(2,1)S(1)}, u32[]{:S(2)}, u32[]{:S(2)}) collective-permute-start(bf16[2,104,768]{2,1,0:T(8,128)(2,1)S(1)} %get-tuple-element.481.refs_0_), channel_id=1, source_target_pairs={{0,8},{4,12},{8,0},{12,4},{16,24},{20,28},{24,16},{28,20},{1,9},{5... | collective-permute-start | bytes 958472 | tf_op jit(solution)/shard_map/ppermute | solution.py:645
  196.1 8.5 %collective-permute-start.56 = (bf16[1,104,768]{2,1,0:T(8,128)(2,1)S(1)}, bf16[1,104,768]{2,1,0:T(8,128)(2,1)S(1)}, u32[]{:S(2)}, u32[]{:S(2)}) collective-permute-start(bf16[1,104,768]{2,1,0:T(8,128)(2,1)S(1)} %get-tuple-element.482.refs_2_), channel_id=1, source_target_pairs={{0,16},{4,20},{8,24},{12,28},{16,0},{20,4},{24,8},{28,12},{1,17},{... | collective-permute-start | bytes 479240 | tf_op jit(solution)/shard_map/ppermute | solution.py:645
  207.2 15.8 %collective-permute-start.61 = (bf16[2,104,768]{2,1,0:T(8,128)(2,1)S(1)}, bf16[2,104,768]{2,1,0:T(8,128)(2,1)S(1)}, u32[]{:S(2)}, u32[]{:S(2)}) collective-permute-start(bf16[2,104,768]{2,1,0:T(8,128)(2,1)S(1)} %get-tuple-element.491.refs_0_), channel_id=1, source_target_pairs={{0,8},{4,12},{8,0},{12,4},{16,24},{20,28},{24,16},{28,20},{1,9},{5... | collective-permute-start | bytes 958472 | tf_op jit(solution)/shard_map/ppermute | solution.py:645
  210.6 13.5 %collective-permute-start.60 = (bf16[2,224,768]{2,1,0:T(8,128)(2,1)S(1)}, bf16[2,224,768]{2,1,0:T(8,128)(2,1)S(1)}, u32[]{:S(2)}, u32[]{:S(2)}) collective-permute-start(bf16[2,224,768]{2,1,0:T(8,128)(2,1)S(1)} %get-tuple-element.490.refs_2_), channel_id=1, source_target_pairs={{0,1},{1,0},{2,3},{3,2},{4,5},{5,4},{6,7},{7,6},{8,9},{9,8},{10,11... | collective-permute-start | bytes 2064392 | tf_op jit(solution)/shard_map/ppermute | solution.py:645
  210.6 25.1 %collective-permute-start.58 = (bf16[2,224,768]{2,1,0:T(8,128)(2,1)S(1)}, bf16[2,224,768]{2,1,0:T(8,128)(2,1)S(1)}, u32[]{:S(2)}, u32[]{:S(2)}) collective-permute-start(bf16[2,224,768]{2,1,0:T(8,128)(2,1)S(1)} %get-tuple-element.485.refs_2_), channel_id=1, source_target_pairs={{0,1},{1,0},{2,3},{3,2},{4,5},{5,4},{6,7},{7,6},{8,9},{9,8},{10,11... | collective-permute-start | bytes 2064392 | tf_op jit(solution)/shard_map/ppermute | solution.py:645
  211.1 22.8 %collective-permute-start.59 = (bf16[4,104,768]{2,1,0:T(8,128)(2,1)S(1)}, bf16[4,104,768]{2,1,0:T(8,128)(2,1)S(1)}, u32[]{:S(2)}, u32[]{:S(2)}) collective-permute-start(bf16[4,104,768]{2,1,0:T(8,128)(2,1)S(1)} %get-tuple-element.487.refs_0_), channel_id=1, source_target_pairs={{0,4},{4,0},{8,12},{12,8},{16,20},{20,16},{24,28},{28,24},{1,5},{5... | collective-permute-start | bytes 1916936 | tf_op jit(solution)/shard_map/ppermute | solution.py:645
  223.1 22.2 %collective-permute-start.63 = (bf16[4,104,768]{2,1,0:T(8,128)(2,1)S(1)}, bf16[4,104,768]{2,1,0:T(8,128)(2,1)S(1)}, u32[]{:S(2)}, u32[]{:S(2)}) collective-permute-start(bf16[4,104,768]{2,1,0:T(8,128)(2,1)S(1)} %get-tuple-element.501.refs_0_), channel_id=1, source_target_pairs={{0,4},{4,0},{8,12},{12,8},{16,20},{20,16},{24,28},{28,24},{1,5},{5... | collective-permute-start | bytes 1916936 | tf_op jit(solution)/shard_map/ppermute | solution.py:645
  (21 other events, 51.5 us)
